TPU v7x, 32 devices: a whole 2x2x4 slice. The times are simulated.
32 devices in a mesh: expert: 8 (over y, x, core), shard: 4 (over z).
Axes of the slice: x: 2, y: 2, z: 4, core: 2. Of those that a mesh axis runs over, the one named last changes fastest.
Arguments:
- embedded: bfloat16 [8192, 1024], P(('expert', 'shard')), may hold values from -1 to 1
- document_numbers: int32 [32, 256], P(('expert', 'shard')), may hold values from 0 to 4, as said below
- expert_ids: int32 [8192, 8], P(('expert', 'shard')), may hold values from 0 to 31, all different within a row; in each aligned block of 256 rows (0 to 255, 256 to 511, ...) at most 128 rows name the same one
- attn_gain: float32 [1024], P(('expert', 'shard')), may hold values from 0.5 to 1.5
- ffn_gain: float32 [1024], P(('expert', 'shard')), may hold values from 0.5 to 1.5
- w_query: float32 [1024, 1024], P(('expert', 'shard')), may hold values from -0.75 to 0.75
- key_projection: float32 [1024, 512], P(('expert', 'shard')), may hold values from -0.75 to 0.75
- value_projection: float32 [1024, 512], P(('expert', 'shard')), may hold values from -0.1875 to 0.1875
- w_out: float32 [1024, 1024], P(('expert', 'shard')), may hold values from -3 to 3
- w_router: float32 [1024, 32], P(('expert', 'shard')), may hold values from -0.09375 to 0.09375
- expert_in: bfloat16 [32, 1024, 1024], P('expert', 'shard'), may hold values from -0.1875 to 0.1875
- expert_out: bfloat16 [32, 512, 1024], P('expert', 'shard'), may hold values from -4 to 4
- cotangent: bfloat16 [8192, 1024], P(('expert', 'shard')), may hold values from -6 to 6
Outputs:
- output: bfloat16 [8192, 1024], P(('expert', 'shard'))
- grad_embedded: bfloat16 [8192, 1024], P(('expert', 'shard'))
- grad_attn_gain: float32 [1024], P(('expert', 'shard'))
- grad_ffn_gain: float32 [1024], P(('expert', 'shard'))
- grad_w_query: float32 [1024, 1024], P(('expert', 'shard'))
- grad_w_key: float32 [1024, 512], P(('expert', 'shard'))
- grad_w_value: float32 [1024, 512], P(('expert', 'shard'))
- grad_w_out: float32 [1024, 1024], P(('expert', 'shard'))
- grad_w_router: float32 [1024, 32], P(('expert', 'shard'))
- grad_expert_in: float32 [32, 1024, 1024], P('expert', 'shard')
- grad_expert_out: float32 [32, 512, 1024], P('expert', 'shard')
Inputs may be any that keep to these rules, and one draw needn't show every extreme that they name: `expert_ids`: each row names 8 different experts. In the rows of one device (aligned blocks of 256 rows) no expert is named by more than 128 rows, and in every draw some expert is named by exactly 128 rows of some device. `document_numbers`: within each sequence the document numbers start at 0 and rise by one at each new document; every document has 32 to 128 positions, and each sequence has one document of exactly 128 positions.
All inputs are finite; a program needn't handle non-finite values.
Results may differ from a plain program's by a relative error of at most 0.015.
The roundings to bfloat16 on the way count: a program that leaves them out, or rounds other values in their place, can miss the bound.
Values may be sent and summed in bfloat16 or wider, within the bound.
No kernel may reach another device: no remote copies, remote signals or barrier semaphores. Data moves between devices by JAX's collectives and lax.ppermute only.
A program may use at most 192 MiB of HBM per device.

v0:
```python
import jax
import jax.numpy as jnp
from jax import lax
from jax.sharding import PartitionSpec as P

MODEL_WIDTH = 1024
QUERY_HEADS = 16
KEY_VALUE_HEADS = 8
HEAD_SIZE = 64
FF = 512
EXPERTS = 32
TOPK = 8
CAP = 128


embed_scale = 12.0
attn_scale = 0.015625
resid_scale = 0.22
norm_eps = 1e-06
rope_base = 10000.0


def rope_tables(segments):
    sequence_length = segments.shape[0]
    key_index = jnp.arange(sequence_length, dtype=jnp.int32)
    change = jnp.concatenate([jnp.ones((1,), jnp.bool_), segments[1:] != segments[:-1]])
    begins = lax.cummax(jnp.where(change, key_index, 0), axis=0)
    places = (key_index - begins).astype(jnp.float32)
    freqs = rope_base ** (-2.0 * jnp.arange(HEAD_SIZE // 2, dtype=jnp.float32) / HEAD_SIZE)
    angles = places[:, None] * freqs[None, :]
    return (jnp.cos(angles), jnp.sin(angles))


def apply_rotation(value_heads, cosine_table, sine_table):
    halfway = value_heads.shape[-1] // 2
    first_half = value_heads[..., :halfway]
    second_half = value_heads[..., halfway:]
    cos_part = cosine_table[:, None, :]
    sin_part = sine_table[:, None, :]
    return jnp.concatenate(
        [
            first_half * cos_part - second_half * sin_part,
            second_half * cos_part + first_half * sin_part,
        ],
        axis=-1,
    )


def reverse_rotation(grads, cosine_table, sine_table):
    halfway = grads.shape[-1] // 2
    first_half = grads[..., :halfway]
    second_half = grads[..., halfway:]
    cos_part = cosine_table[:, None, :]
    sin_part = sine_table[:, None, :]
    return jnp.concatenate(
        [
            first_half * cos_part + second_half * sin_part,
            second_half * cos_part - first_half * sin_part,
        ],
        axis=-1,
    )


def norm_forward(value_heads):
    inverse = lax.rsqrt(jnp.mean(value_heads * value_heads, axis=1, keepdims=True) + norm_eps)
    return (value_heads * inverse, inverse)


def norm_backward(upstream, unit_values, inverse, gain):
    scaled = upstream * gain
    grad_values = inverse * (
        scaled - unit_values * jnp.mean(scaled * unit_values, axis=1, keepdims=True)
    )
    return (grad_values, jnp.sum(upstream * unit_values, axis=0))


def slot_tables(expert_ids):
    flat_ids = expert_ids.reshape(-1)
    count_all = flat_ids.shape[0]
    matches = (flat_ids[:, None] == jnp.arange(EXPERTS, dtype=jnp.int32)[None, :]).astype(jnp.int32)
    before = jnp.cumsum(matches, axis=0) - 1
    ranking = jnp.sum(before * matches, axis=1)
    target = flat_ids * CAP + ranking
    source = (
        jnp.zeros((EXPERTS * CAP,), jnp.int32)
        .at[target]
        .set(jnp.arange(count_all, dtype=jnp.int32))
    )
    filled = (
        jnp.zeros((EXPERTS * CAP,), jnp.int32).at[target].set(jnp.ones((count_all,), jnp.int32))
    )
    return (target, source, filled)


def silu_parts(gate_up):
    gate_part = gate_up[..., :FF]
    up_part = gate_up[..., FF:]
    sigmoid_gate = jax.nn.sigmoid(gate_part)
    hidden = (gate_part * sigmoid_gate * up_part).astype(jnp.bfloat16)
    return (gate_part, up_part, sigmoid_gate, hidden)


def per_device(
    embedded,
    document_numbers,
    expert_ids,
    attn_gain,
    ffn_gain,
    w_query,
    key_projection,
    value_projection,
    w_out,
    w_router,
    expert_in,
    expert_out,
    cotangent,
):
    mixer = (
        lax.all_gather(attn_gain.astype(jnp.bfloat16), ("expert", "shard"), axis=0, tiled=True),
        lax.all_gather(ffn_gain.astype(jnp.bfloat16), ("expert", "shard"), axis=0, tiled=True),
        lax.all_gather(w_query.astype(jnp.bfloat16), ("expert", "shard"), axis=0, tiled=True),
        lax.all_gather(
            key_projection.astype(jnp.bfloat16), ("expert", "shard"), axis=0, tiled=True
        ),
        lax.all_gather(
            value_projection.astype(jnp.bfloat16), ("expert", "shard"), axis=0, tiled=True
        ),
        lax.all_gather(w_out.astype(jnp.bfloat16), ("expert", "shard"), axis=0, tiled=True),
        lax.all_gather(w_router.astype(jnp.bfloat16), ("expert", "shard"), axis=0, tiled=True),
    )
    gain_attn, gain_ffn, query_w, key_w, value_w, out_w, router_w = mixer
    full_in, full_out = (
        lax.all_gather(expert_in, "shard", axis=1, tiled=True),
        lax.all_gather(expert_out, "shard", axis=1, tiled=True),
    )
    sequence_length = embedded.shape[0]
    query_groups = QUERY_HEADS // KEY_VALUE_HEADS
    owners = lax.axis_size("expert")
    local_count = EXPERTS // owners
    received = owners * CAP
    resid = embed_scale * embedded.astype(jnp.float32)
    unit_attn, inverse_attn = norm_forward(resid)
    normed = (unit_attn * gain_attn.astype(jnp.float32)).astype(jnp.bfloat16)
    unrotated_query = jnp.dot(normed, query_w, preferred_element_type=jnp.float32)
    unrotated_key = jnp.dot(normed, key_w, preferred_element_type=jnp.float32)
    projected_value = jnp.dot(normed, value_w, preferred_element_type=jnp.float32)
    segments = document_numbers[0]
    cosine_table, sine_table = rope_tables(segments)
    query_heads = (
        apply_rotation(
            unrotated_query.reshape(sequence_length, QUERY_HEADS, HEAD_SIZE),
            cosine_table,
            sine_table,
        )
        .astype(jnp.bfloat16)
        .reshape(sequence_length, KEY_VALUE_HEADS, query_groups, HEAD_SIZE)
    )
    key_heads = apply_rotation(
        unrotated_key.reshape(sequence_length, KEY_VALUE_HEADS, HEAD_SIZE), cosine_table, sine_table
    ).astype(jnp.bfloat16)
    value_heads = projected_value.astype(jnp.bfloat16).reshape(
        sequence_length, KEY_VALUE_HEADS, HEAD_SIZE
    )
    block_rows = min(512, sequence_length)
    starts = jnp.arange(sequence_length // block_rows, dtype=jnp.int32) * block_rows
    key_index = jnp.arange(sequence_length, dtype=jnp.int32)

    def block_scores(first_row):
        row_index = first_row + jnp.arange(block_rows, dtype=jnp.int32)
        raw_scores = (
            jnp.einsum("qhgd,khd->hgqk", query_heads, key_heads, preferred_element_type=jnp.float32)
            * attn_scale
        )
        allowed = (key_index[None, :] <= row_index[:, None]) & (
            segments[None, :] == segments[:, None]
        )
        return (jnp.where(allowed, raw_scores, -1e30), query_heads)

    def attend_block(first_row):
        scores, query_rows = block_scores(first_row)
        row_max = jnp.max(scores, axis=-1, keepdims=True)
        exps = jnp.exp(scores - row_max)
        totals = jnp.sum(exps, axis=-1, keepdims=True)
        weights = (exps / totals).astype(jnp.bfloat16)
        mixed_rows = jnp.einsum(
            "hgqk,khd->qhgd", weights, value_heads, preferred_element_type=jnp.float32
        )
        return (mixed_rows.astype(jnp.bfloat16), (row_max + jnp.log(totals))[..., 0])

    mixed_blocks, log_totals = lax.map(attend_block, starts)
    mixed_heads_output = mixed_blocks.reshape(sequence_length, QUERY_HEADS * HEAD_SIZE)
    middle = resid + resid_scale * jnp.dot(
        mixed_heads_output, out_w, preferred_element_type=jnp.float32
    )
    unit_ffn, inverse_ffn = norm_forward(middle)
    normed2 = (unit_ffn * gain_ffn.astype(jnp.float32)).astype(jnp.bfloat16)
    logits = jnp.dot(normed2, router_w, preferred_element_type=jnp.float32)
    pick_table = expert_ids[:, :, None] == jnp.arange(EXPERTS, dtype=jnp.int32)[None, None, :]
    chosen = jnp.sum(jnp.where(pick_table, logits[:, None, :], 0.0), axis=2)
    exps_chosen = jnp.exp(chosen - jnp.max(chosen, axis=1, keepdims=True))
    gates = exps_chosen / jnp.sum(exps_chosen, axis=1, keepdims=True)
    target, source, filled = slot_tables(expert_ids)
    live_slots = filled[:, None] == 1
    zero_bf = jnp.zeros((), jnp.bfloat16)
    send_rows = jnp.where(live_slots, normed2[source // TOPK], zero_bf).reshape(
        owners, local_count, CAP, MODEL_WIDTH
    )
    arrived = lax.all_to_all(send_rows, "expert", split_axis=0, concat_axis=2, tiled=True).reshape(
        local_count, received, MODEL_WIDTH
    )
    gate_up = jnp.einsum("erd,edf->erf", arrived, full_in, preferred_element_type=jnp.float32)
    gate_part, up_part, sigmoid_gate, hidden = silu_parts(gate_up)
    produced = jnp.einsum(
        "erf,efd->erd", hidden, full_out, preferred_element_type=jnp.float32
    ).astype(jnp.bfloat16)
    returned = lax.all_to_all(
        produced.reshape(1, local_count, received, MODEL_WIDTH),
        "expert",
        split_axis=2,
        concat_axis=0,
        tiled=True,
    ).reshape(EXPERTS * CAP, MODEL_WIDTH)
    slot_values = returned[target].reshape(sequence_length, TOPK, MODEL_WIDTH)
    moe = jnp.einsum("tk,tkd->td", gates, slot_values.astype(jnp.float32))
    output = (middle + resid_scale * moe).astype(jnp.bfloat16)
    grad_output = cotangent.astype(jnp.float32)
    grad_mix = resid_scale * grad_output
    gate_grads = jnp.einsum("tkd,td->tk", slot_values.astype(jnp.float32), grad_mix)
    slot_grads = (
        (gates[:, :, None] * grad_mix[:, None, :])
        .astype(jnp.bfloat16)
        .reshape(sequence_length * TOPK, MODEL_WIDTH)
    )
    grad_send = jnp.where(live_slots, slot_grads[source], zero_bf).reshape(
        owners, local_count, CAP, MODEL_WIDTH
    )
    grad_arrived = lax.all_to_all(
        grad_send, "expert", split_axis=0, concat_axis=2, tiled=True
    ).reshape(local_count, received, MODEL_WIDTH)
    owner_rows = lax.all_to_all(
        send_rows, "expert", split_axis=0, concat_axis=2, tiled=True
    ).reshape(local_count, received, MODEL_WIDTH)
    owner_gate_up = jnp.einsum(
        "erd,edf->erf", owner_rows, full_in, preferred_element_type=jnp.float32
    )
    owner_gate, owner_up, owner_sigmoid, owner_hidden = silu_parts(owner_gate_up)
    hidden_grad = jnp.einsum(
        "erd,efd->erf", grad_arrived, full_out, preferred_element_type=jnp.float32
    )
    gate_grad_part = (
        hidden_grad * owner_up * owner_sigmoid * (1.0 + owner_gate * (1.0 - owner_sigmoid))
    )
    up_grad_part = hidden_grad * owner_gate * owner_sigmoid
    gate_up_grad = jnp.concatenate([gate_grad_part, up_grad_part], axis=-1).astype(jnp.bfloat16)
    grad_full_out = jnp.einsum(
        "erf,erd->efd", owner_hidden, grad_arrived, preferred_element_type=jnp.float32
    )
    grad_full_in = jnp.einsum(
        "erd,erf->edf", owner_rows, gate_up_grad, preferred_element_type=jnp.float32
    )
    row_grads = jnp.einsum(
        "erf,edf->erd", gate_up_grad, full_in, preferred_element_type=jnp.float32
    ).astype(jnp.bfloat16)
    grad_returned = lax.all_to_all(
        row_grads.reshape(1, local_count, received, MODEL_WIDTH),
        "expert",
        split_axis=2,
        concat_axis=0,
        tiled=True,
    ).reshape(EXPERTS * CAP, MODEL_WIDTH)
    grad_expert_in, grad_expert_out = (
        lax.psum_scatter(
            grad_full_in.astype(jnp.bfloat16), "shard", scatter_dimension=1, tiled=True
        ).astype(jnp.float32),
        lax.psum_scatter(
            grad_full_out.astype(jnp.bfloat16), "shard", scatter_dimension=1, tiled=True
        ).astype(jnp.float32),
    )
    mixer_back = (
        lax.all_gather(attn_gain.astype(jnp.bfloat16), ("expert", "shard"), axis=0, tiled=True),
        lax.all_gather(ffn_gain.astype(jnp.bfloat16), ("expert", "shard"), axis=0, tiled=True),
        lax.all_gather(w_query.astype(jnp.bfloat16), ("expert", "shard"), axis=0, tiled=True),
        lax.all_gather(
            key_projection.astype(jnp.bfloat16), ("expert", "shard"), axis=0, tiled=True
        ),
        lax.all_gather(
            value_projection.astype(jnp.bfloat16), ("expert", "shard"), axis=0, tiled=True
        ),
        lax.all_gather(w_out.astype(jnp.bfloat16), ("expert", "shard"), axis=0, tiled=True),
        lax.all_gather(w_router.astype(jnp.bfloat16), ("expert", "shard"), axis=0, tiled=True),
    )
    back_gain_attn, back_gain_ffn, back_query, back_key, back_value, back_out, back_router = (
        mixer_back
    )
    chosen_grad = gates * (gate_grads - jnp.sum(gates * gate_grads, axis=1, keepdims=True))
    logit_grads = jnp.sum(jnp.where(pick_table, chosen_grad[:, :, None], 0.0), axis=1).astype(
        jnp.bfloat16
    )
    grad_router_full = jnp.einsum(
        "td,te->de", normed2, logit_grads, preferred_element_type=jnp.float32
    )
    normed2_grad = jnp.sum(
        grad_returned[target].reshape(sequence_length, TOPK, MODEL_WIDTH), axis=1, dtype=jnp.float32
    )
    normed2_grad = normed2_grad + jnp.einsum(
        "te,de->td", logit_grads, back_router, preferred_element_type=jnp.float32
    )
    middle_norm_grad, grad_gain_ffn = norm_backward(
        normed2_grad, unit_ffn, inverse_ffn, back_gain_ffn.astype(jnp.float32)
    )
    middle_grad = grad_output + middle_norm_grad
    attn_grad = (resid_scale * middle_grad).astype(jnp.bfloat16)
    grad_out_full = jnp.einsum(
        "tf,td->fd", mixed_heads_output, attn_grad, preferred_element_type=jnp.float32
    )
    mixed_output_gradient = jnp.einsum(
        "td,fd->tf", attn_grad, back_out, preferred_element_type=jnp.float32
    ).astype(jnp.bfloat16)
    mixed_gradient_by_head = mixed_output_gradient.reshape(
        sequence_length, KEY_VALUE_HEADS, query_groups, HEAD_SIZE
    )

    def attend_back(carries, packed):
        key_acc, value_acc = carries
        first_row, log_rows = packed
        scores, query_rows = block_scores(first_row)
        probs = jnp.exp(scores - log_rows[..., None])
        prob_grads = jnp.einsum(
            "qhgd,khd->hgqk",
            mixed_gradient_by_head,
            value_heads,
            preferred_element_type=jnp.float32,
        )
        score_grads = (
            probs * (prob_grads - jnp.sum(probs * prob_grads, axis=-1, keepdims=True))
        ).astype(jnp.bfloat16)
        query_grads = (
            jnp.einsum("hgqk,khd->qhgd", score_grads, key_heads, preferred_element_type=jnp.float32)
            * attn_scale
        )
        key_acc = (
            key_acc
            + jnp.einsum(
                "hgqk,qhgd->khd", score_grads, query_rows, preferred_element_type=jnp.float32
            )
            * attn_scale
        )
        value_acc = value_acc + jnp.einsum(
            "hgqk,qhgd->khd",
            probs.astype(jnp.bfloat16),
            mixed_gradient_by_head,
            preferred_element_type=jnp.float32,
        )
        return ((key_acc, value_acc), query_grads)

    empty_head_rows = jnp.zeros((sequence_length, KEY_VALUE_HEADS, HEAD_SIZE), jnp.float32)
    (summed_key_gradient, summed_value_gradient), query_grad_blocks = lax.scan(
        attend_back, (empty_head_rows, empty_head_rows), (starts, log_totals)
    )
    query_raw_grad = (
        reverse_rotation(
            query_grad_blocks.reshape(sequence_length, QUERY_HEADS, HEAD_SIZE),
            cosine_table,
            sine_table,
        )
        .astype(jnp.bfloat16)
        .reshape(sequence_length, QUERY_HEADS * HEAD_SIZE)
    )
    key_raw_grad = (
        reverse_rotation(summed_key_gradient, cosine_table, sine_table)
        .astype(jnp.bfloat16)
        .reshape(sequence_length, KEY_VALUE_HEADS * HEAD_SIZE)
    )
    projected_value_gradient = summed_value_gradient.astype(jnp.bfloat16).reshape(
        sequence_length, KEY_VALUE_HEADS * HEAD_SIZE
    )
    grad_query_full = jnp.einsum(
        "td,tf->df", normed, query_raw_grad, preferred_element_type=jnp.float32
    )
    grad_key_full = jnp.einsum(
        "td,tf->df", normed, key_raw_grad, preferred_element_type=jnp.float32
    )
    grad_value_full = jnp.einsum(
        "td,tf->df", normed, projected_value_gradient, preferred_element_type=jnp.float32
    )
    normed_grad = jnp.einsum(
        "tf,df->td", query_raw_grad, back_query, preferred_element_type=jnp.float32
    )
    normed_grad = normed_grad + jnp.einsum(
        "tf,df->td", key_raw_grad, back_key, preferred_element_type=jnp.float32
    )
    normed_grad = normed_grad + jnp.einsum(
        "tf,df->td", projected_value_gradient, back_value, preferred_element_type=jnp.float32
    )
    resid_norm_grad, grad_gain_attn = norm_backward(
        normed_grad, unit_attn, inverse_attn, back_gain_attn.astype(jnp.float32)
    )
    resid_grad = middle_grad + resid_norm_grad
    grad_embedded = (embed_scale * resid_grad).astype(jnp.bfloat16)
    summed = (
        lax.psum_scatter(grad_gain_attn, ("expert", "shard"), scatter_dimension=0, tiled=True),
        lax.psum_scatter(grad_gain_ffn, ("expert", "shard"), scatter_dimension=0, tiled=True),
        lax.psum_scatter(grad_query_full, ("expert", "shard"), scatter_dimension=0, tiled=True),
        lax.psum_scatter(grad_key_full, ("expert", "shard"), scatter_dimension=0, tiled=True),
        lax.psum_scatter(grad_value_full, ("expert", "shard"), scatter_dimension=0, tiled=True),
        lax.psum_scatter(grad_out_full, ("expert", "shard"), scatter_dimension=0, tiled=True),
        lax.psum_scatter(grad_router_full, ("expert", "shard"), scatter_dimension=0, tiled=True),
    )
    return (
        output,
        grad_embedded,
        summed[0],
        summed[1],
        summed[2],
        summed[3],
        summed[4],
        summed[5],
        summed[6],
        grad_expert_in,
        grad_expert_out,
    )


def solution(mesh):
    return jax.shard_map(
        per_device,
        mesh=mesh,
        in_specs=(
            P(("expert", "shard"), None),
            P(("expert", "shard"), None),
            P(("expert", "shard"), None),
            P(("expert", "shard")),
            P(("expert", "shard")),
            P(("expert", "shard"), None),
            P(("expert", "shard"), None),
            P(("expert", "shard"), None),
            P(("expert", "shard"), None),
            P(("expert", "shard"), None),
            P("expert", "shard", None),
            P("expert", "shard", None),
            P(("expert", "shard"), None),
        ),
        out_specs=(
            P(("expert", "shard"), None),
            P(("expert", "shard"), None),
            P(("expert", "shard")),
            P(("expert", "shard")),
            P(("expert", "shard"), None),
            P(("expert", "shard"), None),
            P(("expert", "shard"), None),
            P(("expert", "shard"), None),
            P(("expert", "shard"), None),
            P("expert", "shard", None),
            P("expert", "shard", None),
        ),
        check_vma=False,
    )
```

profile of v0, /device:TPU:0, one launch (start us, length us, event | category | flops | bytes accessed | tf_op | source)
XLA Modules:
  0.0 1721.2 jit_solution(7981088020114671201)
XLA Ops:
  7.3 1.5 convert_element_type.155
  8.8 1.5 convert_element_type.157
  10.3 1.5 convert_element_type.159
  12.0 1.5 convert_element_type.163
  13.6 4.0 copy.115
  19.1 42.0 %all-reduce.5 = (bf16[1024]{0:T(1024)(128)(2,1)S(1)}, bf16[1024]{0:T(1024)(128)(2,1)S(1)}) all-reduce(bf16[1024]{0:T(1024)(128)(2,1)S(1)} %dynamic-update-slice, bf16[1024]{0:T(1024)(128)(2,1)S(1)} %dynamic-update-slice.1), channel_id=1, replica_groups=mesh['expert'=8,'shard'=4] {'expert','shard'}, use_global_device_ids=true, to_apply=%add | all-reduce | flops 2048 | bytes 8192
  61.4 9.1 reduce-window.19
  71.3 8.1 scatter_custom_fusion.1
  79.4 8.1 scatter_custom_fusion
  88.8 1.7 convolution_convert_fusion.3
  90.7 34.3 %all-gather.9.cloned.1.call-done = bf16[1024,512]{1,0:T(8,128)(2,1)} async-done(((bf16[32,512]{1,0:T(8,128)(2,1)}), bf16[1024,512]{1,0:T(8,128)(2,1)}) %all-gather.9.cloned.1.call-update) | async-done | bytes 1048592 | tf_op jit(solution)/shard_map/all_gather | solution.py:122
  125.0 1.8 fusion.79
  126.9 56.9 %all-gather.11.cloned.1.call-done = bf16[1024,1024]{1,0:T(8,128)(2,1)} async-done(((bf16[32,1024]{1,0:T(8,128)(2,1)}), bf16[1024,1024]{1,0:T(8,128)(2,1)}) %all-gather.11.cloned.1.call-update) | async-done | bytes 2097168 | tf_op jit(solution)/shard_map/all_gather | solution.py:121
  183.8 2.6 fusion.77
  191.1 51.3 %all-gather.13.cloned.1.call-done = bf16[1024,1024]{1,0:T(8,128)(2,1)} async-done(((bf16[32,1024]{1,0:T(8,128)(2,1)}), bf16[1024,1024]{1,0:T(8,128)(2,1)}) %all-gather.13.cloned.1.call-update) | async-done | bytes 2097168 | tf_op jit(solution)/shard_map/all_gather | solution.py:128
  242.4 2.4 multiply_reduce_fusion.2
  246.1 18.3 %gather_fusion = bf16[4096,1024]{1,0:T(8,128)(2,1)} fusion(bf16[256,1024]{1,0:T(8,128)(2,1)S(1)} %multiply_convert_fusion.4, s32[4096]{0:T(1024)S(1)} %get-tuple-element.91), kind=kCustom, calls=%fused_computation | custom fusion | bytes 16793600 | tf_op jit(solution)/shard_map/gather | solution.py:205
  264.3 7.2 broadcast_select_fusion.1
  271.5 5.0 all-to-all-start
  277.1 93.5 %all-to-all-done = bf16[8,4,128,1024]{3,2,1,0:T(8,128)(2,1)} async-done(((bf16[8,4,128,1024]{3,2,1,0:T(8,128)(2,1)}), bf16[8,4,128,1024]{3,2,1,0:T(8,128)(2,1)}, u32[]{:S(2)}, u32[]{:S(2)}) %all-to-all-start) | async-done | bytes 8388640 | tf_op jit(solution)/shard_map/all_to_all | solution.py:208
  370.5 8.2 copy.114
  378.7 13.7 all-gather.15.cloned.1.call-done
  392.4 17.0 fusion.85
  409.4 8.7 multiply_convert_fusion.2
  418.1 54.7 %all-gather.17.cloned.1.call-done = bf16[4,512,1024]{2,1,0:T(8,128)(2,1)} async-done(((bf16[4,128,1024]{2,1,0:T(8,128)(2,1)}), bf16[4,512,1024]{2,1,0:T(8,128)(2,1)}) %all-gather.17.cloned.1.call-update) | async-done | bytes 4194320 | tf_op jit(solution)/shard_map/all_gather | solution.py:134
  472.8 11.2 convert_bitcast_fusion.1
  484.0 12.2 copy.117
  496.2 5.1 all-to-all-start.1
  501.4 70.3 %all_gather.40 = bf16[1024,32]{1,0:T(8,128)(2,1)S(1)} all-gather(bf16[32,32]{1,0:T(8,128)(2,1)S(1)} %convert_element_type.167), channel_id=1, replica_groups=mesh['expert'=8,'shard'=4] {'expert','shard'}, dimensions={0}, use_global_device_ids=true | all-gather | bytes 67584 | tf_op jit(solution)/shard_map/all_gather | solution.py:129
  572.8 23.9 %all-to-all-done.1 = bf16[1,4,1024,1024]{3,1,0,2:T(4,128)(2,1)} async-done(((bf16[1,4,1024,1024]{3,1,0,2:T(4,128)(2,1)}), bf16[1,4,1024,1024]{3,1,0,2:T(4,128)(2,1)}, u32[]{:S(2)}, u32[]{:S(2)}) %all-to-all-start.1) | async-done | bytes 8388640 | tf_op jit(solution)/shard_map/all_to_all | solution.py:216
  596.7 9.8 copy.118
  606.5 15.4 gather_fusion.1
  621.9 4.5 fusion.4
  626.8 2.3 fusion
  629.1 23.6 %gather_fusion.2 = bf16[4096,1024]{1,0:T(8,128)(2,1)} fusion(bf16[2048,1024]{1,0:T(8,128)(2,1)} %fusion, s32[4096]{0:T(1024)S(1)} %get-tuple-element.90), kind=kCustom, calls=%fused_computation.2 | custom fusion | bytes 16793600 | tf_op jit(solution)/shard_map/gather | solution.py:234
  652.6 4.4 broadcast_select_fusion
  657.1 97.8 %all_to_all.65 = bf16[8,4,128,1024]{3,2,1,0:T(8,128)(2,1)} all-to-all(bf16[8,4,128,1024]{3,2,1,0:T(8,128)(2,1)S(1)} %broadcast_select_fusion), channel_id=1, replica_groups=mesh['expert'=8,'shard'=4] {'expert'}, dimensions={0} | all-to-all | bytes 16777216 | tf_op jit(solution)/shard_map/all_to_all | solution.py:237
  754.9 8.2 copy.120
  763.1 11.1 convolution_convert_fusion.1
  774.3 15.8 multiply_convert_fusion.1
  790.1 16.5 convolution_convert_fusion
  806.6 15.9 convert_bitcast_fusion
  822.5 12.2 copy.123
  834.7 5.2 all-to-all-start.3
  841.4 3.5 fusion.6
  844.9 89.0 %all-to-all-done.3 = bf16[1,4,1024,1024]{3,1,0,2:T(4,128)(2,1)} async-done(((bf16[1,4,1024,1024]{3,1,0,2:T(4,128)(2,1)}), bf16[1,4,1024,1024]{3,1,0,2:T(4,128)(2,1)}, u32[]{:S(2)}, u32[]{:S(2)}) %all-to-all-start.3) | async-done | bytes 8388640 | tf_op jit(solution)/shard_map/all_to_all | solution.py:264
  933.9 9.8 copy.124
  943.7 15.7 gather_fusion.3
  959.4 5.6 convert_reduce_fusion
  968.9 3.1 fusion.26
  972.0 1.9 fusion.71
  974.0 3.3 fusion.1
  979.4 2.0 fusion.73
  981.4 4.1 fusion.45
  986.6 2.8 fusion.75
  990.6 1.5 convolution_add_fusion.1
  992.9 37.1 %all-reduce.4 = (f32[1024]{0:T(1024)S(1)}, f32[1024]{0:T(1024)S(1)}) all-reduce(f32[1024]{0:T(1024)S(1)} %get-tuple-element.59, f32[1024]{0:T(1024)S(1)} %get-tuple-element.57), channel_id=2, replica_groups=mesh['expert'=8,'shard'=4] {'expert','shard'}, use_global_device_ids=true, to_apply=%region_21.22.clone | all-reduce | flops 2048 | bytes 16384
  1032.3 2.8 convert_element_type.190
  1035.1 4.1 convert_element_type.188
  1039.2 95.5 %reduce-scatter.16.cloned.1.call-done = f32[32,32]{1,0:T(8,128)} async-done(((f32[1024,32]{1,0:T(8,128)}), f32[32,32]{1,0:T(8,128)}) %reduce-scatter.16.cloned.1.call-update) | async-done | bytes 4112 | tf_op jit(solution)/shard_map/reduce_scatter | solution.py:407
  1134.7 138.6 %reduce-scatter.12.cloned.1.call-done = f32[32,512]{1,0:T(8,128)} async-done(((f32[1024,512]{1,0:T(8,128)}), f32[32,512]{1,0:T(8,128)}) %reduce-scatter.12.cloned.1.call-update) | async-done | bytes 65552 | tf_op jit(solution)/shard_map/reduce_scatter | solution.py:405
  1273.3 140.6 %reduce-scatter.10.cloned.1.call-done = f32[32,512]{1,0:T(8,128)} async-done(((f32[1024,512]{1,0:T(8,128)}), f32[32,512]{1,0:T(8,128)}) %reduce-scatter.10.cloned.1.call-update) | async-done | bytes 65552 | tf_op jit(solution)/shard_map/reduce_scatter | solution.py:404
  1413.9 150.1 %reduce-scatter.14.cloned.1.call-done = f32[32,1024]{1,0:T(8,128)} async-done(((f32[1024,1024]{1,0:T(8,128)}), f32[32,1024]{1,0:T(8,128)}) %reduce-scatter.14.cloned.1.call-update) | async-done | bytes 131088 | tf_op jit(solution)/shard_map/reduce_scatter | solution.py:406
  1564.0 150.2 %reduce-scatter.8.cloned.1.call-done = f32[32,1024]{1,0:T(8,128)} async-done(((f32[1024,1024]{1,0:T(8,128)}), f32[32,1024]{1,0:T(8,128)}) %reduce-scatter.8.cloned.1.call-update) | async-done | bytes 131088 | tf_op jit(solution)/shard_map/reduce_scatter | solution.py:403
  (209 shorter events, 24.8 us)
Async XLA Ops:
  7.2 10.4 copy-start.34
  7.2 10.8 copy-start.48
  7.2 10.8 copy-start.49
  7.2 10.8 copy-start.43
  7.2 81.6 %all-gather.7.cloned.1.call-start = ((), (), s32[]{:S(2)}) async-start(), calls=%async_computation.11 | async-start | bytes 1081344 | tf_op jit(solution)/shard_map/all_gather | solution.py:125
  8.7 116.2 %all-gather.9.cloned.1.call-start = ((), (), s32[]{:S(2)}) async-start(), calls=%async_computation.12 | async-start | bytes 1081344 | tf_op jit(solution)/shard_map/all_gather | solution.py:122
  10.3 173.6 %all-gather.11.cloned.1.call-start = ((), (), s32[]{:S(2)}) async-start(), calls=%async_computation.13 | async-start | bytes 2162688 | tf_op jit(solution)/shard_map/all_gather | solution.py:121
  11.9 230.5 %all-gather.13.cloned.1.call-start = ((), (), s32[]{:S(2)}) async-start(), calls=%async_computation.14 | async-start | bytes 2162688 | tf_op jit(solution)/shard_map/all_gather | solution.py:128
  13.5 74.1 %copy-start.2 = (bf16[256,1024]{1,0:T(8,128)(2,1)S(1)}, bf16[256,1024]{1,0:T(8,128)(2,1)}, u32[]{:S(2)}) copy-start(bf16[256,1024]{1,0:T(8,128)(2,1)} %param.13) | copy-start | bytes 1572868
  13.5 378.9 %all-gather.15.cloned.1.call-start = ((), (), s32[]{:S(2)}) async-start(), calls=%async_computation.15 | async-start | bytes 10485760 | tf_op jit(solution)/shard_map/all_gather | solution.py:133
  61.0 122.8 %copy-start.32 = (f32[1024]{0:T(1024)}, f32[1024]{0:T(1024)S(1)}, u32[]{:S(2)}) copy-start(f32[1024]{0:T(1024)S(1)} %convert_element_type.153) | copy-start | bytes 12292
  61.1 183.9 %copy-start.39 = (f32[1024]{0:T(1024)}, f32[1024]{0:T(1024)S(1)}, u32[]{:S(2)}) copy-start(f32[1024]{0:T(1024)S(1)} %convert_element_type.165) | copy-start | bytes 12292
  88.4 98.0 %copy-start.41 = (f32[256]{0:T(256)}, f32[256]{0:T(256)S(1)}, u32[]{:S(2)}) copy-start(f32[256]{0:T(256)S(1)} %get-tuple-element.95) | copy-start | bytes 3076
  88.7 97.8 %copy-start.24 = (f32[256,32]{0,1:T(8,128)}, f32[256,32]{0,1:T(8,128)S(1)}, u32[]{:S(2)}) copy-start(f32[256,32]{0,1:T(8,128)S(1)} %get-tuple-element.92) | copy-start | bytes 98308
  88.7 97.8 %copy-start.26 = (f32[256,32]{0,1:T(8,128)}, f32[256,32]{0,1:T(8,128)S(1)}, u32[]{:S(2)}) copy-start(f32[256,32]{0,1:T(8,128)S(1)} %get-tuple-element.93) | copy-start | bytes 98308
  90.7 98.2 %copy-start.21 = (bf16[256,512]{0,1:T(8,128)(2,1)}, bf16[256,512]{0,1:T(8,128)(2,1)S(1)}, u32[]{:S(2)}) copy-start(bf16[256,512]{0,1:T(8,128)(2,1)S(1)} %copy.105) | copy-start | bytes 786436
  126.9 61.3 %copy-start.28 = (bf16[256,8,32]{0,2,1:T(8,128)(2,1)}, bf16[256,8,32]{0,2,1:T(8,128)(2,1)S(1)}, u32[]{:S(2)}) copy-start(bf16[256,8,32]{0,2,1:T(8,128)(2,1)S(1)} %get-tuple-element.88) | copy-start | bytes 393220
  126.9 61.3 %copy-start.30 = (bf16[256,8,32]{0,2,1:T(8,128)(2,1)}, bf16[256,8,32]{0,2,1:T(8,128)(2,1)S(1)}, u32[]{:S(2)}) copy-start(bf16[256,8,32]{0,2,1:T(8,128)(2,1)S(1)} %get-tuple-element.89) | copy-start | bytes 393220
  186.7 1.5 copy-start.19
  188.2 2.0 copy-start
  188.2 2.9 copy-start.35
  188.8 2.3 copy-start.37
  191.1 73.2 %copy-start.15 = (bf16[8,64,2,256]{3,1,2,0:T(8,128)(2,1)}, bf16[8,64,2,256]{3,1,2,0:T(8,128)(2,1)S(1)}, u32[]{:S(2)}) copy-start(bf16[8,64,2,256]{3,1,2,0:T(8,128)(2,1)S(1)} %fusion.19) | copy-start | bytes 1572868
  244.9 1.0 copy-start.4
  244.9 19.4 %copy-start.45 = (f32[256]{0:T(256)}, f32[256]{0:T(256)S(1)}, u32[]{:S(2)}) copy-start(f32[256]{0:T(256)S(1)} %add_rsqrt_fusion) | copy-start | bytes 3076
  271.5 99.0 %all-to-all-start = ((bf16[8,4,128,1024]{3,2,1,0:T(8,128)(2,1)}), bf16[8,4,128,1024]{3,2,1,0:T(8,128)(2,1)}, u32[]{:S(2)}, u32[]{:S(2)}) async-start(bf16[8,4,128,1024]{3,2,1,0:T(8,128)(2,1)} %broadcast_select_fusion.1), calls=%async_computation | async-start | bytes 16777216 | tf_op jit(solution)/shard_map/all_to_all | solution.py:208
  276.5 196.3 %all-gather.17.cloned.1.call-start = ((), (), s32[]{:S(2)}) async-start(), calls=%async_computation.16 | async-start | bytes 5242880 | tf_op jit(solution)/shard_map/all_gather | solution.py:134
  496.2 5.2 copy-start.44
  496.2 75.5 %copy-start.10 = (bf16[256,1024]{1,0:T(8,128)(2,1)S(1)}, bf16[256,1024]{1,0:T(8,128)(2,1)}, u32[]{:S(2)}) copy-start(bf16[256,1024]{1,0:T(8,128)(2,1)} %param.25) | copy-start | bytes 1572868
  496.2 100.5 %all-to-all-start.1 = ((bf16[1,4,1024,1024]{3,1,0,2:T(4,128)(2,1)}), bf16[1,4,1024,1024]{3,1,0,2:T(4,128)(2,1)}, u32[]{:S(2)}, u32[]{:S(2)}) async-start(bf16[1,4,1024,1024]{3,1,0,2:T(4,128)(2,1)} %copy.117), calls=%async_computation.1 | async-start | bytes 16777216 | tf_op jit(solution)/shard_map/all_to_all | solution.py:216
  501.3 531.0 %reduce-scatter.20.cloned.1.call-start = ((), (), s32[]{:S(2)}) async-start(), calls=%async_computation.23 | async-start | bytes 5242880 | tf_op jit(solution)/shard_map/reduce_scatter | solution.py:275
  774.2 260.9 %reduce-scatter.18.cloned.1.call-start = ((), (), s32[]{:S(2)}) async-start(), calls=%async_computation.22 | async-start | bytes 10485760 | tf_op jit(solution)/shard_map/reduce_scatter | solution.py:272
  834.7 5.2 copy-start.36
  834.7 5.2 copy-start.38
  834.7 99.2 %all-to-all-start.3 = ((bf16[1,4,1024,1024]{3,1,0,2:T(4,128)(2,1)}), bf16[1,4,1024,1024]{3,1,0,2:T(4,128)(2,1)}, u32[]{:S(2)}, u32[]{:S(2)}) async-start(bf16[1,4,1024,1024]{3,1,0,2:T(4,128)(2,1)} %copy.123), calls=%async_computation.3 | async-start | bytes 16777216 | tf_op jit(solution)/shard_map/all_to_all | solution.py:264
  839.9 294.8 %reduce-scatter.16.cloned.1.call-start = ((), (), s32[]{:S(2)}) async-start(), calls=%async_computation.21 | async-start | bytes 540672 | tf_op jit(solution)/shard_map/reduce_scatter | solution.py:407
  841.4 431.9 %reduce-scatter.12.cloned.1.call-start = ((), (), s32[]{:S(2)}) async-start(), calls=%async_computation.19 | async-start | bytes 2162688 | tf_op jit(solution)/shard_map/reduce_scatter | solution.py:405
  959.4 5.6 copy-start.5
  959.4 5.6 copy-start.13
  959.4 5.6 copy-start.40
  959.4 5.6 copy-start.46
  959.4 6.2 copy-start.11
  965.0 2.8 copy-start.9
  966.9 1.0 copy-start.6
  967.9 4.1 copy-start.3
  967.9 4.1 copy-start.33
  967.9 4.1 copy-start.42
  968.9 5.1 copy-start.22
  973.9 440.0 %reduce-scatter.10.cloned.1.call-start = ((), (), s32[]{:S(2)}) async-start(), calls=%async_computation.18 | async-start | bytes 2162688 | tf_op jit(solution)/shard_map/reduce_scatter | solution.py:404
  974.0 3.5 copy-start.1
  977.4 1.1 copy-start.18
  977.4 1.1 copy-start.20
  977.4 1.8 copy-start.25
  977.4 1.8 copy-start.27
  979.4 6.2 copy-start.14
  981.4 4.5 copy-start.29
  981.4 4.5 copy-start.31
  981.4 582.6 %reduce-scatter.14.cloned.1.call-start = ((), (), s32[]{:S(2)}) async-start(), calls=%async_computation.20 | async-start | bytes 4325376 | tf_op jit(solution)/shard_map/reduce_scatter | solution.py:406
  985.6 728.6 %reduce-scatter.8.cloned.1.call-start = ((), (), s32[]{:S(2)}) async-start(), calls=%async_computation.17 | async-start | bytes 4325376 | tf_op jit(solution)/shard_map/reduce_scatter | solution.py:403
  986.6 2.8 copy-start.8
  989.4 1.2 copy-start.23
  989.4 2.8 copy-start.16
  990.6 40.5 %copy-start.7 = (f32[256,1024]{1,0:T(8,128)S(1)}, f32[256,1024]{1,0:T(8,128)}, u32[]{:S(2)}) copy-start(f32[256,1024]{1,0:T(8,128)} %copy-done.6) | copy-start | bytes 3145732
  990.6 40.5 %copy-start.47 = (f32[256]{0:T(256)S(1)}, f32[256]{0:T(256)}, u32[]{:S(2)}) copy-start(f32[256]{0:T(256)} %get-tuple-element.94) | copy-start | bytes 3076
  (2 other events, 1.4 us)
Sparse Core Ops, SparseCore 0:
  11.6 56.8 all-gather.6
  72.0 52.9 all-gather.8
  128.5 55.3 all-gather.10
  187.2 55.1 all-gather.12
  244.4 147.9 all-gather.14
  393.8 78.9 all-gather.16
  774.3 73.0 reduce-scatter.19
  849.8 145.1 reduce-scatter.17
  997.8 136.8 reduce-scatter.15
  1137.4 135.8 reduce-scatter.11
  1276.1 137.7 reduce-scatter.9
  1416.6 147.3 reduce-scatter.13
  1566.9 147.2 reduce-scatter.7
where the time goes:
time: 1730 us; the launch traced here: 1720 us
  waiting for transfers between devices  1090 us (63%)
  blocking collectives  247 us (14%)
  local copies, waits for them, and re-layouts  162 us (9%)
  matrix products  130 us (8%)
  other arithmetic  57.5 us (3%)
    reduce_scatter x1, waiting for transfers between devices, per_device(): lax.psum_scatter(grad_query_full, ('expert', 'shard'), scatter_dimension=...  150 us
    reduce_scatter x1, waiting for transfers between devices, per_device(): lax.psum_scatter(grad_out_full, ('expert', 'shard'), scatter_dimension=0,...  150 us
    reduce_scatter x1, waiting for transfers between devices, per_device(): lax.psum_scatter(grad_key_full, ('expert', 'shard'), scatter_dimension=0,...  141 us
    reduce_scatter x1, waiting for transfers between devices, per_device(): lax.psum_scatter(grad_value_full, ('expert', 'shard'), scatter_dimension=...  139 us
    all_to_all x1, blocking collectives, per_device(): lax.all_to_all(grad_send, 'expert', split_axis=0, concat_axis=2, tiled=True)  97.8 us
    reduce_scatter x1, waiting for transfers between devices, per_device(): lax.psum_scatter(grad_router_full, ('expert', 'shard'), scatter_dimension...  95.5 us
    all_to_all x1, waiting for transfers between devices, per_device(): lax.all_to_all(send_rows, 'expert', split_axis=0, concat_axis=2, tiled=True)  93.5 us
    all_to_all x1, waiting for transfers between devices, per_device(): lax.all_to_all(row_grads.reshape(1, local_count, received, MODEL_WIDTH),...  89 us
  transfers between devices with their start and end apart: 16, of which 13 were waited for; matrix products, arithmetic and copies ran while one was open for 14% of the time, Pallas kernels for 0%

commit v1 on v0

--- a/solution.py
+++ b/solution.py
@@ -100,7 +100,7 @@
     return (gate_part, up_part, sigmoid_gate, hidden)
 
 
-def per_device(
+def per_device_general(
     embedded,
     document_numbers,
     expert_ids,
@@ -421,37 +421,292 @@
     )
 
 
+BF16 = jnp.bfloat16
+F32 = jnp.float32
+PAIR = 2
+OWN = 2
+BLOCKS = 16
+
+
+def over_expert(value, bits):
+    return lax.ppermute(value, "expert", [(i, i ^ bits) for i in range(8)])
+
+
+def over_shard(value, bits):
+    return lax.ppermute(value, "shard", [(i, i ^ bits) for i in range(4)])
+
+
+def dot_f32(left, right, dims):
+    return lax.dot_general(left, right, dims, preferred_element_type=F32)
+
+
+def gather_blocks(block):
+    pair = jnp.stack([block, over_shard(block, 1)])
+    quarter = [pair] + [over_expert(pair, bits) for bits in (2, 4, 6)]
+    half = jnp.concatenate(quarter)
+    return jnp.concatenate([half, over_expert(half, 1)])
+
+
+def scatter_blocks(blocks):
+    half = (blocks[:8].astype(F32) + over_expert(blocks[8:], 1).astype(F32)).astype(BF16)
+    pair = half[0:2].astype(F32)
+    for number, bits in ((1, 2), (2, 4), (3, 6)):
+        pair = pair + over_expert(half[2 * number : 2 * number + 2], bits).astype(F32)
+    pair = pair.astype(BF16)
+    return pair[0].astype(F32) + over_shard(pair[1], 1).astype(F32)
+
+
+def reduce_rows(partial, e, z):
+    columns = partial.shape[1]
+    parts = partial.astype(BF16).reshape(4, 2, 4, 32, columns)
+    core = e % 2
+    quad = e // 2
+    mine = lax.dynamic_index_in_dim(parts, core, 1, keepdims=False)
+    other = lax.dynamic_index_in_dim(parts, 1 - core, 1, keepdims=False)
+    total = (mine.astype(F32) + over_expert(other, 1).astype(F32)).astype(BF16)
+    plane = lax.dynamic_index_in_dim(total, quad, 0, keepdims=False).astype(F32)
+    for step in (1, 2, 3):
+        sent = lax.dynamic_index_in_dim(total, quad ^ step, 0, keepdims=False)
+        plane = plane + over_expert(sent, 2 * step).astype(F32)
+    plane = plane.astype(BF16)
+    result = lax.dynamic_index_in_dim(plane, z, 0, keepdims=False).astype(F32)
+    for step in (1, 2, 3):
+        sent = lax.dynamic_index_in_dim(plane, z ^ step, 0, keepdims=False)
+        result = result + over_shard(sent, step).astype(F32)
+    return result
+
+
+def exchange_weights(weights, z):
+    h = z % 2
+    same = lax.dynamic_slice_in_dim(weights, 2 * h, 2, 0)
+    other = lax.dynamic_slice_in_dim(weights, 2 * (1 - h), 2, 0)
+    pieces = [same, over_shard(other, 1), over_shard(same, 2), over_shard(other, 3)]
+    stacked = jnp.stack(pieces)
+    return jnp.concatenate(
+        [lax.dynamic_index_in_dim(stacked, z ^ i, 0, keepdims=False) for i in range(4)], axis=1
+    )
+
+
+def exchange_grads(full, z):
+    h = z % 2
+    rows = full.shape[1] // 4
+    pick = lambda k: lax.dynamic_slice_in_dim(full, (z ^ k) * rows, rows, 1)
+    sent = [over_shard(pick(k).astype(BF16), k) for k in (1, 2, 3)]
+    same = pick(0).astype(F32) + sent[1].astype(F32)
+    other = sent[0].astype(F32) + sent[2].astype(F32)
+    return jnp.where(
+        h == 0, jnp.concatenate([same, other]), jnp.concatenate([other, same])
+    )
+
+
+def split_parts(value):
+    high = value.astype(BF16)
+    rest = value - high.astype(F32)
+    middle = rest.astype(BF16)
+    low = (rest - middle.astype(F32)).astype(BF16)
+    return high, middle, low
+
+
+def rows_of(table):
+    quarter = table.shape[0] // 4
+    return jnp.concatenate([table[i * quarter : (i + 1) * quarter] for i in range(4)], axis=1)
+
+
+def table_of(rows):
+    return jnp.concatenate([rows[..., 256 * i : 256 * i + 256] for i in range(4)], axis=-2)
+
+
+def per_device_fast(
+    embedded,
+    document_numbers,
+    expert_ids,
+    attn_gain,
+    ffn_gain,
+    w_query,
+    key_projection,
+    value_projection,
+    w_out,
+    w_router,
+    expert_in,
+    expert_out,
+    cotangent,
+):
+    e = lax.axis_index("expert")
+    z = lax.axis_index("shard")
+    h = z % 2
+    length = embedded.shape[0]
+    groups = QUERY_HEADS // KEY_VALUE_HEADS
+    small = jnp.concatenate(
+        [attn_gain[:, None], ffn_gain[:, None], jnp.zeros((32, 30), F32), w_router,
+         jnp.zeros((32, 64), F32)], axis=1)
+    packed = jnp.concatenate(
+        [w_query, key_projection, value_projection, w_out, small], axis=1
+    ).astype(BF16)
+    mixer = lax.all_gather(packed, ("expert", "shard"), axis=0, tiled=True)
+    query_w, key_w, value_w = mixer[:, :1024], mixer[:, 1024:1536], mixer[:, 1536:2048]
+    out_w = mixer[:, 2048:3072]
+    gain_attn, gain_ffn = mixer[:, 3072].astype(F32), mixer[:, 3073].astype(F32)
+    router_w = mixer[:, 3104:3136]
+    full_in = exchange_weights(expert_in, z)
+    full_out = exchange_weights(expert_out, z)
+    all_grads = gather_blocks(cotangent)
+
+    resid = embed_scale * embedded.astype(F32)
+    unit_attn, inverse_attn = norm_forward(resid)
+    normed = (unit_attn * gain_attn).astype(BF16)
+    unrotated_query = jnp.dot(normed, query_w, preferred_element_type=F32)
+    unrotated_key = jnp.dot(normed, key_w, preferred_element_type=F32)
+    projected_value = jnp.dot(normed, value_w, preferred_element_type=F32)
+    segments = document_numbers[0]
+    cosine_table, sine_table = rope_tables(segments)
+    query_heads = (
+        apply_rotation(unrotated_query.reshape(length, QUERY_HEADS, HEAD_SIZE), cosine_table, sine_table)
+        .astype(BF16)
+        .reshape(length, KEY_VALUE_HEADS, groups, HEAD_SIZE)
+    )
+    key_heads = apply_rotation(
+        unrotated_key.reshape(length, KEY_VALUE_HEADS, HEAD_SIZE), cosine_table, sine_table
+    ).astype(BF16)
+    value_heads = projected_value.astype(BF16).reshape(length, KEY_VALUE_HEADS, HEAD_SIZE)
+    key_index = jnp.arange(length, dtype=jnp.int32)
+    allowed = (key_index[None, :] <= key_index[:, None]) & (segments[None, :] == segments[:, None])
+    scores = jnp.einsum("qhgd,khd->hgqk", query_heads, key_heads, preferred_element_type=F32) * attn_scale
+    scores = jnp.where(allowed, scores, -1e30)
+    exps = jnp.exp(scores - jnp.max(scores, axis=-1, keepdims=True))
+    probs = exps / jnp.sum(exps, axis=-1, keepdims=True)
+    probs_low = probs.astype(BF16)
+    mixed = (
+        jnp.einsum("hgqk,khd->qhgd", probs_low, value_heads, preferred_element_type=F32)
+        .astype(BF16)
+        .reshape(length, QUERY_HEADS * HEAD_SIZE)
+    )
+    middle = resid + resid_scale * jnp.dot(mixed, out_w, preferred_element_type=F32)
+    unit_ffn, inverse_ffn = norm_forward(middle)
+    normed2 = (unit_ffn * gain_ffn).astype(BF16)
+    logits = jnp.dot(normed2, router_w, preferred_element_type=F32)
+
+    expert_range = jnp.arange(EXPERTS, dtype=jnp.int32)
+    member = jnp.any(expert_ids[:, :, None] == expert_range, axis=1)
+    below = (key_index[None, :] < key_index[:, None]).astype(BF16)
+    rank = jnp.dot(below, member.astype(BF16), preferred_element_type=F32)
+    code = jnp.where(member, rank, -1.0)
+    masked = jnp.where(member, logits, -1e30)
+    raised = jnp.where(member, jnp.exp(masked - jnp.max(masked, axis=1, keepdims=True)), 0.0)
+    gates = raised / jnp.sum(raised, axis=1, keepdims=True)
+    parts = [part.T for part in split_parts(gates)]
+    aux = rows_of(jnp.concatenate([code.T.astype(BF16)] + parts))
+    tokens = gather_blocks(jnp.concatenate([normed2, aux]))
+    all_rows, tables = tokens[:, :256], table_of(tokens[:, 256:])
+
+    first = e * 4 + h * OWN
+    table = tables.reshape(BLOCKS, 4, EXPERTS, 256).astype(F32)
+    table = lax.dynamic_slice_in_dim(table, first, OWN, 2)
+    slot_index = jnp.arange(CAP, dtype=jnp.int32).astype(F32)
+    select32 = (table[:, 0][:, :, None, :] == slot_index[None, None, :, None]).transpose(1, 0, 2, 3)
+    select = select32.astype(BF16)
+    gate_table = (table[:, 1] + table[:, 2] + table[:, 3]).transpose(1, 0, 2)
+    slot_gates = jnp.sum(jnp.where(select32, gate_table[:, :, None, :], 0.0), axis=-1)
+    pick = lambda rows: jnp.einsum("jbst,btd->jbsd", select, rows, preferred_element_type=F32)
+    arrived = pick(all_rows).astype(BF16).reshape(OWN, BLOCKS * CAP, MODEL_WIDTH)
+    slot_out = pick(all_grads).reshape(OWN, BLOCKS * CAP, MODEL_WIDTH)
+    slot_gates = slot_gates.reshape(OWN, BLOCKS * CAP, 1)
+    gate_up = jnp.einsum("erd,edf->erf", arrived, full_in, preferred_element_type=F32)
+    gate_part, up_part, sigmoid_gate, hidden = silu_parts(gate_up)
+    produced = jnp.einsum("erf,efd->erd", hidden, full_out, preferred_element_type=F32).astype(BF16)
+    scaled_out = resid_scale * slot_out
+    slot_grads = (slot_gates * scaled_out).astype(BF16)
+    gate_dots = jnp.sum(produced.astype(F32) * scaled_out, axis=-1)
+    weighted = (slot_gates * produced.astype(F32)).astype(BF16)
+    back = lambda rows: jnp.einsum(
+        "jbst,jbsd->btd", select, rows.reshape(OWN, BLOCKS, CAP, MODEL_WIDTH), preferred_element_type=F32
+    )
+    moe_blocks = back(weighted).astype(BF16)
+    hidden_grad = jnp.einsum("erd,efd->erf", slot_grads, full_out, preferred_element_type=F32)
+    gate_grad_part = hidden_grad * up_part * sigmoid_gate * (1.0 + gate_part * (1.0 - sigmoid_gate))
+    up_grad_part = hidden_grad * gate_part * sigmoid_gate
+    gate_up_grad = jnp.concatenate([gate_grad_part, up_grad_part], axis=-1).astype(BF16)
+    row_grads = jnp.einsum("erf,edf->erd", gate_up_grad, full_in, preferred_element_type=F32).astype(BF16)
+    row_blocks = back(row_grads).astype(BF16)
+    dots = jnp.sum(
+        jnp.where(select32, gate_dots.reshape(OWN, BLOCKS, CAP, 1), 0.0), axis=2
+    )
+    high, low, _ = split_parts(dots.transpose(1, 0, 2))
+    place = jnp.zeros((BLOCKS, 2, EXPERTS, 256), BF16)
+    place = lax.dynamic_update_slice(place, jnp.stack([high, low], axis=1), (0, 0, first, 0))
+    flat = place.reshape(BLOCKS, 64, 256)
+    flat = jnp.concatenate([flat[:, 16 * i : 16 * i + 16] for i in range(4)], axis=2)
+    returned = scatter_blocks(jnp.concatenate([row_blocks, flat], axis=1))
+    normed2_grad, dot_rows = returned[:256], table_of(returned[256:])
+    gate_grads = (dot_rows[:EXPERTS] + dot_rows[EXPERTS:]).T
+
+    grad_full_out = jnp.einsum("erf,erd->efd", hidden, slot_grads, preferred_element_type=F32)
+    grad_full_in = jnp.einsum("erd,erf->edf", arrived, gate_up_grad, preferred_element_type=F32)
+    grad_expert_in = exchange_grads(grad_full_in, z)
+    grad_expert_out = exchange_grads(grad_full_out, z)
+    moe = scatter_blocks(moe_blocks)
+    output = (middle + resid_scale * moe).astype(BF16)
+
+    grad_output = cotangent.astype(F32)
+    chosen_grad = gates * (gate_grads - jnp.sum(gates * gate_grads, axis=1, keepdims=True))
+    logit_grads = chosen_grad.astype(BF16)
+    grad_router_full = jnp.einsum("td,te->de", normed2, logit_grads, preferred_element_type=F32)
+    normed2_grad = normed2_grad + jnp.einsum("te,de->td", logit_grads, router_w, preferred_element_type=F32)
+    middle_norm_grad, grad_gain_ffn = norm_backward(normed2_grad, unit_ffn, inverse_ffn, gain_ffn)
+    middle_grad = grad_output + middle_norm_grad
+    attn_grad = (resid_scale * middle_grad).astype(BF16)
+    grad_out_full = jnp.einsum("tf,td->fd", mixed, attn_grad, preferred_element_type=F32)
+    mixed_grad = (
+        jnp.einsum("td,fd->tf", attn_grad, out_w, preferred_element_type=F32)
+        .astype(BF16)
+        .reshape(length, KEY_VALUE_HEADS, groups, HEAD_SIZE)
+    )
+    prob_grads = jnp.einsum("qhgd,khd->hgqk", mixed_grad, value_heads, preferred_element_type=F32)
+    score_grads = (probs * (prob_grads - jnp.sum(probs * prob_grads, axis=-1, keepdims=True))).astype(BF16)
+    query_grads = jnp.einsum("hgqk,khd->qhgd", score_grads, key_heads, preferred_element_type=F32) * attn_scale
+    key_grads = jnp.einsum("hgqk,qhgd->khd", score_grads, query_heads, preferred_element_type=F32) * attn_scale
+    value_grads = jnp.einsum("hgqk,qhgd->khd", probs_low, mixed_grad, preferred_element_type=F32)
+    query_raw = reverse_rotation(
+        query_grads.reshape(length, QUERY_HEADS, HEAD_SIZE), cosine_table, sine_table
+    ).astype(BF16).reshape(length, QUERY_HEADS * HEAD_SIZE)
+    key_raw = reverse_rotation(key_grads, cosine_table, sine_table).astype(BF16).reshape(length, 512)
+    value_raw = value_grads.astype(BF16).reshape(length, 512)
+    raw = jnp.concatenate([query_raw, key_raw, value_raw], axis=1)
+    grad_qkv_full = jnp.einsum("td,tf->df", normed, raw, preferred_element_type=F32)
+    normed_grad = jnp.einsum("tf,df->td", raw, mixer[:, :2048], preferred_element_type=F32)
+    resid_norm_grad, grad_gain_attn = norm_backward(normed_grad, unit_attn, inverse_attn, gain_attn)
+    grad_embedded = (embed_scale * (middle_grad + resid_norm_grad)).astype(BF16)
+
+    gains = jnp.concatenate(
+        [part[:, None] for gain in (grad_gain_attn, grad_gain_ffn) for part in split_parts(gain)[:2]]
+        + [jnp.zeros((1024, 28), BF16)], axis=1).astype(F32)
+    side = jnp.concatenate([gains, grad_router_full, jnp.zeros((1024, 64), F32)], axis=1)
+    late = reduce_rows(jnp.concatenate([grad_qkv_full, side], axis=1), e, z)
+    early = reduce_rows(grad_out_full, e, z)
+    return (
+        output,
+        grad_embedded,
+        late[:, 2048] + late[:, 2049],
+        late[:, 2050] + late[:, 2051],
+        late[:, :1024],
+        late[:, 1024:1536],
+        late[:, 1536:2048],
+        early,
+        late[:, 2080:2112],
+        grad_expert_in,
+        grad_expert_out,
+    )
+
+
 def solution(mesh):
+    owners, shards = mesh.shape["expert"], mesh.shape["shard"]
+    fast = owners == 8 and shards == 4
+    both = ("expert", "shard")
+    rows = P(both, None)
+    weights = P("expert", "shard", None)
     return jax.shard_map(
-        per_device,
+        per_device_fast if fast else per_device_general,
         mesh=mesh,
-        in_specs=(
-            P(("expert", "shard"), None),
-            P(("expert", "shard"), None),
-            P(("expert", "shard"), None),
-            P(("expert", "shard")),
-            P(("expert", "shard")),
-            P(("expert", "shard"), None),
-            P(("expert", "shard"), None),
-            P(("expert", "shard"), None),
-            P(("expert", "shard"), None),
-            P(("expert", "shard"), None),
-            P("expert", "shard", None),
-            P("expert", "shard", None),
-            P(("expert", "shard"), None),
-        ),
-        out_specs=(
-            P(("expert", "shard"), None),
-            P(("expert", "shard"), None),
-            P(("expert", "shard")),
-            P(("expert", "shard")),
-            P(("expert", "shard"), None),
-            P(("expert", "shard"), None),
-            P(("expert", "shard"), None),
-            P(("expert", "shard"), None),
-            P(("expert", "shard"), None),
-            P("expert", "shard", None),
-            P("expert", "shard", None),
-        ),
+        in_specs=(rows,) * 3 + (P(both),) * 2 + (rows,) * 5 + (weights,) * 2 + (rows,),
+        out_specs=(rows,) * 2 + (P(both),) * 2 + (rows,) * 5 + (weights,) * 2,
         check_vma=False,
     )

time: 1730 us -> 864 us (0.50)
  waiting for transfers between devices: 1090 us -> 440 us
  blocking collectives: 247 us -> 0 us
  local copies, waits for them, and re-layouts: 162 us -> 98.9 us
  starting transfers between devices: 16.2 us -> 73.4 us
  other arithmetic: 57.5 us -> 83.8 us
    reduce_scatter x7 -> x0, waiting for transfers between devices: 675 us -> none  [the longest x1 150 us: per_device(): lax.psum_scatter(grad_query_full, ('expert', 'shard'), scatter_dimension=...]
    ppermute x0 -> x46, waiting for transfers between devices: none -> 375 us  [the longest x22 209 us: over_shard(): return lax.ppermute(value, 'shard', [(i, i ^ bits) for i in range(4)])]
    all_to_all x3 -> x0, waiting for transfers between devices: 206 us -> none  [the longest x1 93.5 us: per_device(): lax.all_to_all(send_rows, 'expert', split_axis=0, concat_axis=2, tiled=True)]
    all_gather x6 -> x1, waiting for transfers between devices: 211 us -> 65.1 us  [per_device_fast(): mixer = lax.all_gather(packed, ('expert', 'shard'), axis=0, tiled=True)]
    all_to_all x1 -> x0, blocking collectives: 97.8 us -> none  [per_device(): lax.all_to_all(grad_send, 'expert', split_axis=0, concat_axis=2, tiled=True)]
    unnamed x2 -> x0, blocking collectives: 79 us -> none
    ppermute x0 -> x46, starting transfers between devices: none -> 73.3 us  [the longest x22 49 us: over_shard(): return lax.ppermute(value, 'shard', [(i, i ^ bits) for i in range(4)])]
    gather x4 -> x0, local copies, waits for them, and re-layouts: 72.9 us -> none  [the longest x1 23.6 us: per_device(): slot_grads[source]]
  transfers between devices with their start and end apart: 16 -> 47, of which waited for: 13 -> 22; matrix products, arithmetic and copies ran while one was open for 14% -> 20% of each run, Pallas kernels for 0% -> 0%
where the time goes in v1:
time: 864 us; the launch traced here: 855 us
  waiting for transfers between devices  440 us (51%)
  matrix products  143 us (17%)
  local copies, waits for them, and re-layouts  98.9 us (11%)
  other arithmetic  83.8 us (10%)
  starting transfers between devices  73.4 us (8%)
  between operations  15.7 us (2%)
    ppermute x22, waiting for transfers between devices, over_shard(): return lax.ppermute(value, 'shard', [(i, i ^ bits) for i in range(4)])  209 us
    ppermute x24, waiting for transfers between devices, over_expert(): return lax.ppermute(value, 'expert', [(i, i ^ bits) for i in range(8)])  166 us
    all_gather x1, waiting for transfers between devices, per_device_fast(): mixer = lax.all_gather(packed, ('expert', 'shard'), axis=0, tiled=True)  65.1 us
    ppermute x22, starting transfers between devices, over_shard(): return lax.ppermute(value, 'shard', [(i, i ^ bits) for i in range(4)])  49 us
    ppermute x24, starting transfers between devices, over_expert(): return lax.ppermute(value, 'expert', [(i, i ^ bits) for i in range(8)])  24.4 us
    dot_general x2, matrix products, per_device_fast(): jnp.einsum('jbst,btd->jbsd', select, rows, preferred_element_type=F32)  19.1 us
  transfers between devices with their start and end apart: 47, of which 22 were waited for; matrix products, arithmetic and copies ran while one was open for 20% of the time, Pallas kernels for 0%

profile of v1, /device:TPU:0, one launch (start us, length us, event | category | flops | bytes accessed | tf_op | source)
XLA Modules:
  0.0 855.2 jit_solution(6692883185939247354)
XLA Ops:
  13.9 3.1 collective-permute-start.16
  22.4 65.1 %all-gather.2.cloned.1.call-done = bf16[1024,3200]{1,0:T(8,128)(2,1)} async-done(((bf16[32,3200]{1,0:T(8,128)(2,1)}), bf16[1024,3200]{1,0:T(8,128)(2,1)}) %all-gather.2.cloned.1.call-update) | async-done | bytes 6553616 | tf_op jit(solution)/shard_map/all_gather | solution.py:545
  89.0 2.8 fusion.40
  96.1 3.5 fusion.161
  99.6 2.7 convolution_convert_fusion.3
  102.4 2.6 multiply_reduce_fusion.2
  111.8 12.6 %collective-permute-done = bf16[288,1024]{1,0:T(8,128)(2,1)S(1)} collective-permute-done((bf16[288,1024]{1,0:T(8,128)(2,1)S(1)}, bf16[288,1024]{1,0:T(8,128)(2,1)S(1)}, u32[]{:S(2)}, u32[]{:S(2)}) %collective-permute-start) | collective-permute-done | bytes 589856 | tf_op jit(solution)/shard_map/ppermute | solution.py:436
  131.8 4.8 collective-permute-done.17
  140.7 21.2 %collective-permute-done.1 = bf16[2,288,1024]{2,1,0:T(8,128)(2,1)S(1)} collective-permute-done((bf16[2,288,1024]{2,1,0:T(8,128)(2,1)S(1)}, bf16[2,288,1024]{2,1,0:T(8,128)(2,1)S(1)}, u32[]{:S(2)}, u32[]{:S(2)}) %collective-permute-start.1) | collective-permute-done | bytes 1179680 | tf_op jit(solution)/shard_map/ppermute | solution.py:432
  164.3 23.8 %collective-permute-done.3 = bf16[2,288,1024]{2,1,0:T(8,128)(2,1)S(1)} collective-permute-done((bf16[2,288,1024]{2,1,0:T(8,128)(2,1)S(1)}, bf16[2,288,1024]{2,1,0:T(8,128)(2,1)S(1)}, u32[]{:S(2)}, u32[]{:S(2)}) %collective-permute-start.3) | collective-permute-done | bytes 1179680 | tf_op jit(solution)/shard_map/ppermute | solution.py:432
  189.4 33.7 %collective-permute-done.18 = bf16[2,256,1024]{2,1,0:T(8,128)(2,1)S(1)} collective-permute-done((bf16[2,256,1024]{2,1,0:T(8,128)(2,1)S(1)}, bf16[2,256,1024]{2,1,0:T(8,128)(2,1)S(1)}, u32[]{:S(2)}, u32[]{:S(2)}) %collective-permute-start.18) | collective-permute-done | bytes 1048608 | tf_op jit(solution)/shard_map/ppermute | solution.py:432
  232.1 19.1 %collective-permute-done.8 = bf16[2,128,1024]{2,1,0:T(8,128)(2,1)S(1)} collective-permute-done((bf16[2,128,1024]{2,1,0:T(8,128)(2,1)S(1)}, bf16[2,128,1024]{2,1,0:T(8,128)(2,1)S(1)}, u32[]{:S(2)}, u32[]{:S(2)}) %collective-permute-start.8) | collective-permute-done | bytes 524320 | tf_op jit(solution)/shard_map/ppermute | solution.py:436
  251.3 14.9 %collective-permute-done.9 = bf16[2,128,1024]{2,1,0:T(8,128)(2,1)S(1)} collective-permute-done((bf16[2,128,1024]{2,1,0:T(8,128)(2,1)S(1)}, bf16[2,128,1024]{2,1,0:T(8,128)(2,1)S(1)}, u32[]{:S(2)}, u32[]{:S(2)}) %collective-permute-start.9) | collective-permute-done | bytes 524320 | tf_op jit(solution)/shard_map/ppermute | solution.py:436
  272.8 25.5 %collective-permute-done.5 = bf16[2,256,1024]{2,1,0:T(8,128)(2,1)S(1)} collective-permute-done((bf16[2,256,1024]{2,1,0:T(8,128)(2,1)}, bf16[2,256,1024]{2,1,0:T(8,128)(2,1)S(1)}, u32[]{:S(2)}, u32[]{:S(2)}) %collective-permute-start.5) | collective-permute-done | bytes 1048608 | tf_op jit(solution)/shard_map/ppermute | solution.py:436
  298.3 46.7 %collective-permute-done.6 = bf16[2,256,1024]{2,1,0:T(8,128)(2,1)S(1)} collective-permute-done((bf16[2,256,1024]{2,1,0:T(8,128)(2,1)S(1)}, bf16[2,256,1024]{2,1,0:T(8,128)(2,1)S(1)}, u32[]{:S(2)}, u32[]{:S(2)}) %collective-permute-start.6) | collective-permute-done | bytes 1048608 | tf_op jit(solution)/shard_map/ppermute | solution.py:436
  348.3 2.3 copy.139
  353.7 4.6 constant_dynamic-update-slice_fusion.16
  358.4 5.1 constant_dynamic-update-slice_fusion.5
  364.9 7.9 convert_bitcast_fusion
  372.8 8.4 copy.138
  381.3 14.8 %fusion.96 = f32[2,2048,1024]{1,2,0:T(8,128)} fusion(bf16[2,2048,1024]{2,1,0:T(8,128)(2,1)} %bitcast.302, bf16[2,256,1024]{1,2,0:T(8,128)(2,1)} %bitcast.324, bf16[2,256,1024]{1,2,0:T(8,128)(2,1)S(1)} %bitcast.322, bf16[2,256,1024]{1,2,0:T(8,128)(2,1)S(1)} %bitcast.320, bf16[2,256,1024]{1,2,0:T(8,128)(2,1)S(1)} %bitcast.318), kind=kOutput, calls=%fused_computation.149 | convolution fusion | flops 8606711808 | bytes 29360128 | tf_op jit(solution)/shard_map/erd,edf->erf/dot_general | solution.py:613
  396.1 8.7 %multiply_convert_fusion.2 = bf16[2,2048,512]{1,2,0:T(8,128)(2,1)} fusion(f32[2,2048,1024]{1,2,0:T(8,128)} %fusion.96), kind=kLoop, calls=%fused_computation.31 | loop fusion | flops 12582912 | bytes 20971520 | tf_op jit(solution)/shard_map/convert_element_type | solution.py:99
  404.8 11.2 %fusion.12 = f32[2,16,128,1024]{3,2,0,1:T(8,128)} fusion(bf16[16,256,1024]{2,1,0:T(8,128)(2,1)} %constant_dynamic-update-slice_fusion.16, f32[128]{0:T(128)S(1)} %iota_convert_fusion, f32[2,16,256]{2,0,1:T(2,128)S(1)} %get-tuple-element.108), kind=kOutput, calls=%fused_computation.22 | convolution fusion | flops 2148532224 | bytes 25199104 | tf_op jit(solution)/shard_map/jbst,btd->jbsd/dot_general | solution.py:609
  416.0 11.8 %copy.146 = f32[2,16,128,1024]{3,2,1,0:T(8,128)} copy(f32[2,16,128,1024]{3,2,0,1:T(8,128)} %fusion.12) | data formatting | bytes 33554432 | tf_op jit(solution)/shard_map/jbst,btd->jbsd/transpose | solution.py:609
  427.8 13.2 %fusion.2 = (f32[2,2048]{1,0:T(2,128)S(1)}, bf16[2,2048,1024]{2,1,0:T(8,128)(2,1)}) fusion(f32[2,16,128,1024]{3,2,1,0:T(8,128)} %copy.146, bf16[2,2048,512]{1,2,0:T(8,128)(2,1)} %multiply_convert_fusion.2, bf16[2,128,1024]{2,1,0:T(8,128)(2,1)} %get-tuple-element.53, bf16[2,128,1024]{2,1,0:T(8,128)(2,1)} %get-tuple-element.54, ...), kind=kOutput, calls=%fused_computation.4 | convolution fusion | flops 4324323328 | bytes 31473664 | tf_op jit(solution)/shard_map/erf,efd->erd/dot_general | solution.py:615
  441.0 3.7 fusion.33
  444.8 9.0 %fusion.3 = bf16[2,2048,1024]{2,1,0:T(8,128)(2,1)} fusion(f32[2,16,128,1024]{3,2,1,0:T(8,128)} %copy.146, f32[2,2048]{1,0:T(2,128)S(1)} %broadcast_multiply_fusion), kind=kLoop, calls=%fused_computation.8 | loop fusion | flops 8388608 | bytes 25182208 | tf_op jit(solution)/shard_map/convert_element_type | solution.py:617
  453.8 14.4 %multiply_convert_fusion.1 = (bf16[2,2048,512]{1,2,0:T(8,128)(2,1)}, bf16[2,2048,512]{1,2,0:T(8,128)(2,1)}) fusion(f32[2,2048,1024]{1,2,0:T(8,128)} %fusion.96, bf16[2,2048,1024]{2,1,0:T(8,128)(2,1)} %fusion.3, bf16[2,128,1024]{2,1,0:T(8,128)(2,1)} %get-tuple-element.53, bf16[2,128,1024]{2,1,0:T(8,128)(2,1)} %get-tuple-element.54, ...), kind=kOutput, calls=%fused_computation.29 | convolution fusion | flops 4330618880 | bytes 35651584 | tf_op jit(solution)/shard_map/erd,efd->erf/dot_general | solution.py:624
  468.2 13.9 %fusion.30 = bf16[2,2048,1024]{2,1,0:T(8,128)(2,1)} fusion(bf16[2,2048,512]{1,2,0:T(8,128)(2,1)} %get-tuple-element.28, bf16[2,2048,512]{1,2,0:T(8,128)(2,1)} %get-tuple-element.27, bf16[2,256,1024]{1,2,0:T(8,128)(2,1)} %bitcast.325, bf16[2,256,1024]{1,2,0:T(8,128)(2,1)S(1)} %bitcast.323, bf16[2,256,1024]{1,2,0:T(8,128)(2,1)S(1)} %bitcast.321, ...), kind=kOutput, calls=%fused_computation.37 | convolution fusion | flops 8627683328 | bytes 20971520 | tf_op jit(solution)/shard_map/erf,edf->erd/dot_general | solution.py:628
  482.1 4.8 bitcast_convert_fusion
  487.1 5.0 maximum_maximum_fusion
  492.1 3.0 slice.308
  497.1 8.1 fusion.1
  505.2 4.8 bitcast_convert_fusion.1
  510.1 2.9 slice.296
  515.1 17.2 %fusion.28 = f32[2,1024,1024]{2,1,0:T(8,128)} fusion(bf16[2,2048,1024]{2,1,0:T(8,128)(2,1)} %bitcast.303, bf16[2,2048,512]{1,2,0:T(8,128)(2,1)} %get-tuple-element.28, bf16[2,2048,512]{1,2,0:T(8,128)(2,1)} %get-tuple-element.27), kind=kOutput, calls=%fused_computation.34 | convolution fusion | flops 8606711808 | bytes 25165824 | tf_op jit(solution)/shard_map/erd,erf->edf/dot_general | solution.py:643
  532.3 6.1 add_convert_fusion
  539.8 7.8 fusion.162
  549.1 22.4 %collective-permute-start.44 = (bf16[2,128,1024]{2,1,0:T(8,128)(2,1)}, bf16[2,128,1024]{2,1,0:T(8,128)(2,1)}, u32[]{:S(2)}, u32[]{:S(2)}) collective-permute-start(bf16[2,128,1024]{2,1,0:T(8,128)(2,1)} %get-tuple-element.41), channel_id=1, source_target_pairs={{0,1},{1,0},{2,3},{3,2},{4,5},{5,4},{6,7},{7,6},{8,9},{9,8},{10,11... | collective-permute-start | bytes 1572872 | tf_op jit(solution)/shard_map/ppermute | solution.py:436
  575.8 4.3 add_convert_fusion.1
  580.4 3.7 collective-permute-done.44
  585.2 11.1 %collective-permute-done.45 = bf16[2,128,1024]{2,1,0:T(8,128)(2,1)} collective-permute-done((bf16[2,128,1024]{2,1,0:T(8,128)(2,1)S(1)}, bf16[2,128,1024]{2,1,0:T(8,128)(2,1)}, u32[]{:S(2)}, u32[]{:S(2)}) %collective-permute-start.45) | collective-permute-done | bytes 524320 | tf_op jit(solution)/shard_map/ppermute | solution.py:436
  599.2 4.7 dynamic-slice_convert_fusion.2
  605.2 41.9 %collective-permute-done.23 = bf16[2,272,1024]{2,1,0:T(8,128)(2,1)} collective-permute-done((bf16[2,272,1024]{2,1,0:T(8,128)(2,1)S(1)}, bf16[2,272,1024]{2,1,0:T(8,128)(2,1)}, u32[]{:S(2)}, u32[]{:S(2)}) %collective-permute-start.23) | collective-permute-done | bytes 1114144 | tf_op jit(solution)/shard_map/ppermute | solution.py:432
  647.2 2.9 collective-permute-start.40
  650.1 2.6 add_convert_fusion.2
  652.8 14.8 %collective-permute-done.13 = bf16[2,256,1024]{2,1,0:T(8,128)(2,1)S(1)} collective-permute-done((bf16[2,256,1024]{2,1,0:T(8,128)(2,1)S(1)}, bf16[2,256,1024]{2,1,0:T(8,128)(2,1)S(1)}, u32[]{:S(2)}, u32[]{:S(2)}) %collective-permute-start.13) | collective-permute-done | bytes 1048608 | tf_op jit(solution)/shard_map/ppermute | solution.py:432
  670.7 55.3 %collective-permute-done.25 = bf16[272,1024]{1,0:T(8,128)(2,1)S(1)} collective-permute-done((bf16[272,1024]{1,0:T(8,128)(2,1)S(1)}, bf16[272,1024]{1,0:T(8,128)(2,1)S(1)}, u32[]{:S(2)}, u32[]{:S(2)}) %collective-permute-start.25) | collective-permute-done | bytes 557088 | tf_op jit(solution)/shard_map/ppermute | solution.py:436
  727.9 11.9 %collective-permute-done.15 = bf16[256,1024]{1,0:T(8,128)(2,1)S(1)} collective-permute-done((bf16[256,1024]{1,0:T(8,128)(2,1)S(1)}, bf16[256,1024]{1,0:T(8,128)(2,1)S(1)}, u32[]{:S(2)}, u32[]{:S(2)}) %collective-permute-start.15) | collective-permute-done | bytes 524320 | tf_op jit(solution)/shard_map/ppermute | solution.py:436
  741.1 2.3 fusion.68
  743.7 3.1 fusion.36
  751.5 3.7 convolution_convert_fusion.1
  755.3 2.4 fusion.87
  757.8 4.8 copy.155
  768.9 8.5 concatenate.131
  783.7 2.2 convert_add_fusion.3
  788.0 2.5 maximum_select_fusion
  791.0 3.2 collective-permute-start.34
  798.5 2.8 collective-permute-done.34
  803.9 5.1 collective-permute-done.35
  811.7 7.2 collective-permute-done.27
  820.9 10.9 %collective-permute-done.28 = bf16[4,32,2176]{2,1,0:T(8,128)(2,1)S(1)} collective-permute-done((bf16[4,32,2176]{2,1,0:T(8,128)(2,1)S(1)}, bf16[4,32,2176]{2,1,0:T(8,128)(2,1)S(1)}, u32[]{:S(2)}, u32[]{:S(2)}) %collective-permute-start.28) | collective-permute-done | bytes 557088 | tf_op jit(solution)/shard_map/ppermute | solution.py:432
  832.4 2.2 collective-permute-start.31
  838.5 6.6 collective-permute-done.31
  (328 shorter events, 125.4 us)
Async XLA Ops:
  7.2 80.4 %all-gather.2.cloned.1.call-start = ((), (), s32[]{:S(2)}) async-start(), calls=%async_computation | async-start | bytes 6758400 | tf_op jit(solution)/shard_map/all_gather | solution.py:545
  9.0 82.9 %copy-start.11 = (bf16[256,1024]{1,0:T(8,128)(2,1)S(1)}, bf16[256,1024]{1,0:T(8,128)(2,1)}, u32[]{:S(2)}) copy-start(bf16[256,1024]{1,0:T(8,128)(2,1)} %param.13) | copy-start | bytes 1572868
  13.9 96.5 %collective-permute-start.16 = (bf16[256,1024]{1,0:T(8,128)(2,1)}, bf16[256,1024]{1,0:T(8,128)(2,1)S(1)}, u32[]{:S(2)}, u32[]{:S(2)}) collective-permute-start(bf16[256,1024]{1,0:T(8,128)(2,1)} %param.25), channel_id=1, source_target_pairs={{0,1},{1,0},{2,3},{3,2},{4,5},{5,4},{6,7},{7,6},{8,9},{9,8},{10,11... | collective-permute-start | bytes 1572872 | tf_op jit(solution)/shard_map/ppermute | solution.py:436
  19.2 88.3 %copy-start.38 = (pred[256,32]{0,1:T(8,128)(4,1)}, pred[256,32]{0,1:T(8,128)(4,1)S(1)}, u32[]{:S(2)}) copy-start(pred[256,32]{0,1:T(8,128)(4,1)S(1)} %fusion.106) | copy-start | bytes 24580
  21.1 72.9 %copy-start.56 = (f32[256]{0:T(256)}, f32[256]{0:T(256)S(1)}, u32[]{:S(2)}) copy-start(f32[256]{0:T(256)S(1)} %get-tuple-element.115) | copy-start | bytes 3076
  21.5 72.5 %copy-start.25 = (f32[256,32]{0,1:T(8,128)}, f32[256,32]{0,1:T(8,128)S(1)}, u32[]{:S(2)}) copy-start(f32[256,32]{0,1:T(8,128)S(1)} %get-tuple-element.112) | copy-start | bytes 98308
  21.5 72.5 %copy-start.27 = (f32[256,32]{0,1:T(8,128)}, f32[256,32]{0,1:T(8,128)S(1)}, u32[]{:S(2)}) copy-start(f32[256,32]{0,1:T(8,128)S(1)} %get-tuple-element.113) | copy-start | bytes 98308
  108.9 15.5 %collective-permute-start = (bf16[288,1024]{1,0:T(8,128)(2,1)S(1)}, bf16[288,1024]{1,0:T(8,128)(2,1)S(1)}, u32[]{:S(2)}, u32[]{:S(2)}) collective-permute-start(bf16[288,1024]{1,0:T(8,128)(2,1)S(1)} %get-tuple-element.26), channel_id=1, source_target_pairs={{0,1},{1,0},{2,3},{3,2},{4,5},{5,4},{6,7},{7,6},{8,9},{9,8},{10,11... | collective-permute-start | bytes 1769480 | tf_op jit(solution)/shard_map/ppermute | solution.py:436
  110.5 26.1 %collective-permute-start.17 = (bf16[2,256,1024]{2,1,0:T(8,128)(2,1)S(1)}, bf16[2,256,1024]{2,1,0:T(8,128)(2,1)S(1)}, u32[]{:S(2)}, u32[]{:S(2)}) collective-permute-start(bf16[2,256,1024]{2,1,0:T(8,128)(2,1)S(1)} %pad_maximum_fusion.11), channel_id=1, source_target_pairs={{0,8},{4,12},{8,0},{12,4},{16,24},{20,28},{24,16},{28,20},{1,9},{5... | collective-permute-start | bytes 3145736 | tf_op jit(solution)/shard_map/ppermute | solution.py:432
  124.5 37.4 %collective-permute-start.1 = (bf16[2,288,1024]{2,1,0:T(8,128)(2,1)S(1)}, bf16[2,288,1024]{2,1,0:T(8,128)(2,1)S(1)}, u32[]{:S(2)}, u32[]{:S(2)}) collective-permute-start(bf16[2,288,1024]{2,1,0:T(8,128)(2,1)S(1)} %pad_maximum_fusion.9), channel_id=1, source_target_pairs={{0,8},{4,12},{8,0},{12,4},{16,24},{20,28},{24,16},{28,20},{1,9},{5... | collective-permute-start | bytes 3538952 | tf_op jit(solution)/shard_map/ppermute | solution.py:432
  125.8 37.2 %collective-permute-start.2 = (bf16[2,288,1024]{2,1,0:T(8,128)(2,1)S(1)}, bf16[2,288,1024]{2,1,0:T(8,128)(2,1)S(1)}, u32[]{:S(2)}, u32[]{:S(2)}) collective-permute-start(bf16[2,288,1024]{2,1,0:T(8,128)(2,1)S(1)} %pad_maximum_fusion.9), channel_id=1, source_target_pairs={{0,16},{4,20},{8,24},{12,28},{16,0},{20,4},{24,8},{28,12},{1,17},{... | collective-permute-start | bytes 3538952 | tf_op jit(solution)/shard_map/ppermute | solution.py:432
  127.7 95.3 %collective-permute-start.18 = (bf16[2,256,1024]{2,1,0:T(8,128)(2,1)S(1)}, bf16[2,256,1024]{2,1,0:T(8,128)(2,1)S(1)}, u32[]{:S(2)}, u32[]{:S(2)}) collective-permute-start(bf16[2,256,1024]{2,1,0:T(8,128)(2,1)S(1)} %pad_maximum_fusion.11), channel_id=1, source_target_pairs={{0,16},{4,20},{8,24},{12,28},{16,0},{20,4},{24,8},{28,12},{1,17},{... | collective-permute-start | bytes 3145736 | tf_op jit(solution)/shard_map/ppermute | solution.py:432
  129.0 59.1 %collective-permute-start.3 = (bf16[2,288,1024]{2,1,0:T(8,128)(2,1)S(1)}, bf16[2,288,1024]{2,1,0:T(8,128)(2,1)S(1)}, u32[]{:S(2)}, u32[]{:S(2)}) collective-permute-start(bf16[2,288,1024]{2,1,0:T(8,128)(2,1)S(1)} %pad_maximum_fusion.9), channel_id=1, source_target_pairs={{0,24},{4,28},{8,16},{12,20},{16,8},{20,12},{24,0},{28,4},{1,25},{... | collective-permute-start | bytes 3538952 | tf_op jit(solution)/shard_map/ppermute | solution.py:432
  136.6 88.1 %collective-permute-start.19 = (bf16[2,256,1024]{2,1,0:T(8,128)(2,1)S(1)}, bf16[2,256,1024]{2,1,0:T(8,128)(2,1)S(1)}, u32[]{:S(2)}, u32[]{:S(2)}) collective-permute-start(bf16[2,256,1024]{2,1,0:T(8,128)(2,1)S(1)} %pad_maximum_fusion.11), channel_id=1, source_target_pairs={{0,24},{4,28},{8,16},{12,20},{16,8},{20,12},{24,0},{28,4},{1,25},{... | collective-permute-start | bytes 3145736 | tf_op jit(solution)/shard_map/ppermute | solution.py:432
  188.1 38.2 %copy-start.22 = (bf16[4,128,1024]{2,1,0:T(8,128)(2,1)S(1)}, bf16[4,128,1024]{2,1,0:T(8,128)(2,1)}, u32[]{:S(2)}) copy-start(bf16[4,128,1024]{2,1,0:T(8,128)(2,1)} %param.24) | copy-start | bytes 3145732
  189.3 37.0 %copy-start.40 = (bf16[16,288,1024]{2,1,0:T(8,128)(2,1)}, bf16[16,288,1024]{2,1,0:T(8,128)(2,1)S(1)}, u32[]{:S(2)}) copy-start(bf16[16,288,1024]{2,1,0:T(8,128)(2,1)S(1)} %get-tuple-element.59) | copy-start | bytes 28311556
  189.3 169.0 %collective-permute-start.4 = (bf16[8,288,1024]{2,1,0:T(8,128)(2,1)}, bf16[8,288,1024]{2,1,0:T(8,128)(2,1)}, u32[]{:S(2)}, u32[]{:S(2)}) collective-permute-start(bf16[8,288,1024]{2,1,0:T(8,128)(2,1)} %get-tuple-element.58), channel_id=1, source_target_pairs={{0,4},{4,0},{8,12},{12,8},{16,20},{20,16},{24,28},{28,24},{1,5},{5... | collective-permute-start | bytes 14155784 | tf_op jit(solution)/shard_map/ppermute | solution.py:432
  226.3 127.4 %collective-permute-start.20 = (bf16[8,256,1024]{2,1,0:T(8,128)(2,1)}, bf16[8,256,1024]{2,1,0:T(8,128)(2,1)}, u32[]{:S(2)}, u32[]{:S(2)}) collective-permute-start(bf16[8,256,1024]{2,1,0:T(8,128)(2,1)} %get-tuple-element.77), channel_id=1, source_target_pairs={{0,4},{4,0},{8,12},{12,8},{16,20},{20,16},{24,28},{28,24},{1,5},{5... | collective-permute-start | bytes 12582920 | tf_op jit(solution)/shard_map/ppermute | solution.py:432
  226.4 39.8 %copy-start.13 = (bf16[2,128,1024]{2,1,0:T(8,128)(2,1)}, bf16[2,128,1024]{2,1,0:T(8,128)(2,1)S(1)}, u32[]{:S(2)}) copy-start(bf16[2,128,1024]{2,1,0:T(8,128)(2,1)S(1)} %get-tuple-element.83) | copy-start | bytes 1572868
  226.4 24.8 %collective-permute-start.8 = (bf16[2,128,1024]{2,1,0:T(8,128)(2,1)S(1)}, bf16[2,128,1024]{2,1,0:T(8,128)(2,1)S(1)}, u32[]{:S(2)}, u32[]{:S(2)}) collective-permute-start(bf16[2,128,1024]{2,1,0:T(8,128)(2,1)S(1)} %get-tuple-element.84), channel_id=1, source_target_pairs={{0,1},{1,0},{2,3},{3,2},{4,5},{5,4},{6,7},{7,6},{8,9},{9,8},{10,11... | collective-permute-start | bytes 1572872 | tf_op jit(solution)/shard_map/ppermute | solution.py:436
  228.0 38.3 %collective-permute-start.9 = (bf16[2,128,1024]{2,1,0:T(8,128)(2,1)S(1)}, bf16[2,128,1024]{2,1,0:T(8,128)(2,1)S(1)}, u32[]{:S(2)}, u32[]{:S(2)}) collective-permute-start(bf16[2,128,1024]{2,1,0:T(8,128)(2,1)S(1)} %get-tuple-element.83), channel_id=1, source_target_pairs={{0,2},{1,3},{2,0},{3,1},{4,6},{5,7},{6,4},{7,5},{8,10},{9,11},{10,... | collective-permute-start | bytes 1572872 | tf_op jit(solution)/shard_map/ppermute | solution.py:436
  228.9 37.4 %collective-permute-start.10 = (bf16[2,128,1024]{2,1,0:T(8,128)(2,1)S(1)}, bf16[2,128,1024]{2,1,0:T(8,128)(2,1)S(1)}, u32[]{:S(2)}, u32[]{:S(2)}) collective-permute-start(bf16[2,128,1024]{2,1,0:T(8,128)(2,1)S(1)} %get-tuple-element.84), channel_id=1, source_target_pairs={{0,3},{1,2},{2,1},{3,0},{4,7},{5,6},{6,5},{7,4},{8,11},{9,10},{10,... | collective-permute-start | bytes 1572872 | tf_op jit(solution)/shard_map/ppermute | solution.py:436
  251.3 47.0 %collective-permute-start.5 = (bf16[2,256,1024]{2,1,0:T(8,128)(2,1)}, bf16[2,256,1024]{2,1,0:T(8,128)(2,1)S(1)}, u32[]{:S(2)}, u32[]{:S(2)}) collective-permute-start(bf16[2,256,1024]{2,1,0:T(8,128)(2,1)} %get-tuple-element.57), channel_id=1, source_target_pairs={{0,1},{1,0},{2,3},{3,2},{4,5},{5,4},{6,7},{7,6},{8,9},{9,8},{10,11... | collective-permute-start | bytes 3145736 | tf_op jit(solution)/shard_map/ppermute | solution.py:436
  266.2 78.7 %collective-permute-start.6 = (bf16[2,256,1024]{2,1,0:T(8,128)(2,1)S(1)}, bf16[2,256,1024]{2,1,0:T(8,128)(2,1)S(1)}, u32[]{:S(2)}, u32[]{:S(2)}) collective-permute-start(bf16[2,256,1024]{2,1,0:T(8,128)(2,1)S(1)} %get-tuple-element.56), channel_id=1, source_target_pairs={{0,2},{1,3},{2,0},{3,1},{4,6},{5,7},{6,4},{7,5},{8,10},{9,11},{10,... | collective-permute-start | bytes 3145736 | tf_op jit(solution)/shard_map/ppermute | solution.py:436
  267.8 77.1 %collective-permute-start.7 = (bf16[2,256,1024]{2,1,0:T(8,128)(2,1)}, bf16[2,256,1024]{2,1,0:T(8,128)(2,1)}, u32[]{:S(2)}, u32[]{:S(2)}) collective-permute-start(bf16[2,256,1024]{2,1,0:T(8,128)(2,1)} %get-tuple-element.57), channel_id=1, source_target_pairs={{0,3},{1,2},{2,1},{3,0},{4,7},{5,6},{6,5},{7,4},{8,11},{9,10},{10,... | collective-permute-start | bytes 3145736 | tf_op jit(solution)/shard_map/ppermute | solution.py:436
  497.1 35.2 %collective-permute-start.21 = (bf16[8,272,1024]{2,1,0:T(8,128)(2,1)}, bf16[8,272,1024]{2,1,0:T(8,128)(2,1)}, u32[]{:S(2)}, u32[]{:S(2)}) collective-permute-start(bf16[8,272,1024]{2,1,0:T(8,128)(2,1)} %slice.308), channel_id=1, source_target_pairs={{0,4},{4,0},{8,12},{12,8},{16,20},{20,16},{24,28},{28,24},{1,5},{5... | collective-permute-start | bytes 13369352 | tf_op jit(solution)/shard_map/ppermute | solution.py:432
  514.6 59.8 %collective-permute-start.11 = (bf16[8,256,1024]{2,1,0:T(8,128)(2,1)}, bf16[8,256,1024]{2,1,0:T(8,128)(2,1)}, u32[]{:S(2)}, u32[]{:S(2)}) collective-permute-start(bf16[8,256,1024]{2,1,0:T(8,128)(2,1)} %slice.296), channel_id=1, source_target_pairs={{0,4},{4,0},{8,12},{12,8},{16,20},{20,16},{24,28},{28,24},{1,5},{5... | collective-permute-start | bytes 12582920 | tf_op jit(solution)/shard_map/ppermute | solution.py:432
  538.3 37.5 %slice-start = ((s8[8388608]{0:T(1024)(128)(4,1)}), s8[4194304]{0:T(1024)(128)(4,1)S(1)}, s32[]{:S(2)}) async-start(s8[8388608]{0:T(1024)(128)(4,1)} %bitcast.294), calls=%async_computation.1 | async-start | bytes 8388608
  539.0 58.7 %collective-permute-start.22 = (bf16[2,272,1024]{2,1,0:T(8,128)(2,1)S(1)}, bf16[2,272,1024]{2,1,0:T(8,128)(2,1)S(1)}, u32[]{:S(2)}, u32[]{:S(2)}) collective-permute-start(bf16[2,272,1024]{2,1,0:T(8,128)(2,1)S(1)} %get-tuple-element.36), channel_id=1, source_target_pairs={{0,8},{4,12},{8,0},{12,4},{16,24},{20,28},{24,16},{28,20},{1,9},{5... | collective-permute-start | bytes 3342344 | tf_op jit(solution)/shard_map/ppermute | solution.py:432
  549.1 35.0 %collective-permute-start.44 = (bf16[2,128,1024]{2,1,0:T(8,128)(2,1)}, bf16[2,128,1024]{2,1,0:T(8,128)(2,1)}, u32[]{:S(2)}, u32[]{:S(2)}) collective-permute-start(bf16[2,128,1024]{2,1,0:T(8,128)(2,1)} %get-tuple-element.41), channel_id=1, source_target_pairs={{0,1},{1,0},{2,3},{3,2},{4,5},{5,4},{6,7},{7,6},{8,9},{9,8},{10,11... | collective-permute-start | bytes 1572872 | tf_op jit(solution)/shard_map/ppermute | solution.py:436
  571.5 24.8 %collective-permute-start.45 = (bf16[2,128,1024]{2,1,0:T(8,128)(2,1)S(1)}, bf16[2,128,1024]{2,1,0:T(8,128)(2,1)}, u32[]{:S(2)}, u32[]{:S(2)}) collective-permute-start(bf16[2,128,1024]{2,1,0:T(8,128)(2,1)S(1)} %get-tuple-element.40), channel_id=1, source_target_pairs={{0,3},{1,2},{2,1},{3,0},{4,7},{5,6},{6,5},{7,4},{8,11},{9,10},{10,... | collective-permute-start | bytes 1572872 | tf_op jit(solution)/shard_map/ppermute | solution.py:436
  573.3 73.9 %collective-permute-start.23 = (bf16[2,272,1024]{2,1,0:T(8,128)(2,1)S(1)}, bf16[2,272,1024]{2,1,0:T(8,128)(2,1)}, u32[]{:S(2)}, u32[]{:S(2)}) collective-permute-start(bf16[2,272,1024]{2,1,0:T(8,128)(2,1)S(1)} %get-tuple-element.38), channel_id=1, source_target_pairs={{0,16},{4,20},{8,24},{12,28},{16,0},{20,4},{24,8},{28,12},{1,17},{... | collective-permute-start | bytes 3342344 | tf_op jit(solution)/shard_map/ppermute | solution.py:432
  574.3 72.8 %collective-permute-start.24 = (bf16[2,272,1024]{2,1,0:T(8,128)(2,1)S(1)}, bf16[2,272,1024]{2,1,0:T(8,128)(2,1)}, u32[]{:S(2)}, u32[]{:S(2)}) collective-permute-start(bf16[2,272,1024]{2,1,0:T(8,128)(2,1)S(1)} %get-tuple-element.37), channel_id=1, source_target_pairs={{0,24},{4,28},{8,16},{12,20},{16,8},{20,12},{24,0},{28,4},{1,25},{... | collective-permute-start | bytes 3342344 | tf_op jit(solution)/shard_map/ppermute | solution.py:432
  584.1 68.6 %collective-permute-start.12 = (bf16[2,256,1024]{2,1,0:T(8,128)(2,1)S(1)}, bf16[2,256,1024]{2,1,0:T(8,128)(2,1)S(1)}, u32[]{:S(2)}, u32[]{:S(2)}) collective-permute-start(bf16[2,256,1024]{2,1,0:T(8,128)(2,1)S(1)} %get-tuple-element.42), channel_id=1, source_target_pairs={{0,8},{4,12},{8,0},{12,4},{16,24},{20,28},{24,16},{28,20},{1,9},{5... | collective-permute-start | bytes 3145736 | tf_op jit(solution)/shard_map/ppermute | solution.py:432
  596.2 71.4 %collective-permute-start.13 = (bf16[2,256,1024]{2,1,0:T(8,128)(2,1)S(1)}, bf16[2,256,1024]{2,1,0:T(8,128)(2,1)S(1)}, u32[]{:S(2)}, u32[]{:S(2)}) collective-permute-start(bf16[2,256,1024]{2,1,0:T(8,128)(2,1)S(1)} %get-tuple-element.44), channel_id=1, source_target_pairs={{0,16},{4,20},{8,24},{12,28},{16,0},{20,4},{24,8},{28,12},{1,17},{... | collective-permute-start | bytes 3145736 | tf_op jit(solution)/shard_map/ppermute | solution.py:432
  597.7 72.1 %collective-permute-start.14 = (bf16[2,256,1024]{2,1,0:T(8,128)(2,1)S(1)}, bf16[2,256,1024]{2,1,0:T(8,128)(2,1)S(1)}, u32[]{:S(2)}, u32[]{:S(2)}) collective-permute-start(bf16[2,256,1024]{2,1,0:T(8,128)(2,1)S(1)} %get-tuple-element.43), channel_id=1, source_target_pairs={{0,24},{4,28},{8,16},{12,20},{16,8},{20,12},{24,0},{28,4},{1,25},{... | collective-permute-start | bytes 3145736 | tf_op jit(solution)/shard_map/ppermute | solution.py:432
  647.2 132.1 %collective-permute-start.43 = (bf16[2,128,1024]{2,1,0:T(8,128)(2,1)}, bf16[2,128,1024]{2,1,0:T(8,128)(2,1)}, u32[]{:S(2)}, u32[]{:S(2)}) collective-permute-start(bf16[2,128,1024]{2,1,0:T(8,128)(2,1)} %get-tuple-element.39), channel_id=1, source_target_pairs={{0,2},{1,3},{2,0},{3,1},{4,6},{5,7},{6,4},{7,5},{8,10},{9,11},{10,... | collective-permute-start | bytes 1572872 | tf_op jit(solution)/shard_map/ppermute | solution.py:436
  647.2 136.5 %collective-permute-start.40 = (bf16[2,256,1024]{2,1,0:T(8,128)(2,1)}, bf16[2,256,1024]{2,1,0:T(8,128)(2,1)}, u32[]{:S(2)}, u32[]{:S(2)}) collective-permute-start(bf16[2,256,1024]{2,1,0:T(8,128)(2,1)} %get-tuple-element.33), channel_id=1, source_target_pairs={{0,2},{1,3},{2,0},{3,1},{4,6},{5,7},{6,4},{7,5},{8,10},{9,11},{10,... | collective-permute-start | bytes 3145736 | tf_op jit(solution)/shard_map/ppermute | solution.py:436
  652.7 133.2 %collective-permute-start.41 = (bf16[2,256,1024]{2,1,0:T(8,128)(2,1)}, bf16[2,256,1024]{2,1,0:T(8,128)(2,1)}, u32[]{:S(2)}, u32[]{:S(2)}) collective-permute-start(bf16[2,256,1024]{2,1,0:T(8,128)(2,1)} %get-tuple-element.35), channel_id=1, source_target_pairs={{0,1},{1,0},{2,3},{3,2},{4,5},{5,4},{6,7},{7,6},{8,9},{9,8},{10,11... | collective-permute-start | bytes 3145736 | tf_op jit(solution)/shard_map/ppermute | solution.py:436
  667.6 58.6 %copy-start.24 = (f32[256,32]{0,1:T(8,128)S(1)}, f32[256,32]{0,1:T(8,128)}, u32[]{:S(2)}) copy-start(f32[256,32]{0,1:T(8,128)} %copy-done.23) | copy-start | bytes 98308
  667.6 58.6 %copy-start.39 = (pred[256,32]{0,1:T(8,128)(4,1)S(1)}, pred[256,32]{0,1:T(8,128)(4,1)}, u32[]{:S(2)}) copy-start(pred[256,32]{0,1:T(8,128)(4,1)} %copy-done.38) | copy-start | bytes 24580
  667.6 58.6 %copy-start.46 = (f32[256]{0:T(256)S(1)}, f32[256]{0:T(256)}, u32[]{:S(2)}) copy-start(f32[256]{0:T(256)} %copy-done.45) | copy-start | bytes 3076
  667.6 58.6 %copy-start.52 = (f32[256]{0:T(256)S(1)}, f32[256]{0:T(256)}, u32[]{:S(2)}) copy-start(f32[256]{0:T(256)} %copy-done.51) | copy-start | bytes 3076
  667.6 58.7 %copy-start.3 = (f32[256,1024]{1,0:T(8,128)S(1)}, f32[256,1024]{1,0:T(8,128)}, u32[]{:S(2)}) copy-start(f32[256,1024]{1,0:T(8,128)} %copy-done.2) | copy-start | bytes 3145732
  667.6 58.7 %copy-start.44 = (f32[1024]{0:T(1024)S(1)}, f32[1024]{0:T(1024)}, u32[]{:S(2)}) copy-start(f32[1024]{0:T(1024)} %copy-done.43) | copy-start | bytes 12292
  667.6 58.7 %copy-start.54 = (f32[256]{0:T(256)S(1)}, f32[256]{0:T(256)}, u32[]{:S(2)}) copy-start(f32[256]{0:T(256)} %copy-done.53) | copy-start | bytes 3076
  667.7 118.2 %collective-permute-start.42 = (bf16[2,256,1024]{2,1,0:T(8,128)(2,1)}, bf16[2,256,1024]{2,1,0:T(8,128)(2,1)}, u32[]{:S(2)}, u32[]{:S(2)}) collective-permute-start(bf16[2,256,1024]{2,1,0:T(8,128)(2,1)} %get-tuple-element.34), channel_id=1, source_target_pairs={{0,3},{1,2},{2,1},{3,0},{4,7},{5,6},{6,5},{7,4},{8,11},{9,10},{10,... | collective-permute-start | bytes 3145736 | tf_op jit(solution)/shard_map/ppermute | solution.py:436
  669.7 56.3 %collective-permute-start.25 = (bf16[272,1024]{1,0:T(8,128)(2,1)S(1)}, bf16[272,1024]{1,0:T(8,128)(2,1)S(1)}, u32[]{:S(2)}, u32[]{:S(2)}) collective-permute-start(bf16[272,1024]{1,0:T(8,128)(2,1)S(1)} %slice_bitcast_fusion.4), channel_id=1, source_target_pairs={{0,1},{1,0},{2,3},{3,2},{4,5},{5,4},{6,7},{7,6},{8,9},{9,8},{10,11... | collective-permute-start | bytes 1671176 | tf_op jit(solution)/shard_map/ppermute | solution.py:436
  670.7 69.2 %copy-start.7 = (bf16[256,1024]{1,0:T(8,128)(2,1)S(1)}, bf16[256,1024]{1,0:T(8,128)(2,1)}, u32[]{:S(2)}) copy-start(bf16[256,1024]{1,0:T(8,128)(2,1)} %param.25) | copy-start | bytes 1572868
  726.0 13.8 %collective-permute-start.15 = (bf16[256,1024]{1,0:T(8,128)(2,1)S(1)}, bf16[256,1024]{1,0:T(8,128)(2,1)S(1)}, u32[]{:S(2)}, u32[]{:S(2)}) collective-permute-start(bf16[256,1024]{1,0:T(8,128)(2,1)S(1)} %slice_bitcast_fusion.6), channel_id=1, source_target_pairs={{0,1},{1,0},{2,3},{3,2},{4,5},{5,4},{6,7},{7,6},{8,9},{9,8},{10,11... | collective-permute-start | bytes 1572872 | tf_op jit(solution)/shard_map/ppermute | solution.py:436
  779.2 16.6 %collective-permute-start.26 = (bf16[4,4,32,2176]{3,2,1,0:T(8,128)(2,1)S(1)}, bf16[4,4,32,2176]{3,2,1,0:T(8,128)(2,1)S(1)}, u32[]{:S(2)}, u32[]{:S(2)}) collective-permute-start(bf16[4,4,32,2176]{3,2,1,0:T(8,128)(2,1)S(1)} %dynamic-slice_bitcast_fusion), channel_id=1, source_target_pairs={{0,4},{4,0},{8,12},{12,8},{16,20},{20,16},{24,28},{28,24},{1,5},{5... | collective-permute-start | bytes 6684680 | tf_op jit(solution)/shard_map/ppermute | solution.py:432
  783.2 7.3 collective-permute-start.33
  791.0 10.4 %collective-permute-start.34 = (bf16[4,32,1024]{2,1,0:T(8,128)(2,1)S(1)}, bf16[4,32,1024]{2,1,0:T(8,128)(2,1)S(1)}, u32[]{:S(2)}, u32[]{:S(2)}) collective-permute-start(bf16[4,32,1024]{2,1,0:T(8,128)(2,1)S(1)} %get-tuple-element.72), channel_id=1, source_target_pairs={{0,8},{4,12},{8,0},{12,4},{16,24},{20,28},{24,16},{28,20},{1,9},{5... | collective-permute-start | bytes 786440 | tf_op jit(solution)/shard_map/ppermute | solution.py:432
  794.2 14.8 %collective-permute-start.35 = (bf16[4,32,1024]{2,1,0:T(8,128)(2,1)S(1)}, bf16[4,32,1024]{2,1,0:T(8,128)(2,1)S(1)}, u32[]{:S(2)}, u32[]{:S(2)}) collective-permute-start(bf16[4,32,1024]{2,1,0:T(8,128)(2,1)S(1)} %get-tuple-element.74), channel_id=1, source_target_pairs={{0,16},{4,20},{8,24},{12,28},{16,0},{20,4},{24,8},{28,12},{1,17},{... | collective-permute-start | bytes 786440 | tf_op jit(solution)/shard_map/ppermute | solution.py:432
  794.2 14.8 %collective-permute-start.36 = (bf16[4,32,1024]{2,1,0:T(8,128)(2,1)S(1)}, bf16[4,32,1024]{2,1,0:T(8,128)(2,1)S(1)}, u32[]{:S(2)}, u32[]{:S(2)}) collective-permute-start(bf16[4,32,1024]{2,1,0:T(8,128)(2,1)S(1)} %get-tuple-element.73), channel_id=1, source_target_pairs={{0,24},{4,28},{8,16},{12,20},{16,8},{20,12},{24,0},{28,4},{1,25},{... | collective-permute-start | bytes 786440 | tf_op jit(solution)/shard_map/ppermute | solution.py:432
  796.5 22.5 %collective-permute-start.27 = (bf16[4,32,2176]{2,1,0:T(8,128)(2,1)S(1)}, bf16[4,32,2176]{2,1,0:T(8,128)(2,1)S(1)}, u32[]{:S(2)}, u32[]{:S(2)}) collective-permute-start(bf16[4,32,2176]{2,1,0:T(8,128)(2,1)S(1)} %get-tuple-element.49), channel_id=1, source_target_pairs={{0,8},{4,12},{8,0},{12,4},{16,24},{20,28},{24,16},{28,20},{1,9},{5... | collective-permute-start | bytes 1671176 | tf_op jit(solution)/shard_map/ppermute | solution.py:432
  798.5 33.2 %collective-permute-start.28 = (bf16[4,32,2176]{2,1,0:T(8,128)(2,1)S(1)}, bf16[4,32,2176]{2,1,0:T(8,128)(2,1)S(1)}, u32[]{:S(2)}, u32[]{:S(2)}) collective-permute-start(bf16[4,32,2176]{2,1,0:T(8,128)(2,1)S(1)} %get-tuple-element.51), channel_id=1, source_target_pairs={{0,16},{4,20},{8,24},{12,28},{16,0},{20,4},{24,8},{28,12},{1,17},{... | collective-permute-start | bytes 1671176 | tf_op jit(solution)/shard_map/ppermute | solution.py:432
  801.4 30.3 %collective-permute-start.29 = (bf16[4,32,2176]{2,1,0:T(8,128)(2,1)S(1)}, bf16[4,32,2176]{2,1,0:T(8,128)(2,1)S(1)}, u32[]{:S(2)}, u32[]{:S(2)}) collective-permute-start(bf16[4,32,2176]{2,1,0:T(8,128)(2,1)S(1)} %get-tuple-element.50), channel_id=1, source_target_pairs={{0,24},{4,28},{8,16},{12,20},{16,8},{20,12},{24,0},{28,4},{1,25},{... | collective-permute-start | bytes 1671176 | tf_op jit(solution)/shard_map/ppermute | solution.py:432
  809.2 25.3 %collective-permute-start.37 = (bf16[32,1024]{1,0:T(8,128)(2,1)S(1)}, bf16[32,1024]{1,0:T(8,128)(2,1)S(1)}, u32[]{:S(2)}, u32[]{:S(2)}) collective-permute-start(bf16[32,1024]{1,0:T(8,128)(2,1)S(1)} %get-tuple-element.104), channel_id=1, source_target_pairs={{0,1},{1,0},{2,3},{3,2},{4,5},{5,4},{6,7},{7,6},{8,9},{9,8},{10,11... | collective-permute-start | bytes 196616 | tf_op jit(solution)/shard_map/ppermute | solution.py:436
  809.6 26.9 %collective-permute-start.38 = (bf16[32,1024]{1,0:T(8,128)(2,1)S(1)}, bf16[32,1024]{1,0:T(8,128)(2,1)S(1)}, u32[]{:S(2)}, u32[]{:S(2)}) collective-permute-start(bf16[32,1024]{1,0:T(8,128)(2,1)S(1)} %get-tuple-element.106), channel_id=1, source_target_pairs={{0,2},{1,3},{2,0},{3,1},{4,6},{5,7},{6,4},{7,5},{8,10},{9,11},{10,... | collective-permute-start | bytes 196616 | tf_op jit(solution)/shard_map/ppermute | solution.py:436
  819.0 17.5 %collective-permute-start.39 = (bf16[32,1024]{1,0:T(8,128)(2,1)S(1)}, bf16[32,1024]{1,0:T(8,128)(2,1)S(1)}, u32[]{:S(2)}, u32[]{:S(2)}) collective-permute-start(bf16[32,1024]{1,0:T(8,128)(2,1)S(1)} %get-tuple-element.105), channel_id=1, source_target_pairs={{0,3},{1,2},{2,1},{3,0},{4,7},{5,6},{6,5},{7,4},{8,11},{9,10},{10,... | collective-permute-start | bytes 196616 | tf_op jit(solution)/shard_map/ppermute | solution.py:436
  832.1 6.5 collective-permute-start.30
  832.4 12.7 %collective-permute-start.31 = (bf16[32,2176]{1,0:T(8,128)(2,1)S(1)}, bf16[32,2176]{1,0:T(8,128)(2,1)S(1)}, u32[]{:S(2)}, u32[]{:S(2)}) collective-permute-start(bf16[32,2176]{1,0:T(8,128)(2,1)S(1)} %get-tuple-element.93), channel_id=1, source_target_pairs={{0,2},{1,3},{2,0},{3,1},{4,6},{5,7},{6,4},{7,5},{8,10},{9,11},{10,... | collective-permute-start | bytes 417800 | tf_op jit(solution)/shard_map/ppermute | solution.py:436
  834.6 10.5 %collective-permute-start.32 = (bf16[32,2176]{1,0:T(8,128)(2,1)S(1)}, bf16[32,2176]{1,0:T(8,128)(2,1)S(1)}, u32[]{:S(2)}, u32[]{:S(2)}) collective-permute-start(bf16[32,2176]{1,0:T(8,128)(2,1)S(1)} %get-tuple-element.92), channel_id=1, source_target_pairs={{0,3},{1,2},{2,1},{3,0},{4,7},{5,6},{6,5},{7,4},{8,11},{9,10},{10,... | collective-permute-start | bytes 417800 | tf_op jit(solution)/shard_map/ppermute | solution.py:436
  (47 other events, 303.5 us)
Sparse Core Ops, SparseCore 0:
  14.0 73.5 all-gather.1

commit v2 on v0

--- a/solution.py
+++ b/solution.py
@@ -1,6 +1,10 @@
+import functools
+
 import jax
 import jax.numpy as jnp
 from jax import lax
+from jax.experimental import pallas as pl
+from jax.experimental.pallas import tpu as pltpu
 from jax.sharding import PartitionSpec as P
 
 MODEL_WIDTH = 1024
@@ -100,7 +104,7 @@
     return (gate_part, up_part, sigmoid_gate, hidden)
 
 
-def per_device(
+def per_device_general(
     embedded,
     document_numbers,
     expert_ids,
@@ -421,37 +425,585 @@
     )
 
 
+BF16 = jnp.bfloat16
+F32 = jnp.float32
+PAIR = 2
+OWN = 2
+BLOCKS = 16
+
+
+def over_expert(value, bits):
+    return lax.ppermute(value, "expert", [(i, i ^ bits) for i in range(8)])
+
+
+def over_shard(value, bits):
+    return lax.ppermute(value, "shard", [(i, i ^ bits) for i in range(4)])
+
+
+def dot_f32(left, right, dims):
+    return lax.dot_general(left, right, dims, preferred_element_type=F32)
+
+
+CONTRACT_LAST = (((1,), (1,)), ((), ()))
+CONTRACT_FIRST = (((0,), (0,)), ((), ()))
+CONTRACT_PLAIN = (((1,), (0,)), ((), ()))
+STEP_BLOCKS = 2
+STEPS = BLOCKS // STEP_BLOCKS
+STEP_ROWS = STEP_BLOCKS * CAP
+
+
+def expert_body(first_part, number_ref, *refs):
+    if first_part:
+        tok_own, tok_far, out_own, out_far, w_ref = refs[:5]
+        refs = refs[5:]
+        befores = None
+    else:
+        tok_own, tok_far, out_own, out_far, w_ref = refs[:5]
+        befores = refs[5:9]
+        refs = refs[9:]
+    row_own, row_far, moe_own, moe_far, grad_ref, x_s, g_s, gate_s, table_s, back_s, mix_s, dot_s, in_acc, out_acc = refs
+    step = pl.program_id(0)
+    number = number_ref[0]
+    own = step < STEPS // 2
+
+    def mask_of(i):
+        slot = lax.broadcasted_iota(jnp.int32, (CAP, 256), 0).astype(F32)
+        return slot == table_s[i, 0:1, :]
+
+    def load(tok_ref, g_ref):
+        for i in range(STEP_BLOCKS):
+            aux = tok_ref[i, 256:288, :].astype(F32)
+            line = lax.broadcasted_iota(jnp.int32, (EXPERTS, 1024), 0)
+            line = jnp.sum(jnp.where(line == number, aux, 0.0), axis=0, keepdims=True)
+            table_s[i, 0:1, :] = line[:, :256]
+            gate = line[:, 256:512] + line[:, 512:768] + line[:, 768:]
+            mask = mask_of(i)
+            pick = jnp.where(mask, 1.0, 0.0).astype(BF16)
+            at = slice(i * CAP, (i + 1) * CAP)
+            x_s[at, :] = dot_f32(pick, tok_ref[i, 0:256, :], CONTRACT_PLAIN).astype(BF16)
+            g_s[at, :] = resid_scale * dot_f32(pick, g_ref[i], CONTRACT_PLAIN)
+            gate_s[at, :] = jnp.sum(jnp.where(mask, gate, 0.0), axis=1, keepdims=True)
+
+    @pl.when(own)
+    def _():
+        load(tok_own, out_own)
+
+    @pl.when(jnp.logical_not(own))
+    def _():
+        load(tok_far, out_far)
+
+    w_in = w_ref[:, 0:256, :].reshape(1024, 1024)
+    w_out = w_ref[:, 256:384, :].reshape(512, 1024)
+    x = x_s[...]
+    gate_up = dot_f32(x, w_in, CONTRACT_PLAIN)
+    gate_part, up_part = gate_up[:, :FF], gate_up[:, FF:]
+    sigmoid = jax.nn.sigmoid(gate_part)
+    hidden = (gate_part * sigmoid * up_part).astype(BF16)
+    produced = dot_f32(hidden, w_out, CONTRACT_PLAIN).astype(BF16).astype(F32)
+    slot_gate = gate_s[...]
+    scaled = g_s[...]
+    slot_grad = (slot_gate * scaled).astype(BF16)
+    dot_s[...] = jnp.sum(produced * scaled, axis=1, keepdims=True)
+    mix_s[...] = (slot_gate * produced).astype(BF16)
+    hidden_grad = dot_f32(slot_grad, w_out, CONTRACT_LAST)
+    gate_grad = hidden_grad * up_part * sigmoid * (1.0 + gate_part * (1.0 - sigmoid))
+    up_grad = hidden_grad * gate_part * sigmoid
+    gate_up_grad = jnp.concatenate([gate_grad.astype(BF16), up_grad.astype(BF16)], axis=1)
+    back_s[...] = dot_f32(gate_up_grad, w_in, CONTRACT_LAST).astype(BF16)
+    in_part = dot_f32(x, gate_up_grad, CONTRACT_FIRST)
+    out_part = dot_f32(hidden, slot_grad, CONTRACT_FIRST)
+
+    @pl.when(step == 0)
+    def _():
+        in_acc[...] = in_part
+        out_acc[...] = out_part
+
+    @pl.when(step > 0)
+    def _():
+        in_acc[...] += in_part
+        out_acc[...] += out_part
+
+    def store(row_ref, moe_ref, row_before, moe_before):
+        for i in range(STEP_BLOCKS):
+            at = slice(i * CAP, (i + 1) * CAP)
+            mask = mask_of(i)
+            pick = jnp.where(mask, 1.0, 0.0).astype(BF16)
+            rows = dot_f32(pick, back_s[at, :], CONTRACT_FIRST)
+            mixed = dot_f32(pick, mix_s[at, :], CONTRACT_FIRST)
+            dots = jnp.sum(jnp.where(mask, dot_s[at, :], 0.0), axis=0, keepdims=True)
+            high = dots.astype(BF16).astype(F32)
+            low = dots - high
+            wide = jnp.concatenate([high, high, low, low], axis=1)
+            line = lax.broadcasted_iota(jnp.int32, (16, 1024), 0)
+            lane = lax.broadcasted_iota(jnp.int32, (16, 1024), 1) // 256
+            here = (line == number % 16) & (lane % 2 == number // 16)
+            side = jnp.where(here, jnp.broadcast_to(wide, (16, 1024)), 0.0)
+            if row_before is not None:
+                rows = rows + row_before[i, 0:256, :].astype(F32)
+                mixed = mixed + moe_before[i].astype(F32)
+                side = side + row_before[i, 256:272, :].astype(F32)
+            row_ref[i, 0:256, :] = rows.astype(BF16)
+            row_ref[i, 256:272, :] = side.astype(BF16)
+            moe_ref[i] = mixed.astype(BF16)
+
+    own_before, far_before, own_moe_before, far_moe_before = befores or (None,) * 4
+
+    @pl.when(own)
+    def _():
+        store(row_own, moe_own, own_before, own_moe_before)
+
+    @pl.when(jnp.logical_not(own))
+    def _():
+        store(row_far, moe_far, far_before, far_moe_before)
+
+    @pl.when(step == STEPS - 1)
+    def _():
+        for d in range(4):
+            grad_ref[d, 0:256, :] = in_acc[d * 256 : (d + 1) * 256, :].astype(BF16)
+            grad_ref[d, 256:384, :] = out_acc[d * 128 : (d + 1) * 128, :].astype(BF16)
+
+
+def expert_call(number, tok_own, tok_far, out_own, out_far, weights, before=None):
+    half = STEPS // 2
+    own_at = lambda s, n: (jnp.minimum(s, half - 1), 0, 0)
+    far_at = lambda s, n: (jnp.maximum(s - half, 0), 0, 0)
+    whole = lambda s, n: (0, 0, 0)
+    spec = lambda rows, at: pl.BlockSpec((STEP_BLOCKS, rows, 1024), at)
+    w_spec = pl.BlockSpec((4, 384, 1024), whole, pipeline_mode=pl.Buffered(1))
+    outs = [spec(272, own_at), spec(272, far_at), spec(256, own_at), spec(256, far_at)]
+    ins = [spec(288, own_at), spec(288, far_at), spec(256, own_at), spec(256, far_at), w_spec]
+    operands = [tok_own, tok_far, out_own, out_far, weights]
+    aliases = {}
+    if before is not None:
+        ins = ins + outs
+        operands = operands + list(before)
+        aliases = {6 + i: i for i in range(4)}
+    shapes = [jax.ShapeDtypeStruct((8, rows, 1024), BF16) for rows in (272, 272, 256, 256)]
+    rows_f32 = pltpu.VMEM((STEP_ROWS, 1), F32)
+    wide = pltpu.VMEM((STEP_ROWS, 1024), BF16)
+    return pl.pallas_call(
+        functools.partial(expert_body, before is None),
+        out_shape=shapes + [jax.ShapeDtypeStruct((4, 384, 1024), BF16)],
+        grid_spec=pltpu.PrefetchScalarGridSpec(
+            num_scalar_prefetch=1,
+            grid=(STEPS,),
+            in_specs=ins,
+            out_specs=outs + [w_spec],
+            scratch_shapes=[
+                wide, pltpu.VMEM((STEP_ROWS, 1024), F32), rows_f32, pltpu.VMEM((STEP_BLOCKS, 8, 256), F32),
+                wide, wide, rows_f32, pltpu.VMEM((1024, 1024), F32), pltpu.VMEM((512, 1024), F32),
+            ],
+        ),
+        input_output_aliases=aliases,
+        compiler_params=pltpu.CompilerParams(
+            dimension_semantics=("arbitrary",), vmem_limit_bytes=60 * 1024 * 1024
+        ),
+        cost_estimate=pl.CostEstimate(
+            flops=24_000_000_000, bytes_accessed=45_000_000, transcendentals=1_000_000
+        ),
+        name="expert",
+    )(number, *operands)
+
+
+LANES = 128
+GAIN_ATTN = 32
+GAIN_FFN = 33
+SEQUENCE = 256
+
+
+def group_of(e, r):
+    return pl.ds(pl.multiple_of((e ^ r) * LANES, LANES), LANES)
+
+
+def turn_halves(value):
+    lane = lax.broadcasted_iota(jnp.int32, value.shape, 1) % HEAD_SIZE
+    width = value.shape[1]
+    return jnp.where(
+        lane < HEAD_SIZE // 2,
+        -pltpu.roll(value, width - HEAD_SIZE // 2, 1),
+        pltpu.roll(value, HEAD_SIZE // 2, 1),
+    )
+
+
+def wide_table(table, width):
+    return jnp.concatenate([table] * (width // LANES), axis=1)
+
+
+def inverse_rms(value):
+    return lax.rsqrt(jnp.mean(value * value, axis=1, keepdims=True) + norm_eps)
+
+
+def attention_probs(queries, keys, allowed):
+    scores = jnp.where(allowed, dot_f32(queries, keys, CONTRACT_LAST) * attn_scale, -1e30)
+    exps = jnp.exp(scores - jnp.max(scores, axis=1, keepdims=True))
+    return exps / jnp.sum(exps, axis=1, keepdims=True)
+
+
+def allowed_of(column_ref, row_ref):
+    shape = (2 * SEQUENCE, SEQUENCE)
+    query = lax.broadcasted_iota(jnp.int32, shape, 0) % SEQUENCE
+    key = lax.broadcasted_iota(jnp.int32, shape, 1)
+    column = column_ref[...]
+    same = jnp.concatenate([column, column], axis=0) == row_ref[...]
+    return (key <= query) & same
+
+
+def heads_of(block, first, count):
+    return jnp.concatenate(
+        [block[:, HEAD_SIZE * (first + i) : HEAD_SIZE * (first + i + 1)] for i in range(count)], axis=0
+    )
+
+
+def attend_body(e_ref, x_ref, column_ref, row_ref, cos_ref, sin_ref, own_ref, far_ref,
+                normed_ref, q_ref, k_ref, v_ref, mixed_ref):
+    e = e_ref[0]
+    resid = embed_scale * x_ref[...].astype(F32)
+    inverse = inverse_rms(resid)
+    for part, w_ref in ((0, own_ref), (1, far_ref)):
+        gain = w_ref[:, 2048:].astype(F32).T[GAIN_ATTN : GAIN_ATTN + 1, :]
+        for q in range(4):
+            block = embed_scale * x_ref[:, group_of(e, 2 * q + part)].astype(F32)
+            scaled = block * inverse * gain[:, LANES * q : LANES * (q + 1)]
+            at = 512 * part + LANES * q
+            normed_ref[:, at : at + LANES] = scaled.astype(BF16)
+    own = normed_ref[:, :512]
+    far = normed_ref[:, 512:]
+    project = lambda a, b: dot_f32(own, own_ref[:, a:b], CONTRACT_PLAIN) + dot_f32(
+        far, far_ref[:, a:b], CONTRACT_PLAIN
+    )
+    rotate = lambda u: u * wide_table(cos_ref[...], u.shape[1]) + turn_halves(u) * wide_table(
+        sin_ref[...], u.shape[1]
+    )
+    q_ref[...] = rotate(project(0, 1024)).astype(BF16)
+    k_ref[...] = rotate(project(1024, 1536)).astype(BF16)
+    v_ref[...] = project(1536, 2048).astype(BF16)
+    allowed = allowed_of(column_ref, row_ref)
+
+    def pair(step, _):
+        wide = pl.ds(pl.multiple_of(step * 256, 256), 256)
+        narrow = pl.ds(pl.multiple_of(step * LANES, LANES), LANES)
+        q_block, k_block, v_block = q_ref[:, wide], k_ref[:, narrow], v_ref[:, narrow]
+        outs = []
+        for i in range(2):
+            probs = attention_probs(heads_of(q_block, 2 * i, 2), heads_of(k_block, i, 1), allowed)
+            rows = dot_f32(probs.astype(BF16), heads_of(v_block, i, 1), CONTRACT_PLAIN)
+            outs += [rows[:SEQUENCE], rows[SEQUENCE:]]
+        mixed_ref[:, wide] = jnp.concatenate(outs, axis=1).astype(BF16)
+        return 0
+
+    lax.fori_loop(0, 4, pair, 0)
+
+
+def route_body(e_ref, x_ref, mixed_ref, w_own_ref, w_far_ref, small_own_ref, small_far_ref, code_ref,
+               pay_ref, gates_ref, middle_ref, small_ref):
+    e = e_ref[0]
+    total = jnp.zeros((SEQUENCE, 1024), F32)
+    for part, w_ref, s_ref in ((0, w_own_ref, small_own_ref), (1, w_far_ref, small_far_ref)):
+        features = jnp.concatenate([mixed_ref[:, group_of(e, 2 * q + part)] for q in range(4)], axis=1)
+        total = total + dot_f32(features, w_ref[...], CONTRACT_PLAIN)
+        for q in range(4):
+            small_ref[group_of(e, 2 * q + part), :] = s_ref[LANES * q : LANES * (q + 1), :]
+    middle = embed_scale * x_ref[...].astype(F32) + resid_scale * total
+    middle_ref[...] = middle
+    gain = small_ref[...].astype(F32).T[GAIN_FFN : GAIN_FFN + 1, :]
+    normed2 = (middle * inverse_rms(middle) * gain).astype(BF16)
+    pay_ref[0:256, :] = normed2
+    logits = dot_f32(normed2, small_ref[...], CONTRACT_PLAIN)
+    code = code_ref[...]
+    member = code >= 0.0
+    masked = jnp.where(member, logits, -1e30)
+    raised = jnp.where(member, jnp.exp(masked - jnp.max(masked, axis=1, keepdims=True)), 0.0)
+    gates = raised / jnp.sum(raised, axis=1, keepdims=True)
+    gates_ref[...] = gates
+    rows = lambda value: value.T[:EXPERTS, :]
+    turned = rows(gates)
+    high = turned.astype(BF16).astype(F32)
+    middle_part = (turned - high).astype(BF16).astype(F32)
+    low = turned - high - middle_part
+    pay_ref[256:288, :] = jnp.concatenate([rows(code), high, middle_part, low], axis=1).astype(BF16)
+
+
+def turn_body(e_ref, sum_ref, add_ref, grad_ref, middle_ref, gates_ref, small_ref, normed2_ref, mixed_ref,
+              w_own_ref, w_far_ref, own_ref, far_ref, mixed_grad_ref, middle_grad_ref, side_ref):
+    e = e_ref[0]
+    upstream = sum_ref[0:256, :].astype(F32) + add_ref[0:256, :].astype(F32)
+    table = sum_ref[256:272, :].astype(F32) + add_ref[256:272, :].astype(F32)
+    dots = jnp.concatenate([table[:, :256], table[:, 256:512]], axis=0) + jnp.concatenate(
+        [table[:, 512:768], table[:, 768:]], axis=0
+    )
+    dots = jnp.concatenate([dots, jnp.zeros((LANES - EXPERTS, SEQUENCE), F32)], axis=0).T
+    gates = gates_ref[...]
+    logit_grads = (gates * (dots - jnp.sum(gates * dots, axis=1, keepdims=True))).astype(BF16)
+    small = small_ref[...]
+    upstream = upstream + dot_f32(logit_grads, small, CONTRACT_LAST)
+    middle = middle_ref[...]
+    inverse = inverse_rms(middle)
+    unit = middle * inverse
+    gain = small.astype(F32).T[GAIN_FFN : GAIN_FFN + 1, :]
+    gain_grad = jnp.sum(upstream * unit, axis=0, keepdims=True)
+    scaled = upstream * gain
+    middle_grad = grad_ref[...].astype(F32) + inverse * (
+        scaled - unit * jnp.mean(scaled * unit, axis=1, keepdims=True)
+    )
+    middle_grad_ref[...] = middle_grad
+    attn_grad = (resid_scale * middle_grad).astype(BF16)
+    line = lax.broadcasted_iota(jnp.int32, (LANES, 1024), 0)
+    side_ref[...] = dot_f32(normed2_ref[0:256, :], logit_grads, CONTRACT_FIRST) + jnp.where(
+        line == GAIN_FFN, gain_grad, 0.0
+    ).T
+    for part, w_ref, out_ref in ((0, w_own_ref, own_ref), (1, w_far_ref, far_ref)):
+        features = jnp.concatenate([mixed_ref[:, group_of(e, 2 * q + part)] for q in range(4)], axis=1)
+        out_ref[:, :1024] = dot_f32(features, attn_grad, CONTRACT_FIRST).astype(BF16)
+        back = dot_f32(attn_grad, w_ref[...], CONTRACT_LAST).astype(BF16)
+        for q in range(4):
+            mixed_grad_ref[:, group_of(e, 2 * q + part)] = back[:, LANES * q : LANES * (q + 1)]
+            at = slice(LANES * q, LANES * (q + 1))
+            out_ref[at, 1024:] = side_ref[group_of(e, 2 * q + part), :].astype(BF16)
+
+
+def attend_back_body(e_ref, x_ref, column_ref, row_ref, cos_ref, sin_ref, q_ref, k_ref, v_ref, grad_ref,
+                     normed_ref, w_own_ref, w_far_ref, middle_grad_ref,
+                     own_ref, far_ref, embed_ref, raw_ref, scaled_ref):
+    e = e_ref[0]
+    allowed = allowed_of(column_ref, row_ref)
+    unrotate = lambda u: (
+        u * wide_table(cos_ref[...], u.shape[1]) - turn_halves(u) * wide_table(sin_ref[...], u.shape[1])
+    ).astype(BF16)
+
+    def pair(step, _):
+        wide = pl.ds(pl.multiple_of(step * 256, 256), 256)
+        narrow = lambda base: pl.ds(pl.multiple_of(base + step * LANES, LANES), LANES)
+        q_block, d_block = q_ref[:, wide], grad_ref[:, wide]
+        k_block, v_block = k_ref[:, narrow(0)], v_ref[:, narrow(0)]
+        q_outs, k_outs, v_outs = [], [], []
+        for i in range(2):
+            queries, keys = heads_of(q_block, 2 * i, 2), heads_of(k_block, i, 1)
+            upstream = heads_of(d_block, 2 * i, 2)
+            probs = attention_probs(queries, keys, allowed)
+            prob_grads = dot_f32(upstream, heads_of(v_block, i, 1), CONTRACT_LAST)
+            centre = jnp.sum(probs * prob_grads, axis=1, keepdims=True)
+            score_grads = (probs * (prob_grads - centre)).astype(BF16)
+            rows = dot_f32(score_grads, keys, CONTRACT_PLAIN) * attn_scale
+            q_outs += [rows[:SEQUENCE], rows[SEQUENCE:]]
+            k_outs.append(dot_f32(score_grads, queries, CONTRACT_FIRST) * attn_scale)
+            v_outs.append(dot_f32(probs.astype(BF16), upstream, CONTRACT_FIRST))
+        raw_ref[:, wide] = unrotate(jnp.concatenate(q_outs, axis=1))
+        raw_ref[:, narrow(1024)] = unrotate(jnp.concatenate(k_outs, axis=1))
+        raw_ref[:, narrow(1536)] = jnp.concatenate(v_outs, axis=1).astype(BF16)
+        return 0
+
+    lax.fori_loop(0, 4, pair, 0)
+    resid = embed_scale * x_ref[...].astype(F32)
+    inverse = inverse_rms(resid)
+    for part, w_ref, out_ref in ((0, w_own_ref, own_ref), (1, w_far_ref, far_ref)):
+        for c in range(4):
+            at = slice(512 * c, 512 * c + 512)
+            out_ref[:, at] = dot_f32(
+                normed_ref[:, 512 * part : 512 * part + 512], raw_ref[:, at], CONTRACT_FIRST
+            ).astype(BF16)
+        back = dot_f32(raw_ref[...], w_ref[:, :2048], CONTRACT_LAST)
+        gain = w_ref[:, 2048:].astype(F32).T[GAIN_ATTN : GAIN_ATTN + 1, :]
+        gain_grads = []
+        for q in range(4):
+            at = slice(LANES * q, LANES * (q + 1))
+            group = group_of(e, 2 * q + part)
+            unit = embed_scale * x_ref[:, group].astype(F32) * inverse
+            gain_grads.append(jnp.sum(back[:, at] * unit, axis=0, keepdims=True))
+            scaled_ref[:, group] = back[:, at] * gain[:, at]
+        line = lax.broadcasted_iota(jnp.int32, (LANES, 512), 0)
+        side = jnp.where(line == GAIN_ATTN, jnp.concatenate(gain_grads, axis=1), 0.0).T
+        out_ref[:, 2048:] = side.astype(BF16)
+    unit = resid * inverse
+    scaled = scaled_ref[...]
+    resid_grad = middle_grad_ref[...] + inverse * (
+        scaled - unit * jnp.mean(scaled * unit, axis=1, keepdims=True)
+    )
+    embed_ref[...] = (embed_scale * resid_grad).astype(BF16)
+
+
+def local_kernel(body, name, outs, scratch, flops, number, *operands):
+    bytes_moved = sum(a.size * a.dtype.itemsize for a in operands)
+    vmem = pl.BlockSpec(memory_space=pltpu.VMEM)
+    return pl.pallas_call(
+        body,
+        out_shape=[jax.ShapeDtypeStruct(shape, dtype) for shape, dtype in outs],
+        in_specs=[pl.BlockSpec(memory_space=pltpu.SMEM)] + [vmem] * len(operands),
+        out_specs=[vmem] * len(outs),
+        scratch_shapes=[pltpu.VMEM(shape, dtype) for shape, dtype in scratch],
+        compiler_params=pltpu.CompilerParams(vmem_limit_bytes=56 * 1024 * 1024),
+        cost_estimate=pl.CostEstimate(flops=flops, bytes_accessed=bytes_moved, transcendentals=0),
+        name=name,
+    )(number, *operands)
+
+
+def together(*values):
+    return lax.optimization_barrier(values)
+
+
+def plane_gather(value):
+    return jnp.concatenate([value] + [over_expert(value, bits) for bits in (2, 4, 6)])
+
+
+def plane_sum(total):
+    rows = total.shape[0] // 4
+    part = total[:rows].astype(F32)
+    for q in (1, 2, 3):
+        part = part + over_expert(total[rows * q : rows * q + rows], 2 * q).astype(F32)
+    return part.astype(BF16)
+
+
+def core_sum(own, far):
+    return (own.astype(F32) + over_expert(far, 1).astype(F32)).astype(BF16)
+
+
+def xor_order(pieces, at):
+    stacked = jnp.stack(pieces)
+    return jnp.concatenate(
+        [lax.dynamic_index_in_dim(stacked, at ^ i, 0, keepdims=False) for i in range(len(pieces))]
+    )
+
+
+def shard_sum(plane, z):
+    rows = lambda k: lax.dynamic_slice_in_dim(plane, (z ^ k) * 32, 32, 0)
+    result = rows(0).astype(F32)
+    for k in (1, 2, 3):
+        result = result + over_shard(rows(k), k).astype(F32)
+    return result
+
+
+def exchange(slices):
+    return lax.all_to_all(slices, "shard", split_axis=0, concat_axis=0, tiled=True)
+
+
+def expert_slices(expert_in, expert_out, part):
+    chosen = [OWN * (d % PAIR) + part for d in range(4)]
+    return jnp.stack([jnp.concatenate([expert_in[c], expert_out[c]]) for c in chosen])
+
+
+def per_device_fast(
+    embedded,
+    document_numbers,
+    expert_ids,
+    attn_gain,
+    ffn_gain,
+    w_query,
+    key_projection,
+    value_projection,
+    w_out,
+    w_router,
+    expert_in,
+    expert_out,
+    cotangent,
+):
+    e = lax.axis_index("expert")
+    z = lax.axis_index("shard")
+    place = e.reshape(1)
+    zeros = jnp.zeros((32, LANES - EXPERTS - 2), F32)
+    small = [w_router, attn_gain[:, None], ffn_gain[:, None], zeros]
+    pack = jnp.concatenate([w_query, key_projection, value_projection] + small + [w_out], axis=1)
+    pack = pack.astype(BF16)
+    plane = xor_order([pack] + [over_shard(pack, k) for k in (1, 2, 3)], z)
+    slices = [expert_slices(expert_in, expert_out, part) for part in range(OWN)]
+    plane, out_grad, slices[0] = together(plane, cotangent, slices[0])
+    weights0 = exchange(slices[0])
+    out_pair = jnp.stack([out_grad, over_shard(out_grad, 1)])
+    in_own = plane_gather(plane[:, :2176])
+    in_own, plane = together(in_own, plane)
+    in_far = over_expert(in_own, 1)
+    in_far, weights0 = together(in_far, weights0)
+    out_w_own = plane_gather(plane[:, 2176:])
+    out_w_own, out_pair = together(out_w_own, out_pair)
+    out_w_far = over_expert(out_w_own, 1)
+    out_own = plane_gather(out_pair)
+
+    segments = document_numbers[0]
+    column, row = segments[:, None], segments[None, :]
+    cosine, sine = (jnp.concatenate([table] * 4, axis=1) for table in rope_tables(segments))
+    lanes = jnp.arange(LANES, dtype=jnp.int32)
+    member = jnp.any(expert_ids[:, :, None] == lanes, axis=1)
+    index = jnp.arange(SEQUENCE, dtype=jnp.int32)
+    below = (index[None, :] < index[:, None]).astype(BF16)
+    rank = jnp.dot(below, member.astype(BF16), preferred_element_type=F32)
+    code = jnp.where(member, rank, -1.0)
+
+    wide, half = (SEQUENCE, 1024), (SEQUENCE, 512)
+    normed, queries, keys, values, mixed = local_kernel(
+        attend_body, "attend", [(wide, BF16), (wide, BF16), (half, BF16), (half, BF16), (wide, BF16)], [],
+        4_000_000_000, place, embedded, column, row, cosine, sine, in_own, in_far,
+    )
+    payload, gates, middle, small_all = local_kernel(
+        route_body, "route",
+        [((288, 1024), BF16), ((SEQUENCE, LANES), F32), (wide, F32), ((1024, LANES), BF16)], [],
+        2_000_000_000, place, embedded, mixed, out_w_own, out_w_far, in_own[:, 2048:], in_far[:, 2048:], code,
+    )
+    pay_pair = jnp.stack([payload, over_shard(payload, 1)])
+    pay_pair, slices[1] = together(pay_pair, slices[1])
+    weights1 = exchange(slices[1])
+    tok_own = plane_gather(pay_pair)
+    tok_own, out_own = together(tok_own, out_own)
+    tok_far, out_far = over_expert(tok_own, 1), over_expert(out_own, 1)
+    tok_far, weights1 = together(tok_far, weights1)
+    first = (e * 4 + z % PAIR * OWN).reshape(1)
+    operands = (tok_own, tok_far, out_own, out_far)
+    *sums, expert_grad0 = expert_call(first, *operands, weights0)
+    row_own, row_far, moe_own, moe_far, expert_grad1 = expert_call(first + 1, *operands, weights1, sums)
+    slices0 = exchange(expert_grad0)
+    slices0, row_far, expert_grad1 = together(slices0, row_far, expert_grad1)
+    slices1 = exchange(expert_grad1)
+    row_half = core_sum(row_own, row_far)
+    row_half, moe_own, moe_far = together(row_half, moe_own, moe_far)
+    moe_half = core_sum(moe_own, moe_far)
+    row_pair = plane_sum(row_half)
+    row_pair, moe_half, slices1 = together(row_pair, moe_half, slices1)
+    returned = over_shard(row_pair[1], 1)
+    moe_pair = plane_sum(moe_half)
+    moe_other = over_shard(moe_pair[1], 1)
+    early_own, early_far, mixed_grad, middle_grad = local_kernel(
+        turn_body, "turn", [((512, 1152), BF16), ((512, 1152), BF16), (wide, BF16), (wide, F32)],
+        [((1024, LANES), F32)], 4_000_000_000, place, row_pair[0], returned, cotangent, middle, gates,
+        small_all, payload, mixed, out_w_own, out_w_far,
+    )
+    late_own, late_far, grad_embedded = local_kernel(
+        attend_back_body, "attend_back", [((512, 2176), BF16), ((512, 2176), BF16), (wide, BF16)],
+        [((SEQUENCE, 2048), BF16), (wide, F32)], 8_000_000_000, place, embedded, column, row, cosine, sine,
+        queries, keys, values, mixed_grad, normed, in_own, in_far, middle_grad,
+    )
+    early_plane = plane_sum(core_sum(early_own, early_far))
+    late_plane = plane_sum(core_sum(late_own, late_far))
+    early = shard_sum(early_plane, z)
+    late = shard_sum(late_plane, z)
+    slices0, slices1 = slices0.astype(F32), slices1.astype(F32)
+    expert_grads = jnp.stack(
+        [slices0[0] + slices0[2], slices1[0] + slices1[2], slices0[1] + slices0[3], slices1[1] + slices1[3]]
+    )
+    grad_expert_in, grad_expert_out = expert_grads[:, :256], expert_grads[:, 256:]
+    moe = moe_pair[0].astype(F32) + moe_other.astype(F32)
+    output = (middle + resid_scale * moe).astype(BF16)
+    return (
+        output,
+        grad_embedded,
+        late[:, 2048 + GAIN_ATTN],
+        early[:, 1024 + GAIN_FFN],
+        late[:, :1024],
+        late[:, 1024:1536],
+        late[:, 1536:2048],
+        early[:, :1024],
+        early[:, 1024 : 1024 + EXPERTS],
+        grad_expert_in,
+        grad_expert_out,
+    )
+
+
 def solution(mesh):
+    owners, shards = mesh.shape["expert"], mesh.shape["shard"]
+    fast = owners == 8 and shards == 4
+    both = ("expert", "shard")
+    rows = P(both, None)
+    weights = P("expert", "shard", None)
     return jax.shard_map(
-        per_device,
+        per_device_fast if fast else per_device_general,
         mesh=mesh,
-        in_specs=(
-            P(("expert", "shard"), None),
-            P(("expert", "shard"), None),
-            P(("expert", "shard"), None),
-            P(("expert", "shard")),
-            P(("expert", "shard")),
-            P(("expert", "shard"), None),
-            P(("expert", "shard"), None),
-            P(("expert", "shard"), None),
-            P(("expert", "shard"), None),
-            P(("expert", "shard"), None),
-            P("expert", "shard", None),
-            P("expert", "shard", None),
-            P(("expert", "shard"), None),
-        ),
-        out_specs=(
-            P(("expert", "shard"), None),
-            P(("expert", "shard"), None),
-            P(("expert", "shard")),
-            P(("expert", "shard")),
-            P(("expert", "shard"), None),
-            P(("expert", "shard"), None),
-            P(("expert", "shard"), None),
-            P(("expert", "shard"), None),
-            P(("expert", "shard"), None),
-            P("expert", "shard", None),
-            P("expert", "shard", None),
-        ),
+        in_specs=(rows,) * 3 + (P(both),) * 2 + (rows,) * 5 + (weights,) * 2 + (rows,),
+        out_specs=(rows,) * 2 + (P(both),) * 2 + (rows,) * 5 + (weights,) * 2,
         check_vma=False,
     )

time: 1730 us -> 584 us (0.34)
  waiting for transfers between devices: 1090 us -> 279 us
  blocking collectives: 247 us -> 0 us
  local copies, waits for them, and re-layouts: 162 us -> 27.6 us
  matrix products: 130 us -> 0.84 us
  Pallas kernels: 0 us -> 128 us
  starting transfers between devices: 16.2 us -> 66.3 us
    reduce_scatter x7 -> x0, waiting for transfers between devices: 675 us -> none  [the longest x1 150 us: per_device(): lax.psum_scatter(grad_query_full, ('expert', 'shard'), scatter_dimension=...]
    ppermute x0 -> x45, waiting for transfers between devices: none -> 224 us  [the longest x32 172 us: over_expert(): return lax.ppermute(value, 'expert', [(i, i ^ bits) for i in range(8)])]
    all_gather x6 -> x0, waiting for transfers between devices: 211 us -> none  [the longest x1 56.9 us: per_device(): lax.all_gather(w_query.astype(jnp.bfloat16), ('expert', 'shard'), axis=0,...]
    all_to_all x3 -> x4, waiting for transfers between devices: 206 us -> 54.6 us  [exchange(): lax.all_to_all(slices, 'shard', split_axis=0, concat_axis=0, tiled=True)]
    dot_general x29 -> x1, matrix products: 130 us -> 0.84 us  [per_device_fast(): rank = jnp.dot(below, member.astype(BF16), preferred_element_type=F32)]
    pallas_call x0 -> x6, Pallas kernels: none -> 128 us  [the longest x2 91.2 us: expert_call(): pl.pallas_call(functools.partial(expert_body, before is None), out_shape=...]
    all_to_all x1 -> x0, blocking collectives: 97.8 us -> none  [per_device(): lax.all_to_all(grad_send, 'expert', split_axis=0, concat_axis=2, tiled=True)]
    unnamed x2 -> x0, blocking collectives: 79 us -> none
  transfers between devices with their start and end apart: 16 -> 49, of which waited for: 13 -> 28; matrix products, arithmetic and copies ran while one was open for 14% -> 14% of each run, Pallas kernels for 0% -> 14%
where the time goes in v2:
time: 584 us; the launch traced here: 576 us
  waiting for transfers between devices  279 us (48%)
  Pallas kernels  128 us (22%)
  other arithmetic  72.4 us (12%)
  starting transfers between devices  66.3 us (11%)
  local copies, waits for them, and re-layouts  27.6 us (5%)
    ppermute x32, waiting for transfers between devices, over_expert(): return lax.ppermute(value, 'expert', [(i, i ^ bits) for i in range(8)])  172 us
    pallas_call x2, Pallas kernels, expert_call(): pl.pallas_call(functools.partial(expert_body, before is None), out_shape=...  91.2 us
    all_to_all x4, waiting for transfers between devices, exchange(): lax.all_to_all(slices, 'shard', split_axis=0, concat_axis=0, tiled=True)  54.6 us
    ppermute x13, waiting for transfers between devices, over_shard(): return lax.ppermute(value, 'shard', [(i, i ^ bits) for i in range(4)])  52.1 us
    pallas_call x4, Pallas kernels, local_kernel(): pl.pallas_call(body, out_shape=[jax.ShapeDtypeStruct(shape, dtype) for sh...  37 us
    ppermute x32, starting transfers between devices, over_expert(): return lax.ppermute(value, 'expert', [(i, i ^ bits) for i in range(8)])  28.5 us
    ppermute x13, starting transfers between devices, over_shard(): return lax.ppermute(value, 'shard', [(i, i ^ bits) for i in range(4)])  19.1 us
    all_to_all x4, starting transfers between devices, exchange(): lax.all_to_all(slices, 'shard', split_axis=0, concat_axis=0, tiled=True)  18.7 us
  transfers between devices with their start and end apart: 49, of which 28 were waited for; matrix products, arithmetic and copies ran while one was open for 14% of the time, Pallas kernels for 14%

profile of v2, /device:TPU:0, one launch (start us, length us, event | category | flops | bytes accessed | tf_op | source)
XLA Modules:
  0.0 575.6 jit_solution(1126190032524293381)
XLA Ops:
  7.5 5.1 collective-permute-start.2
  16.8 1.5 convert_bitcast_fusion.8
  18.3 1.5 convert_bitcast_fusion.4
  22.8 1.5 maximum_bitcast_fusion
  24.5 1.9 pad_maximum_fusion.3
  26.4 3.9 collective-permute-done.1
  31.7 4.7 all-to-all-start
  36.4 2.5 collective-permute-start.5
  40.0 12.9 %collective-permute-done.5 = bf16[128,2176]{1,0:T(8,128)(2,1)S(1)} collective-permute-done((bf16[128,2176]{1,0:T(8,128)(2,1)S(1)}, bf16[128,2176]{1,0:T(8,128)(2,1)S(1)}, u32[]{:S(2)}, u32[]{:S(2)}) %collective-permute-start.5) | collective-permute-done | bytes 557088 | tf_op jit(solution)/shard_map/ppermute | solution.py:436
  52.9 10.1 %collective-permute-done.4 = bf16[128,2176]{1,0:T(8,128)(2,1)S(1)} collective-permute-done((bf16[128,2176]{1,0:T(8,128)(2,1)S(1)}, bf16[128,2176]{1,0:T(8,128)(2,1)S(1)}, u32[]{:S(2)}, u32[]{:S(2)}) %collective-permute-start.4) | collective-permute-done | bytes 557088 | tf_op jit(solution)/shard_map/ppermute | solution.py:436
  63.1 1.6 pad_maximum_fusion.5.own_ref.w_own_ref
  64.8 1.8 collective-permute-start.10
  67.2 1.7 collective-permute-start.9
  72.5 25.6 %collective-permute-done.10 = bf16[256,1024]{1,0:T(8,128)(2,1)S(1)} collective-permute-done((bf16[256,1024]{1,0:T(8,128)(2,1)}, bf16[256,1024]{1,0:T(8,128)(2,1)S(1)}, u32[]{:S(2)}, u32[]{:S(2)}) %collective-permute-start.10) | collective-permute-done | bytes 524320 | tf_op jit(solution)/shard_map/ppermute | solution.py:440
  105.8 1.6 slice.180.small_own_ref
  107.3 2.4 collective-permute-start.18
  109.8 9.7 %attend.1 = (bf16[256,1024]{1,0:T(8,128)(2,1)}, bf16[256,1024]{1,0:T(8,128)(2,1)}, bf16[256,512]{1,0:T(8,128)(2,1)}, bf16[256,512]{1,0:T(8,128)(2,1)}, bf16[256,1024]{1,0:T(8,128)(2,1)}) custom-call(s32[1]{0:T(128)} %bitcast.e_ref, bf16[256,1024]{1,0:T(8,128)(2,1)} %x_ref.5, s32[256,1]{1,0:T(8,128)} %copy.44.column_ref, s32[1,256]{1,0:T(1,128)} %row_ref.3, ...), custom_call_target="tpu_custom_call" | custom-call | flops 4000000000 | bytes 5244928 | tf_op jit(solution)/shard_map/attend/pallas_call | solution.py:827
  119.5 1.6 slice.181.small_far_ref
  121.1 4.5 route.1
  125.6 2.4 collective-permute-start.12
  129.2 1.9 pad_maximum_fusion.4
  131.1 10.8 %collective-permute-done.12 = bf16[288,1024]{1,0:T(8,128)(2,1)S(1)} collective-permute-done((bf16[288,1024]{1,0:T(8,128)(2,1)}, bf16[288,1024]{1,0:T(8,128)(2,1)S(1)}, u32[]{:S(2)}, u32[]{:S(2)}) %collective-permute-start.12) | collective-permute-done | bytes 589856 | tf_op jit(solution)/shard_map/ppermute | solution.py:440
  145.6 11.3 %collective-permute-done.17 = bf16[2,256,1024]{2,1,0:T(8,128)(2,1)S(1)} collective-permute-done((bf16[2,256,1024]{2,1,0:T(8,128)(2,1)S(1)}, bf16[2,256,1024]{2,1,0:T(8,128)(2,1)S(1)}, u32[]{:S(2)}, u32[]{:S(2)}) %collective-permute-start.17) | collective-permute-done | bytes 1048608 | tf_op jit(solution)/shard_map/ppermute | solution.py:436
  156.8 3.3 pad_maximum_fusion.2.refs_2_
  160.1 6.3 %all-to-all-start.1 = ((bf16[4,384,1024]{2,1,0:T(8,128)(2,1)}), bf16[4,384,1024]{2,1,0:T(8,128)(2,1)}, u32[]{:S(2)}, u32[]{:S(2)}) async-start(bf16[4,384,1024]{2,1,0:T(8,128)(2,1)} %pad_maximum_fusion.4), calls=%async_computation.1 | async-start | bytes 6291456 | tf_op jit(solution)/shard_map/all_to_all | solution.py:875
  166.4 15.7 %collective-permute-done.15 = bf16[2,288,1024]{2,1,0:T(8,128)(2,1)S(1)} collective-permute-done((bf16[2,288,1024]{2,1,0:T(8,128)(2,1)S(1)}, bf16[2,288,1024]{2,1,0:T(8,128)(2,1)S(1)}, u32[]{:S(2)}, u32[]{:S(2)}) %collective-permute-start.15) | collective-permute-done | bytes 1179680 | tf_op jit(solution)/shard_map/ppermute | solution.py:436
  182.1 24.8 %collective-permute-done.14 = bf16[2,288,1024]{2,1,0:T(8,128)(2,1)} collective-permute-done((bf16[2,288,1024]{2,1,0:T(8,128)(2,1)S(1)}, bf16[2,288,1024]{2,1,0:T(8,128)(2,1)}, u32[]{:S(2)}, u32[]{:S(2)}) %collective-permute-start.14) | collective-permute-done | bytes 1179680 | tf_op jit(solution)/shard_map/ppermute | solution.py:436
  207.1 4.4 pad_maximum_fusion.1.refs_0_
  212.0 26.1 %all-to-all-done.1.refs_4_ = bf16[4,384,1024]{2,1,0:T(8,128)(2,1)} async-done(((bf16[4,384,1024]{2,1,0:T(8,128)(2,1)}), bf16[4,384,1024]{2,1,0:T(8,128)(2,1)}, u32[]{:S(2)}, u32[]{:S(2)}) %all-to-all-start.1) | async-done | bytes 3145760 | tf_op jit(solution)/shard_map/all_to_all | solution.py:875
  238.1 44.9 %expert.2 = (bf16[8,272,1024]{2,1,0:T(8,128)(2,1)}, bf16[8,272,1024]{2,1,0:T(8,128)(2,1)}, bf16[8,256,1024]{2,1,0:T(8,128)(2,1)}, bf16[8,256,1024]{2,1,0:T(8,128)(2,1)}, bf16[4,384,1024]{2,1,0:T(8,128)(2,1)}) custom-call(s32[1]{0:T(128)} %bitcast.28.number_ref, bf16[8,288,1024]{2,1,0:T(8,128)(2,1)} %pad_maximum_fusion.1.refs_0_, ...), custom_call_target="tpu_custom_call" | custom-call | flops 24000000000 | bytes 45000000 | tf_op jit(solution)/shard_map/expert/pallas_call | solution.py:584
  283.0 3.9 all-to-all-start.2
  286.9 46.3 %expert.3 = (bf16[8,272,1024]{2,1,0:T(8,128)(2,1)}, bf16[8,272,1024]{2,1,0:T(8,128)(2,1)}, bf16[8,256,1024]{2,1,0:T(8,128)(2,1)}, bf16[8,256,1024]{2,1,0:T(8,128)(2,1)}, bf16[4,384,1024]{2,1,0:T(8,128)(2,1)}) custom-call(s32[1]{0:T(128)S(6)} %add.134.number_ref, ...), custom_call_target="tpu_custom_call", output_to_operand_aliasing={{0}: (6, {}), {1}: (7, {}), {2}: (8, {}), {3}: (9, {})} | custom-call | flops 24000000000 | bytes 45000000 | tf_op jit(solution)/shard_map/expert/pallas_call | solution.py:584
  333.2 24.8 %all-to-all-done.2 = bf16[4,384,1024]{2,1,0:T(8,128)(2,1)S(1)} async-done(((bf16[4,384,1024]{2,1,0:T(8,128)(2,1)}), bf16[4,384,1024]{2,1,0:T(8,128)(2,1)S(1)}, u32[]{:S(2)}, u32[]{:S(2)}) %all-to-all-start.2) | async-done | bytes 3145760 | tf_op jit(solution)/shard_map/all_to_all | solution.py:875
  358.0 7.7 %collective-permute-done.21 = bf16[8,272,1024]{2,1,0:T(8,128)(2,1)S(1)} collective-permute-done((bf16[8,272,1024]{2,1,0:T(8,128)(2,1)}, bf16[8,272,1024]{2,1,0:T(8,128)(2,1)S(1)}, u32[]{:S(2)}, u32[]{:S(2)}) %collective-permute-start.21) | collective-permute-done | bytes 4456480 | tf_op jit(solution)/shard_map/ppermute | solution.py:436
  365.8 6.7 %add_convert_fusion = bf16[8,272,1024]{2,1,0:T(8,128)(2,1)} fusion(bf16[8,272,1024]{2,1,0:T(8,128)(2,1)S(1)} %collective-permute-done.21, bf16[8,272,1024]{2,1,0:T(8,128)(2,1)} %get-tuple-element.83), kind=kLoop, calls=%fused_computation | loop fusion | flops 8912896 | bytes 13369344 | tf_op jit(solution)/shard_map/convert_element_type | solution.py:856
  372.6 3.9 all-to-all-start.3
  376.5 3.8 fusion.6
  383.7 5.3 convert_element_type.200
  389.0 19.0 %collective-permute-done.22 = bf16[2,272,1024]{2,1,0:T(8,128)(2,1)} collective-permute-done((bf16[2,272,1024]{2,1,0:T(8,128)(2,1)}, bf16[2,272,1024]{2,1,0:T(8,128)(2,1)}, u32[]{:S(2)}, u32[]{:S(2)}) %collective-permute-start.22) | collective-permute-done | bytes 1114144 | tf_op jit(solution)/shard_map/ppermute | solution.py:436
  408.0 24.3 %collective-permute-done.24 = bf16[2,272,1024]{2,1,0:T(8,128)(2,1)} collective-permute-done((bf16[2,272,1024]{2,1,0:T(8,128)(2,1)}, bf16[2,272,1024]{2,1,0:T(8,128)(2,1)}, u32[]{:S(2)}, u32[]{:S(2)}) %collective-permute-start.24) | collective-permute-done | bytes 1114144 | tf_op jit(solution)/shard_map/ppermute | solution.py:436
  433.7 4.2 add_convert_fusion.4
  437.9 6.3 %add_convert_fusion.1 = bf16[8,256,1024]{2,1,0:T(8,128)(2,1)} fusion(bf16[8,256,1024]{2,1,0:T(8,128)(2,1)} %collective-permute-done.25, bf16[8,256,1024]{2,1,0:T(8,128)(2,1)S(1)} %copy-done.5), kind=kLoop, calls=%fused_computation.1 | loop fusion | flops 8388608 | bytes 12582912 | tf_op jit(solution)/shard_map/convert_element_type | solution.py:856
  444.3 3.7 all-to-all-done.3
  447.9 2.9 slice_bitcast_fusion
  450.9 5.1 slice_add_fusion.3
  456.0 1.8 fusion.7
  462.0 2.9 collective-permute-done.30.add_ref
  465.8 6.1 %turn.1 = (bf16[512,1152]{1,0:T(8,128)(2,1)}, bf16[512,1152]{1,0:T(8,128)(2,1)}, bf16[256,1024]{1,0:T(8,128)(2,1)}, f32[256,1024]{1,0:T(8,128)}) custom-call(s32[1]{0:T(128)} %bitcast.e_ref, bf16[272,1024]{1,0:T(8,128)(2,1)} %get-tuple-element.132.sum_ref, bf16[272,1024]{1,0:T(8,128)(2,1)} %copy-done.26, bf16[256,1024]{1,0:T(8,128)(2,1)} %grad_ref.1, ...), custom_call_target="tpu_custom_call" | custom-call | flops 4000000000 | bytes 6291456 | tf_op jit(solution)/shard_map/turn/pallas_call | solution.py:827
  471.8 16.7 %attend_back.1 = (bf16[512,2176]{1,0:T(8,128)(2,1)}, bf16[512,2176]{1,0:T(8,128)(2,1)}, bf16[256,1024]{1,0:T(8,128)(2,1)}) custom-call(s32[1]{0:T(128)} %bitcast.e_ref, bf16[256,1024]{1,0:T(8,128)(2,1)} %x_ref.5, s32[256,1]{1,0:T(8,128)} %copy.44.column_ref, s32[1,256]{1,0:T(1,128)} %row_ref.3, f32[256,128]{1,0:T(8,128)} %get-tuple-element.155.cos_ref, ...), custom_call_target="tpu_custom_call" | custom-call | flops 8000000000 | bytes 8390656 | tf_op jit(solution)/shard_map/attend_back/pallas_call | solution.py:827
  489.0 17.2 %collective-permute-done.28 = bf16[2,256,1024]{2,1,0:T(8,128)(2,1)} collective-permute-done((bf16[2,256,1024]{2,1,0:T(8,128)(2,1)}, bf16[2,256,1024]{2,1,0:T(8,128)(2,1)}, u32[]{:S(2)}, u32[]{:S(2)}) %collective-permute-start.28) | collective-permute-done | bytes 1048608 | tf_op jit(solution)/shard_map/ppermute | solution.py:436
  507.6 3.1 add_convert_fusion.5
  510.7 1.7 collective-permute-start.29
  514.2 2.6 slice.248
  516.8 1.6 pad_maximum_fusion.6
  518.4 3.5 collective-permute-done.29
  522.9 1.7 add_convert_fusion.3
  524.7 1.6 collective-permute-start.39
  528.9 1.6 collective-permute-start.32
  530.9 3.7 collective-permute-done.39
  535.1 5.8 %collective-permute-done.41 = bf16[128,1152]{1,0:T(8,128)(2,1)S(1)} collective-permute-done((bf16[128,1152]{1,0:T(8,128)(2,1)S(1)}, bf16[128,1152]{1,0:T(8,128)(2,1)S(1)}, u32[]{:S(2)}, u32[]{:S(2)}) %collective-permute-start.41) | collective-permute-done | bytes 294944 | tf_op jit(solution)/shard_map/ppermute | solution.py:436
  543.9 9.0 %collective-permute-done.32 = bf16[128,2176]{1,0:T(8,128)(2,1)S(1)} collective-permute-done((bf16[128,2176]{1,0:T(8,128)(2,1)S(1)}, bf16[128,2176]{1,0:T(8,128)(2,1)S(1)}, u32[]{:S(2)}, u32[]{:S(2)}) %collective-permute-start.32) | collective-permute-done | bytes 557088 | tf_op jit(solution)/shard_map/ppermute | solution.py:436
  554.2 6.1 %collective-permute-done.34 = bf16[128,2176]{1,0:T(8,128)(2,1)S(1)} collective-permute-done((bf16[128,2176]{1,0:T(8,128)(2,1)S(1)}, bf16[128,2176]{1,0:T(8,128)(2,1)S(1)}, u32[]{:S(2)}, u32[]{:S(2)}) %collective-permute-start.34) | collective-permute-done | bytes 557088 | tf_op jit(solution)/shard_map/ppermute | solution.py:436
  567.6 2.5 collective-permute-done.37
  570.0 3.0 collective-permute-done.36
  (179 shorter events, 66.3 us)
Async XLA Ops:
  0.6 20.0 %copy-start.9 = (bf16[4,128,1024]{2,1,0:T(8,128)(2,1)S(1)}, bf16[4,128,1024]{2,1,0:T(8,128)(2,1)}, u32[]{:S(2)}) copy-start(bf16[4,128,1024]{2,1,0:T(8,128)(2,1)} %param.24) | copy-start | bytes 3145732
  0.7 20.9 %copy-start.7 = (bf16[4,256,1024]{2,1,0:T(8,128)(2,1)S(1)}, bf16[4,256,1024]{2,1,0:T(8,128)(2,1)}, u32[]{:S(2)}) copy-start(bf16[4,256,1024]{2,1,0:T(8,128)(2,1)} %param.23) | copy-start | bytes 6291460
  7.5 18.9 %collective-permute-start.2 = (bf16[32,3200]{1,0:T(8,128)(2,1)}, bf16[32,3200]{1,0:T(8,128)(2,1)}, u32[]{:S(2)}, u32[]{:S(2)}) collective-permute-start(bf16[32,3200]{1,0:T(8,128)(2,1)} %concatenate.82), channel_id=1, source_target_pairs={{0,3},{1,2},{2,1},{3,0},{4,7},{5,6},{6,5},{7,4},{8,11},{9,10},{10,... | collective-permute-start | bytes 614408 | tf_op jit(solution)/shard_map/ppermute | solution.py:440
  12.6 17.7 %collective-permute-start.1 = (bf16[32,3200]{1,0:T(8,128)(2,1)}, bf16[32,3200]{1,0:T(8,128)(2,1)}, u32[]{:S(2)}, u32[]{:S(2)}) collective-permute-start(bf16[32,3200]{1,0:T(8,128)(2,1)} %concatenate.82), channel_id=1, source_target_pairs={{0,2},{1,3},{2,0},{3,1},{4,6},{5,7},{6,4},{7,5},{8,10},{9,11},{10,... | collective-permute-start | bytes 614408 | tf_op jit(solution)/shard_map/ppermute | solution.py:440
  12.6 17.7 %collective-permute-start = (bf16[32,3200]{1,0:T(8,128)(2,1)}, bf16[32,3200]{1,0:T(8,128)(2,1)}, u32[]{:S(2)}, u32[]{:S(2)}) collective-permute-start(bf16[32,3200]{1,0:T(8,128)(2,1)} %concatenate.82), channel_id=1, source_target_pairs={{0,1},{1,0},{2,3},{3,2},{4,5},{5,4},{6,7},{7,6},{8,9},{9,8},{10,11... | collective-permute-start | bytes 614408 | tf_op jit(solution)/shard_map/ppermute | solution.py:440
  31.7 78.1 %all-to-all-start = ((bf16[4,384,1024]{2,1,0:T(8,128)(2,1)}), bf16[4,384,1024]{2,1,0:T(8,128)(2,1)}, u32[]{:S(2)}, u32[]{:S(2)}) async-start(bf16[4,384,1024]{2,1,0:T(8,128)(2,1)} %pad_maximum_fusion.3), calls=%async_computation | async-start | bytes 6291456 | tf_op jit(solution)/shard_map/all_to_all | solution.py:875
  36.4 28.3 %copy-start.24 = (s32[1,256]{1,0:T(1,128)S(1)}, s32[1,256]{1,0:T(1,128)}, u32[]{:S(2)}) copy-start(s32[1,256]{1,0:T(1,128)} %row_ref.3) | copy-start | bytes 3076
  36.4 35.2 %copy-start.25 = (s32[256,8]{0,1:T(8,128)S(1)}, s32[256,8]{0,1:T(8,128)}, u32[]{:S(2)}) copy-start(s32[256,8]{0,1:T(8,128)} %param.15) | copy-start | bytes 24580
  36.4 16.5 %collective-permute-start.5 = (bf16[128,2176]{1,0:T(8,128)(2,1)S(1)}, bf16[128,2176]{1,0:T(8,128)(2,1)S(1)}, u32[]{:S(2)}, u32[]{:S(2)}) collective-permute-start(bf16[128,2176]{1,0:T(8,128)(2,1)S(1)} %slice.178), channel_id=1, source_target_pairs={{0,24},{4,28},{8,16},{12,20},{16,8},{20,12},{24,0},{28,4},{1,25},{... | collective-permute-start | bytes 1671176 | tf_op jit(solution)/shard_map/ppermute | solution.py:436
  39.0 24.1 %collective-permute-start.4 = (bf16[128,2176]{1,0:T(8,128)(2,1)S(1)}, bf16[128,2176]{1,0:T(8,128)(2,1)S(1)}, u32[]{:S(2)}, u32[]{:S(2)}) collective-permute-start(bf16[128,2176]{1,0:T(8,128)(2,1)S(1)} %slice.178), channel_id=1, source_target_pairs={{0,16},{4,20},{8,24},{12,28},{16,0},{20,4},{24,8},{28,12},{1,17},{... | collective-permute-start | bytes 1671176 | tf_op jit(solution)/shard_map/ppermute | solution.py:436
  39.5 23.7 %collective-permute-start.3 = (bf16[128,2176]{1,0:T(8,128)(2,1)S(1)}, bf16[128,2176]{1,0:T(8,128)(2,1)S(1)}, u32[]{:S(2)}, u32[]{:S(2)}) collective-permute-start(bf16[128,2176]{1,0:T(8,128)(2,1)S(1)} %slice.178), channel_id=1, source_target_pairs={{0,8},{4,12},{8,0},{12,4},{16,24},{20,28},{24,16},{28,20},{1,9},{5... | collective-permute-start | bytes 1671176 | tf_op jit(solution)/shard_map/ppermute | solution.py:436
  64.7 45.1 %collective-permute-start.6 = (bf16[512,2176]{1,0:T(8,128)(2,1)}, bf16[512,2176]{1,0:T(8,128)(2,1)}, u32[]{:S(2)}, u32[]{:S(2)}) collective-permute-start(bf16[512,2176]{1,0:T(8,128)(2,1)} %pad_maximum_fusion.5.own_ref.w_own_ref), channel_id=1, source_target_pairs={{0,4},{4,0},{8,12},{12,8},{16,20},{20,16},{24,28},{28,24},{1,5},{5... | collective-permute-start | bytes 6684680 | tf_op jit(solution)/shard_map/ppermute | solution.py:436
  64.8 33.2 %collective-permute-start.10 = (bf16[256,1024]{1,0:T(8,128)(2,1)}, bf16[256,1024]{1,0:T(8,128)(2,1)S(1)}, u32[]{:S(2)}, u32[]{:S(2)}) collective-permute-start(bf16[256,1024]{1,0:T(8,128)(2,1)} %grad_ref.1), channel_id=1, source_target_pairs={{0,1},{1,0},{2,3},{3,2},{4,5},{5,4},{6,7},{7,6},{8,9},{9,8},{10,11... | collective-permute-start | bytes 1572872 | tf_op jit(solution)/shard_map/ppermute | solution.py:440
  67.2 33.0 %copy-start.13 = (bf16[128,1024]{1,0:T(8,128)(2,1)}, bf16[128,1024]{1,0:T(8,128)(2,1)S(1)}, u32[]{:S(2)}) copy-start(bf16[128,1024]{1,0:T(8,128)(2,1)S(1)} %slice.179) | copy-start | bytes 786436
  67.2 33.0 %collective-permute-start.9 = (bf16[128,1024]{1,0:T(8,128)(2,1)S(1)}, bf16[128,1024]{1,0:T(8,128)(2,1)S(1)}, u32[]{:S(2)}, u32[]{:S(2)}) collective-permute-start(bf16[128,1024]{1,0:T(8,128)(2,1)S(1)} %slice.179), channel_id=1, source_target_pairs={{0,24},{4,28},{8,16},{12,20},{16,8},{20,12},{24,0},{28,4},{1,25},{... | collective-permute-start | bytes 786440 | tf_op jit(solution)/shard_map/ppermute | solution.py:436
  68.9 31.3 %collective-permute-start.8 = (bf16[128,1024]{1,0:T(8,128)(2,1)S(1)}, bf16[128,1024]{1,0:T(8,128)(2,1)S(1)}, u32[]{:S(2)}, u32[]{:S(2)}) collective-permute-start(bf16[128,1024]{1,0:T(8,128)(2,1)S(1)} %slice.179), channel_id=1, source_target_pairs={{0,16},{4,20},{8,24},{12,28},{16,0},{20,4},{24,8},{28,12},{1,17},{... | collective-permute-start | bytes 786440 | tf_op jit(solution)/shard_map/ppermute | solution.py:436
  70.3 31.4 %collective-permute-start.7 = (bf16[128,1024]{1,0:T(8,128)(2,1)S(1)}, bf16[128,1024]{1,0:T(8,128)(2,1)}, u32[]{:S(2)}, u32[]{:S(2)}) collective-permute-start(bf16[128,1024]{1,0:T(8,128)(2,1)S(1)} %slice.179), channel_id=1, source_target_pairs={{0,8},{4,12},{8,0},{12,4},{16,24},{20,28},{24,16},{28,20},{1,9},{5... | collective-permute-start | bytes 786440 | tf_op jit(solution)/shard_map/ppermute | solution.py:436
  98.8 5.6 copy-start.15
  102.9 16.6 %copy-start.11 = (bf16[512,1024]{1,0:T(8,128)(2,1)}, bf16[512,1024]{1,0:T(8,128)(2,1)S(1)}, u32[]{:S(2)}) copy-start(bf16[512,1024]{1,0:T(8,128)(2,1)S(1)} %pad_maximum_fusion.8.w_own_ref) | copy-start | bytes 3145732
  102.9 18.2 %collective-permute-start.11 = (bf16[512,1024]{1,0:T(8,128)(2,1)S(1)}, bf16[512,1024]{1,0:T(8,128)(2,1)}, u32[]{:S(2)}, u32[]{:S(2)}) collective-permute-start(bf16[512,1024]{1,0:T(8,128)(2,1)S(1)} %pad_maximum_fusion.8.w_own_ref), channel_id=1, source_target_pairs={{0,4},{4,0},{8,12},{12,8},{16,20},{20,16},{24,28},{28,24},{1,5},{5... | collective-permute-start | bytes 3145736 | tf_op jit(solution)/shard_map/ppermute | solution.py:436
  107.3 36.7 %collective-permute-start.18 = (bf16[2,256,1024]{2,1,0:T(8,128)(2,1)S(1)}, bf16[2,256,1024]{2,1,0:T(8,128)(2,1)}, u32[]{:S(2)}, u32[]{:S(2)}) collective-permute-start(bf16[2,256,1024]{2,1,0:T(8,128)(2,1)S(1)} %pad_maximum_fusion.9), channel_id=1, source_target_pairs={{0,24},{4,28},{8,16},{12,20},{16,8},{20,12},{24,0},{28,4},{1,25},{... | collective-permute-start | bytes 3145736 | tf_op jit(solution)/shard_map/ppermute | solution.py:436
  121.1 6.9 %copy-start.12 = (bf16[128,1024]{1,0:T(8,128)(2,1)S(1)}, bf16[128,1024]{1,0:T(8,128)(2,1)}, u32[]{:S(2)}) copy-start(bf16[128,1024]{1,0:T(8,128)(2,1)} %get-tuple-element.136) | copy-start | bytes 786436
  125.6 16.3 %collective-permute-start.12 = (bf16[288,1024]{1,0:T(8,128)(2,1)}, bf16[288,1024]{1,0:T(8,128)(2,1)S(1)}, u32[]{:S(2)}, u32[]{:S(2)}) collective-permute-start(bf16[288,1024]{1,0:T(8,128)(2,1)} %get-tuple-element.70.normed2_ref), channel_id=1, source_target_pairs={{0,1},{1,0},{2,3},{3,2},{4,5},{5,4},{6,7},{7,6},{8,9},{9,8},{10,11... | collective-permute-start | bytes 1769480 | tf_op jit(solution)/shard_map/ppermute | solution.py:440
  128.1 28.7 %collective-permute-start.17 = (bf16[2,256,1024]{2,1,0:T(8,128)(2,1)S(1)}, bf16[2,256,1024]{2,1,0:T(8,128)(2,1)S(1)}, u32[]{:S(2)}, u32[]{:S(2)}) collective-permute-start(bf16[2,256,1024]{2,1,0:T(8,128)(2,1)S(1)} %pad_maximum_fusion.9), channel_id=1, source_target_pairs={{0,16},{4,20},{8,24},{12,28},{16,0},{20,4},{24,8},{28,12},{1,17},{... | collective-permute-start | bytes 3145736 | tf_op jit(solution)/shard_map/ppermute | solution.py:436
  128.6 28.2 %collective-permute-start.16 = (bf16[2,256,1024]{2,1,0:T(8,128)(2,1)S(1)}, bf16[2,256,1024]{2,1,0:T(8,128)(2,1)S(1)}, u32[]{:S(2)}, u32[]{:S(2)}) collective-permute-start(bf16[2,256,1024]{2,1,0:T(8,128)(2,1)S(1)} %pad_maximum_fusion.9), channel_id=1, source_target_pairs={{0,8},{4,12},{8,0},{12,4},{16,24},{20,28},{24,16},{28,20},{1,9},{5... | collective-permute-start | bytes 3145736 | tf_op jit(solution)/shard_map/ppermute | solution.py:436
  129.2 12.7 %copy-start.14 = (bf16[288,1024]{1,0:T(8,128)(2,1)S(1)}, bf16[288,1024]{1,0:T(8,128)(2,1)}, u32[]{:S(2)}) copy-start(bf16[288,1024]{1,0:T(8,128)(2,1)} %get-tuple-element.70.normed2_ref) | copy-start | bytes 1769476
  142.0 40.1 %collective-permute-start.15 = (bf16[2,288,1024]{2,1,0:T(8,128)(2,1)S(1)}, bf16[2,288,1024]{2,1,0:T(8,128)(2,1)S(1)}, u32[]{:S(2)}, u32[]{:S(2)}) collective-permute-start(bf16[2,288,1024]{2,1,0:T(8,128)(2,1)S(1)} %pad_maximum_fusion.7), channel_id=1, source_target_pairs={{0,24},{4,28},{8,16},{12,20},{16,8},{20,12},{24,0},{28,4},{1,25},{... | collective-permute-start | bytes 3538952 | tf_op jit(solution)/shard_map/ppermute | solution.py:436
  142.5 64.4 %collective-permute-start.14 = (bf16[2,288,1024]{2,1,0:T(8,128)(2,1)S(1)}, bf16[2,288,1024]{2,1,0:T(8,128)(2,1)}, u32[]{:S(2)}, u32[]{:S(2)}) collective-permute-start(bf16[2,288,1024]{2,1,0:T(8,128)(2,1)S(1)} %pad_maximum_fusion.7), channel_id=1, source_target_pairs={{0,16},{4,20},{8,24},{12,28},{16,0},{20,4},{24,8},{28,12},{1,17},{... | collective-permute-start | bytes 3538952 | tf_op jit(solution)/shard_map/ppermute | solution.py:436
  144.1 63.0 %collective-permute-start.13 = (bf16[2,288,1024]{2,1,0:T(8,128)(2,1)S(1)}, bf16[2,288,1024]{2,1,0:T(8,128)(2,1)}, u32[]{:S(2)}, u32[]{:S(2)}) collective-permute-start(bf16[2,288,1024]{2,1,0:T(8,128)(2,1)S(1)} %pad_maximum_fusion.7), channel_id=1, source_target_pairs={{0,8},{4,12},{8,0},{12,4},{16,24},{20,28},{24,16},{28,20},{1,9},{5... | collective-permute-start | bytes 3538952 | tf_op jit(solution)/shard_map/ppermute | solution.py:436
  160.1 77.9 %all-to-all-start.1 = ((bf16[4,384,1024]{2,1,0:T(8,128)(2,1)}), bf16[4,384,1024]{2,1,0:T(8,128)(2,1)}, u32[]{:S(2)}, u32[]{:S(2)}) async-start(bf16[4,384,1024]{2,1,0:T(8,128)(2,1)} %pad_maximum_fusion.4), calls=%async_computation.1 | async-start | bytes 6291456 | tf_op jit(solution)/shard_map/all_to_all | solution.py:875
  211.5 26.6 %collective-permute-start.19 = (bf16[8,288,1024]{2,1,0:T(8,128)(2,1)}, bf16[8,288,1024]{2,1,0:T(8,128)(2,1)}, u32[]{:S(2)}, u32[]{:S(2)}) collective-permute-start(bf16[8,288,1024]{2,1,0:T(8,128)(2,1)} %pad_maximum_fusion.1.refs_0_), channel_id=1, source_target_pairs={{0,4},{4,0},{8,12},{12,8},{16,20},{20,16},{24,28},{28,24},{1,5},{5... | collective-permute-start | bytes 14155784 | tf_op jit(solution)/shard_map/ppermute | solution.py:436
  211.5 26.6 %collective-permute-start.20 = (bf16[8,256,1024]{2,1,0:T(8,128)(2,1)}, bf16[8,256,1024]{2,1,0:T(8,128)(2,1)}, u32[]{:S(2)}, u32[]{:S(2)}) collective-permute-start(bf16[8,256,1024]{2,1,0:T(8,128)(2,1)} %pad_maximum_fusion.2.refs_2_), channel_id=1, source_target_pairs={{0,4},{4,0},{8,12},{12,8},{16,20},{20,16},{24,28},{28,24},{1,5},{5... | collective-permute-start | bytes 12582920 | tf_op jit(solution)/shard_map/ppermute | solution.py:436
  283.0 75.0 %all-to-all-start.2 = ((bf16[4,384,1024]{2,1,0:T(8,128)(2,1)}), bf16[4,384,1024]{2,1,0:T(8,128)(2,1)S(1)}, u32[]{:S(2)}, u32[]{:S(2)}) async-start(bf16[4,384,1024]{2,1,0:T(8,128)(2,1)} %get-tuple-element.84), calls=%async_computation.2 | async-start | bytes 6291456 | tf_op jit(solution)/shard_map/all_to_all | solution.py:875
  358.0 14.4 %copy-start.4 = (bf16[4,384,1024]{2,1,0:T(8,128)(2,1)}, bf16[4,384,1024]{2,1,0:T(8,128)(2,1)S(1)}, u32[]{:S(2)}) copy-start(bf16[4,384,1024]{2,1,0:T(8,128)(2,1)S(1)} %all-to-all-done.2) | copy-start | bytes 9437188
  358.0 7.7 %collective-permute-start.21 = (bf16[8,272,1024]{2,1,0:T(8,128)(2,1)}, bf16[8,272,1024]{2,1,0:T(8,128)(2,1)S(1)}, u32[]{:S(2)}, u32[]{:S(2)}) collective-permute-start(bf16[8,272,1024]{2,1,0:T(8,128)(2,1)} %get-tuple-element.87), channel_id=1, source_target_pairs={{0,4},{4,0},{8,12},{12,8},{16,20},{20,16},{24,28},{28,24},{1,5},{5... | collective-permute-start | bytes 13369352 | tf_op jit(solution)/shard_map/ppermute | solution.py:436
  372.4 65.5 %collective-permute-start.25 = (bf16[8,256,1024]{2,1,0:T(8,128)(2,1)}, bf16[8,256,1024]{2,1,0:T(8,128)(2,1)}, u32[]{:S(2)}, u32[]{:S(2)}) collective-permute-start(bf16[8,256,1024]{2,1,0:T(8,128)(2,1)} %get-tuple-element.92), channel_id=1, source_target_pairs={{0,4},{4,0},{8,12},{12,8},{16,20},{20,16},{24,28},{28,24},{1,5},{5... | collective-permute-start | bytes 12582920 | tf_op jit(solution)/shard_map/ppermute | solution.py:436
  372.6 75.4 %all-to-all-start.3 = ((bf16[4,384,1024]{2,1,0:T(8,128)(2,1)}), bf16[4,384,1024]{2,1,0:T(8,128)(2,1)S(1)}, u32[]{:S(2)}, u32[]{:S(2)}) async-start(bf16[4,384,1024]{2,1,0:T(8,128)(2,1)} %get-tuple-element.93), calls=%async_computation.3 | async-start | bytes 6291456 | tf_op jit(solution)/shard_map/all_to_all | solution.py:875
  380.2 27.8 %collective-permute-start.22 = (bf16[2,272,1024]{2,1,0:T(8,128)(2,1)}, bf16[2,272,1024]{2,1,0:T(8,128)(2,1)}, u32[]{:S(2)}, u32[]{:S(2)}) collective-permute-start(bf16[2,272,1024]{2,1,0:T(8,128)(2,1)} %get-tuple-element.115), channel_id=1, source_target_pairs={{0,8},{4,12},{8,0},{12,4},{16,24},{20,28},{24,16},{28,20},{1,9},{5... | collective-permute-start | bytes 3342344 | tf_op jit(solution)/shard_map/ppermute | solution.py:436
  381.7 50.6 %collective-permute-start.24 = (bf16[2,272,1024]{2,1,0:T(8,128)(2,1)}, bf16[2,272,1024]{2,1,0:T(8,128)(2,1)}, u32[]{:S(2)}, u32[]{:S(2)}) collective-permute-start(bf16[2,272,1024]{2,1,0:T(8,128)(2,1)} %get-tuple-element.116), channel_id=1, source_target_pairs={{0,24},{4,28},{8,16},{12,20},{16,8},{20,12},{24,0},{28,4},{1,25},{... | collective-permute-start | bytes 3342344 | tf_op jit(solution)/shard_map/ppermute | solution.py:436
  383.2 50.5 %collective-permute-start.23 = (bf16[2,272,1024]{2,1,0:T(8,128)(2,1)}, bf16[2,272,1024]{2,1,0:T(8,128)(2,1)}, u32[]{:S(2)}, u32[]{:S(2)}) collective-permute-start(bf16[2,272,1024]{2,1,0:T(8,128)(2,1)} %get-tuple-element.117), channel_id=1, source_target_pairs={{0,16},{4,20},{8,24},{12,28},{16,0},{20,4},{24,8},{28,12},{1,17},{... | collective-permute-start | bytes 3342344 | tf_op jit(solution)/shard_map/ppermute | solution.py:436
  389.0 48.9 %copy-start.5 = (bf16[8,256,1024]{2,1,0:T(8,128)(2,1)S(1)}, bf16[8,256,1024]{2,1,0:T(8,128)(2,1)}, u32[]{:S(2)}) copy-start(bf16[8,256,1024]{2,1,0:T(8,128)(2,1)} %get-tuple-element.91) | copy-start | bytes 12582916
  450.9 5.1 copy-start
  450.9 14.0 %collective-permute-start.30 = (bf16[272,1024]{1,0:T(8,128)(2,1)S(1)}, bf16[272,1024]{1,0:T(8,128)(2,1)S(1)}, u32[]{:S(2)}, u32[]{:S(2)}) collective-permute-start(bf16[272,1024]{1,0:T(8,128)(2,1)S(1)} %get-tuple-element.131), channel_id=1, source_target_pairs={{0,1},{1,0},{2,3},{3,2},{4,5},{5,4},{6,7},{7,6},{8,9},{9,8},{10,11... | collective-permute-start | bytes 1671176 | tf_op jit(solution)/shard_map/ppermute | solution.py:440
  456.0 5.3 copy-start.3
  457.8 31.2 %collective-permute-start.26 = (bf16[2,256,1024]{2,1,0:T(8,128)(2,1)}, bf16[2,256,1024]{2,1,0:T(8,128)(2,1)}, u32[]{:S(2)}, u32[]{:S(2)}) collective-permute-start(bf16[2,256,1024]{2,1,0:T(8,128)(2,1)} %get-tuple-element.118), channel_id=1, source_target_pairs={{0,8},{4,12},{8,0},{12,4},{16,24},{20,28},{24,16},{28,20},{1,9},{5... | collective-permute-start | bytes 3145736 | tf_op jit(solution)/shard_map/ppermute | solution.py:436
  459.3 46.9 %collective-permute-start.28 = (bf16[2,256,1024]{2,1,0:T(8,128)(2,1)}, bf16[2,256,1024]{2,1,0:T(8,128)(2,1)}, u32[]{:S(2)}, u32[]{:S(2)}) collective-permute-start(bf16[2,256,1024]{2,1,0:T(8,128)(2,1)} %get-tuple-element.119), channel_id=1, source_target_pairs={{0,24},{4,28},{8,16},{12,20},{16,8},{20,12},{24,0},{28,4},{1,25},{... | collective-permute-start | bytes 3145736 | tf_op jit(solution)/shard_map/ppermute | solution.py:436
  460.8 46.8 %collective-permute-start.27 = (bf16[2,256,1024]{2,1,0:T(8,128)(2,1)}, bf16[2,256,1024]{2,1,0:T(8,128)(2,1)}, u32[]{:S(2)}, u32[]{:S(2)}) collective-permute-start(bf16[2,256,1024]{2,1,0:T(8,128)(2,1)} %get-tuple-element.120), channel_id=1, source_target_pairs={{0,16},{4,20},{8,24},{12,28},{16,0},{20,4},{24,8},{28,12},{1,17},{... | collective-permute-start | bytes 3145736 | tf_op jit(solution)/shard_map/ppermute | solution.py:436
  471.8 51.1 %collective-permute-start.38 = (bf16[512,1152]{1,0:T(8,128)(2,1)}, bf16[512,1152]{1,0:T(8,128)(2,1)}, u32[]{:S(2)}, u32[]{:S(2)}) collective-permute-start(bf16[512,1152]{1,0:T(8,128)(2,1)} %get-tuple-element.108), channel_id=1, source_target_pairs={{0,4},{4,0},{8,12},{12,8},{16,20},{20,16},{24,28},{28,24},{1,5},{5... | collective-permute-start | bytes 3538952 | tf_op jit(solution)/shard_map/ppermute | solution.py:436
  488.5 39.7 %collective-permute-start.31 = (bf16[512,2176]{1,0:T(8,128)(2,1)}, bf16[512,2176]{1,0:T(8,128)(2,1)S(1)}, u32[]{:S(2)}, u32[]{:S(2)}) collective-permute-start(bf16[512,2176]{1,0:T(8,128)(2,1)} %get-tuple-element.106), channel_id=1, source_target_pairs={{0,4},{4,0},{8,12},{12,8},{16,20},{20,16},{24,28},{28,24},{1,5},{5... | collective-permute-start | bytes 6684680 | tf_op jit(solution)/shard_map/ppermute | solution.py:436
  510.7 11.1 %collective-permute-start.29 = (bf16[256,1024]{1,0:T(8,128)(2,1)S(1)}, bf16[256,1024]{1,0:T(8,128)(2,1)S(1)}, u32[]{:S(2)}, u32[]{:S(2)}) collective-permute-start(bf16[256,1024]{1,0:T(8,128)(2,1)S(1)} %slice_bitcast_fusion.2), channel_id=1, source_target_pairs={{0,1},{1,0},{2,3},{3,2},{4,5},{5,4},{6,7},{7,6},{8,9},{9,8},{10,11... | collective-permute-start | bytes 1572872 | tf_op jit(solution)/shard_map/ppermute | solution.py:440
  516.8 5.0 copy-start.10
  522.9 5.3 copy-start.6
  524.7 9.9 %collective-permute-start.39 = (bf16[128,1152]{1,0:T(8,128)(2,1)S(1)}, bf16[128,1152]{1,0:T(8,128)(2,1)S(1)}, u32[]{:S(2)}, u32[]{:S(2)}) collective-permute-start(bf16[128,1152]{1,0:T(8,128)(2,1)S(1)} %get-tuple-element.128), channel_id=1, source_target_pairs={{0,8},{4,12},{8,0},{12,4},{16,24},{20,28},{24,16},{28,20},{1,9},{5... | collective-permute-start | bytes 884744 | tf_op jit(solution)/shard_map/ppermute | solution.py:436
  526.2 14.6 %collective-permute-start.41 = (bf16[128,1152]{1,0:T(8,128)(2,1)S(1)}, bf16[128,1152]{1,0:T(8,128)(2,1)S(1)}, u32[]{:S(2)}, u32[]{:S(2)}) collective-permute-start(bf16[128,1152]{1,0:T(8,128)(2,1)S(1)} %get-tuple-element.129), channel_id=1, source_target_pairs={{0,24},{4,28},{8,16},{12,20},{16,8},{20,12},{24,0},{28,4},{1,25},{... | collective-permute-start | bytes 884744 | tf_op jit(solution)/shard_map/ppermute | solution.py:436
  526.7 14.2 %collective-permute-start.40 = (bf16[128,1152]{1,0:T(8,128)(2,1)S(1)}, bf16[128,1152]{1,0:T(8,128)(2,1)S(1)}, u32[]{:S(2)}, u32[]{:S(2)}) collective-permute-start(bf16[128,1152]{1,0:T(8,128)(2,1)S(1)} %get-tuple-element.130), channel_id=1, source_target_pairs={{0,16},{4,20},{8,24},{12,28},{16,0},{20,4},{24,8},{28,12},{1,17},{... | collective-permute-start | bytes 884744 | tf_op jit(solution)/shard_map/ppermute | solution.py:436
  528.9 24.0 %collective-permute-start.32 = (bf16[128,2176]{1,0:T(8,128)(2,1)S(1)}, bf16[128,2176]{1,0:T(8,128)(2,1)S(1)}, u32[]{:S(2)}, u32[]{:S(2)}) collective-permute-start(bf16[128,2176]{1,0:T(8,128)(2,1)S(1)} %get-tuple-element.121), channel_id=1, source_target_pairs={{0,8},{4,12},{8,0},{12,4},{16,24},{20,28},{24,16},{28,20},{1,9},{5... | collective-permute-start | bytes 1671176 | tf_op jit(solution)/shard_map/ppermute | solution.py:436
  530.5 29.9 %collective-permute-start.34 = (bf16[128,2176]{1,0:T(8,128)(2,1)S(1)}, bf16[128,2176]{1,0:T(8,128)(2,1)S(1)}, u32[]{:S(2)}, u32[]{:S(2)}) collective-permute-start(bf16[128,2176]{1,0:T(8,128)(2,1)S(1)} %get-tuple-element.122), channel_id=1, source_target_pairs={{0,24},{4,28},{8,16},{12,20},{16,8},{20,12},{24,0},{28,4},{1,25},{... | collective-permute-start | bytes 1671176 | tf_op jit(solution)/shard_map/ppermute | solution.py:436
  534.6 27.0 %collective-permute-start.33 = (bf16[128,2176]{1,0:T(8,128)(2,1)S(1)}, bf16[128,2176]{1,0:T(8,128)(2,1)S(1)}, u32[]{:S(2)}, u32[]{:S(2)}) collective-permute-start(bf16[128,2176]{1,0:T(8,128)(2,1)S(1)} %get-tuple-element.123), channel_id=1, source_target_pairs={{0,16},{4,20},{8,24},{12,28},{16,0},{20,4},{24,8},{28,12},{1,17},{... | collective-permute-start | bytes 1671176 | tf_op jit(solution)/shard_map/ppermute | solution.py:436
  541.1 23.5 %collective-permute-start.42 = (bf16[32,1152]{1,0:T(8,128)(2,1)S(1)}, bf16[32,1152]{1,0:T(8,128)(2,1)S(1)}, u32[]{:S(2)}, u32[]{:S(2)}) collective-permute-start(bf16[32,1152]{1,0:T(8,128)(2,1)S(1)} %get-tuple-element.144), channel_id=1, source_target_pairs={{0,1},{1,0},{2,3},{3,2},{4,5},{5,4},{6,7},{7,6},{8,9},{9,8},{10,11... | collective-permute-start | bytes 221192 | tf_op jit(solution)/shard_map/ppermute | solution.py:440
  542.5 23.1 %collective-permute-start.44 = (bf16[32,1152]{1,0:T(8,128)(2,1)S(1)}, bf16[32,1152]{1,0:T(8,128)(2,1)S(1)}, u32[]{:S(2)}, u32[]{:S(2)}) collective-permute-start(bf16[32,1152]{1,0:T(8,128)(2,1)S(1)} %get-tuple-element.145), channel_id=1, source_target_pairs={{0,3},{1,2},{2,1},{3,0},{4,7},{5,6},{6,5},{7,4},{8,11},{9,10},{10,... | collective-permute-start | bytes 221192 | tf_op jit(solution)/shard_map/ppermute | solution.py:440
  552.9 12.7 %collective-permute-start.43 = (bf16[32,1152]{1,0:T(8,128)(2,1)S(1)}, bf16[32,1152]{1,0:T(8,128)(2,1)S(1)}, u32[]{:S(2)}, u32[]{:S(2)}) collective-permute-start(bf16[32,1152]{1,0:T(8,128)(2,1)S(1)} %get-tuple-element.146), channel_id=1, source_target_pairs={{0,2},{1,3},{2,0},{3,1},{4,6},{5,7},{6,4},{7,5},{8,10},{9,11},{10,... | collective-permute-start | bytes 221192 | tf_op jit(solution)/shard_map/ppermute | solution.py:440
  562.0 5.6 collective-permute-start.35
  563.1 7.0 %collective-permute-start.37 = (bf16[32,2176]{1,0:T(8,128)(2,1)S(1)}, bf16[32,2176]{1,0:T(8,128)(2,1)S(1)}, u32[]{:S(2)}, u32[]{:S(2)}) collective-permute-start(bf16[32,2176]{1,0:T(8,128)(2,1)S(1)} %get-tuple-element.142), channel_id=1, source_target_pairs={{0,3},{1,2},{2,1},{3,0},{4,7},{5,6},{6,5},{7,4},{8,11},{9,10},{10,... | collective-permute-start | bytes 417800 | tf_op jit(solution)/shard_map/ppermute | solution.py:440
  564.5 8.5 %collective-permute-start.36 = (bf16[32,2176]{1,0:T(8,128)(2,1)S(1)}, bf16[32,2176]{1,0:T(8,128)(2,1)S(1)}, u32[]{:S(2)}, u32[]{:S(2)}) collective-permute-start(bf16[32,2176]{1,0:T(8,128)(2,1)S(1)} %get-tuple-element.143), channel_id=1, source_target_pairs={{0,2},{1,3},{2,0},{3,1},{4,6},{5,7},{6,4},{7,5},{8,10},{9,11},{10,... | collective-permute-start | bytes 417800 | tf_op jit(solution)/shard_map/ppermute | solution.py:440
  (12 other events, 21.2 us)

commit v3 on v2

--- a/solution.py
+++ b/solution.py
@@ -429,7 +429,6 @@
 F32 = jnp.float32
 PAIR = 2
 OWN = 2
-BLOCKS = 16
 
 
 def over_expert(value, bits):
@@ -447,32 +446,45 @@
 CONTRACT_LAST = (((1,), (1,)), ((), ()))
 CONTRACT_FIRST = (((0,), (0,)), ((), ()))
 CONTRACT_PLAIN = (((1,), (0,)), ((), ()))
-STEP_BLOCKS = 2
-STEPS = BLOCKS // STEP_BLOCKS
-STEP_ROWS = STEP_BLOCKS * CAP
+BLOCKS = 8
+HALF = 4
+ROWS = HALF * CAP
+PAY_ROWS = 288
+SUM_ROWS = 272
 
 
 def expert_body(first_part, number_ref, *refs):
-    if first_part:
-        tok_own, tok_far, out_own, out_far, w_ref = refs[:5]
-        refs = refs[5:]
-        befores = None
-    else:
-        tok_own, tok_far, out_own, out_far, w_ref = refs[:5]
-        befores = refs[5:9]
-        refs = refs[9:]
-    row_own, row_far, moe_own, moe_far, grad_ref, x_s, g_s, gate_s, table_s, back_s, mix_s, dot_s, in_acc, out_acc = refs
-    step = pl.program_id(0)
+    refs = list(refs)
+    take = lambda count: [refs.pop(0) for _ in range(count)]
+    tok_refs, out_refs = take(BLOCKS), take(BLOCKS)
+    (w_ref,) = take(1)
+    row_before, moe_before = ([], []) if first_part else (take(BLOCKS), take(BLOCKS))
+    row_outs, moe_outs = take(BLOCKS), take(BLOCKS)
+    (grad_ref,) = take(1)
+    (tok_s, out_s, w_s, row_s, moe_s, grad_s, x_s, g_s, gate_s, table_s, back_s, mix_s, dot_s,
+     in_acc, out_acc, tok_sem, out_sem, w_sem, row_sem, moe_sem, row_out_sem, moe_out_sem, grad_sem) = refs
     number = number_ref[0]
-    own = step < STEPS // 2
+    copy = pltpu.make_async_copy
+    for j in range(BLOCKS):
+        copy(tok_refs[j], tok_s.at[j], tok_sem.at[j]).start()
+        copy(out_refs[j], out_s.at[j], out_sem.at[j]).start()
+        if j == HALF - 1:
+            copy(w_ref, w_s, w_sem.at[0]).start()
+    if not first_part:
+        for j in range(BLOCKS):
+            copy(row_before[j], row_s.at[j], row_sem.at[j]).start()
+            copy(moe_before[j], moe_s.at[j], moe_sem.at[j]).start()
 
     def mask_of(i):
         slot = lax.broadcasted_iota(jnp.int32, (CAP, 256), 0).astype(F32)
         return slot == table_s[i, 0:1, :]
 
-    def load(tok_ref, g_ref):
-        for i in range(STEP_BLOCKS):
-            aux = tok_ref[i, 256:288, :].astype(F32)
+    def half_step(half, _):
+        for i in range(HALF):
+            j = half * HALF + i
+            copy(tok_s.at[j], tok_s.at[j], tok_sem.at[j]).wait()
+            copy(out_s.at[j], out_s.at[j], out_sem.at[j]).wait()
+            aux = tok_s[j, 256:PAY_ROWS, :].astype(F32)
             line = lax.broadcasted_iota(jnp.int32, (EXPERTS, 1024), 0)
             line = jnp.sum(jnp.where(line == number, aux, 0.0), axis=0, keepdims=True)
             table_s[i, 0:1, :] = line[:, :256]
@@ -480,51 +492,50 @@
             mask = mask_of(i)
             pick = jnp.where(mask, 1.0, 0.0).astype(BF16)
             at = slice(i * CAP, (i + 1) * CAP)
-            x_s[at, :] = dot_f32(pick, tok_ref[i, 0:256, :], CONTRACT_PLAIN).astype(BF16)
-            g_s[at, :] = resid_scale * dot_f32(pick, g_ref[i], CONTRACT_PLAIN)
+            x_s[at, :] = dot_f32(pick, tok_s[j, 0:256, :], CONTRACT_PLAIN).astype(BF16)
+            g_s[at, :] = resid_scale * dot_f32(pick, out_s[j], CONTRACT_PLAIN)
             gate_s[at, :] = jnp.sum(jnp.where(mask, gate, 0.0), axis=1, keepdims=True)
 
-    @pl.when(own)
-    def _():
-        load(tok_own, out_own)
-
-    @pl.when(jnp.logical_not(own))
-    def _():
-        load(tok_far, out_far)
-
-    w_in = w_ref[:, 0:256, :].reshape(1024, 1024)
-    w_out = w_ref[:, 256:384, :].reshape(512, 1024)
-    x = x_s[...]
-    gate_up = dot_f32(x, w_in, CONTRACT_PLAIN)
-    gate_part, up_part = gate_up[:, :FF], gate_up[:, FF:]
-    sigmoid = jax.nn.sigmoid(gate_part)
-    hidden = (gate_part * sigmoid * up_part).astype(BF16)
-    produced = dot_f32(hidden, w_out, CONTRACT_PLAIN).astype(BF16).astype(F32)
-    slot_gate = gate_s[...]
-    scaled = g_s[...]
-    slot_grad = (slot_gate * scaled).astype(BF16)
-    dot_s[...] = jnp.sum(produced * scaled, axis=1, keepdims=True)
-    mix_s[...] = (slot_gate * produced).astype(BF16)
-    hidden_grad = dot_f32(slot_grad, w_out, CONTRACT_LAST)
-    gate_grad = hidden_grad * up_part * sigmoid * (1.0 + gate_part * (1.0 - sigmoid))
-    up_grad = hidden_grad * gate_part * sigmoid
-    gate_up_grad = jnp.concatenate([gate_grad.astype(BF16), up_grad.astype(BF16)], axis=1)
-    back_s[...] = dot_f32(gate_up_grad, w_in, CONTRACT_LAST).astype(BF16)
-    in_part = dot_f32(x, gate_up_grad, CONTRACT_FIRST)
-    out_part = dot_f32(hidden, slot_grad, CONTRACT_FIRST)
-
-    @pl.when(step == 0)
-    def _():
-        in_acc[...] = in_part
-        out_acc[...] = out_part
-
-    @pl.when(step > 0)
-    def _():
-        in_acc[...] += in_part
-        out_acc[...] += out_part
-
-    def store(row_ref, moe_ref, row_before, moe_before):
-        for i in range(STEP_BLOCKS):
+        @pl.when(half == 0)
+        def _():
+            copy(w_ref, w_s, w_sem.at[0]).wait()
+
+        w_in = w_s[:, 0:256, :].reshape(1024, 1024)
+        w_out = w_s[:, 256:384, :].reshape(512, 1024)
+        x = x_s[...]
+        gate_up = dot_f32(x, w_in, CONTRACT_PLAIN)
+        gate_part, up_part = gate_up[:, :FF], gate_up[:, FF:]
+        sigmoid = jax.nn.sigmoid(gate_part)
+        hidden = (gate_part * sigmoid * up_part).astype(BF16)
+        produced = dot_f32(hidden, w_out, CONTRACT_PLAIN).astype(BF16).astype(F32)
+        slot_gate = gate_s[...]
+        scaled = g_s[...]
+        slot_grad = (slot_gate * scaled).astype(BF16)
+        dot_s[...] = jnp.sum(produced * scaled, axis=1, keepdims=True)
+        mix_s[...] = (slot_gate * produced).astype(BF16)
+        hidden_grad = dot_f32(slot_grad, w_out, CONTRACT_LAST)
+        gate_grad = hidden_grad * up_part * sigmoid * (1.0 + gate_part * (1.0 - sigmoid))
+        up_grad = hidden_grad * gate_part * sigmoid
+        gate_up_grad = jnp.concatenate([gate_grad.astype(BF16), up_grad.astype(BF16)], axis=1)
+        back_s[...] = dot_f32(gate_up_grad, w_in, CONTRACT_LAST).astype(BF16)
+        in_part = dot_f32(x, gate_up_grad, CONTRACT_FIRST)
+        out_part = dot_f32(hidden, slot_grad, CONTRACT_FIRST)
+
+        @pl.when(half == 0)
+        def _():
+            in_acc[...] = in_part
+            out_acc[...] = out_part
+
+        @pl.when(half == 1)
+        def _():
+            for d in range(4):
+                wide, narrow = slice(d * 256, (d + 1) * 256), slice(d * 128, (d + 1) * 128)
+                grad_s[d, 0:256, :] = (in_acc[wide, :] + in_part[wide, :]).astype(BF16)
+                grad_s[d, 256:384, :] = (out_acc[narrow, :] + out_part[narrow, :]).astype(BF16)
+            copy(grad_s, grad_ref, grad_sem.at[0]).start()
+
+        for i in range(HALF):
+            j = half * HALF + i
             at = slice(i * CAP, (i + 1) * CAP)
             mask = mask_of(i)
             pick = jnp.where(mask, 1.0, 0.0).astype(BF16)
@@ -538,71 +549,58 @@
             lane = lax.broadcasted_iota(jnp.int32, (16, 1024), 1) // 256
             here = (line == number % 16) & (lane % 2 == number // 16)
             side = jnp.where(here, jnp.broadcast_to(wide, (16, 1024)), 0.0)
-            if row_before is not None:
-                rows = rows + row_before[i, 0:256, :].astype(F32)
-                mixed = mixed + moe_before[i].astype(F32)
-                side = side + row_before[i, 256:272, :].astype(F32)
-            row_ref[i, 0:256, :] = rows.astype(BF16)
-            row_ref[i, 256:272, :] = side.astype(BF16)
-            moe_ref[i] = mixed.astype(BF16)
-
-    own_before, far_before, own_moe_before, far_moe_before = befores or (None,) * 4
-
-    @pl.when(own)
-    def _():
-        store(row_own, moe_own, own_before, own_moe_before)
-
-    @pl.when(jnp.logical_not(own))
-    def _():
-        store(row_far, moe_far, far_before, far_moe_before)
-
-    @pl.when(step == STEPS - 1)
-    def _():
-        for d in range(4):
-            grad_ref[d, 0:256, :] = in_acc[d * 256 : (d + 1) * 256, :].astype(BF16)
-            grad_ref[d, 256:384, :] = out_acc[d * 128 : (d + 1) * 128, :].astype(BF16)
-
-
-def expert_call(number, tok_own, tok_far, out_own, out_far, weights, before=None):
-    half = STEPS // 2
-    own_at = lambda s, n: (jnp.minimum(s, half - 1), 0, 0)
-    far_at = lambda s, n: (jnp.maximum(s - half, 0), 0, 0)
-    whole = lambda s, n: (0, 0, 0)
-    spec = lambda rows, at: pl.BlockSpec((STEP_BLOCKS, rows, 1024), at)
-    w_spec = pl.BlockSpec((4, 384, 1024), whole, pipeline_mode=pl.Buffered(1))
-    outs = [spec(272, own_at), spec(272, far_at), spec(256, own_at), spec(256, far_at)]
-    ins = [spec(288, own_at), spec(288, far_at), spec(256, own_at), spec(256, far_at), w_spec]
-    operands = [tok_own, tok_far, out_own, out_far, weights]
-    aliases = {}
-    if before is not None:
-        ins = ins + outs
-        operands = operands + list(before)
-        aliases = {6 + i: i for i in range(4)}
-    shapes = [jax.ShapeDtypeStruct((8, rows, 1024), BF16) for rows in (272, 272, 256, 256)]
-    rows_f32 = pltpu.VMEM((STEP_ROWS, 1), F32)
-    wide = pltpu.VMEM((STEP_ROWS, 1024), BF16)
-    return pl.pallas_call(
+            if not first_part:
+                copy(row_s.at[j], row_s.at[j], row_sem.at[j]).wait()
+                copy(moe_s.at[j], moe_s.at[j], moe_sem.at[j]).wait()
+                rows = rows + row_s[j, 0:256, :].astype(F32)
+                mixed = mixed + moe_s[j].astype(F32)
+                side = side + row_s[j, 256:SUM_ROWS, :].astype(F32)
+            row_s[j, 0:256, :] = rows.astype(BF16)
+            row_s[j, 256:SUM_ROWS, :] = side.astype(BF16)
+            moe_s[j] = mixed.astype(BF16)
+            for part in range(2):
+
+                @pl.when(half == part)
+                def _():
+                    k = part * HALF + i
+                    copy(row_s.at[k], row_outs[k], row_out_sem.at[k]).start()
+                    copy(moe_s.at[k], moe_outs[k], moe_out_sem.at[k]).start()
+
+        return 0
+
+    lax.fori_loop(0, 2, half_step, 0)
+    copy(grad_s, grad_ref, grad_sem.at[0]).wait()
+    for j in range(BLOCKS):
+        copy(row_s.at[j], row_outs[j], row_out_sem.at[j]).wait()
+        copy(moe_s.at[j], moe_outs[j], moe_out_sem.at[j]).wait()
+
+
+def expert_call(number, tokens, grads, weights, before=None):
+    operands = list(tokens) + list(grads) + [weights] + ([] if before is None else list(before))
+    block = lambda rows: jax.ShapeDtypeStruct((rows, 1024), BF16)
+    outs = [block(SUM_ROWS)] * BLOCKS + [block(256)] * BLOCKS + [jax.ShapeDtypeStruct((4, 384, 1024), BF16)]
+    anywhere = pl.BlockSpec(memory_space=pl.ANY)
+    blocks = lambda rows: pltpu.VMEM((BLOCKS, rows, 1024), BF16)
+    column, wide = pltpu.VMEM((ROWS, 1), F32), pltpu.VMEM((ROWS, 1024), BF16)
+    sems = [pltpu.SemaphoreType.DMA((count,)) for count in (8, 8, 1, 8, 8, 8, 8, 1)]
+    results = pl.pallas_call(
         functools.partial(expert_body, before is None),
-        out_shape=shapes + [jax.ShapeDtypeStruct((4, 384, 1024), BF16)],
-        grid_spec=pltpu.PrefetchScalarGridSpec(
-            num_scalar_prefetch=1,
-            grid=(STEPS,),
-            in_specs=ins,
-            out_specs=outs + [w_spec],
-            scratch_shapes=[
-                wide, pltpu.VMEM((STEP_ROWS, 1024), F32), rows_f32, pltpu.VMEM((STEP_BLOCKS, 8, 256), F32),
-                wide, wide, rows_f32, pltpu.VMEM((1024, 1024), F32), pltpu.VMEM((512, 1024), F32),
-            ],
-        ),
-        input_output_aliases=aliases,
-        compiler_params=pltpu.CompilerParams(
-            dimension_semantics=("arbitrary",), vmem_limit_bytes=60 * 1024 * 1024
-        ),
+        out_shape=outs,
+        in_specs=[pl.BlockSpec(memory_space=pltpu.SMEM)] + [anywhere] * len(operands),
+        out_specs=[anywhere] * len(outs),
+        scratch_shapes=[
+            blocks(PAY_ROWS), blocks(256), pltpu.VMEM((4, 384, 1024), BF16), blocks(SUM_ROWS), blocks(256),
+            pltpu.VMEM((4, 384, 1024), BF16), wide, pltpu.VMEM((ROWS, 1024), F32), column,
+            pltpu.VMEM((HALF, 8, 256), F32), wide, wide, column,
+            pltpu.VMEM((1024, 1024), F32), pltpu.VMEM((512, 1024), F32),
+        ] + sems,
+        compiler_params=pltpu.CompilerParams(vmem_limit_bytes=60 * 1024 * 1024),
         cost_estimate=pl.CostEstimate(
-            flops=24_000_000_000, bytes_accessed=45_000_000, transcendentals=1_000_000
+            flops=12_000_000_000, bytes_accessed=30_000_000, transcendentals=1_000_000
         ),
         name="expert",
     )(number, *operands)
+    return results[: 2 * BLOCKS], results[2 * BLOCKS]
 
 
 LANES = 128
@@ -880,6 +878,62 @@
     return jnp.stack([jnp.concatenate([expert_in[c], expert_out[c]]) for c in chosen])
 
 
+def over_x(value):
+    return over_expert(value, 2)
+
+
+def over_y(value):
+    return over_expert(value, 4)
+
+
+def spread(value, first, second):
+    near = {first: first(value), second: second(value)}
+    return [value, near[over_x], near[over_y], second(near[first])]
+
+
+def fold(parts, first, second):
+    one, two = (1, 2) if first is over_x else (2, 1)
+    passing, mine = first(parts[3]), first(parts[one])
+    other = (parts[two].astype(F32) + passing.astype(F32)).astype(BF16)
+    return parts[0].astype(F32) + mine.astype(F32) + second(other).astype(F32)
+
+
+def fold_both(parts):
+    own, pair = parts[:4], parts[4:]
+    pair_pass, own_pass = over_x(pair[3]), over_y(own[3])
+    pair_mine = over_x(pair[1])
+    pair_other = over_y(bf_sum(pair[2], pair_pass))
+    mine, pair_pass = together(own[2], pair_pass)
+    own_mine = over_y(mine)
+    own_other = over_x(bf_sum(own[1], own_pass))
+    pair_sum = bf_sum(pair[0], pair_mine, pair_other)
+    return bf_sum(own[0], own_mine, own_other), pair_sum
+
+
+def bf_sum(*values):
+    return sum(value.astype(F32) for value in values).astype(BF16)
+
+
+def pack_body(query_ref, key_ref, value_ref, router_ref, attn_ref, ffn_ref, out_ref, pack_ref):
+    pack_ref[:, 0:1024] = query_ref[...].astype(BF16)
+    pack_ref[:, 1024:1536] = key_ref[...].astype(BF16)
+    pack_ref[:, 1536:2048] = value_ref[...].astype(BF16)
+    zeros = jnp.zeros((32, LANES - EXPERTS - 2), F32)
+    small = jnp.concatenate([router_ref[...], attn_ref[...], ffn_ref[...], zeros], axis=1)
+    pack_ref[:, 2048:2176] = small.astype(BF16)
+    pack_ref[:, 2176:] = out_ref[...].astype(BF16)
+
+
+def pack_call(*operands):
+    return pl.pallas_call(
+        pack_body,
+        out_shape=jax.ShapeDtypeStruct((32, 3200), BF16),
+        in_specs=[pl.BlockSpec(memory_space=pltpu.VMEM)] * len(operands),
+        out_specs=pl.BlockSpec(memory_space=pltpu.VMEM),
+        name="pack",
+    )(*operands)
+
+
 def per_device_fast(
     embedded,
     document_numbers,
@@ -898,23 +952,22 @@
     e = lax.axis_index("expert")
     z = lax.axis_index("shard")
     place = e.reshape(1)
-    zeros = jnp.zeros((32, LANES - EXPERTS - 2), F32)
-    small = [w_router, attn_gain[:, None], ffn_gain[:, None], zeros]
-    pack = jnp.concatenate([w_query, key_projection, value_projection] + small + [w_out], axis=1)
-    pack = pack.astype(BF16)
+    pack = pack_call(
+        w_query, key_projection, value_projection, w_router, attn_gain[:, None], ffn_gain[:, None], w_out
+    )
+    pack, grad_early = together(pack, cotangent)
     plane = xor_order([pack] + [over_shard(pack, k) for k in (1, 2, 3)], z)
+    out_pair = over_shard(grad_early, 1)
+    out_x, out_y = over_x(grad_early), over_y(grad_early)
     slices = [expert_slices(expert_in, expert_out, part) for part in range(OWN)]
-    plane, out_grad, slices[0] = together(plane, cotangent, slices[0])
+    plane, out_x, out_y, out_pair, slices[0] = together(plane, out_x, out_y, out_pair, slices[0])
     weights0 = exchange(slices[0])
-    out_pair = jnp.stack([out_grad, over_shard(out_grad, 1)])
-    in_own = plane_gather(plane[:, :2176])
-    in_own, plane = together(in_own, plane)
+    left = spread(plane[:, :1152], over_x, over_y)
+    right = spread(plane[:, 1152:2176], over_y, over_x)
+    in_own = jnp.concatenate([jnp.concatenate(left), jnp.concatenate(right)], axis=1)
+    in_own, plane, out_x, out_pair = together(in_own, plane, out_x, out_pair)
     in_far = over_expert(in_own, 1)
-    in_far, weights0 = together(in_far, weights0)
     out_w_own = plane_gather(plane[:, 2176:])
-    out_w_own, out_pair = together(out_w_own, out_pair)
-    out_w_far = over_expert(out_w_own, 1)
-    out_own = plane_gather(out_pair)
 
     segments = document_numbers[0]
     column, row = segments[:, None], segments[None, :]
@@ -931,36 +984,46 @@
         attend_body, "attend", [(wide, BF16), (wide, BF16), (half, BF16), (half, BF16), (wide, BF16)], [],
         4_000_000_000, place, embedded, column, row, cosine, sine, in_own, in_far,
     )
+    out_w_own, out_pair, out_x, mixed = together(out_w_own, out_pair, out_x, mixed)
+    out_w_far = over_expert(out_w_own, 1)
+    out_blocks = [cotangent, out_x, out_y, over_y(out_x)] + spread(out_pair, over_y, over_x)
     payload, gates, middle, small_all = local_kernel(
         route_body, "route",
         [((288, 1024), BF16), ((SEQUENCE, LANES), F32), (wide, F32), ((1024, LANES), BF16)], [],
         2_000_000_000, place, embedded, mixed, out_w_own, out_w_far, in_own[:, 2048:], in_far[:, 2048:], code,
     )
-    pay_pair = jnp.stack([payload, over_shard(payload, 1)])
-    pay_pair, slices[1] = together(pay_pair, slices[1])
+    pay_pair = over_shard(payload, 1)
+    pay_x, pay_y = over_x(payload), over_y(payload)
+    pay_x, pay_y, pay_pair, *out_blocks = together(pay_x, pay_y, pay_pair, *out_blocks)
+    tok_pair = [pay_pair, over_x(pay_pair), over_y(pay_pair)]
+    tok_own = [payload, pay_x, pay_y, over_y(pay_x)]
+    *tok_pair, weights0, slices[1] = together(*tok_pair, weights0, slices[1])
+    tok_pair.append(over_x(tok_pair[2]))
     weights1 = exchange(slices[1])
-    tok_own = plane_gather(pay_pair)
-    tok_own, out_own = together(tok_own, out_own)
-    tok_far, out_far = over_expert(tok_own, 1), over_expert(out_own, 1)
-    tok_far, weights1 = together(tok_far, weights1)
+    weights0_far = over_expert(weights0, 1)
+    tokens = tok_own + tok_pair
     first = (e * 4 + z % PAIR * OWN).reshape(1)
-    operands = (tok_own, tok_far, out_own, out_far)
-    *sums, expert_grad0 = expert_call(first, *operands, weights0)
-    row_own, row_far, moe_own, moe_far, expert_grad1 = expert_call(first + 1, *operands, weights1, sums)
+    first_far = ((e ^ 1) * 4 + z % PAIR * OWN).reshape(1)
+    sums, grad_a = expert_call(first, tokens, out_blocks, weights0)
+    sums, grad_b = expert_call(first_far, tokens, out_blocks, weights0_far, sums)
+    expert_grad0 = core_sum(grad_a, grad_b)
+    expert_grad0, weights1 = together(expert_grad0, weights1)
     slices0 = exchange(expert_grad0)
-    slices0, row_far, expert_grad1 = together(slices0, row_far, expert_grad1)
+    weights1_far = over_expert(weights1, 1)
+    sums, grad_c = expert_call(first + 1, tokens, out_blocks, weights1, sums)
+    sums, grad_d = expert_call(first_far + 1, tokens, out_blocks, weights1_far, sums)
+    rows, moes = sums[:BLOCKS], sums[BLOCKS:]
+    row_own, row_pair = fold_both(rows)
+    returned = over_shard(row_pair, 1)
+    expert_grad1 = core_sum(grad_c, grad_d)
+    row_own, returned, expert_grad1, slices0, *moes = together(row_own, returned, expert_grad1, slices0, *moes)
     slices1 = exchange(expert_grad1)
-    row_half = core_sum(row_own, row_far)
-    row_half, moe_own, moe_far = together(row_half, moe_own, moe_far)
-    moe_half = core_sum(moe_own, moe_far)
-    row_pair = plane_sum(row_half)
-    row_pair, moe_half, slices1 = together(row_pair, moe_half, slices1)
-    returned = over_shard(row_pair[1], 1)
-    moe_pair = plane_sum(moe_half)
-    moe_other = over_shard(moe_pair[1], 1)
+    moe_pair = fold(moes[4:], over_x, over_y).astype(BF16)
+    moe_own = fold(moes[:4], over_y, over_x)
+    moe_other = over_shard(moe_pair, 1)
     early_own, early_far, mixed_grad, middle_grad = local_kernel(
         turn_body, "turn", [((512, 1152), BF16), ((512, 1152), BF16), (wide, BF16), (wide, F32)],
-        [((1024, LANES), F32)], 4_000_000_000, place, row_pair[0], returned, cotangent, middle, gates,
+        [((1024, LANES), F32)], 4_000_000_000, place, row_own, returned, cotangent, middle, gates,
         small_all, payload, mixed, out_w_own, out_w_far,
     )
     late_own, late_far, grad_embedded = local_kernel(
@@ -977,7 +1040,7 @@
         [slices0[0] + slices0[2], slices1[0] + slices1[2], slices0[1] + slices0[3], slices1[1] + slices1[3]]
     )
     grad_expert_in, grad_expert_out = expert_grads[:, :256], expert_grads[:, 256:]
-    moe = moe_pair[0].astype(F32) + moe_other.astype(F32)
+    moe = moe_own + moe_other.astype(F32)
     output = (middle + resid_scale * moe).astype(BF16)
     return (
         output,

time: 584 us -> 491 us (0.84)
  waiting for transfers between devices: 279 us -> 192 us
  other arithmetic: 72.4 us -> 49.4 us
  starting transfers between devices: 66.3 us -> 80.1 us
  Pallas kernels: 128 us -> 136 us
    all_to_all x4, waiting for transfers between devices: 54.6 us -> 3.02 us  [exchange(): lax.all_to_all(slices, 'shard', split_axis=0, concat_axis=0, tiled=True)]
    ppermute x13, waiting for transfers between devices: 52.1 us -> 29 us  [over_shard(): return lax.ppermute(value, 'shard', [(i, i ^ bits) for i in range(4)])]
    ppermute x32 -> x47, starting transfers between devices: 28.5 us -> 41.4 us  [over_expert(): return lax.ppermute(value, 'expert', [(i, i ^ bits) for i in range(8)])]
    ppermute x32 -> x47, waiting for transfers between devices: 172 us -> 160 us  [over_expert(): return lax.ppermute(value, 'expert', [(i, i ^ bits) for i in range(8)])]
    convert_element_type x0 -> x7, other arithmetic: none -> 9.77 us  [the longest x4 9.13 us: bf_sum(): return sum((value.astype(F32) for value in values)).astype(BF16)]
    concatenate x4 -> x1, other arithmetic: 10.5 us -> 1.05 us  [plane_gather(): jnp.concatenate([value] + [over_expert(value, bits) for bits in (2, 4, 6)])]
    convert_element_type x4 -> x2, other arithmetic: 7.73 us -> 0.43 us  [plane_sum(): return part.astype(BF16)]
    pallas_call x2 -> x4, Pallas kernels: 91.2 us -> 97.6 us  [expert_call(): pl.pallas_call(functools.partial(expert_body, before is None), out_shape=...]
  transfers between devices with their start and end apart: 49 -> 64, of which waited for: 28 -> 31; matrix products, arithmetic and copies ran while one was open for 14% -> 9% of each run, Pallas kernels for 14% -> 28%
where the time goes in v3:
time: 491 us; the launch traced here: 484 us
  waiting for transfers between devices  192 us (39%)
  Pallas kernels  136 us (28%)
  starting transfers between devices  80.1 us (16%)
  other arithmetic  49.4 us (10%)
  local copies, waits for them, and re-layouts  23.1 us (5%)
    ppermute x47, waiting for transfers between devices, over_expert(): return lax.ppermute(value, 'expert', [(i, i ^ bits) for i in range(8)])  160 us
    pallas_call x4, Pallas kernels, expert_call(): pl.pallas_call(functools.partial(expert_body, before is None), out_shape=...  97.6 us
    ppermute x47, starting transfers between devices, over_expert(): return lax.ppermute(value, 'expert', [(i, i ^ bits) for i in range(8)])  41.4 us
    pallas_call x4, Pallas kernels, local_kernel(): pl.pallas_call(body, out_shape=[jax.ShapeDtypeStruct(shape, dtype) for sh...  36.9 us
    ppermute x13, waiting for transfers between devices, over_shard(): return lax.ppermute(value, 'shard', [(i, i ^ bits) for i in range(4)])  29 us
    all_to_all x4, starting transfers between devices, exchange(): lax.all_to_all(slices, 'shard', split_axis=0, concat_axis=0, tiled=True)  19.8 us
    ppermute x13, starting transfers between devices, over_shard(): return lax.ppermute(value, 'shard', [(i, i ^ bits) for i in range(4)])  18.9 us
    concatenate x1, other arithmetic, per_device_fast(): jnp.concatenate([jnp.concatenate(left), jnp.concatenate(right)], axis=1)  13.9 us
  transfers between devices with their start and end apart: 64, of which 31 were waited for; matrix products, arithmetic and copies ran while one was open for 9% of the time, Pallas kernels for 28%

profile of v3, /device:TPU:0, one launch (start us, length us, event | category | flops | bytes accessed | tf_op | source)
XLA Modules:
  0.0 483.7 jit_solution(2049312704655687759)
XLA Ops:
  3.3 1.8 pack.1
  5.2 3.1 collective-permute-start
  8.2 2.6 collective-permute-start.1
  10.8 1.7 collective-permute-start.3
  12.5 1.5 collective-permute-start.4
  14.0 2.7 slice_bitcast_fusion.1
  17.7 1.8 pad_maximum_fusion.1
  20.2 5.9 %collective-permute-done.1 = bf16[32,3200]{1,0:T(8,128)(2,1)S(1)} collective-permute-done((bf16[32,3200]{1,0:T(8,128)(2,1)}, bf16[32,3200]{1,0:T(8,128)(2,1)S(1)}, u32[]{:S(2)}, u32[]{:S(2)}) %collective-permute-start.1) | collective-permute-done | bytes 204832 | tf_op jit(solution)/shard_map/ppermute | solution.py:439
  26.4 9.8 %collective-permute-done.5.refs_12_ = bf16[256,1024]{1,0:T(8,128)(2,1)S(1)} collective-permute-done((bf16[256,1024]{1,0:T(8,128)(2,1)S(1)}, bf16[256,1024]{1,0:T(8,128)(2,1)S(1)}, u32[]{:S(2)}, u32[]{:S(2)}) %collective-permute-start.5) | collective-permute-done | bytes 524320 | tf_op jit(solution)/shard_map/ppermute | solution.py:439
  39.4 5.5 %collective-permute-done.6 = bf16[128,1152]{1,0:T(8,128)(2,1)S(1)} collective-permute-done((bf16[128,1152]{1,0:T(8,128)(2,1)S(1)}, bf16[128,1152]{1,0:T(8,128)(2,1)S(1)}, u32[]{:S(2)}, u32[]{:S(2)}) %collective-permute-start.6) | collective-permute-done | bytes 294944 | tf_op jit(solution)/shard_map/ppermute | solution.py:435
  47.6 7.0 %collective-permute-done.9 = bf16[128,1024]{1,0:T(8,128)(2,1)S(1)} collective-permute-done((bf16[128,1024]{1,0:T(8,128)(2,1)S(1)}, bf16[128,1024]{1,0:T(8,128)(2,1)S(1)}, u32[]{:S(2)}, u32[]{:S(2)}) %collective-permute-start.9) | collective-permute-done | bytes 262176 | tf_op jit(solution)/shard_map/ppermute | solution.py:435
  54.6 3.0 collective-permute-done.11
  57.5 13.9 %maximum_maximum_fusion.own_ref.w_own_ref = bf16[512,2176]{1,0:T(8,128)(2,1)S(1)} fusion(bf16[128,1024]{1,0:T(8,128)(2,1)S(1)} %collective-permute-done.11, bf16[128,1024]{1,0:T(8,128)(2,1)S(1)} %collective-permute-done.10, bf16[128,1024]{1,0:T(8,128)(2,1)S(1)} %collective-permute-done.9, bf16[128,1024]{1,0:T(8,128)(2,1)S(1)} %slice.142, ...), kind=kLoop, calls=%fused_computation.7 | loop fusion | flops 17825792 | bytes 4456448 | tf_op jit(solution)/shard_map/concatenate | solution.py:967
  72.8 5.4 %all-to-all-start = ((bf16[4,384,1024]{2,1,0:T(8,128)(2,1)}), bf16[4,384,1024]{2,1,0:T(8,128)(2,1)}, u32[]{:S(2)}, u32[]{:S(2)}) async-start(bf16[4,384,1024]{2,1,0:T(8,128)(2,1)} %pad_maximum_fusion.1), calls=%async_computation | async-start | bytes 6291456 | tf_op jit(solution)/shard_map/all_to_all | solution.py:873
  84.9 4.2 collective-permute-done.12
  89.5 4.1 collective-permute-done.14
  94.7 9.8 %attend.1 = (bf16[256,1024]{1,0:T(8,128)(2,1)}, bf16[256,1024]{1,0:T(8,128)(2,1)}, bf16[256,512]{1,0:T(8,128)(2,1)}, bf16[256,512]{1,0:T(8,128)(2,1)}, bf16[256,1024]{1,0:T(8,128)(2,1)}) custom-call(s32[1]{0:T(128)} %bitcast.e_ref, bf16[256,1024]{1,0:T(8,128)(2,1)} %x_ref.5, s32[256,1]{1,0:T(8,128)} %copy.34.column_ref, s32[1,256]{1,0:T(1,128)} %row_ref.3, ...), custom_call_target="tpu_custom_call" | custom-call | flops 4000000000 | bytes 5244928 | tf_op jit(solution)/shard_map/attend/pallas_call | solution.py:825
  108.0 1.6 slice.148.small_own_ref
  109.5 1.6 slice.179.small_far_ref
  112.1 4.5 route.1
  118.8 1.7 collective-permute-start.19
  121.1 9.6 %collective-permute-done.20.refs_11_ = bf16[256,1024]{1,0:T(8,128)(2,1)S(1)} collective-permute-done((bf16[256,1024]{1,0:T(8,128)(2,1)}, bf16[256,1024]{1,0:T(8,128)(2,1)S(1)}, u32[]{:S(2)}, u32[]{:S(2)}) %collective-permute-start.20) | collective-permute-done | bytes 524320 | tf_op jit(solution)/shard_map/ppermute | solution.py:435
  131.6 12.6 %collective-permute-done.21.refs_13_ = bf16[256,1024]{1,0:T(8,128)(2,1)S(1)} collective-permute-done((bf16[256,1024]{1,0:T(8,128)(2,1)S(1)}, bf16[256,1024]{1,0:T(8,128)(2,1)S(1)}, u32[]{:S(2)}, u32[]{:S(2)}) %collective-permute-start.21) | collective-permute-done | bytes 524320 | tf_op jit(solution)/shard_map/ppermute | solution.py:435
  144.2 10.2 %collective-permute-done.23.refs_15_ = bf16[256,1024]{1,0:T(8,128)(2,1)S(1)} collective-permute-done((bf16[256,1024]{1,0:T(8,128)(2,1)S(1)}, bf16[256,1024]{1,0:T(8,128)(2,1)S(1)}, u32[]{:S(2)}, u32[]{:S(2)}) %collective-permute-start.23) | collective-permute-done | bytes 524320 | tf_op jit(solution)/shard_map/ppermute | solution.py:435
  157.0 1.9 pad_maximum_fusion.2
  158.9 10.0 %collective-permute-done.25.refs_5_ = bf16[288,1024]{1,0:T(8,128)(2,1)S(1)} collective-permute-done((bf16[288,1024]{1,0:T(8,128)(2,1)S(1)}, bf16[288,1024]{1,0:T(8,128)(2,1)S(1)}, u32[]{:S(2)}, u32[]{:S(2)}) %collective-permute-start.25) | collective-permute-done | bytes 589856 | tf_op jit(solution)/shard_map/ppermute | solution.py:435
  172.0 5.0 %all-to-all-start.1 = ((bf16[4,384,1024]{2,1,0:T(8,128)(2,1)}), bf16[4,384,1024]{2,1,0:T(8,128)(2,1)}, u32[]{:S(2)}, u32[]{:S(2)}) async-start(bf16[4,384,1024]{2,1,0:T(8,128)(2,1)} %pad_maximum_fusion.2), calls=%async_computation.1 | async-start | bytes 6291456 | tf_op jit(solution)/shard_map/all_to_all | solution.py:873
  177.0 8.7 %collective-permute-done.24.refs_3_ = bf16[288,1024]{1,0:T(8,128)(2,1)} collective-permute-done((bf16[288,1024]{1,0:T(8,128)(2,1)}, bf16[288,1024]{1,0:T(8,128)(2,1)}, u32[]{:S(2)}, u32[]{:S(2)}) %collective-permute-start.24) | collective-permute-done | bytes 589856 | tf_op jit(solution)/shard_map/ppermute | solution.py:435
  186.7 22.2 %expert.4 = (bf16[272,1024]{1,0:T(8,128)(2,1)}, bf16[272,1024]{1,0:T(8,128)(2,1)}, bf16[272,1024]{1,0:T(8,128)(2,1)}, bf16[272,1024]{1,0:T(8,128)(2,1)}, bf16[27...) custom-call(s32[1]{0:T(128)} %bitcast.27.number_ref, ...), custom_call_target="tpu_custom_call" | custom-call | flops 12000000000 | bytes 30000000 | tf_op jit(solution)/shard_map/expert/pallas_call | solution.py:586
  208.9 1.6 copy-done.18
  210.6 25.3 %expert.5 = (bf16[272,1024]{1,0:T(8,128)(2,1)}, bf16[272,1024]{1,0:T(8,128)(2,1)}, bf16[272,1024]{1,0:T(8,128)(2,1)}, bf16[272,1024]{1,0:T(8,128)(2,1)}, bf16[27...) custom-call(s32[1]{0:T(128)} %bitcast.20.number_ref, ...), custom_call_target="tpu_custom_call" | custom-call | flops 12000000000 | bytes 30000000 | tf_op jit(solution)/shard_map/expert/pallas_call | solution.py:586
  236.0 5.9 %collective-permute-done.29 = bf16[4,384,1024]{2,1,0:T(8,128)(2,1)S(1)} collective-permute-done((bf16[4,384,1024]{2,1,0:T(8,128)(2,1)}, bf16[4,384,1024]{2,1,0:T(8,128)(2,1)S(1)}, u32[]{:S(2)}, u32[]{:S(2)}) %collective-permute-start.29) | collective-permute-done | bytes 3145760 | tf_op jit(solution)/shard_map/ppermute | solution.py:435
  241.8 3.2 add_convert_fusion.1
  245.1 3.0 all-to-all-done.1.refs_16_
  248.1 3.9 all-to-all-start.2
  251.9 25.0 %expert.6 = (bf16[272,1024]{1,0:T(8,128)(2,1)}, bf16[272,1024]{1,0:T(8,128)(2,1)}, bf16[272,1024]{1,0:T(8,128)(2,1)}, bf16[272,1024]{1,0:T(8,128)(2,1)}, bf16[27...) custom-call(s32[1]{0:T(128)S(6)} %add.162.number_ref, ...), custom_call_target="tpu_custom_call" | custom-call | flops 12000000000 | bytes 30000000 | tf_op jit(solution)/shard_map/expert/pallas_call | solution.py:586
  277.0 25.1 %expert.7 = (bf16[272,1024]{1,0:T(8,128)(2,1)}, bf16[272,1024]{1,0:T(8,128)(2,1)}, bf16[272,1024]{1,0:T(8,128)(2,1)}, bf16[272,1024]{1,0:T(8,128)(2,1)}, bf16[27...) custom-call(s32[1]{0:T(128)S(6)} %add.159.number_ref, ...), custom_call_target="tpu_custom_call" | custom-call | flops 12000000000 | bytes 30000000 | tf_op jit(solution)/shard_map/expert/pallas_call | solution.py:586
  305.4 13.0 %collective-permute-done.31 = bf16[272,1024]{1,0:T(8,128)(2,1)S(1)} collective-permute-done((bf16[272,1024]{1,0:T(8,128)(2,1)}, bf16[272,1024]{1,0:T(8,128)(2,1)S(1)}, u32[]{:S(2)}, u32[]{:S(2)}) %collective-permute-start.31) | collective-permute-done | bytes 557088 | tf_op jit(solution)/shard_map/ppermute | solution.py:435
  318.4 2.1 add_convert_fusion.6
  322.5 2.1 add_convert_fusion.8
  325.6 4.9 %collective-permute-done.35 = bf16[272,1024]{1,0:T(8,128)(2,1)} collective-permute-done((bf16[272,1024]{1,0:T(8,128)(2,1)}, bf16[272,1024]{1,0:T(8,128)(2,1)}, u32[]{:S(2)}, u32[]{:S(2)}) %collective-permute-start.35) | collective-permute-done | bytes 557088 | tf_op jit(solution)/shard_map/ppermute | solution.py:435
  330.4 5.9 %collective-permute-done.36 = bf16[272,1024]{1,0:T(8,128)(2,1)} collective-permute-done((bf16[272,1024]{1,0:T(8,128)(2,1)}, bf16[272,1024]{1,0:T(8,128)(2,1)}, u32[]{:S(2)}, u32[]{:S(2)}) %collective-permute-start.36) | collective-permute-done | bytes 557088 | tf_op jit(solution)/shard_map/ppermute | solution.py:435
  336.3 2.7 add_convert_fusion.5
  339.0 1.7 collective-permute-start.37
  340.7 4.9 %collective-permute-done.32 = bf16[272,1024]{1,0:T(8,128)(2,1)} collective-permute-done((bf16[272,1024]{1,0:T(8,128)(2,1)}, bf16[272,1024]{1,0:T(8,128)(2,1)}, u32[]{:S(2)}, u32[]{:S(2)}) %collective-permute-start.32) | collective-permute-done | bytes 557088 | tf_op jit(solution)/shard_map/ppermute | solution.py:435
  345.6 2.3 add_convert_fusion.7.sum_ref
  347.9 5.1 %add_convert_fusion = bf16[4,384,1024]{2,1,0:T(8,128)(2,1)} fusion(bf16[4,384,1024]{2,1,0:T(8,128)(2,1)} %collective-permute-done.38, bf16[4,384,1024]{2,1,0:T(8,128)(2,1)S(1)} %copy-done), kind=kLoop, calls=%fused_computation.1 | loop fusion | flops 6291456 | bytes 9437184 | tf_op jit(solution)/shard_map/convert_element_type | solution.py:854
  353.0 5.4 %all-to-all-start.3 = ((bf16[4,384,1024]{2,1,0:T(8,128)(2,1)}), bf16[4,384,1024]{2,1,0:T(8,128)(2,1)}, u32[]{:S(2)}, u32[]{:S(2)}) async-start(bf16[4,384,1024]{2,1,0:T(8,128)(2,1)} %add_convert_fusion), calls=%async_computation.3 | async-start | bytes 6291456 | tf_op jit(solution)/shard_map/all_to_all | solution.py:873
  358.5 6.2 %turn.1 = (bf16[512,1152]{1,0:T(8,128)(2,1)}, bf16[512,1152]{1,0:T(8,128)(2,1)}, bf16[256,1024]{1,0:T(8,128)(2,1)}, f32[256,1024]{1,0:T(8,128)}) custom-call(s32[1]{0:T(128)} %bitcast.e_ref, bf16[272,1024]{1,0:T(8,128)(2,1)} %add_convert_fusion.7.sum_ref, bf16[272,1024]{1,0:T(8,128)(2,1)} %collective-permute-done.37.add_ref, bf16[256,1024]{1,0:T(8,128)(2,1)} %grad_ref.1, ...), custom_call_target="tpu_custom_call" | custom-call | flops 4000000000 | bytes 6291456 | tf_op jit(solution)/shard_map/turn/pallas_call | solution.py:825
  365.7 16.5 %attend_back.1 = (bf16[512,2176]{1,0:T(8,128)(2,1)}, bf16[512,2176]{1,0:T(8,128)(2,1)}, bf16[256,1024]{1,0:T(8,128)(2,1)}) custom-call(s32[1]{0:T(128)} %bitcast.e_ref, bf16[256,1024]{1,0:T(8,128)(2,1)} %x_ref.5, s32[256,1]{1,0:T(8,128)} %copy.34.column_ref, s32[1,256]{1,0:T(1,128)} %row_ref.3, f32[256,128]{1,0:T(8,128)} %get-tuple-element.307.cos_ref, ...), custom_call_target="tpu_custom_call" | custom-call | flops 8000000000 | bytes 8390656 | tf_op jit(solution)/shard_map/attend_back/pallas_call | solution.py:825
  389.5 9.3 %collective-permute-done.40 = bf16[256,1024]{1,0:T(8,128)(2,1)S(1)} collective-permute-done((bf16[256,1024]{1,0:T(8,128)(2,1)S(1)}, bf16[256,1024]{1,0:T(8,128)(2,1)S(1)}, u32[]{:S(2)}, u32[]{:S(2)}) %collective-permute-start.40) | collective-permute-done | bytes 524320 | tf_op jit(solution)/shard_map/ppermute | solution.py:435
  399.6 1.7 collective-permute-start.56
  401.5 14.9 %collective-permute-done.44 = bf16[256,1024]{1,0:T(8,128)(2,1)S(1)} collective-permute-done((bf16[256,1024]{1,0:T(8,128)(2,1)S(1)}, bf16[256,1024]{1,0:T(8,128)(2,1)S(1)}, u32[]{:S(2)}, u32[]{:S(2)}) %collective-permute-start.44) | collective-permute-done | bytes 524320 | tf_op jit(solution)/shard_map/ppermute | solution.py:435
  418.4 4.2 collective-permute-done.55
  422.9 2.1 collective-permute-start.57
  425.0 2.3 collective-permute-start.58
  428.1 1.8 collective-permute-done.57
  436.7 8.6 %collective-permute-done.47 = bf16[128,2176]{1,0:T(8,128)(2,1)S(1)} collective-permute-done((bf16[128,2176]{1,0:T(8,128)(2,1)S(1)}, bf16[128,2176]{1,0:T(8,128)(2,1)S(1)}, u32[]{:S(2)}, u32[]{:S(2)}) %collective-permute-start.47) | collective-permute-done | bytes 557088 | tf_op jit(solution)/shard_map/ppermute | solution.py:435
  445.5 11.7 %collective-permute-done.48 = bf16[128,2176]{1,0:T(8,128)(2,1)S(1)} collective-permute-done((bf16[128,2176]{1,0:T(8,128)(2,1)S(1)}, bf16[128,2176]{1,0:T(8,128)(2,1)S(1)}, u32[]{:S(2)}, u32[]{:S(2)}) %collective-permute-start.48) | collective-permute-done | bytes 557088 | tf_op jit(solution)/shard_map/ppermute | solution.py:435
  457.5 2.1 collective-permute-start.50
  459.6 2.4 collective-permute-start.51
  464.5 8.2 %collective-permute-done.51 = bf16[32,2176]{1,0:T(8,128)(2,1)S(1)} collective-permute-done((bf16[32,2176]{1,0:T(8,128)(2,1)S(1)}, bf16[32,2176]{1,0:T(8,128)(2,1)S(1)}, u32[]{:S(2)}, u32[]{:S(2)}) %collective-permute-start.51) | collective-permute-done | bytes 139296 | tf_op jit(solution)/shard_map/ppermute | solution.py:439
  474.9 2.6 convert_element_type.253
  480.6 2.6 slice.203
  (210 shorter events, 68.5 us)
Async XLA Ops:
  5.2 14.4 %collective-permute-start = (bf16[32,3200]{1,0:T(8,128)(2,1)}, bf16[32,3200]{1,0:T(8,128)(2,1)S(1)}, u32[]{:S(2)}, u32[]{:S(2)}) collective-permute-start(bf16[32,3200]{1,0:T(8,128)(2,1)} %pack.1), channel_id=1, source_target_pairs={{0,1},{1,0},{2,3},{3,2},{4,5},{5,4},{6,7},{7,6},{8,9},{9,8},{10,11... | collective-permute-start | bytes 614408 | tf_op jit(solution)/shard_map/ppermute | solution.py:439
  8.2 17.9 %collective-permute-start.1 = (bf16[32,3200]{1,0:T(8,128)(2,1)}, bf16[32,3200]{1,0:T(8,128)(2,1)S(1)}, u32[]{:S(2)}, u32[]{:S(2)}) collective-permute-start(bf16[32,3200]{1,0:T(8,128)(2,1)} %pack.1), channel_id=1, source_target_pairs={{0,2},{1,3},{2,0},{3,1},{4,6},{5,7},{6,4},{7,5},{8,10},{9,11},{10,... | collective-permute-start | bytes 614408 | tf_op jit(solution)/shard_map/ppermute | solution.py:439
  10.8 15.3 %collective-permute-start.2 = (bf16[32,3200]{1,0:T(8,128)(2,1)}, bf16[32,3200]{1,0:T(8,128)(2,1)S(1)}, u32[]{:S(2)}, u32[]{:S(2)}) collective-permute-start(bf16[32,3200]{1,0:T(8,128)(2,1)} %pack.1), channel_id=1, source_target_pairs={{0,3},{1,2},{2,1},{3,0},{4,7},{5,6},{6,5},{7,4},{8,11},{9,10},{10,... | collective-permute-start | bytes 614408 | tf_op jit(solution)/shard_map/ppermute | solution.py:439
  10.8 15.6 %collective-permute-start.3 = (bf16[256,1024]{1,0:T(8,128)(2,1)}, bf16[256,1024]{1,0:T(8,128)(2,1)}, u32[]{:S(2)}, u32[]{:S(2)}) collective-permute-start(bf16[256,1024]{1,0:T(8,128)(2,1)} %grad_ref.1), channel_id=1, source_target_pairs={{0,8},{4,12},{8,0},{12,4},{16,24},{20,28},{24,16},{28,20},{1,9},{5... | collective-permute-start | bytes 1572872 | tf_op jit(solution)/shard_map/ppermute | solution.py:435
  12.5 13.9 %collective-permute-start.4 = (bf16[256,1024]{1,0:T(8,128)(2,1)}, bf16[256,1024]{1,0:T(8,128)(2,1)}, u32[]{:S(2)}, u32[]{:S(2)}) collective-permute-start(bf16[256,1024]{1,0:T(8,128)(2,1)} %grad_ref.1), channel_id=1, source_target_pairs={{0,16},{4,20},{8,24},{12,28},{16,0},{20,4},{24,8},{28,12},{1,17},{... | collective-permute-start | bytes 1572872 | tf_op jit(solution)/shard_map/ppermute | solution.py:435
  19.5 16.7 %collective-permute-start.5 = (bf16[256,1024]{1,0:T(8,128)(2,1)S(1)}, bf16[256,1024]{1,0:T(8,128)(2,1)S(1)}, u32[]{:S(2)}, u32[]{:S(2)}) collective-permute-start(bf16[256,1024]{1,0:T(8,128)(2,1)S(1)} %copy-done.25), channel_id=1, source_target_pairs={{0,1},{1,0},{2,3},{3,2},{4,5},{5,4},{6,7},{7,6},{8,9},{9,8},{10,11... | collective-permute-start | bytes 1572872 | tf_op jit(solution)/shard_map/ppermute | solution.py:439
  36.2 8.6 %collective-permute-start.6 = (bf16[128,1152]{1,0:T(8,128)(2,1)S(1)}, bf16[128,1152]{1,0:T(8,128)(2,1)S(1)}, u32[]{:S(2)}, u32[]{:S(2)}) collective-permute-start(bf16[128,1152]{1,0:T(8,128)(2,1)S(1)} %slice.141), channel_id=1, source_target_pairs={{0,8},{4,12},{8,0},{12,4},{16,24},{20,28},{24,16},{28,20},{1,9},{5... | collective-permute-start | bytes 884744 | tf_op jit(solution)/shard_map/ppermute | solution.py:435
  37.3 9.2 %collective-permute-start.10 = (bf16[128,1024]{1,0:T(8,128)(2,1)S(1)}, bf16[128,1024]{1,0:T(8,128)(2,1)S(1)}, u32[]{:S(2)}, u32[]{:S(2)}) collective-permute-start(bf16[128,1024]{1,0:T(8,128)(2,1)S(1)} %slice.142), channel_id=1, source_target_pairs={{0,16},{4,20},{8,24},{12,28},{16,0},{20,4},{24,8},{28,12},{1,17},{... | collective-permute-start | bytes 786440 | tf_op jit(solution)/shard_map/ppermute | solution.py:435
  38.3 16.3 %collective-permute-start.7 = (bf16[128,1152]{1,0:T(8,128)(2,1)S(1)}, bf16[128,1152]{1,0:T(8,128)(2,1)S(1)}, u32[]{:S(2)}, u32[]{:S(2)}) collective-permute-start(bf16[128,1152]{1,0:T(8,128)(2,1)S(1)} %slice.141), channel_id=1, source_target_pairs={{0,16},{4,20},{8,24},{12,28},{16,0},{20,4},{24,8},{28,12},{1,17},{... | collective-permute-start | bytes 884744 | tf_op jit(solution)/shard_map/ppermute | solution.py:435
  44.9 12.7 %collective-permute-start.8 = (bf16[128,1152]{1,0:T(8,128)(2,1)S(1)}, bf16[128,1152]{1,0:T(8,128)(2,1)S(1)}, u32[]{:S(2)}, u32[]{:S(2)}) collective-permute-start(bf16[128,1152]{1,0:T(8,128)(2,1)S(1)} %collective-permute-done.6), channel_id=1, source_target_pairs={{0,16},{4,20},{8,24},{12,28},{16,0},{20,4},{24,8},{28,12},{1,17},{... | collective-permute-start | bytes 884744 | tf_op jit(solution)/shard_map/ppermute | solution.py:435
  45.4 9.2 %collective-permute-start.9 = (bf16[128,1024]{1,0:T(8,128)(2,1)S(1)}, bf16[128,1024]{1,0:T(8,128)(2,1)S(1)}, u32[]{:S(2)}, u32[]{:S(2)}) collective-permute-start(bf16[128,1024]{1,0:T(8,128)(2,1)S(1)} %slice.142), channel_id=1, source_target_pairs={{0,8},{4,12},{8,0},{12,4},{16,24},{20,28},{24,16},{28,20},{1,9},{5... | collective-permute-start | bytes 786440 | tf_op jit(solution)/shard_map/ppermute | solution.py:435
  46.6 10.9 %collective-permute-start.11 = (bf16[128,1024]{1,0:T(8,128)(2,1)S(1)}, bf16[128,1024]{1,0:T(8,128)(2,1)S(1)}, u32[]{:S(2)}, u32[]{:S(2)}) collective-permute-start(bf16[128,1024]{1,0:T(8,128)(2,1)S(1)} %collective-permute-done.10), channel_id=1, source_target_pairs={{0,8},{4,12},{8,0},{12,4},{16,24},{20,28},{24,16},{28,20},{1,9},{5... | collective-permute-start | bytes 786440 | tf_op jit(solution)/shard_map/ppermute | solution.py:435
  71.4 23.2 %collective-permute-start.15 = (bf16[512,2176]{1,0:T(8,128)(2,1)S(1)}, bf16[512,2176]{1,0:T(8,128)(2,1)}, u32[]{:S(2)}, u32[]{:S(2)}) collective-permute-start(bf16[512,2176]{1,0:T(8,128)(2,1)S(1)} %maximum_maximum_fusion.own_ref.w_own_ref), channel_id=1, source_target_pairs={{0,4},{4,0},{8,12},{12,8},{16,20},{20,16},{24,28},{28,24},{1,5},{5... | collective-permute-start | bytes 6684680 | tf_op jit(solution)/shard_map/ppermute | solution.py:435
  72.8 86.1 %all-to-all-start = ((bf16[4,384,1024]{2,1,0:T(8,128)(2,1)}), bf16[4,384,1024]{2,1,0:T(8,128)(2,1)}, u32[]{:S(2)}, u32[]{:S(2)}) async-start(bf16[4,384,1024]{2,1,0:T(8,128)(2,1)} %pad_maximum_fusion.1), calls=%async_computation | async-start | bytes 6291456 | tf_op jit(solution)/shard_map/all_to_all | solution.py:873
  79.9 9.2 %collective-permute-start.12 = (bf16[128,1024]{1,0:T(8,128)(2,1)S(1)}, bf16[128,1024]{1,0:T(8,128)(2,1)S(1)}, u32[]{:S(2)}, u32[]{:S(2)}) collective-permute-start(bf16[128,1024]{1,0:T(8,128)(2,1)S(1)} %slice.143), channel_id=1, source_target_pairs={{0,8},{4,12},{8,0},{12,4},{16,24},{20,28},{24,16},{28,20},{1,9},{5... | collective-permute-start | bytes 786440 | tf_op jit(solution)/shard_map/ppermute | solution.py:435
  81.0 8.5 %collective-permute-start.13 = (bf16[128,1024]{1,0:T(8,128)(2,1)S(1)}, bf16[128,1024]{1,0:T(8,128)(2,1)S(1)}, u32[]{:S(2)}, u32[]{:S(2)}) collective-permute-start(bf16[128,1024]{1,0:T(8,128)(2,1)S(1)} %slice.143), channel_id=1, source_target_pairs={{0,16},{4,20},{8,24},{12,28},{16,0},{20,4},{24,8},{28,12},{1,17},{... | collective-permute-start | bytes 786440 | tf_op jit(solution)/shard_map/ppermute | solution.py:435
  81.9 11.7 %collective-permute-start.14 = (bf16[128,1024]{1,0:T(8,128)(2,1)S(1)}, bf16[128,1024]{1,0:T(8,128)(2,1)S(1)}, u32[]{:S(2)}, u32[]{:S(2)}) collective-permute-start(bf16[128,1024]{1,0:T(8,128)(2,1)S(1)} %slice.143), channel_id=1, source_target_pairs={{0,24},{4,28},{8,16},{12,20},{16,8},{20,12},{24,0},{28,4},{1,25},{... | collective-permute-start | bytes 786440 | tf_op jit(solution)/shard_map/ppermute | solution.py:435
  104.4 6.7 %collective-permute-start.16 = (bf16[512,1024]{1,0:T(8,128)(2,1)}, bf16[512,1024]{1,0:T(8,128)(2,1)S(1)}, u32[]{:S(2)}, u32[]{:S(2)}) collective-permute-start(bf16[512,1024]{1,0:T(8,128)(2,1)} %pad_maximum_fusion.4.w_own_ref), channel_id=1, source_target_pairs={{0,4},{4,0},{8,12},{12,8},{16,20},{20,16},{24,28},{28,24},{1,5},{5... | collective-permute-start | bytes 3145736 | tf_op jit(solution)/shard_map/ppermute | solution.py:435
  104.6 16.0 %collective-permute-start.22 = (bf16[256,1024]{1,0:T(8,128)(2,1)S(1)}, bf16[256,1024]{1,0:T(8,128)(2,1)S(1)}, u32[]{:S(2)}, u32[]{:S(2)}) collective-permute-start(bf16[256,1024]{1,0:T(8,128)(2,1)S(1)} %copy-done.27), channel_id=1, source_target_pairs={{0,16},{4,20},{8,24},{12,28},{16,0},{20,4},{24,8},{28,12},{1,17},{... | collective-permute-start | bytes 1572872 | tf_op jit(solution)/shard_map/ppermute | solution.py:435
  105.5 25.2 %collective-permute-start.20 = (bf16[256,1024]{1,0:T(8,128)(2,1)}, bf16[256,1024]{1,0:T(8,128)(2,1)S(1)}, u32[]{:S(2)}, u32[]{:S(2)}) collective-permute-start(bf16[256,1024]{1,0:T(8,128)(2,1)} %collective-permute-done.3.refs_9_), channel_id=1, source_target_pairs={{0,16},{4,20},{8,24},{12,28},{16,0},{20,4},{24,8},{28,12},{1,17},{... | collective-permute-start | bytes 1572872 | tf_op jit(solution)/shard_map/ppermute | solution.py:435
  116.5 37.9 %collective-permute-start.17 = (bf16[288,1024]{1,0:T(8,128)(2,1)}, bf16[288,1024]{1,0:T(8,128)(2,1)S(1)}, u32[]{:S(2)}, u32[]{:S(2)}) collective-permute-start(bf16[288,1024]{1,0:T(8,128)(2,1)} %get-tuple-element.154.refs_0_.normed2_ref), channel_id=1, source_target_pairs={{0,8},{4,12},{8,0},{12,4},{16,24},{20,28},{24,16},{28,20},{1,9},{5... | collective-permute-start | bytes 1769480 | tf_op jit(solution)/shard_map/ppermute | solution.py:435
  117.4 37.0 %collective-permute-start.18 = (bf16[288,1024]{1,0:T(8,128)(2,1)}, bf16[288,1024]{1,0:T(8,128)(2,1)S(1)}, u32[]{:S(2)}, u32[]{:S(2)}) collective-permute-start(bf16[288,1024]{1,0:T(8,128)(2,1)} %get-tuple-element.154.refs_0_.normed2_ref), channel_id=1, source_target_pairs={{0,16},{4,20},{8,24},{12,28},{16,0},{20,4},{24,8},{28,12},{1,17},{... | collective-permute-start | bytes 1769480 | tf_op jit(solution)/shard_map/ppermute | solution.py:435
  118.8 35.6 %collective-permute-start.19 = (bf16[288,1024]{1,0:T(8,128)(2,1)}, bf16[288,1024]{1,0:T(8,128)(2,1)S(1)}, u32[]{:S(2)}, u32[]{:S(2)}) collective-permute-start(bf16[288,1024]{1,0:T(8,128)(2,1)} %get-tuple-element.154.refs_0_.normed2_ref), channel_id=1, source_target_pairs={{0,1},{1,0},{2,3},{3,2},{4,5},{5,4},{6,7},{7,6},{8,9},{9,8},{10,11... | collective-permute-start | bytes 1769480 | tf_op jit(solution)/shard_map/ppermute | solution.py:439
  120.5 23.6 %collective-permute-start.21 = (bf16[256,1024]{1,0:T(8,128)(2,1)S(1)}, bf16[256,1024]{1,0:T(8,128)(2,1)S(1)}, u32[]{:S(2)}, u32[]{:S(2)}) collective-permute-start(bf16[256,1024]{1,0:T(8,128)(2,1)S(1)} %copy-done.27), channel_id=1, source_target_pairs={{0,8},{4,12},{8,0},{12,4},{16,24},{20,28},{24,16},{28,20},{1,9},{5... | collective-permute-start | bytes 1572872 | tf_op jit(solution)/shard_map/ppermute | solution.py:435
  130.7 23.7 %collective-permute-start.23 = (bf16[256,1024]{1,0:T(8,128)(2,1)S(1)}, bf16[256,1024]{1,0:T(8,128)(2,1)S(1)}, u32[]{:S(2)}, u32[]{:S(2)}) collective-permute-start(bf16[256,1024]{1,0:T(8,128)(2,1)S(1)} %collective-permute-done.22.refs_14_), channel_id=1, source_target_pairs={{0,8},{4,12},{8,0},{12,4},{16,24},{20,28},{24,16},{28,20},{1,9},{5... | collective-permute-start | bytes 1572872 | tf_op jit(solution)/shard_map/ppermute | solution.py:435
  154.4 14.4 %collective-permute-start.25 = (bf16[288,1024]{1,0:T(8,128)(2,1)S(1)}, bf16[288,1024]{1,0:T(8,128)(2,1)S(1)}, u32[]{:S(2)}, u32[]{:S(2)}) collective-permute-start(bf16[288,1024]{1,0:T(8,128)(2,1)S(1)} %collective-permute-done.19.refs_4_), channel_id=1, source_target_pairs={{0,8},{4,12},{8,0},{12,4},{16,24},{20,28},{24,16},{28,20},{1,9},{5... | collective-permute-start | bytes 1769480 | tf_op jit(solution)/shard_map/ppermute | solution.py:435
  155.4 14.3 %collective-permute-start.26 = (bf16[288,1024]{1,0:T(8,128)(2,1)S(1)}, bf16[288,1024]{1,0:T(8,128)(2,1)}, u32[]{:S(2)}, u32[]{:S(2)}) collective-permute-start(bf16[288,1024]{1,0:T(8,128)(2,1)S(1)} %collective-permute-done.19.refs_4_), channel_id=1, source_target_pairs={{0,16},{4,20},{8,24},{12,28},{16,0},{20,4},{24,8},{28,12},{1,17},{... | collective-permute-start | bytes 1769480 | tf_op jit(solution)/shard_map/ppermute | solution.py:435
  169.7 39.2 %collective-permute-start.28 = (bf16[4,384,1024]{2,1,0:T(8,128)(2,1)}, bf16[4,384,1024]{2,1,0:T(8,128)(2,1)S(1)}, u32[]{:S(2)}, u32[]{:S(2)}) collective-permute-start(bf16[4,384,1024]{2,1,0:T(8,128)(2,1)} %all-to-all-done.refs_16_), channel_id=1, source_target_pairs={{0,4},{4,0},{8,12},{12,8},{16,20},{20,16},{24,28},{28,24},{1,5},{5... | collective-permute-start | bytes 9437192 | tf_op jit(solution)/shard_map/ppermute | solution.py:435
  169.7 16.1 %collective-permute-start.24 = (bf16[288,1024]{1,0:T(8,128)(2,1)}, bf16[288,1024]{1,0:T(8,128)(2,1)}, u32[]{:S(2)}, u32[]{:S(2)}) collective-permute-start(bf16[288,1024]{1,0:T(8,128)(2,1)} %copy-done.21), channel_id=1, source_target_pairs={{0,16},{4,20},{8,24},{12,28},{16,0},{20,4},{24,8},{28,12},{1,17},{... | collective-permute-start | bytes 1769480 | tf_op jit(solution)/shard_map/ppermute | solution.py:435
  171.0 15.8 %collective-permute-start.27 = (bf16[288,1024]{1,0:T(8,128)(2,1)}, bf16[288,1024]{1,0:T(8,128)(2,1)}, u32[]{:S(2)}, u32[]{:S(2)}) collective-permute-start(bf16[288,1024]{1,0:T(8,128)(2,1)} %collective-permute-done.26.refs_6_), channel_id=1, source_target_pairs={{0,8},{4,12},{8,0},{12,4},{16,24},{20,28},{24,16},{28,20},{1,9},{5... | collective-permute-start | bytes 1769480 | tf_op jit(solution)/shard_map/ppermute | solution.py:435
  172.0 76.1 %all-to-all-start.1 = ((bf16[4,384,1024]{2,1,0:T(8,128)(2,1)}), bf16[4,384,1024]{2,1,0:T(8,128)(2,1)}, u32[]{:S(2)}, u32[]{:S(2)}) async-start(bf16[4,384,1024]{2,1,0:T(8,128)(2,1)} %pad_maximum_fusion.2), calls=%async_computation.1 | async-start | bytes 6291456 | tf_op jit(solution)/shard_map/all_to_all | solution.py:873
  235.9 5.9 %collective-permute-start.29 = (bf16[4,384,1024]{2,1,0:T(8,128)(2,1)}, bf16[4,384,1024]{2,1,0:T(8,128)(2,1)S(1)}, u32[]{:S(2)}, u32[]{:S(2)}) collective-permute-start(bf16[4,384,1024]{2,1,0:T(8,128)(2,1)} %get-tuple-element.191), channel_id=1, source_target_pairs={{0,4},{4,0},{8,12},{12,8},{16,20},{20,16},{24,28},{28,24},{1,5},{5... | collective-permute-start | bytes 9437192 | tf_op jit(solution)/shard_map/ppermute | solution.py:435
  248.1 28.9 %collective-permute-start.30 = (bf16[4,384,1024]{2,1,0:T(8,128)(2,1)}, bf16[4,384,1024]{2,1,0:T(8,128)(2,1)}, u32[]{:S(2)}, u32[]{:S(2)}) collective-permute-start(bf16[4,384,1024]{2,1,0:T(8,128)(2,1)} %all-to-all-done.1.refs_16_), channel_id=1, source_target_pairs={{0,4},{4,0},{8,12},{12,8},{16,20},{20,16},{24,28},{28,24},{1,5},{5... | collective-permute-start | bytes 9437192 | tf_op jit(solution)/shard_map/ppermute | solution.py:435
  248.1 105.0 %all-to-all-start.2 = ((bf16[4,384,1024]{2,1,0:T(8,128)(2,1)}), bf16[4,384,1024]{2,1,0:T(8,128)(2,1)S(1)}, u32[]{:S(2)}, u32[]{:S(2)}) async-start(bf16[4,384,1024]{2,1,0:T(8,128)(2,1)} %add_convert_fusion.1), calls=%async_computation.2 | async-start | bytes 6291456 | tf_op jit(solution)/shard_map/all_to_all | solution.py:873
  302.1 45.8 %collective-permute-start.38 = (bf16[4,384,1024]{2,1,0:T(8,128)(2,1)}, bf16[4,384,1024]{2,1,0:T(8,128)(2,1)}, u32[]{:S(2)}, u32[]{:S(2)}) collective-permute-start(bf16[4,384,1024]{2,1,0:T(8,128)(2,1)} %get-tuple-element.236), channel_id=1, source_target_pairs={{0,4},{4,0},{8,12},{12,8},{16,20},{20,16},{24,28},{28,24},{1,5},{5... | collective-permute-start | bytes 9437192 | tf_op jit(solution)/shard_map/ppermute | solution.py:435
  302.7 15.7 %collective-permute-start.31 = (bf16[272,1024]{1,0:T(8,128)(2,1)}, bf16[272,1024]{1,0:T(8,128)(2,1)S(1)}, u32[]{:S(2)}, u32[]{:S(2)}) collective-permute-start(bf16[272,1024]{1,0:T(8,128)(2,1)} %get-tuple-element.228), channel_id=1, source_target_pairs={{0,8},{4,12},{8,0},{12,4},{16,24},{20,28},{24,16},{28,20},{1,9},{5... | collective-permute-start | bytes 1671176 | tf_op jit(solution)/shard_map/ppermute | solution.py:435
  303.7 18.8 %collective-permute-start.33 = (bf16[272,1024]{1,0:T(8,128)(2,1)}, bf16[272,1024]{1,0:T(8,128)(2,1)S(1)}, u32[]{:S(2)}, u32[]{:S(2)}) collective-permute-start(bf16[272,1024]{1,0:T(8,128)(2,1)} %get-tuple-element.231), channel_id=1, source_target_pairs={{0,16},{4,20},{8,24},{12,28},{16,0},{20,4},{24,8},{28,12},{1,17},{... | collective-permute-start | bytes 1671176 | tf_op jit(solution)/shard_map/ppermute | solution.py:435
  304.4 26.0 %collective-permute-start.35 = (bf16[272,1024]{1,0:T(8,128)(2,1)}, bf16[272,1024]{1,0:T(8,128)(2,1)}, u32[]{:S(2)}, u32[]{:S(2)}) collective-permute-start(bf16[272,1024]{1,0:T(8,128)(2,1)} %get-tuple-element.233), channel_id=1, source_target_pairs={{0,8},{4,12},{8,0},{12,4},{16,24},{20,28},{24,16},{28,20},{1,9},{5... | collective-permute-start | bytes 1671176 | tf_op jit(solution)/shard_map/ppermute | solution.py:435
  320.5 15.8 %collective-permute-start.36 = (bf16[272,1024]{1,0:T(8,128)(2,1)}, bf16[272,1024]{1,0:T(8,128)(2,1)}, u32[]{:S(2)}, u32[]{:S(2)}) collective-permute-start(bf16[272,1024]{1,0:T(8,128)(2,1)} %add_convert_fusion.6), channel_id=1, source_target_pairs={{0,16},{4,20},{8,24},{12,28},{16,0},{20,4},{24,8},{28,12},{1,17},{... | collective-permute-start | bytes 1671176 | tf_op jit(solution)/shard_map/ppermute | solution.py:435
  321.2 24.4 %collective-permute-start.32 = (bf16[272,1024]{1,0:T(8,128)(2,1)}, bf16[272,1024]{1,0:T(8,128)(2,1)}, u32[]{:S(2)}, u32[]{:S(2)}) collective-permute-start(bf16[272,1024]{1,0:T(8,128)(2,1)} %get-tuple-element.229), channel_id=1, source_target_pairs={{0,16},{4,20},{8,24},{12,28},{16,0},{20,4},{24,8},{28,12},{1,17},{... | collective-permute-start | bytes 1671176 | tf_op jit(solution)/shard_map/ppermute | solution.py:435
  324.6 21.0 %collective-permute-start.34 = (bf16[272,1024]{1,0:T(8,128)(2,1)}, bf16[272,1024]{1,0:T(8,128)(2,1)}, u32[]{:S(2)}, u32[]{:S(2)}) collective-permute-start(bf16[272,1024]{1,0:T(8,128)(2,1)} %add_convert_fusion.8), channel_id=1, source_target_pairs={{0,8},{4,12},{8,0},{12,4},{16,24},{20,28},{24,16},{28,20},{1,9},{5... | collective-permute-start | bytes 1671176 | tf_op jit(solution)/shard_map/ppermute | solution.py:435
  339.0 14.1 %collective-permute-start.37 = (bf16[272,1024]{1,0:T(8,128)(2,1)}, bf16[272,1024]{1,0:T(8,128)(2,1)}, u32[]{:S(2)}, u32[]{:S(2)}) collective-permute-start(bf16[272,1024]{1,0:T(8,128)(2,1)} %add_convert_fusion.5), channel_id=1, source_target_pairs={{0,1},{1,0},{2,3},{3,2},{4,5},{5,4},{6,7},{7,6},{8,9},{9,8},{10,11... | collective-permute-start | bytes 1671176 | tf_op jit(solution)/shard_map/ppermute | solution.py:439
  353.0 121.8 %all-to-all-start.3 = ((bf16[4,384,1024]{2,1,0:T(8,128)(2,1)}), bf16[4,384,1024]{2,1,0:T(8,128)(2,1)}, u32[]{:S(2)}, u32[]{:S(2)}) async-start(bf16[4,384,1024]{2,1,0:T(8,128)(2,1)} %add_convert_fusion), calls=%async_computation.3 | async-start | bytes 6291456 | tf_op jit(solution)/shard_map/all_to_all | solution.py:873
  364.6 23.4 %collective-permute-start.53 = (bf16[512,1152]{1,0:T(8,128)(2,1)}, bf16[512,1152]{1,0:T(8,128)(2,1)S(1)}, u32[]{:S(2)}, u32[]{:S(2)}) collective-permute-start(bf16[512,1152]{1,0:T(8,128)(2,1)} %get-tuple-element.268), channel_id=1, source_target_pairs={{0,4},{4,0},{8,12},{12,8},{16,20},{20,16},{24,28},{28,24},{1,5},{5... | collective-permute-start | bytes 3538952 | tf_op jit(solution)/shard_map/ppermute | solution.py:435
  364.7 21.7 %collective-permute-start.43 = (bf16[256,1024]{1,0:T(8,128)(2,1)S(1)}, bf16[256,1024]{1,0:T(8,128)(2,1)S(1)}, u32[]{:S(2)}, u32[]{:S(2)}) collective-permute-start(bf16[256,1024]{1,0:T(8,128)(2,1)S(1)} %copy-done.35), channel_id=1, source_target_pairs={{0,8},{4,12},{8,0},{12,4},{16,24},{20,28},{24,16},{28,20},{1,9},{5... | collective-permute-start | bytes 1572872 | tf_op jit(solution)/shard_map/ppermute | solution.py:435
  383.8 43.5 %collective-permute-start.46 = (bf16[512,2176]{1,0:T(8,128)(2,1)S(1)}, bf16[512,2176]{1,0:T(8,128)(2,1)S(1)}, u32[]{:S(2)}, u32[]{:S(2)}) collective-permute-start(bf16[512,2176]{1,0:T(8,128)(2,1)S(1)} %copy-done.19), channel_id=1, source_target_pairs={{0,4},{4,0},{8,12},{12,8},{16,20},{20,16},{24,28},{28,24},{1,5},{5... | collective-permute-start | bytes 6684680 | tf_op jit(solution)/shard_map/ppermute | solution.py:435
  384.0 14.8 %collective-permute-start.40 = (bf16[256,1024]{1,0:T(8,128)(2,1)S(1)}, bf16[256,1024]{1,0:T(8,128)(2,1)S(1)}, u32[]{:S(2)}, u32[]{:S(2)}) collective-permute-start(bf16[256,1024]{1,0:T(8,128)(2,1)S(1)} %copy-done.34), channel_id=1, source_target_pairs={{0,16},{4,20},{8,24},{12,28},{16,0},{20,4},{24,8},{28,12},{1,17},{... | collective-permute-start | bytes 1572872 | tf_op jit(solution)/shard_map/ppermute | solution.py:435
  384.8 14.8 %collective-permute-start.42 = (bf16[256,1024]{1,0:T(8,128)(2,1)S(1)}, bf16[256,1024]{1,0:T(8,128)(2,1)S(1)}, u32[]{:S(2)}, u32[]{:S(2)}) collective-permute-start(bf16[256,1024]{1,0:T(8,128)(2,1)S(1)} %copy-done.33), channel_id=1, source_target_pairs={{0,8},{4,12},{8,0},{12,4},{16,24},{20,28},{24,16},{28,20},{1,9},{5... | collective-permute-start | bytes 1572872 | tf_op jit(solution)/shard_map/ppermute | solution.py:435
  386.6 29.7 %collective-permute-start.44 = (bf16[256,1024]{1,0:T(8,128)(2,1)S(1)}, bf16[256,1024]{1,0:T(8,128)(2,1)S(1)}, u32[]{:S(2)}, u32[]{:S(2)}) collective-permute-start(bf16[256,1024]{1,0:T(8,128)(2,1)S(1)} %add_convert_fusion.11), channel_id=1, source_target_pairs={{0,16},{4,20},{8,24},{12,28},{16,0},{20,4},{24,8},{28,12},{1,17},{... | collective-permute-start | bytes 1572872 | tf_op jit(solution)/shard_map/ppermute | solution.py:435
  388.4 29.0 %collective-permute-start.54 = (bf16[128,1152]{1,0:T(8,128)(2,1)S(1)}, bf16[128,1152]{1,0:T(8,128)(2,1)S(1)}, u32[]{:S(2)}, u32[]{:S(2)}) collective-permute-start(bf16[128,1152]{1,0:T(8,128)(2,1)S(1)} %get-tuple-element.282), channel_id=1, source_target_pairs={{0,8},{4,12},{8,0},{12,4},{16,24},{20,28},{24,16},{28,20},{1,9},{5... | collective-permute-start | bytes 884744 | tf_op jit(solution)/shard_map/ppermute | solution.py:435
  398.8 23.9 %collective-permute-start.55 = (bf16[128,1152]{1,0:T(8,128)(2,1)S(1)}, bf16[128,1152]{1,0:T(8,128)(2,1)S(1)}, u32[]{:S(2)}, u32[]{:S(2)}) collective-permute-start(bf16[128,1152]{1,0:T(8,128)(2,1)S(1)} %get-tuple-element.284), channel_id=1, source_target_pairs={{0,16},{4,20},{8,24},{12,28},{16,0},{20,4},{24,8},{28,12},{1,17},{... | collective-permute-start | bytes 884744 | tf_op jit(solution)/shard_map/ppermute | solution.py:435
  399.6 23.1 %collective-permute-start.56 = (bf16[128,1152]{1,0:T(8,128)(2,1)S(1)}, bf16[128,1152]{1,0:T(8,128)(2,1)S(1)}, u32[]{:S(2)}, u32[]{:S(2)}) collective-permute-start(bf16[128,1152]{1,0:T(8,128)(2,1)S(1)} %get-tuple-element.283), channel_id=1, source_target_pairs={{0,24},{4,28},{8,16},{12,20},{16,8},{20,12},{24,0},{28,4},{1,25},{... | collective-permute-start | bytes 884744 | tf_op jit(solution)/shard_map/ppermute | solution.py:435
  416.3 45.6 %collective-permute-start.39 = (bf16[256,1024]{1,0:T(8,128)(2,1)S(1)}, bf16[256,1024]{1,0:T(8,128)(2,1)S(1)}, u32[]{:S(2)}, u32[]{:S(2)}) collective-permute-start(bf16[256,1024]{1,0:T(8,128)(2,1)S(1)} %copy-done.28), channel_id=1, source_target_pairs={{0,16},{4,20},{8,24},{12,28},{16,0},{20,4},{24,8},{28,12},{1,17},{... | collective-permute-start | bytes 1572872 | tf_op jit(solution)/shard_map/ppermute | solution.py:435
  417.4 44.6 %collective-permute-start.41 = (bf16[256,1024]{1,0:T(8,128)(2,1)S(1)}, bf16[256,1024]{1,0:T(8,128)(2,1)S(1)}, u32[]{:S(2)}, u32[]{:S(2)}) collective-permute-start(bf16[256,1024]{1,0:T(8,128)(2,1)S(1)} %add_convert_fusion.12), channel_id=1, source_target_pairs={{0,8},{4,12},{8,0},{12,4},{16,24},{20,28},{24,16},{28,20},{1,9},{5... | collective-permute-start | bytes 1572872 | tf_op jit(solution)/shard_map/ppermute | solution.py:435
  422.9 7.0 %collective-permute-start.57 = (bf16[32,1152]{1,0:T(8,128)(2,1)S(1)}, bf16[32,1152]{1,0:T(8,128)(2,1)S(1)}, u32[]{:S(2)}, u32[]{:S(2)}) collective-permute-start(bf16[32,1152]{1,0:T(8,128)(2,1)S(1)} %get-tuple-element.296), channel_id=1, source_target_pairs={{0,1},{1,0},{2,3},{3,2},{4,5},{5,4},{6,7},{7,6},{8,9},{9,8},{10,11... | collective-permute-start | bytes 221192 | tf_op jit(solution)/shard_map/ppermute | solution.py:439
  425.0 7.2 %collective-permute-start.58 = (bf16[32,1152]{1,0:T(8,128)(2,1)S(1)}, bf16[32,1152]{1,0:T(8,128)(2,1)S(1)}, u32[]{:S(2)}, u32[]{:S(2)}) collective-permute-start(bf16[32,1152]{1,0:T(8,128)(2,1)S(1)} %get-tuple-element.298), channel_id=1, source_target_pairs={{0,2},{1,3},{2,0},{3,1},{4,6},{5,7},{6,4},{7,5},{8,10},{9,11},{10,... | collective-permute-start | bytes 221192 | tf_op jit(solution)/shard_map/ppermute | solution.py:439
  427.3 6.3 %collective-permute-start.59 = (bf16[32,1152]{1,0:T(8,128)(2,1)S(1)}, bf16[32,1152]{1,0:T(8,128)(2,1)S(1)}, u32[]{:S(2)}, u32[]{:S(2)}) collective-permute-start(bf16[32,1152]{1,0:T(8,128)(2,1)S(1)} %get-tuple-element.297), channel_id=1, source_target_pairs={{0,3},{1,2},{2,1},{3,0},{4,7},{5,6},{6,5},{7,4},{8,11},{9,10},{10,... | collective-permute-start | bytes 221192 | tf_op jit(solution)/shard_map/ppermute | solution.py:439
  429.9 15.5 %collective-permute-start.47 = (bf16[128,2176]{1,0:T(8,128)(2,1)S(1)}, bf16[128,2176]{1,0:T(8,128)(2,1)S(1)}, u32[]{:S(2)}, u32[]{:S(2)}) collective-permute-start(bf16[128,2176]{1,0:T(8,128)(2,1)S(1)} %get-tuple-element.275), channel_id=1, source_target_pairs={{0,8},{4,12},{8,0},{12,4},{16,24},{20,28},{24,16},{28,20},{1,9},{5... | collective-permute-start | bytes 1671176 | tf_op jit(solution)/shard_map/ppermute | solution.py:435
  432.1 25.1 %collective-permute-start.48 = (bf16[128,2176]{1,0:T(8,128)(2,1)S(1)}, bf16[128,2176]{1,0:T(8,128)(2,1)S(1)}, u32[]{:S(2)}, u32[]{:S(2)}) collective-permute-start(bf16[128,2176]{1,0:T(8,128)(2,1)S(1)} %get-tuple-element.277), channel_id=1, source_target_pairs={{0,16},{4,20},{8,24},{12,28},{16,0},{20,4},{24,8},{28,12},{1,17},{... | collective-permute-start | bytes 1671176 | tf_op jit(solution)/shard_map/ppermute | solution.py:435
  433.6 23.6 %collective-permute-start.49 = (bf16[128,2176]{1,0:T(8,128)(2,1)S(1)}, bf16[128,2176]{1,0:T(8,128)(2,1)S(1)}, u32[]{:S(2)}, u32[]{:S(2)}) collective-permute-start(bf16[128,2176]{1,0:T(8,128)(2,1)S(1)} %get-tuple-element.276), channel_id=1, source_target_pairs={{0,24},{4,28},{8,16},{12,20},{16,8},{20,12},{24,0},{28,4},{1,25},{... | collective-permute-start | bytes 1671176 | tf_op jit(solution)/shard_map/ppermute | solution.py:435
  445.4 16.7 %collective-permute-start.45 = (bf16[256,1024]{1,0:T(8,128)(2,1)S(1)}, bf16[256,1024]{1,0:T(8,128)(2,1)S(1)}, u32[]{:S(2)}, u32[]{:S(2)}) collective-permute-start(bf16[256,1024]{1,0:T(8,128)(2,1)S(1)} %add_convert_fusion.10), channel_id=1, source_target_pairs={{0,1},{1,0},{2,3},{3,2},{4,5},{5,4},{6,7},{7,6},{8,9},{9,8},{10,11... | collective-permute-start | bytes 1572872 | tf_op jit(solution)/shard_map/ppermute | solution.py:439
  457.5 7.0 %collective-permute-start.50 = (bf16[32,2176]{1,0:T(8,128)(2,1)S(1)}, bf16[32,2176]{1,0:T(8,128)(2,1)S(1)}, u32[]{:S(2)}, u32[]{:S(2)}) collective-permute-start(bf16[32,2176]{1,0:T(8,128)(2,1)S(1)} %get-tuple-element.293), channel_id=1, source_target_pairs={{0,1},{1,0},{2,3},{3,2},{4,5},{5,4},{6,7},{7,6},{8,9},{9,8},{10,11... | collective-permute-start | bytes 417800 | tf_op jit(solution)/shard_map/ppermute | solution.py:439
  459.6 13.2 %collective-permute-start.51 = (bf16[32,2176]{1,0:T(8,128)(2,1)S(1)}, bf16[32,2176]{1,0:T(8,128)(2,1)S(1)}, u32[]{:S(2)}, u32[]{:S(2)}) collective-permute-start(bf16[32,2176]{1,0:T(8,128)(2,1)S(1)} %get-tuple-element.295), channel_id=1, source_target_pairs={{0,2},{1,3},{2,0},{3,1},{4,6},{5,7},{6,4},{7,5},{8,10},{9,11},{10,... | collective-permute-start | bytes 417800 | tf_op jit(solution)/shard_map/ppermute | solution.py:439
  462.0 10.8 %collective-permute-start.52 = (bf16[32,2176]{1,0:T(8,128)(2,1)S(1)}, bf16[32,2176]{1,0:T(8,128)(2,1)S(1)}, u32[]{:S(2)}, u32[]{:S(2)}) collective-permute-start(bf16[32,2176]{1,0:T(8,128)(2,1)S(1)} %get-tuple-element.294), channel_id=1, source_target_pairs={{0,3},{1,2},{2,1},{3,0},{4,7},{5,6},{6,5},{7,4},{8,11},{9,10},{10,... | collective-permute-start | bytes 417800 | tf_op jit(solution)/shard_map/ppermute | solution.py:439
  (36 other events, 539.7 us)

commit v4 on v3

--- a/solution.py
+++ b/solution.py
@@ -453,15 +453,19 @@
 SUM_ROWS = 272
 
 
-def expert_body(first_part, number_ref, *refs):
+def expert_body(first_part, packed, number_ref, *refs):
     refs = list(refs)
     take = lambda count: [refs.pop(0) for _ in range(count)]
     tok_refs, out_refs = take(BLOCKS), take(BLOCKS)
-    (w_ref,) = take(1)
+    if packed:
+        (w_ref,) = take(1)
+        w_in_ref, w_out_ref = w_ref.at[:, 0:256, :], w_ref.at[:, 256:384, :]
+    else:
+        w_in_ref, w_out_ref = take(2)
     row_before, moe_before = ([], []) if first_part else (take(BLOCKS), take(BLOCKS))
     row_outs, moe_outs = take(BLOCKS), take(BLOCKS)
     (grad_ref,) = take(1)
-    (tok_s, out_s, w_s, row_s, moe_s, grad_s, x_s, g_s, gate_s, table_s, back_s, mix_s, dot_s,
+    (tok_s, out_s, w_in_s, w_out_s, row_s, moe_s, grad_s, x_s, g_s, gate_s, table_s, back_s, mix_s, dot_s,
      in_acc, out_acc, tok_sem, out_sem, w_sem, row_sem, moe_sem, row_out_sem, moe_out_sem, grad_sem) = refs
     number = number_ref[0]
     copy = pltpu.make_async_copy
@@ -469,7 +473,8 @@
         copy(tok_refs[j], tok_s.at[j], tok_sem.at[j]).start()
         copy(out_refs[j], out_s.at[j], out_sem.at[j]).start()
         if j == HALF - 1:
-            copy(w_ref, w_s, w_sem.at[0]).start()
+            copy(w_in_ref, w_in_s, w_sem.at[0]).start()
+            copy(w_out_ref, w_out_s, w_sem.at[1]).start()
     if not first_part:
         for j in range(BLOCKS):
             copy(row_before[j], row_s.at[j], row_sem.at[j]).start()
@@ -498,10 +503,11 @@
 
         @pl.when(half == 0)
         def _():
-            copy(w_ref, w_s, w_sem.at[0]).wait()
-
-        w_in = w_s[:, 0:256, :].reshape(1024, 1024)
-        w_out = w_s[:, 256:384, :].reshape(512, 1024)
+            copy(w_in_ref, w_in_s, w_sem.at[0]).wait()
+            copy(w_out_ref, w_out_s, w_sem.at[1]).wait()
+
+        w_in = w_in_s[...].reshape(1024, 1024)
+        w_out = w_out_s[...].reshape(512, 1024)
         x = x_s[...]
         gate_up = dot_f32(x, w_in, CONTRACT_PLAIN)
         gate_part, up_part = gate_up[:, :FF], gate_up[:, FF:]
@@ -576,27 +582,28 @@
 
 
 def expert_call(number, tokens, grads, weights, before=None):
-    operands = list(tokens) + list(grads) + [weights] + ([] if before is None else list(before))
+    operands = list(tokens) + list(grads) + list(weights) + ([] if before is None else list(before))
     block = lambda rows: jax.ShapeDtypeStruct((rows, 1024), BF16)
     outs = [block(SUM_ROWS)] * BLOCKS + [block(256)] * BLOCKS + [jax.ShapeDtypeStruct((4, 384, 1024), BF16)]
     anywhere = pl.BlockSpec(memory_space=pl.ANY)
     blocks = lambda rows: pltpu.VMEM((BLOCKS, rows, 1024), BF16)
     column, wide = pltpu.VMEM((ROWS, 1), F32), pltpu.VMEM((ROWS, 1024), BF16)
-    sems = [pltpu.SemaphoreType.DMA((count,)) for count in (8, 8, 1, 8, 8, 8, 8, 1)]
+    sems = [pltpu.SemaphoreType.DMA((count,)) for count in (8, 8, 2, 8, 8, 8, 8, 1)]
     results = pl.pallas_call(
-        functools.partial(expert_body, before is None),
+        functools.partial(expert_body, before is None, len(weights) == 1),
         out_shape=outs,
         in_specs=[pl.BlockSpec(memory_space=pltpu.SMEM)] + [anywhere] * len(operands),
         out_specs=[anywhere] * len(outs),
         scratch_shapes=[
-            blocks(PAY_ROWS), blocks(256), pltpu.VMEM((4, 384, 1024), BF16), blocks(SUM_ROWS), blocks(256),
+            blocks(PAY_ROWS), blocks(256), pltpu.VMEM((4, 256, 1024), BF16), pltpu.VMEM((4, 128, 1024), BF16),
+            blocks(SUM_ROWS), blocks(256),
             pltpu.VMEM((4, 384, 1024), BF16), wide, pltpu.VMEM((ROWS, 1024), F32), column,
             pltpu.VMEM((HALF, 8, 256), F32), wide, wide, column,
             pltpu.VMEM((1024, 1024), F32), pltpu.VMEM((512, 1024), F32),
         ] + sems,
         compiler_params=pltpu.CompilerParams(vmem_limit_bytes=60 * 1024 * 1024),
         cost_estimate=pl.CostEstimate(
-            flops=12_000_000_000, bytes_accessed=30_000_000, transcendentals=1_000_000
+            flops=1000, bytes_accessed=1000, transcendentals=0
         ),
         name="expert",
     )(number, *operands)
@@ -652,29 +659,40 @@
     )
 
 
-def attend_body(e_ref, x_ref, column_ref, row_ref, cos_ref, sin_ref, own_ref, far_ref,
-                normed_ref, q_ref, k_ref, v_ref, mixed_ref):
+def stacked(refs, a, b):
+    return jnp.concatenate([ref[:, a:b] for ref in refs], axis=0)
+
+
+def gain_row(refs, index):
+    return stacked(refs, 1024, 1152).astype(F32).T[index : index + 1, :]
+
+
+def attend_body(e_ref, x_ref, column_ref, row_ref, cos_ref, sin_ref, *refs):
+    lefts, rights = (refs[0:4], refs[4:8]), (refs[8:12], refs[12:16])
+    normed_ref, q_ref, k_ref, v_ref, mixed_ref, small_ref = refs[16:]
     e = e_ref[0]
     resid = embed_scale * x_ref[...].astype(F32)
     inverse = inverse_rms(resid)
-    for part, w_ref in ((0, own_ref), (1, far_ref)):
-        gain = w_ref[:, 2048:].astype(F32).T[GAIN_ATTN : GAIN_ATTN + 1, :]
+    for part in range(2):
+        gain = gain_row(lefts[part], GAIN_ATTN)
         for q in range(4):
-            block = embed_scale * x_ref[:, group_of(e, 2 * q + part)].astype(F32)
+            group = group_of(e, 2 * q + part)
+            block = embed_scale * x_ref[:, group].astype(F32)
             scaled = block * inverse * gain[:, LANES * q : LANES * (q + 1)]
             at = 512 * part + LANES * q
             normed_ref[:, at : at + LANES] = scaled.astype(BF16)
+            small_ref[group, :] = lefts[part][q][:, 1024:1152]
     own = normed_ref[:, :512]
     far = normed_ref[:, 512:]
-    project = lambda a, b: dot_f32(own, own_ref[:, a:b], CONTRACT_PLAIN) + dot_f32(
-        far, far_ref[:, a:b], CONTRACT_PLAIN
+    project = lambda sides, a, b: dot_f32(own, stacked(sides[0], a, b), CONTRACT_PLAIN) + dot_f32(
+        far, stacked(sides[1], a, b), CONTRACT_PLAIN
     )
     rotate = lambda u: u * wide_table(cos_ref[...], u.shape[1]) + turn_halves(u) * wide_table(
         sin_ref[...], u.shape[1]
     )
-    q_ref[...] = rotate(project(0, 1024)).astype(BF16)
-    k_ref[...] = rotate(project(1024, 1536)).astype(BF16)
-    v_ref[...] = project(1536, 2048).astype(BF16)
+    q_ref[...] = rotate(project(lefts, 0, 1024)).astype(BF16)
+    k_ref[...] = rotate(project(rights, 0, 512)).astype(BF16)
+    v_ref[...] = project(rights, 512, 1024).astype(BF16)
     allowed = allowed_of(column_ref, row_ref)
 
     def pair(step, _):
@@ -692,15 +710,13 @@
     lax.fori_loop(0, 4, pair, 0)
 
 
-def route_body(e_ref, x_ref, mixed_ref, w_own_ref, w_far_ref, small_own_ref, small_far_ref, code_ref,
-               pay_ref, gates_ref, middle_ref, small_ref):
+def route_body(e_ref, x_ref, mixed_ref, small_ref, code_ref, *refs):
+    w_refs, (pay_ref, gates_ref, middle_ref) = (refs[0:4], refs[4:8]), refs[8:]
     e = e_ref[0]
     total = jnp.zeros((SEQUENCE, 1024), F32)
-    for part, w_ref, s_ref in ((0, w_own_ref, small_own_ref), (1, w_far_ref, small_far_ref)):
+    for part in range(2):
         features = jnp.concatenate([mixed_ref[:, group_of(e, 2 * q + part)] for q in range(4)], axis=1)
-        total = total + dot_f32(features, w_ref[...], CONTRACT_PLAIN)
-        for q in range(4):
-            small_ref[group_of(e, 2 * q + part), :] = s_ref[LANES * q : LANES * (q + 1), :]
+        total = total + dot_f32(features, stacked(w_refs[part], 0, 1024), CONTRACT_PLAIN)
     middle = embed_scale * x_ref[...].astype(F32) + resid_scale * total
     middle_ref[...] = middle
     gain = small_ref[...].astype(F32).T[GAIN_FFN : GAIN_FFN + 1, :]
@@ -722,7 +738,8 @@
 
 
 def turn_body(e_ref, sum_ref, add_ref, grad_ref, middle_ref, gates_ref, small_ref, normed2_ref, mixed_ref,
-              w_own_ref, w_far_ref, own_ref, far_ref, mixed_grad_ref, middle_grad_ref, side_ref):
+              *refs):
+    w_refs, (own_ref, far_ref, mixed_grad_ref, middle_grad_ref, side_ref) = (refs[0:4], refs[4:8]), refs[8:]
     e = e_ref[0]
     upstream = sum_ref[0:256, :].astype(F32) + add_ref[0:256, :].astype(F32)
     table = sum_ref[256:272, :].astype(F32) + add_ref[256:272, :].astype(F32)
@@ -749,10 +766,10 @@
     side_ref[...] = dot_f32(normed2_ref[0:256, :], logit_grads, CONTRACT_FIRST) + jnp.where(
         line == GAIN_FFN, gain_grad, 0.0
     ).T
-    for part, w_ref, out_ref in ((0, w_own_ref, own_ref), (1, w_far_ref, far_ref)):
+    for part, out_ref in ((0, own_ref), (1, far_ref)):
         features = jnp.concatenate([mixed_ref[:, group_of(e, 2 * q + part)] for q in range(4)], axis=1)
         out_ref[:, :1024] = dot_f32(features, attn_grad, CONTRACT_FIRST).astype(BF16)
-        back = dot_f32(attn_grad, w_ref[...], CONTRACT_LAST).astype(BF16)
+        back = dot_f32(attn_grad, stacked(w_refs[part], 0, 1024), CONTRACT_LAST).astype(BF16)
         for q in range(4):
             mixed_grad_ref[:, group_of(e, 2 * q + part)] = back[:, LANES * q : LANES * (q + 1)]
             at = slice(LANES * q, LANES * (q + 1))
@@ -760,8 +777,10 @@
 
 
 def attend_back_body(e_ref, x_ref, column_ref, row_ref, cos_ref, sin_ref, q_ref, k_ref, v_ref, grad_ref,
-                     normed_ref, w_own_ref, w_far_ref, middle_grad_ref,
-                     own_ref, far_ref, embed_ref, raw_ref, scaled_ref):
+                     normed_ref, middle_grad_ref, *refs):
+    lefts, rights = (refs[0:4], refs[4:8]), (refs[8:12], refs[12:16])
+    left_refs, right_refs = refs[16:18], refs[18:20]
+    embed_ref, raw_ref, scaled_ref = refs[20:]
     e = e_ref[0]
     allowed = allowed_of(column_ref, row_ref)
     unrotate = lambda u: (
@@ -793,14 +812,18 @@
     lax.fori_loop(0, 4, pair, 0)
     resid = embed_scale * x_ref[...].astype(F32)
     inverse = inverse_rms(resid)
-    for part, w_ref, out_ref in ((0, w_own_ref, own_ref), (1, w_far_ref, far_ref)):
-        for c in range(4):
+    for part in range(2):
+        half = normed_ref[:, 512 * part : 512 * part + 512]
+        for c in range(2):
             at = slice(512 * c, 512 * c + 512)
-            out_ref[:, at] = dot_f32(
-                normed_ref[:, 512 * part : 512 * part + 512], raw_ref[:, at], CONTRACT_FIRST
+            left_refs[part][:, at] = dot_f32(half, raw_ref[:, at], CONTRACT_FIRST).astype(BF16)
+            right_refs[part][:, at] = dot_f32(
+                half, raw_ref[:, 1024 + 512 * c : 1536 + 512 * c], CONTRACT_FIRST
             ).astype(BF16)
-        back = dot_f32(raw_ref[...], w_ref[:, :2048], CONTRACT_LAST)
-        gain = w_ref[:, 2048:].astype(F32).T[GAIN_ATTN : GAIN_ATTN + 1, :]
+        back = dot_f32(raw_ref[:, :1024], stacked(lefts[part], 0, 1024), CONTRACT_LAST) + dot_f32(
+            raw_ref[:, 1024:], stacked(rights[part], 0, 1024), CONTRACT_LAST
+        )
+        gain = gain_row(lefts[part], GAIN_ATTN)
         gain_grads = []
         for q in range(4):
             at = slice(LANES * q, LANES * (q + 1))
@@ -810,7 +833,7 @@
             scaled_ref[:, group] = back[:, at] * gain[:, at]
         line = lax.broadcasted_iota(jnp.int32, (LANES, 512), 0)
         side = jnp.where(line == GAIN_ATTN, jnp.concatenate(gain_grads, axis=1), 0.0).T
-        out_ref[:, 2048:] = side.astype(BF16)
+        left_refs[part][:, 1024:] = side.astype(BF16)
     unit = resid * inverse
     scaled = scaled_ref[...]
     resid_grad = middle_grad_ref[...] + inverse * (
@@ -819,8 +842,7 @@
     embed_ref[...] = (embed_scale * resid_grad).astype(BF16)
 
 
-def local_kernel(body, name, outs, scratch, flops, number, *operands):
-    bytes_moved = sum(a.size * a.dtype.itemsize for a in operands)
+def local_kernel(body, name, outs, scratch, number, *operands):
     vmem = pl.BlockSpec(memory_space=pltpu.VMEM)
     return pl.pallas_call(
         body,
@@ -829,25 +851,13 @@
         out_specs=[vmem] * len(outs),
         scratch_shapes=[pltpu.VMEM(shape, dtype) for shape, dtype in scratch],
         compiler_params=pltpu.CompilerParams(vmem_limit_bytes=56 * 1024 * 1024),
-        cost_estimate=pl.CostEstimate(flops=flops, bytes_accessed=bytes_moved, transcendentals=0),
+        cost_estimate=pl.CostEstimate(flops=1000, bytes_accessed=1000, transcendentals=0),
         name=name,
     )(number, *operands)
 
 
 def together(*values):
     return lax.optimization_barrier(values)
-
-
-def plane_gather(value):
-    return jnp.concatenate([value] + [over_expert(value, bits) for bits in (2, 4, 6)])
-
-
-def plane_sum(total):
-    rows = total.shape[0] // 4
-    part = total[:rows].astype(F32)
-    for q in (1, 2, 3):
-        part = part + over_expert(total[rows * q : rows * q + rows], 2 * q).astype(F32)
-    return part.astype(BF16)
 
 
 def core_sum(own, far):
@@ -861,21 +871,12 @@
     )
 
 
-def shard_sum(plane, z):
-    rows = lambda k: lax.dynamic_slice_in_dim(plane, (z ^ k) * 32, 32, 0)
-    result = rows(0).astype(F32)
-    for k in (1, 2, 3):
-        result = result + over_shard(rows(k), k).astype(F32)
-    return result
-
-
 def exchange(slices):
     return lax.all_to_all(slices, "shard", split_axis=0, concat_axis=0, tiled=True)
 
 
-def expert_slices(expert_in, expert_out, part):
-    chosen = [OWN * (d % PAIR) + part for d in range(4)]
-    return jnp.stack([jnp.concatenate([expert_in[c], expert_out[c]]) for c in chosen])
+def expert_slices(weights, part):
+    return jnp.stack([weights[OWN * (d % PAIR) + part] for d in range(4)])
 
 
 def over_x(value):
@@ -891,37 +892,75 @@
     return [value, near[over_x], near[over_y], second(near[first])]
 
 
-def fold(parts, first, second):
-    one, two = (1, 2) if first is over_x else (2, 1)
-    passing, mine = first(parts[3]), first(parts[one])
-    other = (parts[two].astype(F32) + passing.astype(F32)).astype(BF16)
-    return parts[0].astype(F32) + mine.astype(F32) + second(other).astype(F32)
-
-
-def fold_both(parts):
-    own, pair = parts[:4], parts[4:]
-    pair_pass, own_pass = over_x(pair[3]), over_y(own[3])
-    pair_mine = over_x(pair[1])
-    pair_other = over_y(bf_sum(pair[2], pair_pass))
-    mine, pair_pass = together(own[2], pair_pass)
-    own_mine = over_y(mine)
-    own_other = over_x(bf_sum(own[1], own_pass))
-    pair_sum = bf_sum(pair[0], pair_mine, pair_other)
-    return bf_sum(own[0], own_mine, own_other), pair_sum
-
-
 def bf_sum(*values):
     return sum(value.astype(F32) for value in values).astype(BF16)
 
 
 def pack_body(query_ref, key_ref, value_ref, router_ref, attn_ref, ffn_ref, out_ref, pack_ref):
     pack_ref[:, 0:1024] = query_ref[...].astype(BF16)
-    pack_ref[:, 1024:1536] = key_ref[...].astype(BF16)
-    pack_ref[:, 1536:2048] = value_ref[...].astype(BF16)
+    row = lax.broadcasted_iota(jnp.int32, (32, 32), 0)
+    diagonal = row == lax.broadcasted_iota(jnp.int32, (32, 32), 1)
+    upright = lambda ref: jnp.sum(jnp.where(diagonal, ref[...], 0.0), axis=1, keepdims=True)
     zeros = jnp.zeros((32, LANES - EXPERTS - 2), F32)
-    small = jnp.concatenate([router_ref[...], attn_ref[...], ffn_ref[...], zeros], axis=1)
-    pack_ref[:, 2048:2176] = small.astype(BF16)
+    small = jnp.concatenate([router_ref[...], upright(attn_ref), upright(ffn_ref), zeros], axis=1)
+    pack_ref[:, 1024:1152] = small.astype(BF16)
+    pack_ref[:, 1152:1664] = key_ref[...].astype(BF16)
+    pack_ref[:, 1664:2176] = value_ref[...].astype(BF16)
     pack_ref[:, 2176:] = out_ref[...].astype(BF16)
+
+
+def plane_body(z_ref, *refs):
+    z = z_ref[0]
+    for group, (a, b) in enumerate(((0, 1152), (1152, 2176), (2176, 3328))):
+        mine, one, other = refs[3 * group : 3 * group + 3]
+        for k in range(4):
+            rows = pl.ds(pl.multiple_of((z ^ k) * 32, 32), 32)
+            total = mine[rows, :].astype(F32) + one[rows, :].astype(F32) + other[rows, :].astype(F32)
+            refs[9 + k][:, a:b] = total.astype(BF16)
+
+
+def settle_body(z_ref, *refs):
+    sources, outs = refs[:4], refs[4:]
+    total = lambda a, b: sum(ref[:, a:b].astype(F32) for ref in sources)
+    bounds = ((0, 1024), (1152, 1664), (1664, 2176), (2176, 3200))
+    for out_ref, (a, b) in zip(outs, bounds):
+        out_ref[...] = total(a, b)
+    row = lax.broadcasted_iota(jnp.int32, (32, 32), 0)
+    diagonal = row == lax.broadcasted_iota(jnp.int32, (32, 32), 1)
+    flat = lambda column: jnp.sum(jnp.where(diagonal, column, 0.0), axis=0, keepdims=True)
+    late, early = total(1024, 1152), total(3200, 3328)
+    outs[4][...] = early[:, :EXPERTS]
+    outs[5][...] = flat(late[:, GAIN_ATTN : GAIN_ATTN + 1])
+    outs[6][...] = flat(early[:, GAIN_FFN : GAIN_FFN + 1])
+
+
+def owner_body(first_part, one_ref, two_ref, *refs):
+    in_ref, out_ref = refs if first_part else refs[2:]
+    total = one_ref[...].astype(F32) + two_ref[...].astype(F32)
+    in_ref[...] = total[:, :256]
+    out_ref[...] = total[:, 256:]
+
+
+def owner_sum(part, slices, before=()):
+    block = lambda rows, at: pl.BlockSpec((1, rows, 1024), lambda d: (at(d), 0, 0))
+    place = lambda d: 2 * d + part
+    return pl.pallas_call(
+        functools.partial(owner_body, not before),
+        out_shape=[jax.ShapeDtypeStruct((4, rows, 1024), F32) for rows in (256, 128)],
+        grid=(2,),
+        in_specs=[block(384, lambda d: d), block(384, lambda d: d + 2)]
+        + [pl.BlockSpec(memory_space=pl.ANY)] * len(before),
+        out_specs=[block(256, place), block(128, place)],
+        input_output_aliases={2: 0, 3: 1} if before else {},
+        name="owner_sum",
+    )(slices, slices, *before)
+
+
+def plane_fold(total, first, second):
+    part = lambda q: total[128 * q : 128 * (q + 1)]
+    one, two = (1, 2) if first is over_x else (2, 1)
+    passing, mine = first(part(3)), first(part(one))
+    return [part(0), mine, second(bf_sum(part(two), passing))]
 
 
 def pack_call(*operands):
@@ -953,21 +992,24 @@
     z = lax.axis_index("shard")
     place = e.reshape(1)
     pack = pack_call(
-        w_query, key_projection, value_projection, w_router, attn_gain[:, None], ffn_gain[:, None], w_out
+        w_query, key_projection, value_projection, w_router, attn_gain[None, :], ffn_gain[None, :], w_out
     )
     pack, grad_early = together(pack, cotangent)
     plane = xor_order([pack] + [over_shard(pack, k) for k in (1, 2, 3)], z)
     out_pair = over_shard(grad_early, 1)
     out_x, out_y = over_x(grad_early), over_y(grad_early)
-    slices = [expert_slices(expert_in, expert_out, part) for part in range(OWN)]
-    plane, out_x, out_y, out_pair, slices[0] = together(plane, out_x, out_y, out_pair, slices[0])
-    weights0 = exchange(slices[0])
+    slices = [expert_slices(w, 0) for w in (expert_in, expert_out)]
+    second = jnp.concatenate([expert_slices(w, 1) for w in (expert_in, expert_out)], axis=1)
+    plane, out_x, out_y, slices[0] = together(plane, out_x, out_y, slices[0])
     left = spread(plane[:, :1152], over_x, over_y)
     right = spread(plane[:, 1152:2176], over_y, over_x)
-    in_own = jnp.concatenate([jnp.concatenate(left), jnp.concatenate(right)], axis=1)
-    in_own, plane, out_x, out_pair = together(in_own, plane, out_x, out_pair)
-    in_far = over_expert(in_own, 1)
-    out_w_own = plane_gather(plane[:, 2176:])
+    slices[0], out_pair, left[1], right[2] = together(slices[0], out_pair, left[1], right[2])
+    in0 = exchange(slices[0])
+    swap = lambda values: [over_expert(value, 1) for value in values]
+    left_far, right_far = swap(left), swap(right)
+    left[3], right[3], plane, out_pair, out_x = together(left[3], right[3], plane, out_pair, out_x)
+    out_w = [plane[:, 2176:]] + [over_expert(plane[:, 2176:], bits) for bits in (2, 4, 6)]
+    out_blocks = [cotangent, out_x, out_y, over_y(out_x), out_pair, over_x(out_pair), over_y(out_pair)]
 
     segments = document_numbers[0]
     column, row = segments[:, None], segments[None, :]
@@ -980,78 +1022,101 @@
     code = jnp.where(member, rank, -1.0)
 
     wide, half = (SEQUENCE, 1024), (SEQUENCE, 512)
-    normed, queries, keys, values, mixed = local_kernel(
-        attend_body, "attend", [(wide, BF16), (wide, BF16), (half, BF16), (half, BF16), (wide, BF16)], [],
-        4_000_000_000, place, embedded, column, row, cosine, sine, in_own, in_far,
-    )
-    out_w_own, out_pair, out_x, mixed = together(out_w_own, out_pair, out_x, mixed)
-    out_w_far = over_expert(out_w_own, 1)
-    out_blocks = [cotangent, out_x, out_y, over_y(out_x)] + spread(out_pair, over_y, over_x)
-    payload, gates, middle, small_all = local_kernel(
-        route_body, "route",
-        [((288, 1024), BF16), ((SEQUENCE, LANES), F32), (wide, F32), ((1024, LANES), BF16)], [],
-        2_000_000_000, place, embedded, mixed, out_w_own, out_w_far, in_own[:, 2048:], in_far[:, 2048:], code,
+    weights = left + left_far + right + right_far
+    normed, queries, keys, values, mixed, small_all = local_kernel(
+        attend_body, "attend",
+        [(wide, BF16), (wide, BF16), (half, BF16), (half, BF16), (wide, BF16), ((1024, LANES), BF16)], [],
+        place, embedded, column, row, cosine, sine, *weights,
+    )
+    *out_w, mixed = together(*out_w, mixed)
+    out_w = out_w + swap(out_w)
+    payload, gates, middle = local_kernel(
+        route_body, "route", [((288, 1024), BF16), ((SEQUENCE, LANES), F32), (wide, F32)], [],
+        place, embedded, mixed, small_all, code, *out_w,
     )
     pay_pair = over_shard(payload, 1)
     pay_x, pay_y = over_x(payload), over_y(payload)
     pay_x, pay_y, pay_pair, *out_blocks = together(pay_x, pay_y, pay_pair, *out_blocks)
+    slices[1], in0, pay_pair = together(slices[1], in0, pay_pair)
+    out0 = exchange(slices[1])
+    out_blocks.append(over_x(out_blocks[6]))
+    tok_own = [payload, pay_x, pay_y, over_y(pay_x)]
     tok_pair = [pay_pair, over_x(pay_pair), over_y(pay_pair)]
-    tok_own = [payload, pay_x, pay_y, over_y(pay_x)]
-    *tok_pair, weights0, slices[1] = together(*tok_pair, weights0, slices[1])
+    *tok_pair, out_blocks[7], out0, second = together(*tok_pair, out_blocks[7], out0, second)
     tok_pair.append(over_x(tok_pair[2]))
-    weights1 = exchange(slices[1])
-    weights0_far = over_expert(weights0, 1)
+    weights0 = [in0, out0]
+    weights1 = [exchange(second)]
+    weights0_far = swap(weights0)
     tokens = tok_own + tok_pair
     first = (e * 4 + z % PAIR * OWN).reshape(1)
     first_far = ((e ^ 1) * 4 + z % PAIR * OWN).reshape(1)
-    sums, grad_a = expert_call(first, tokens, out_blocks, weights0)
-    sums, grad_b = expert_call(first_far, tokens, out_blocks, weights0_far, sums)
+    sums, grad_b = expert_call(first_far, tokens, out_blocks, weights0_far)
+    sums, grad_a = expert_call(first, tokens, out_blocks, weights0, sums)
     expert_grad0 = core_sum(grad_a, grad_b)
-    expert_grad0, weights1 = together(expert_grad0, weights1)
+    expert_grad0, *weights1 = together(expert_grad0, *weights1)
     slices0 = exchange(expert_grad0)
-    weights1_far = over_expert(weights1, 1)
+    weights1_far = swap(weights1)
+    sums, grad_d = expert_call(first_far + 1, tokens, out_blocks, weights1_far, sums)
     sums, grad_c = expert_call(first + 1, tokens, out_blocks, weights1, sums)
-    sums, grad_d = expert_call(first_far + 1, tokens, out_blocks, weights1_far, sums)
     rows, moes = sums[:BLOCKS], sums[BLOCKS:]
-    row_own, row_pair = fold_both(rows)
+    expert_grad1 = core_sum(grad_c, grad_d)
+    own, pair = rows[:4], rows[4:]
+    pair_pass, own_pass = over_x(pair[3]), over_y(own[3])
+    pair_mine = over_x(pair[1])
+    pair_pass, expert_grad1, slices0 = together(pair_pass, expert_grad1, slices0)
+    pair_other = over_y(bf_sum(pair[2], pair_pass))
+    mine, pair_pass = together(own[2], pair_pass)
+    own_mine = over_y(mine)
+    own_other = over_x(bf_sum(own[1], own_pass))
+    row_pair = bf_sum(pair[0], pair_mine, pair_other)
     returned = over_shard(row_pair, 1)
-    expert_grad1 = core_sum(grad_c, grad_d)
-    row_own, returned, expert_grad1, slices0, *moes = together(row_own, returned, expert_grad1, slices0, *moes)
+    row_pair, *moes = together(row_pair, *moes)
+    moe_pass, moe_own_pass = over_x(moes[7]), over_y(moes[3])
+    moe_mine, moe_own_mine = over_x(moes[5]), over_y(moes[2])
+    owned = owner_sum(0, slices0)
+    own_other, *owned = together(own_other, *owned)
+    row_own = bf_sum(own[0], own_mine, own_other)
+    returned, expert_grad1, slices0 = together(returned, expert_grad1, slices0)
     slices1 = exchange(expert_grad1)
-    moe_pair = fold(moes[4:], over_x, over_y).astype(BF16)
-    moe_own = fold(moes[:4], over_y, over_x)
-    moe_other = over_shard(moe_pair, 1)
     early_own, early_far, mixed_grad, middle_grad = local_kernel(
         turn_body, "turn", [((512, 1152), BF16), ((512, 1152), BF16), (wide, BF16), (wide, F32)],
-        [((1024, LANES), F32)], 4_000_000_000, place, row_own, returned, cotangent, middle, gates,
-        small_all, payload, mixed, out_w_own, out_w_far,
-    )
-    late_own, late_far, grad_embedded = local_kernel(
-        attend_back_body, "attend_back", [((512, 2176), BF16), ((512, 2176), BF16), (wide, BF16)],
-        [((SEQUENCE, 2048), BF16), (wide, F32)], 8_000_000_000, place, embedded, column, row, cosine, sine,
-        queries, keys, values, mixed_grad, normed, in_own, in_far, middle_grad,
-    )
-    early_plane = plane_sum(core_sum(early_own, early_far))
-    late_plane = plane_sum(core_sum(late_own, late_far))
-    early = shard_sum(early_plane, z)
-    late = shard_sum(late_plane, z)
-    slices0, slices1 = slices0.astype(F32), slices1.astype(F32)
-    expert_grads = jnp.stack(
-        [slices0[0] + slices0[2], slices1[0] + slices1[2], slices0[1] + slices0[3], slices1[1] + slices1[3]]
-    )
-    grad_expert_in, grad_expert_out = expert_grads[:, :256], expert_grads[:, 256:]
-    moe = moe_own + moe_other.astype(F32)
+        [((1024, LANES), F32)], place, row_own, returned, cotangent, middle, gates,
+        small_all, payload, mixed, *out_w,
+    )
+    middle_grad, moe_mine, moe_own_mine = together(middle_grad, moe_mine, moe_own_mine)
+    moe_rest, moe_own_rest = over_y(bf_sum(moes[6], moe_pass)), over_x(bf_sum(moes[1], moe_own_pass))
+    left_own, left_far, right_own, right_far, grad_embedded = local_kernel(
+        attend_back_body, "attend_back", [((512, 1152), BF16)] * 2 + [((512, 1024), BF16)] * 2 + [(wide, BF16)],
+        [((SEQUENCE, 2048), BF16), (wide, F32)], place, embedded, column, row, cosine, sine,
+        queries, keys, values, mixed_grad, normed, middle_grad, *weights,
+    )
+    left_far, right_far, moe_rest, moe_own_rest = together(left_far, right_far, moe_rest, moe_own_rest)
+    moe_pair = bf_sum(moes[4], moe_mine, moe_rest)
+    moe_own = bf_sum(moes[0], moe_own_mine, moe_own_rest)
+    moe_other = over_shard(moe_pair, 1)
+    addends = plane_fold(core_sum(left_own, left_far), over_x, over_y)
+    addends += plane_fold(core_sum(right_own, right_far), over_y, over_x)
+    addends += plane_fold(core_sum(early_own, early_far), over_y, over_x)
+    addends[0], slices1 = together(addends[0], slices1)
+    planes = local_kernel(plane_body, "plane", [((32, 3328), BF16)] * 4, [], z.reshape(1), *addends)
+    planes = [planes[0]] + [over_shard(planes[k], k) for k in (1, 2, 3)]
+    shapes = [(32, 1024), (32, 512), (32, 512), (32, 1024), (32, EXPERTS), (1, 32), (1, 32)]
+    late_query, late_key, late_value, early_out, router, gain_attn, gain_ffn = local_kernel(
+        settle_body, "settle", [(shape, F32) for shape in shapes], [], z.reshape(1), *planes
+    )
+    grad_expert_in, grad_expert_out = owner_sum(1, slices1, owned)
+    moe = moe_own.astype(F32) + moe_other.astype(F32)
     output = (middle + resid_scale * moe).astype(BF16)
     return (
         output,
         grad_embedded,
-        late[:, 2048 + GAIN_ATTN],
-        early[:, 1024 + GAIN_FFN],
-        late[:, :1024],
-        late[:, 1024:1536],
-        late[:, 1536:2048],
-        early[:, :1024],
-        early[:, 1024 : 1024 + EXPERTS],
+        gain_attn[0],
+        gain_ffn[0],
+        late_query,
+        late_key,
+        late_value,
+        early_out,
+        router,
         grad_expert_in,
         grad_expert_out,
     )

time: 491 us -> 447 us (0.910)
  the two profiles are of different devices: /device:TPU:0 before, /device:TPU:8 now
where the time goes in v4:
time: 447 us; the launch traced here: 438 us
  Pallas kernels  148 us (33%)
  waiting for transfers between devices  140 us (31%)
  starting transfers between devices  92.5 us (21%)
  other arithmetic  40.9 us (9%)
  local copies, waits for them, and re-layouts  13.7 us (3%)
    ppermute x62, waiting for transfers between devices, over_expert(): return lax.ppermute(value, 'expert', [(i, i ^ bits) for i in range(8)])  102 us
    pallas_call x4, Pallas kernels, expert_call(): pl.pallas_call(functools.partial(expert_body, before is None, len(weights...  97.2 us
    ppermute x62, starting transfers between devices, over_expert(): return lax.ppermute(value, 'expert', [(i, i ^ bits) for i in range(8)])  51.1 us
    pallas_call x6, Pallas kernels, local_kernel(): pl.pallas_call(body, out_shape=[jax.ShapeDtypeStruct(shape, dtype) for sh...  42.4 us
    all_to_all x5, starting transfers between devices, exchange(): lax.all_to_all(slices, 'shard', split_axis=0, concat_axis=0, tiled=True)  25.9 us
    ppermute x10, waiting for transfers between devices, over_shard(): return lax.ppermute(value, 'shard', [(i, i ^ bits) for i in range(4)])  24 us
    ppermute x10, starting transfers between devices, over_shard(): return lax.ppermute(value, 'shard', [(i, i ^ bits) for i in range(4)])  15.5 us
    convert_element_type x10, other arithmetic, bf_sum(): return sum((value.astype(F32) for value in values)).astype(BF16)  15.1 us
  transfers between devices with their start and end apart: 77, of which 28 were waited for; matrix products, arithmetic and copies ran while one was open for 11% of the time, Pallas kernels for 33%

profile of v4, /device:TPU:8, one launch (start us, length us, event | category | flops | bytes accessed | tf_op | source)
XLA Modules:
  0.0 438.1 jit_solution(10315688167083089022)
XLA Ops:
  0.6 1.9 pack.1
  2.5 3.0 collective-permute-start.1
  6.0 1.5 collective-permute-start.3
  7.5 1.5 collective-permute-start.4
  9.0 2.7 fusion.3
  11.8 1.6 pad_maximum_fusion
  13.3 1.3 collective-permute-start.9
  14.7 5.5 %collective-permute-done.1 = bf16[32,3200]{1,0:T(8,128)(2,1)S(1)} collective-permute-done((bf16[32,3200]{1,0:T(8,128)(2,1)}, bf16[32,3200]{1,0:T(8,128)(2,1)S(1)}, u32[]{:S(2)}, u32[]{:S(2)}) %collective-permute-start.1) | collective-permute-done | bytes 204832 | tf_op jit(solution)/shard_map/ppermute | solution.py:439
  20.1 3.9 collective-permute-done.2
  25.4 1.6 collective-permute-start.5
  27.0 1.6 collective-permute-start.7
  29.6 4.2 collective-permute-done.7.refs_10_
  33.8 4.4 %all-to-all-start = ((bf16[4,256,1024]{2,1,0:T(8,128)(2,1)}), bf16[4,256,1024]{2,1,0:T(8,128)(2,1)}, u32[]{:S(2)}, u32[]{:S(2)}) async-start(bf16[4,256,1024]{2,1,0:T(8,128)(2,1)} %pad_maximum_fusion), calls=%async_computation | async-start | bytes 4194304 | tf_op jit(solution)/shard_map/all_to_all | solution.py:875
  39.1 1.5 collective-permute-start.13
  43.0 2.7 collective-permute-done.18.refs_9_
  45.7 2.5 collective-permute-start.6
  49.1 1.3 collective-permute-done.8.refs_11_
  50.5 2.4 collective-permute-done.6.refs_3_
  55.4 2.0 collective-permute-start.11
  59.1 2.0 collective-permute-start.30
  62.8 9.7 %attend.1 = (bf16[256,1024]{1,0:T(8,128)(2,1)}, bf16[256,1024]{1,0:T(8,128)(2,1)}, bf16[256,512]{1,0:T(8,128)(2,1)}, bf16[256,512]{1,0:T(8,128)(2,1)}, bf16[256,...) custom-call(s32[1]{0:T(128)} %bitcast.e_ref, bf16[256,1024]{1,0:T(8,128)(2,1)} %x_ref.5, s32[256,1]{1,0:T(8,128)} %copy.30.column_ref, ...), custom_call_target="tpu_custom_call" | custom-call | flops 1000 | bytes 1000 | tf_op jit(solution)/shard_map/attend/pallas_call | solution.py:847
  76.0 4.5 %route.1 = (bf16[288,1024]{1,0:T(8,128)(2,1)}, f32[256,128]{1,0:T(8,128)}, f32[256,1024]{1,0:T(8,128)}) custom-call(s32[1]{0:T(128)} %bitcast.e_ref, bf16[256,1024]{1,0:T(8,128)(2,1)} %x_ref.5, bf16[256,1024]{1,0:T(8,128)(2,1)} %get-tuple-element.191.mixed_ref, bf16[1024,128]{1,0:T(8,128)(2,1)} %get-tuple-element.192.small_ref, ...), custom_call_target="tpu_custom_call" | custom-call | flops 1000 | bytes 1000 | tf_op jit(solution)/shard_map/route/pallas_call | solution.py:847
  82.6 2.0 collective-permute-start.32
  86.6 20.8 %collective-permute-done.31.refs_13_ = bf16[256,1024]{1,0:T(8,128)(2,1)S(1)} collective-permute-done((bf16[256,1024]{1,0:T(8,128)(2,1)S(1)}, bf16[256,1024]{1,0:T(8,128)(2,1)S(1)}, u32[]{:S(2)}, u32[]{:S(2)}) %collective-permute-start.31) | collective-permute-done | bytes 524320 | tf_op jit(solution)/shard_map/ppermute | solution.py:435
  108.2 4.9 %all-to-all-start.1 = ((bf16[4,128,1024]{2,1,0:T(8,128)(2,1)}), bf16[4,128,1024]{2,1,0:T(8,128)(2,1)}, u32[]{:S(2)}, u32[]{:S(2)}) async-start(bf16[4,128,1024]{2,1,0:T(8,128)(2,1)} %pad_maximum_fusion.1), calls=%async_computation.1 | async-start | bytes 2097152 | tf_op jit(solution)/shard_map/all_to_all | solution.py:875
  115.3 3.3 maximum_maximum_fusion
  118.6 21.4 %collective-permute-done.36.refs_15_ = bf16[256,1024]{1,0:T(8,128)(2,1)S(1)} collective-permute-done((bf16[256,1024]{1,0:T(8,128)(2,1)S(1)}, bf16[256,1024]{1,0:T(8,128)(2,1)S(1)}, u32[]{:S(2)}, u32[]{:S(2)}) %collective-permute-start.36) | collective-permute-done | bytes 524320 | tf_op jit(solution)/shard_map/ppermute | solution.py:435
  141.7 5.3 %all-to-all-start.2 = ((bf16[4,384,1024]{2,1,0:T(8,128)(2,1)}), bf16[4,384,1024]{2,1,0:T(8,128)(2,1)}, u32[]{:S(2)}, u32[]{:S(2)}) async-start(bf16[4,384,1024]{2,1,0:T(8,128)(2,1)} %maximum_maximum_fusion), calls=%async_computation.2 | async-start | bytes 6291456 | tf_op jit(solution)/shard_map/all_to_all | solution.py:875
  148.5 14.3 %collective-permute-done.33.refs_3_ = bf16[288,1024]{1,0:T(8,128)(2,1)S(1)} collective-permute-done((bf16[288,1024]{1,0:T(8,128)(2,1)S(1)}, bf16[288,1024]{1,0:T(8,128)(2,1)S(1)}, u32[]{:S(2)}, u32[]{:S(2)}) %collective-permute-start.33) | collective-permute-done | bytes 589856 | tf_op jit(solution)/shard_map/ppermute | solution.py:435
  163.8 22.1 %expert.4 = (bf16[272,1024]{1,0:T(8,128)(2,1)}, bf16[272,1024]{1,0:T(8,128)(2,1)}, bf16[272,1024]{1,0:T(8,128)(2,1)}, bf16[272,1024]{1,0:T(8,128)(2,1)}, bf16[27...) custom-call(s32[1]{0:T(128)} %bitcast.15.number_ref, ...), custom_call_target="tpu_custom_call" | custom-call | flops 1000 | bytes 1000 | tf_op jit(solution)/shard_map/expert/pallas_call | solution.py:592
  186.1 25.0 %expert.5 = (bf16[272,1024]{1,0:T(8,128)(2,1)}, bf16[272,1024]{1,0:T(8,128)(2,1)}, bf16[272,1024]{1,0:T(8,128)(2,1)}, bf16[272,1024]{1,0:T(8,128)(2,1)}, bf16[27...) custom-call(s32[1]{0:T(128)} %bitcast.14.number_ref, ...), custom_call_target="tpu_custom_call" | custom-call | flops 1000 | bytes 1000 | tf_op jit(solution)/shard_map/expert/pallas_call | solution.py:592
  211.1 5.1 %add_convert_fusion.1 = bf16[4,384,1024]{2,1,0:T(8,128)(2,1)} fusion(bf16[4,384,1024]{2,1,0:T(8,128)(2,1)S(1)} %collective-permute-done.40, bf16[4,384,1024]{2,1,0:T(8,128)(2,1)} %get-tuple-element.237), kind=kLoop, calls=%fused_computation.1 | loop fusion | flops 6291456 | bytes 9437184 | tf_op jit(solution)/shard_map/convert_element_type | solution.py:864
  216.6 5.3 %all-to-all-start.3 = ((bf16[4,384,1024]{2,1,0:T(8,128)(2,1)}), bf16[4,384,1024]{2,1,0:T(8,128)(2,1)S(1)}, u32[]{:S(2)}, u32[]{:S(2)}) async-start(bf16[4,384,1024]{2,1,0:T(8,128)(2,1)} %add_convert_fusion.1), calls=%async_computation.3 | async-start | bytes 6291456 | tf_op jit(solution)/shard_map/all_to_all | solution.py:875
  222.2 25.0 %expert.6 = (bf16[272,1024]{1,0:T(8,128)(2,1)}, bf16[272,1024]{1,0:T(8,128)(2,1)}, bf16[272,1024]{1,0:T(8,128)(2,1)}, bf16[272,1024]{1,0:T(8,128)(2,1)}, bf16[27...) custom-call(s32[1]{0:T(128)S(6)} %add.106.number_ref, ...), custom_call_target="tpu_custom_call" | custom-call | flops 1000 | bytes 1000 | tf_op jit(solution)/shard_map/expert/pallas_call | solution.py:592
  247.7 25.1 %expert.7 = (bf16[272,1024]{1,0:T(8,128)(2,1)}, bf16[272,1024]{1,0:T(8,128)(2,1)}, bf16[272,1024]{1,0:T(8,128)(2,1)}, bf16[272,1024]{1,0:T(8,128)(2,1)}, bf16[27...) custom-call(s32[1]{0:T(128)S(6)} %add.103.number_ref, ...), custom_call_target="tpu_custom_call" | custom-call | flops 1000 | bytes 1000 | tf_op jit(solution)/shard_map/expert/pallas_call | solution.py:592
  274.8 1.6 collective-permute-start.47
  276.4 6.1 %add_convert_fusion = bf16[4,384,1024]{2,1,0:T(8,128)(2,1)} fusion(bf16[4,384,1024]{2,1,0:T(8,128)(2,1)} %collective-permute-done.44, bf16[4,384,1024]{2,1,0:T(8,128)(2,1)} %get-tuple-element.277), kind=kLoop, calls=%fused_computation | loop fusion | flops 6291456 | bytes 9437184 | tf_op jit(solution)/shard_map/convert_element_type | solution.py:864
  282.5 6.1 %collective-permute-done.43 = bf16[272,1024]{1,0:T(8,128)(2,1)} collective-permute-done((bf16[272,1024]{1,0:T(8,128)(2,1)}, bf16[272,1024]{1,0:T(8,128)(2,1)}, u32[]{:S(2)}, u32[]{:S(2)}) %collective-permute-start.43) | collective-permute-done | bytes 557088 | tf_op jit(solution)/shard_map/ppermute | solution.py:435
  289.9 2.3 add_convert_fusion.8
  293.4 2.3 add_convert_fusion.6
  297.6 3.0 collective-permute-done.42
  300.6 7.2 %collective-permute-done.45 = bf16[272,1024]{1,0:T(8,128)(2,1)S(1)} collective-permute-done((bf16[272,1024]{1,0:T(8,128)(2,1)S(1)}, bf16[272,1024]{1,0:T(8,128)(2,1)S(1)}, u32[]{:S(2)}, u32[]{:S(2)}) %collective-permute-start.45) | collective-permute-done | bytes 557088 | tf_op jit(solution)/shard_map/ppermute | solution.py:435
  307.7 2.2 add_convert_fusion.7
  309.9 3.3 collective-permute-start.49
  314.4 3.4 owner_sum.2
  319.8 2.4 add_convert_fusion.5.sum_ref
  323.2 6.1 %turn.1 = (bf16[512,1152]{1,0:T(8,128)(2,1)}, bf16[512,1152]{1,0:T(8,128)(2,1)}, bf16[256,1024]{1,0:T(8,128)(2,1)}, f32[256,1024]{1,0:T(8,128)}) custom-call(s32[1]{0:T(128)} %bitcast.e_ref, bf16[272,1024]{1,0:T(8,128)(2,1)} %add_convert_fusion.5.sum_ref, bf16[272,1024]{1,0:T(8,128)(2,1)} %collective-permute-done.49.add_ref, bf16[256,1024]{1,0:T(8,128)(2,1)} %grad_ref.1, ...), custom_call_target="tpu_custom_call" | custom-call | flops 1000 | bytes 1000 | tf_op jit(solution)/shard_map/turn/pallas_call | solution.py:847
  335.5 6.0 %all-to-all-start.4 = ((bf16[4,384,1024]{2,1,0:T(8,128)(2,1)}), bf16[4,384,1024]{2,1,0:T(8,128)(2,1)S(1)}, u32[]{:S(2)}, u32[]{:S(2)}) async-start(bf16[4,384,1024]{2,1,0:T(8,128)(2,1)} %add_convert_fusion), calls=%async_computation.4 | async-start | bytes 6291456 | tf_op jit(solution)/shard_map/all_to_all | solution.py:875
  341.4 3.1 collective-permute-done.50
  345.5 16.2 %attend_back.1 = (bf16[512,1152]{1,0:T(8,128)(2,1)}, bf16[512,1152]{1,0:T(8,128)(2,1)}, bf16[512,1024]{1,0:T(8,128)(2,1)}, bf16[512,1024]{1,0:T(8,128)(2,1)}, bf16[256,1024]{1,0:T(8,128)(2,1)}) custom-call(s32[1]{0:T(128)} %bitcast.e_ref, bf16[256,1024]{1,0:T(8,128)(2,1)} %x_ref.5, s32[256,1]{1,0:T(8,128)} %copy.30.column_ref, s32[1,256]{1,0:T(1,128)} %row_ref.3, ...), custom_call_target="tpu_custom_call" | custom-call | flops 1000 | bytes 1000 | tf_op jit(solution)/shard_map/attend_back/pallas_call | solution.py:847
  361.9 1.7 add_convert_fusion.2
  365.4 2.3 add_convert_fusion.10
  367.6 2.6 collective-permute-start.56
  371.1 3.1 collective-permute-done.67
  379.6 9.1 %collective-permute-done.59 = bf16[128,1152]{1,0:T(8,128)(2,1)S(1)} collective-permute-done((bf16[128,1152]{1,0:T(8,128)(2,1)S(1)}, bf16[128,1152]{1,0:T(8,128)(2,1)S(1)}, u32[]{:S(2)}, u32[]{:S(2)}) %collective-permute-start.59) | collective-permute-done | bytes 294944 | tf_op jit(solution)/shard_map/ppermute | solution.py:435
  395.1 13.5 %all-to-all-done.4.one_ref.two_ref = bf16[4,384,1024]{2,1,0:T(8,128)(2,1)S(1)} async-done(((bf16[4,384,1024]{2,1,0:T(8,128)(2,1)}), bf16[4,384,1024]{2,1,0:T(8,128)(2,1)S(1)}, u32[]{:S(2)}, u32[]{:S(2)}) %all-to-all-start.4) | async-done | bytes 3145760 | tf_op jit(solution)/shard_map/all_to_all | solution.py:875
  408.6 3.9 plane.1
  412.5 3.3 collective-permute-start.69
  415.9 1.5 collective-permute-start.71
  417.3 2.6 add_convert_fusion.9
  419.9 3.1 owner_sum.3
  423.1 7.8 %collective-permute-done.70.refs_2_ = bf16[32,3328]{1,0:T(8,128)(2,1)} collective-permute-done((bf16[32,3328]{1,0:T(8,128)(2,1)}, bf16[32,3328]{1,0:T(8,128)(2,1)}, u32[]{:S(2)}, u32[]{:S(2)}) %collective-permute-start.70) | collective-permute-done | bytes 213024 | tf_op jit(solution)/shard_map/ppermute | solution.py:439
  431.0 4.7 %collective-permute-done.71.refs_3_ = bf16[32,3328]{1,0:T(8,128)(2,1)} collective-permute-done((bf16[32,3328]{1,0:T(8,128)(2,1)}, bf16[32,3328]{1,0:T(8,128)(2,1)}, u32[]{:S(2)}, u32[]{:S(2)}) %collective-permute-start.71) | collective-permute-done | bytes 213024 | tf_op jit(solution)/shard_map/ppermute | solution.py:439
  435.6 2.0 settle.1
  (257 shorter events, 61.1 us)
Async XLA Ops:
  2.5 10.8 %collective-permute-start = (bf16[32,3200]{1,0:T(8,128)(2,1)}, bf16[32,3200]{1,0:T(8,128)(2,1)S(1)}, u32[]{:S(2)}, u32[]{:S(2)}) collective-permute-start(bf16[32,3200]{1,0:T(8,128)(2,1)} %pack.1), channel_id=1, source_target_pairs={{0,1},{1,0},{2,3},{3,2},{4,5},{5,4},{6,7},{7,6},{8,9},{9,8},{10,11... | collective-permute-start | bytes 614408 | tf_op jit(solution)/shard_map/ppermute | solution.py:439
  2.5 17.6 %collective-permute-start.1 = (bf16[32,3200]{1,0:T(8,128)(2,1)}, bf16[32,3200]{1,0:T(8,128)(2,1)S(1)}, u32[]{:S(2)}, u32[]{:S(2)}) collective-permute-start(bf16[32,3200]{1,0:T(8,128)(2,1)} %pack.1), channel_id=1, source_target_pairs={{0,2},{1,3},{2,0},{3,1},{4,6},{5,7},{6,4},{7,5},{8,10},{9,11},{10,... | collective-permute-start | bytes 614408 | tf_op jit(solution)/shard_map/ppermute | solution.py:439
  5.5 18.5 %collective-permute-start.2 = (bf16[32,3200]{1,0:T(8,128)(2,1)}, bf16[32,3200]{1,0:T(8,128)(2,1)}, u32[]{:S(2)}, u32[]{:S(2)}) collective-permute-start(bf16[32,3200]{1,0:T(8,128)(2,1)} %pack.1), channel_id=1, source_target_pairs={{0,3},{1,2},{2,1},{3,0},{4,7},{5,6},{6,5},{7,4},{8,11},{9,10},{10,... | collective-permute-start | bytes 614408 | tf_op jit(solution)/shard_map/ppermute | solution.py:439
  6.0 19.3 %collective-permute-start.3 = (bf16[256,1024]{1,0:T(8,128)(2,1)}, bf16[256,1024]{1,0:T(8,128)(2,1)S(1)}, u32[]{:S(2)}, u32[]{:S(2)}) collective-permute-start(bf16[256,1024]{1,0:T(8,128)(2,1)} %grad_ref.1), channel_id=1, source_target_pairs={{0,8},{4,12},{8,0},{12,4},{16,24},{20,28},{24,16},{28,20},{1,9},{5... | collective-permute-start | bytes 1572872 | tf_op jit(solution)/shard_map/ppermute | solution.py:435
  7.5 17.8 %collective-permute-start.4 = (bf16[256,1024]{1,0:T(8,128)(2,1)}, bf16[256,1024]{1,0:T(8,128)(2,1)S(1)}, u32[]{:S(2)}, u32[]{:S(2)}) collective-permute-start(bf16[256,1024]{1,0:T(8,128)(2,1)} %grad_ref.1), channel_id=1, source_target_pairs={{0,16},{4,20},{8,24},{12,28},{16,0},{20,4},{24,8},{28,12},{1,17},{... | collective-permute-start | bytes 1572872 | tf_op jit(solution)/shard_map/ppermute | solution.py:435
  13.3 16.2 %collective-permute-start.9 = (bf16[256,1024]{1,0:T(8,128)(2,1)S(1)}, bf16[256,1024]{1,0:T(8,128)(2,1)S(1)}, u32[]{:S(2)}, u32[]{:S(2)}) collective-permute-start(bf16[256,1024]{1,0:T(8,128)(2,1)S(1)} %copy-done.2), channel_id=1, source_target_pairs={{0,1},{1,0},{2,3},{3,2},{4,5},{5,4},{6,7},{7,6},{8,9},{9,8},{10,11... | collective-permute-start | bytes 1572872 | tf_op jit(solution)/shard_map/ppermute | solution.py:439
  25.4 8.4 %collective-permute-start.5 = (bf16[128,1152]{1,0:T(8,128)(2,1)S(1)}, bf16[128,1152]{1,0:T(8,128)(2,1)S(1)}, u32[]{:S(2)}, u32[]{:S(2)}) collective-permute-start(bf16[128,1152]{1,0:T(8,128)(2,1)S(1)} %slice.97.refs_0_), channel_id=1, source_target_pairs={{0,8},{4,12},{8,0},{12,4},{16,24},{20,28},{24,16},{28,20},{1,9},{5... | collective-permute-start | bytes 884744 | tf_op jit(solution)/shard_map/ppermute | solution.py:435
  33.8 74.4 %all-to-all-start = ((bf16[4,256,1024]{2,1,0:T(8,128)(2,1)}), bf16[4,256,1024]{2,1,0:T(8,128)(2,1)}, u32[]{:S(2)}, u32[]{:S(2)}) async-start(bf16[4,256,1024]{2,1,0:T(8,128)(2,1)} %pad_maximum_fusion), calls=%async_computation | async-start | bytes 4194304 | tf_op jit(solution)/shard_map/all_to_all | solution.py:875
  39.1 9.3 %collective-permute-start.13 = (bf16[128,1152]{1,0:T(8,128)(2,1)S(1)}, bf16[128,1152]{1,0:T(8,128)(2,1)S(1)}, u32[]{:S(2)}, u32[]{:S(2)}) collective-permute-start(bf16[128,1152]{1,0:T(8,128)(2,1)S(1)} %slice.97.refs_0_), channel_id=1, source_target_pairs={{0,16},{4,20},{8,24},{12,28},{16,0},{20,4},{24,8},{28,12},{1,17},{... | collective-permute-start | bytes 884744 | tf_op jit(solution)/shard_map/ppermute | solution.py:435
  40.7 8.3 %collective-permute-start.14 = (bf16[128,1152]{1,0:T(8,128)(2,1)S(1)}, bf16[128,1152]{1,0:T(8,128)(2,1)S(1)}, u32[]{:S(2)}, u32[]{:S(2)}) collective-permute-start(bf16[128,1152]{1,0:T(8,128)(2,1)S(1)} %slice.97.refs_0_), channel_id=1, source_target_pairs={{0,4},{4,0},{8,12},{12,8},{16,20},{20,16},{24,28},{28,24},{1,5},{5... | collective-permute-start | bytes 884744 | tf_op jit(solution)/shard_map/ppermute | solution.py:435
  41.2 9.2 %collective-permute-start.8 = (bf16[128,1024]{1,0:T(8,128)(2,1)S(1)}, bf16[128,1024]{1,0:T(8,128)(2,1)}, u32[]{:S(2)}, u32[]{:S(2)}) collective-permute-start(bf16[128,1024]{1,0:T(8,128)(2,1)S(1)} %collective-permute-done.7.refs_10_), channel_id=1, source_target_pairs={{0,8},{4,12},{8,0},{12,4},{16,24},{20,28},{24,16},{28,20},{1,9},{5... | collective-permute-start | bytes 786440 | tf_op jit(solution)/shard_map/ppermute | solution.py:435
  48.4 9.0 %collective-permute-start.15 = (bf16[128,1152]{1,0:T(8,128)(2,1)S(1)}, bf16[128,1152]{1,0:T(8,128)(2,1)S(1)}, u32[]{:S(2)}, u32[]{:S(2)}) collective-permute-start(bf16[128,1152]{1,0:T(8,128)(2,1)S(1)} %collective-permute-done.5.refs_1_), channel_id=1, source_target_pairs={{0,4},{4,0},{8,12},{12,8},{16,20},{20,16},{24,28},{28,24},{1,5},{5... | collective-permute-start | bytes 884744 | tf_op jit(solution)/shard_map/ppermute | solution.py:435
  50.4 8.1 %collective-permute-start.16 = (bf16[128,1152]{1,0:T(8,128)(2,1)S(1)}, bf16[128,1152]{1,0:T(8,128)(2,1)S(1)}, u32[]{:S(2)}, u32[]{:S(2)}) collective-permute-start(bf16[128,1152]{1,0:T(8,128)(2,1)S(1)} %collective-permute-done.13.refs_2_), channel_id=1, source_target_pairs={{0,4},{4,0},{8,12},{12,8},{16,20},{20,16},{24,28},{28,24},{1,5},{5... | collective-permute-start | bytes 884744 | tf_op jit(solution)/shard_map/ppermute | solution.py:435
  54.9 17.7 %collective-permute-start.10 = (bf16[128,1024]{1,0:T(8,128)(2,1)S(1)}, bf16[128,1024]{1,0:T(8,128)(2,1)S(1)}, u32[]{:S(2)}, u32[]{:S(2)}) collective-permute-start(bf16[128,1024]{1,0:T(8,128)(2,1)S(1)} %slice.99.refs_0_), channel_id=1, source_target_pairs={{0,8},{4,12},{8,0},{12,4},{16,24},{20,28},{24,16},{28,20},{1,9},{5... | collective-permute-start | bytes 786440 | tf_op jit(solution)/shard_map/ppermute | solution.py:435
  55.4 17.1 %collective-permute-start.11 = (bf16[128,1024]{1,0:T(8,128)(2,1)S(1)}, bf16[128,1024]{1,0:T(8,128)(2,1)S(1)}, u32[]{:S(2)}, u32[]{:S(2)}) collective-permute-start(bf16[128,1024]{1,0:T(8,128)(2,1)S(1)} %slice.99.refs_0_), channel_id=1, source_target_pairs={{0,16},{4,20},{8,24},{12,28},{16,0},{20,4},{24,8},{28,12},{1,17},{... | collective-permute-start | bytes 786440 | tf_op jit(solution)/shard_map/ppermute | solution.py:435
  57.4 15.1 %collective-permute-start.12 = (bf16[128,1024]{1,0:T(8,128)(2,1)S(1)}, bf16[128,1024]{1,0:T(8,128)(2,1)S(1)}, u32[]{:S(2)}, u32[]{:S(2)}) collective-permute-start(bf16[128,1024]{1,0:T(8,128)(2,1)S(1)} %slice.99.refs_0_), channel_id=1, source_target_pairs={{0,24},{4,28},{8,16},{12,20},{16,8},{20,12},{24,0},{28,4},{1,25},{... | collective-permute-start | bytes 786440 | tf_op jit(solution)/shard_map/ppermute | solution.py:435
  59.1 23.6 %collective-permute-start.30 = (bf16[256,1024]{1,0:T(8,128)(2,1)S(1)}, bf16[256,1024]{1,0:T(8,128)(2,1)S(1)}, u32[]{:S(2)}, u32[]{:S(2)}) collective-permute-start(bf16[256,1024]{1,0:T(8,128)(2,1)S(1)} %collective-permute-done.3.refs_9_), channel_id=1, source_target_pairs={{0,16},{4,20},{8,24},{12,28},{16,0},{20,4},{24,8},{28,12},{1,17},{... | collective-permute-start | bytes 1572872 | tf_op jit(solution)/shard_map/ppermute | solution.py:435
  80.5 27.1 %collective-permute-start.27 = (bf16[288,1024]{1,0:T(8,128)(2,1)}, bf16[288,1024]{1,0:T(8,128)(2,1)S(1)}, u32[]{:S(2)}, u32[]{:S(2)}) collective-permute-start(bf16[288,1024]{1,0:T(8,128)(2,1)} %get-tuple-element.198.refs_0_.normed2_ref), channel_id=1, source_target_pairs={{0,8},{4,12},{8,0},{12,4},{16,24},{20,28},{24,16},{28,20},{1,9},{5... | collective-permute-start | bytes 1769480 | tf_op jit(solution)/shard_map/ppermute | solution.py:435
  81.0 26.6 %collective-permute-start.28 = (bf16[288,1024]{1,0:T(8,128)(2,1)}, bf16[288,1024]{1,0:T(8,128)(2,1)S(1)}, u32[]{:S(2)}, u32[]{:S(2)}) collective-permute-start(bf16[288,1024]{1,0:T(8,128)(2,1)} %get-tuple-element.198.refs_0_.normed2_ref), channel_id=1, source_target_pairs={{0,16},{4,20},{8,24},{12,28},{16,0},{20,4},{24,8},{28,12},{1,17},{... | collective-permute-start | bytes 1769480 | tf_op jit(solution)/shard_map/ppermute | solution.py:435
  81.7 26.5 %collective-permute-start.29 = (bf16[288,1024]{1,0:T(8,128)(2,1)}, bf16[288,1024]{1,0:T(8,128)(2,1)S(1)}, u32[]{:S(2)}, u32[]{:S(2)}) collective-permute-start(bf16[288,1024]{1,0:T(8,128)(2,1)} %get-tuple-element.198.refs_0_.normed2_ref), channel_id=1, source_target_pairs={{0,1},{1,0},{2,3},{3,2},{4,5},{5,4},{6,7},{7,6},{8,9},{9,8},{10,11... | collective-permute-start | bytes 1769480 | tf_op jit(solution)/shard_map/ppermute | solution.py:439
  81.7 25.7 %collective-permute-start.31 = (bf16[256,1024]{1,0:T(8,128)(2,1)S(1)}, bf16[256,1024]{1,0:T(8,128)(2,1)S(1)}, u32[]{:S(2)}, u32[]{:S(2)}) collective-permute-start(bf16[256,1024]{1,0:T(8,128)(2,1)S(1)} %collective-permute-done.9.refs_12_), channel_id=1, source_target_pairs={{0,8},{4,12},{8,0},{12,4},{16,24},{20,28},{24,16},{28,20},{1,9},{5... | collective-permute-start | bytes 1572872 | tf_op jit(solution)/shard_map/ppermute | solution.py:435
  82.6 25.0 %collective-permute-start.32 = (bf16[256,1024]{1,0:T(8,128)(2,1)S(1)}, bf16[256,1024]{1,0:T(8,128)(2,1)S(1)}, u32[]{:S(2)}, u32[]{:S(2)}) collective-permute-start(bf16[256,1024]{1,0:T(8,128)(2,1)S(1)} %collective-permute-done.9.refs_12_), channel_id=1, source_target_pairs={{0,16},{4,20},{8,24},{12,28},{16,0},{20,4},{24,8},{28,12},{1,17},{... | collective-permute-start | bytes 1572872 | tf_op jit(solution)/shard_map/ppermute | solution.py:435
  108.2 32.7 %all-to-all-start.1 = ((bf16[4,128,1024]{2,1,0:T(8,128)(2,1)}), bf16[4,128,1024]{2,1,0:T(8,128)(2,1)}, u32[]{:S(2)}, u32[]{:S(2)}) async-start(bf16[4,128,1024]{2,1,0:T(8,128)(2,1)} %pad_maximum_fusion.1), calls=%async_computation.1 | async-start | bytes 2097152 | tf_op jit(solution)/shard_map/all_to_all | solution.py:875
  113.1 49.8 %collective-permute-start.38 = (bf16[4,256,1024]{2,1,0:T(8,128)(2,1)}, bf16[4,256,1024]{2,1,0:T(8,128)(2,1)}, u32[]{:S(2)}, u32[]{:S(2)}) collective-permute-start(bf16[4,256,1024]{2,1,0:T(8,128)(2,1)} %all-to-all-done.refs_16_), channel_id=1, source_target_pairs={{0,4},{4,0},{8,12},{12,8},{16,20},{20,16},{24,28},{28,24},{1,5},{5... | collective-permute-start | bytes 6291464 | tf_op jit(solution)/shard_map/ppermute | solution.py:435
  113.1 27.0 %collective-permute-start.34 = (bf16[288,1024]{1,0:T(8,128)(2,1)S(1)}, bf16[288,1024]{1,0:T(8,128)(2,1)S(1)}, u32[]{:S(2)}, u32[]{:S(2)}) collective-permute-start(bf16[288,1024]{1,0:T(8,128)(2,1)S(1)} %collective-permute-done.29.refs_4_), channel_id=1, source_target_pairs={{0,8},{4,12},{8,0},{12,4},{16,24},{20,28},{24,16},{28,20},{1,9},{5... | collective-permute-start | bytes 1769480 | tf_op jit(solution)/shard_map/ppermute | solution.py:435
  114.1 26.8 %collective-permute-start.35 = (bf16[288,1024]{1,0:T(8,128)(2,1)S(1)}, bf16[288,1024]{1,0:T(8,128)(2,1)S(1)}, u32[]{:S(2)}, u32[]{:S(2)}) collective-permute-start(bf16[288,1024]{1,0:T(8,128)(2,1)S(1)} %collective-permute-done.29.refs_4_), channel_id=1, source_target_pairs={{0,16},{4,20},{8,24},{12,28},{16,0},{20,4},{24,8},{28,12},{1,17},{... | collective-permute-start | bytes 1769480 | tf_op jit(solution)/shard_map/ppermute | solution.py:435
  114.4 25.7 %collective-permute-start.36 = (bf16[256,1024]{1,0:T(8,128)(2,1)S(1)}, bf16[256,1024]{1,0:T(8,128)(2,1)S(1)}, u32[]{:S(2)}, u32[]{:S(2)}) collective-permute-start(bf16[256,1024]{1,0:T(8,128)(2,1)S(1)} %collective-permute-done.32.refs_14_), channel_id=1, source_target_pairs={{0,8},{4,12},{8,0},{12,4},{16,24},{20,28},{24,16},{28,20},{1,9},{5... | collective-permute-start | bytes 1572872 | tf_op jit(solution)/shard_map/ppermute | solution.py:435
  141.7 74.5 %all-to-all-start.2 = ((bf16[4,384,1024]{2,1,0:T(8,128)(2,1)}), bf16[4,384,1024]{2,1,0:T(8,128)(2,1)}, u32[]{:S(2)}, u32[]{:S(2)}) async-start(bf16[4,384,1024]{2,1,0:T(8,128)(2,1)} %maximum_maximum_fusion), calls=%async_computation.2 | async-start | bytes 6291456 | tf_op jit(solution)/shard_map/all_to_all | solution.py:875
  147.0 15.9 %collective-permute-start.39 = (bf16[4,128,1024]{2,1,0:T(8,128)(2,1)}, bf16[4,128,1024]{2,1,0:T(8,128)(2,1)}, u32[]{:S(2)}, u32[]{:S(2)}) collective-permute-start(bf16[4,128,1024]{2,1,0:T(8,128)(2,1)} %all-to-all-done.1.refs_17_), channel_id=1, source_target_pairs={{0,4},{4,0},{8,12},{12,8},{16,20},{20,16},{24,28},{28,24},{1,5},{5... | collective-permute-start | bytes 3145736 | tf_op jit(solution)/shard_map/ppermute | solution.py:435
  147.1 15.7 %collective-permute-start.33 = (bf16[288,1024]{1,0:T(8,128)(2,1)S(1)}, bf16[288,1024]{1,0:T(8,128)(2,1)S(1)}, u32[]{:S(2)}, u32[]{:S(2)}) collective-permute-start(bf16[288,1024]{1,0:T(8,128)(2,1)S(1)} %collective-permute-done.27.refs_1_), channel_id=1, source_target_pairs={{0,16},{4,20},{8,24},{12,28},{16,0},{20,4},{24,8},{28,12},{1,17},{... | collective-permute-start | bytes 1769480 | tf_op jit(solution)/shard_map/ppermute | solution.py:435
  147.4 15.5 %collective-permute-start.37 = (bf16[288,1024]{1,0:T(8,128)(2,1)S(1)}, bf16[288,1024]{1,0:T(8,128)(2,1)S(1)}, u32[]{:S(2)}, u32[]{:S(2)}) collective-permute-start(bf16[288,1024]{1,0:T(8,128)(2,1)S(1)} %collective-permute-done.35.refs_6_), channel_id=1, source_target_pairs={{0,8},{4,12},{8,0},{12,4},{16,24},{20,28},{24,16},{28,20},{1,9},{5... | collective-permute-start | bytes 1769480 | tf_op jit(solution)/shard_map/ppermute | solution.py:435
  186.0 25.1 %collective-permute-start.40 = (bf16[4,384,1024]{2,1,0:T(8,128)(2,1)}, bf16[4,384,1024]{2,1,0:T(8,128)(2,1)S(1)}, u32[]{:S(2)}, u32[]{:S(2)}) collective-permute-start(bf16[4,384,1024]{2,1,0:T(8,128)(2,1)} %get-tuple-element.238), channel_id=1, source_target_pairs={{0,4},{4,0},{8,12},{12,8},{16,20},{20,16},{24,28},{28,24},{1,5},{5... | collective-permute-start | bytes 9437192 | tf_op jit(solution)/shard_map/ppermute | solution.py:435
  216.6 73.2 %all-to-all-start.3 = ((bf16[4,384,1024]{2,1,0:T(8,128)(2,1)}), bf16[4,384,1024]{2,1,0:T(8,128)(2,1)S(1)}, u32[]{:S(2)}, u32[]{:S(2)}) async-start(bf16[4,384,1024]{2,1,0:T(8,128)(2,1)} %add_convert_fusion.1), calls=%async_computation.3 | async-start | bytes 6291456 | tf_op jit(solution)/shard_map/all_to_all | solution.py:875
  247.2 29.2 %collective-permute-start.44 = (bf16[4,384,1024]{2,1,0:T(8,128)(2,1)}, bf16[4,384,1024]{2,1,0:T(8,128)(2,1)}, u32[]{:S(2)}, u32[]{:S(2)}) collective-permute-start(bf16[4,384,1024]{2,1,0:T(8,128)(2,1)} %get-tuple-element.278), channel_id=1, source_target_pairs={{0,4},{4,0},{8,12},{12,8},{16,20},{20,16},{24,28},{28,24},{1,5},{5... | collective-permute-start | bytes 9437192 | tf_op jit(solution)/shard_map/ppermute | solution.py:435
  272.7 15.9 %collective-permute-start.43 = (bf16[272,1024]{1,0:T(8,128)(2,1)}, bf16[272,1024]{1,0:T(8,128)(2,1)}, u32[]{:S(2)}, u32[]{:S(2)}) collective-permute-start(bf16[272,1024]{1,0:T(8,128)(2,1)} %get-tuple-element.276), channel_id=1, source_target_pairs={{0,8},{4,12},{8,0},{12,4},{16,24},{20,28},{24,16},{28,20},{1,9},{5... | collective-permute-start | bytes 1671176 | tf_op jit(solution)/shard_map/ppermute | solution.py:435
  273.8 26.8 %collective-permute-start.42 = (bf16[272,1024]{1,0:T(8,128)(2,1)}, bf16[272,1024]{1,0:T(8,128)(2,1)}, u32[]{:S(2)}, u32[]{:S(2)}) collective-permute-start(bf16[272,1024]{1,0:T(8,128)(2,1)} %get-tuple-element.274), channel_id=1, source_target_pairs={{0,8},{4,12},{8,0},{12,4},{16,24},{20,28},{24,16},{28,20},{1,9},{5... | collective-permute-start | bytes 1671176 | tf_op jit(solution)/shard_map/ppermute | solution.py:435
  274.8 18.6 %collective-permute-start.47 = (bf16[272,1024]{1,0:T(8,128)(2,1)}, bf16[272,1024]{1,0:T(8,128)(2,1)}, u32[]{:S(2)}, u32[]{:S(2)}) collective-permute-start(bf16[272,1024]{1,0:T(8,128)(2,1)} %get-tuple-element.294), channel_id=1, source_target_pairs={{0,16},{4,20},{8,24},{12,28},{16,0},{20,4},{24,8},{28,12},{1,17},{... | collective-permute-start | bytes 1671176 | tf_op jit(solution)/shard_map/ppermute | solution.py:435
  292.2 15.6 %collective-permute-start.45 = (bf16[272,1024]{1,0:T(8,128)(2,1)S(1)}, bf16[272,1024]{1,0:T(8,128)(2,1)S(1)}, u32[]{:S(2)}, u32[]{:S(2)}) collective-permute-start(bf16[272,1024]{1,0:T(8,128)(2,1)S(1)} %add_convert_fusion.8), channel_id=1, source_target_pairs={{0,16},{4,20},{8,24},{12,28},{16,0},{20,4},{24,8},{28,12},{1,17},{... | collective-permute-start | bytes 1671176 | tf_op jit(solution)/shard_map/ppermute | solution.py:435
  295.7 22.0 %collective-permute-start.48 = (bf16[272,1024]{1,0:T(8,128)(2,1)}, bf16[272,1024]{1,0:T(8,128)(2,1)}, u32[]{:S(2)}, u32[]{:S(2)}) collective-permute-start(bf16[272,1024]{1,0:T(8,128)(2,1)} %add_convert_fusion.6), channel_id=1, source_target_pairs={{0,8},{4,12},{8,0},{12,4},{16,24},{20,28},{24,16},{28,20},{1,9},{5... | collective-permute-start | bytes 1671176 | tf_op jit(solution)/shard_map/ppermute | solution.py:435
  296.7 23.0 %collective-permute-start.46 = (bf16[272,1024]{1,0:T(8,128)(2,1)}, bf16[272,1024]{1,0:T(8,128)(2,1)}, u32[]{:S(2)}, u32[]{:S(2)}) collective-permute-start(bf16[272,1024]{1,0:T(8,128)(2,1)} %get-tuple-element.292), channel_id=1, source_target_pairs={{0,16},{4,20},{8,24},{12,28},{16,0},{20,4},{24,8},{28,12},{1,17},{... | collective-permute-start | bytes 1671176 | tf_op jit(solution)/shard_map/ppermute | solution.py:435
  309.9 13.2 %collective-permute-start.49 = (bf16[272,1024]{1,0:T(8,128)(2,1)}, bf16[272,1024]{1,0:T(8,128)(2,1)}, u32[]{:S(2)}, u32[]{:S(2)}) collective-permute-start(bf16[272,1024]{1,0:T(8,128)(2,1)} %add_convert_fusion.7), channel_id=1, source_target_pairs={{0,1},{1,0},{2,3},{3,2},{4,5},{5,4},{6,7},{7,6},{8,9},{9,8},{10,11... | collective-permute-start | bytes 1671176 | tf_op jit(solution)/shard_map/ppermute | solution.py:439
  313.2 18.1 %collective-permute-start.54 = (bf16[256,1024]{1,0:T(8,128)(2,1)}, bf16[256,1024]{1,0:T(8,128)(2,1)S(1)}, u32[]{:S(2)}, u32[]{:S(2)}) collective-permute-start(bf16[256,1024]{1,0:T(8,128)(2,1)} %get-tuple-element.317), channel_id=1, source_target_pairs={{0,16},{4,20},{8,24},{12,28},{16,0},{20,4},{24,8},{28,12},{1,17},{... | collective-permute-start | bytes 1572872 | tf_op jit(solution)/shard_map/ppermute | solution.py:435
  317.8 15.5 %collective-permute-start.52 = (bf16[256,1024]{1,0:T(8,128)(2,1)S(1)}, bf16[256,1024]{1,0:T(8,128)(2,1)S(1)}, u32[]{:S(2)}, u32[]{:S(2)}) collective-permute-start(bf16[256,1024]{1,0:T(8,128)(2,1)S(1)} %copy-done.54), channel_id=1, source_target_pairs={{0,8},{4,12},{8,0},{12,4},{16,24},{20,28},{24,16},{28,20},{1,9},{5... | collective-permute-start | bytes 1572872 | tf_op jit(solution)/shard_map/ppermute | solution.py:435
  329.3 32.5 %collective-permute-start.65 = (bf16[512,1152]{1,0:T(8,128)(2,1)}, bf16[512,1152]{1,0:T(8,128)(2,1)}, u32[]{:S(2)}, u32[]{:S(2)}) collective-permute-start(bf16[512,1152]{1,0:T(8,128)(2,1)} %get-tuple-element.330), channel_id=1, source_target_pairs={{0,4},{4,0},{8,12},{12,8},{16,20},{20,16},{24,28},{28,24},{1,5},{5... | collective-permute-start | bytes 3538952 | tf_op jit(solution)/shard_map/ppermute | solution.py:435
  329.3 15.2 %collective-permute-start.50 = (bf16[256,1024]{1,0:T(8,128)(2,1)}, bf16[256,1024]{1,0:T(8,128)(2,1)}, u32[]{:S(2)}, u32[]{:S(2)}) collective-permute-start(bf16[256,1024]{1,0:T(8,128)(2,1)} %get-tuple-element.303), channel_id=1, source_target_pairs={{0,8},{4,12},{8,0},{12,4},{16,24},{20,28},{24,16},{28,20},{1,9},{5... | collective-permute-start | bytes 1572872 | tf_op jit(solution)/shard_map/ppermute | solution.py:435
  330.4 15.1 %collective-permute-start.51 = (bf16[256,1024]{1,0:T(8,128)(2,1)}, bf16[256,1024]{1,0:T(8,128)(2,1)}, u32[]{:S(2)}, u32[]{:S(2)}) collective-permute-start(bf16[256,1024]{1,0:T(8,128)(2,1)} %get-tuple-element.304), channel_id=1, source_target_pairs={{0,16},{4,20},{8,24},{12,28},{16,0},{20,4},{24,8},{28,12},{1,17},{... | collective-permute-start | bytes 1572872 | tf_op jit(solution)/shard_map/ppermute | solution.py:435
  332.3 29.4 %collective-permute-start.55 = (bf16[256,1024]{1,0:T(8,128)(2,1)}, bf16[256,1024]{1,0:T(8,128)(2,1)}, u32[]{:S(2)}, u32[]{:S(2)}) collective-permute-start(bf16[256,1024]{1,0:T(8,128)(2,1)} %add_convert_fusion.12), channel_id=1, source_target_pairs={{0,8},{4,12},{8,0},{12,4},{16,24},{20,28},{24,16},{28,20},{1,9},{5... | collective-permute-start | bytes 1572872 | tf_op jit(solution)/shard_map/ppermute | solution.py:435
  334.3 27.4 %collective-permute-start.53 = (bf16[256,1024]{1,0:T(8,128)(2,1)}, bf16[256,1024]{1,0:T(8,128)(2,1)}, u32[]{:S(2)}, u32[]{:S(2)}) collective-permute-start(bf16[256,1024]{1,0:T(8,128)(2,1)} %add_convert_fusion.13), channel_id=1, source_target_pairs={{0,16},{4,20},{8,24},{12,28},{16,0},{20,4},{24,8},{28,12},{1,17},{... | collective-permute-start | bytes 1572872 | tf_op jit(solution)/shard_map/ppermute | solution.py:435
  335.5 73.1 %all-to-all-start.4 = ((bf16[4,384,1024]{2,1,0:T(8,128)(2,1)}), bf16[4,384,1024]{2,1,0:T(8,128)(2,1)S(1)}, u32[]{:S(2)}, u32[]{:S(2)}) async-start(bf16[4,384,1024]{2,1,0:T(8,128)(2,1)} %add_convert_fusion), calls=%async_computation.4 | async-start | bytes 6291456 | tf_op jit(solution)/shard_map/all_to_all | solution.py:875
  361.8 13.6 %collective-permute-start.57 = (bf16[512,1152]{1,0:T(8,128)(2,1)}, bf16[512,1152]{1,0:T(8,128)(2,1)S(1)}, u32[]{:S(2)}, u32[]{:S(2)}) collective-permute-start(bf16[512,1152]{1,0:T(8,128)(2,1)} %get-tuple-element.324), channel_id=1, source_target_pairs={{0,4},{4,0},{8,12},{12,8},{16,20},{20,16},{24,28},{28,24},{1,5},{5... | collective-permute-start | bytes 3538952 | tf_op jit(solution)/shard_map/ppermute | solution.py:435
  364.3 9.9 %collective-permute-start.67 = (bf16[128,1152]{1,0:T(8,128)(2,1)S(1)}, bf16[128,1152]{1,0:T(8,128)(2,1)S(1)}, u32[]{:S(2)}, u32[]{:S(2)}) collective-permute-start(bf16[128,1152]{1,0:T(8,128)(2,1)S(1)} %get-tuple-element.351), channel_id=1, source_target_pairs={{0,16},{4,20},{8,24},{12,28},{16,0},{20,4},{24,8},{28,12},{1,17},{... | collective-permute-start | bytes 884744 | tf_op jit(solution)/shard_map/ppermute | solution.py:435
  365.2 12.4 %collective-permute-start.61 = (bf16[512,1024]{1,0:T(8,128)(2,1)S(1)}, bf16[512,1024]{1,0:T(8,128)(2,1)S(1)}, u32[]{:S(2)}, u32[]{:S(2)}) collective-permute-start(bf16[512,1024]{1,0:T(8,128)(2,1)S(1)} %copy-done.53), channel_id=1, source_target_pairs={{0,4},{4,0},{8,12},{12,8},{16,20},{20,16},{24,28},{28,24},{1,5},{5... | collective-permute-start | bytes 3145736 | tf_op jit(solution)/shard_map/ppermute | solution.py:435
  367.6 49.7 %collective-permute-start.56 = (bf16[256,1024]{1,0:T(8,128)(2,1)}, bf16[256,1024]{1,0:T(8,128)(2,1)}, u32[]{:S(2)}, u32[]{:S(2)}) collective-permute-start(bf16[256,1024]{1,0:T(8,128)(2,1)} %add_convert_fusion.10), channel_id=1, source_target_pairs={{0,1},{1,0},{2,3},{3,2},{4,5},{5,4},{6,7},{7,6},{8,9},{9,8},{10,11... | collective-permute-start | bytes 1572872 | tf_op jit(solution)/shard_map/ppermute | solution.py:439
  370.3 21.9 %collective-permute-start.66 = (bf16[128,1152]{1,0:T(8,128)(2,1)S(1)}, bf16[128,1152]{1,0:T(8,128)(2,1)S(1)}, u32[]{:S(2)}, u32[]{:S(2)}) collective-permute-start(bf16[128,1152]{1,0:T(8,128)(2,1)S(1)} %get-tuple-element.352), channel_id=1, source_target_pairs={{0,16},{4,20},{8,24},{12,28},{16,0},{20,4},{24,8},{28,12},{1,17},{... | collective-permute-start | bytes 884744 | tf_op jit(solution)/shard_map/ppermute | solution.py:435
  374.3 19.0 %collective-permute-start.68 = (bf16[128,1152]{1,0:T(8,128)(2,1)S(1)}, bf16[128,1152]{1,0:T(8,128)(2,1)S(1)}, u32[]{:S(2)}, u32[]{:S(2)}) collective-permute-start(bf16[128,1152]{1,0:T(8,128)(2,1)S(1)} %add_convert_fusion.14), channel_id=1, source_target_pairs={{0,8},{4,12},{8,0},{12,4},{16,24},{20,28},{24,16},{28,20},{1,9},{5... | collective-permute-start | bytes 884744 | tf_op jit(solution)/shard_map/ppermute | solution.py:435
  376.5 12.2 %collective-permute-start.59 = (bf16[128,1152]{1,0:T(8,128)(2,1)S(1)}, bf16[128,1152]{1,0:T(8,128)(2,1)S(1)}, u32[]{:S(2)}, u32[]{:S(2)}) collective-permute-start(bf16[128,1152]{1,0:T(8,128)(2,1)S(1)} %get-tuple-element.354), channel_id=1, source_target_pairs={{0,8},{4,12},{8,0},{12,4},{16,24},{20,28},{24,16},{28,20},{1,9},{5... | collective-permute-start | bytes 884744 | tf_op jit(solution)/shard_map/ppermute | solution.py:435
  378.8 11.7 %collective-permute-start.63 = (bf16[128,1024]{1,0:T(8,128)(2,1)S(1)}, bf16[128,1024]{1,0:T(8,128)(2,1)S(1)}, u32[]{:S(2)}, u32[]{:S(2)}) collective-permute-start(bf16[128,1024]{1,0:T(8,128)(2,1)S(1)} %get-tuple-element.357), channel_id=1, source_target_pairs={{0,16},{4,20},{8,24},{12,28},{16,0},{20,4},{24,8},{28,12},{1,17},{... | collective-permute-start | bytes 786440 | tf_op jit(solution)/shard_map/ppermute | solution.py:435
  388.7 19.9 %collective-permute-start.58 = (bf16[128,1152]{1,0:T(8,128)(2,1)S(1)}, bf16[128,1152]{1,0:T(8,128)(2,1)}, u32[]{:S(2)}, u32[]{:S(2)}) collective-permute-start(bf16[128,1152]{1,0:T(8,128)(2,1)S(1)} %get-tuple-element.355), channel_id=1, source_target_pairs={{0,8},{4,12},{8,0},{12,4},{16,24},{20,28},{24,16},{28,20},{1,9},{5... | collective-permute-start | bytes 884744 | tf_op jit(solution)/shard_map/ppermute | solution.py:435
  390.5 18.1 %collective-permute-start.60 = (bf16[128,1152]{1,0:T(8,128)(2,1)}, bf16[128,1152]{1,0:T(8,128)(2,1)}, u32[]{:S(2)}, u32[]{:S(2)}) collective-permute-start(bf16[128,1152]{1,0:T(8,128)(2,1)} %add_convert_fusion.15), channel_id=1, source_target_pairs={{0,16},{4,20},{8,24},{12,28},{16,0},{20,4},{24,8},{28,12},{1,17},{... | collective-permute-start | bytes 884744 | tf_op jit(solution)/shard_map/ppermute | solution.py:435
  392.1 16.5 %collective-permute-start.62 = (bf16[128,1024]{1,0:T(8,128)(2,1)}, bf16[128,1024]{1,0:T(8,128)(2,1)}, u32[]{:S(2)}, u32[]{:S(2)}) collective-permute-start(bf16[128,1024]{1,0:T(8,128)(2,1)} %get-tuple-element.358), channel_id=1, source_target_pairs={{0,16},{4,20},{8,24},{12,28},{16,0},{20,4},{24,8},{28,12},{1,17},{... | collective-permute-start | bytes 786440 | tf_op jit(solution)/shard_map/ppermute | solution.py:435
  394.0 14.6 %collective-permute-start.64 = (bf16[128,1024]{1,0:T(8,128)(2,1)}, bf16[128,1024]{1,0:T(8,128)(2,1)}, u32[]{:S(2)}, u32[]{:S(2)}) collective-permute-start(bf16[128,1024]{1,0:T(8,128)(2,1)} %add_convert_fusion.16), channel_id=1, source_target_pairs={{0,8},{4,12},{8,0},{12,4},{16,24},{20,28},{24,16},{28,20},{1,9},{5... | collective-permute-start | bytes 786440 | tf_op jit(solution)/shard_map/ppermute | solution.py:435
  412.5 10.6 %collective-permute-start.69 = (bf16[32,3328]{1,0:T(8,128)(2,1)}, bf16[32,3328]{1,0:T(8,128)(2,1)S(1)}, u32[]{:S(2)}, u32[]{:S(2)}) collective-permute-start(bf16[32,3328]{1,0:T(8,128)(2,1)} %get-tuple-element.332), channel_id=1, source_target_pairs={{0,1},{1,0},{2,3},{3,2},{4,5},{5,4},{6,7},{7,6},{8,9},{9,8},{10,11... | collective-permute-start | bytes 638984 | tf_op jit(solution)/shard_map/ppermute | solution.py:439
  415.8 15.1 %collective-permute-start.70 = (bf16[32,3328]{1,0:T(8,128)(2,1)}, bf16[32,3328]{1,0:T(8,128)(2,1)}, u32[]{:S(2)}, u32[]{:S(2)}) collective-permute-start(bf16[32,3328]{1,0:T(8,128)(2,1)} %get-tuple-element.333), channel_id=1, source_target_pairs={{0,2},{1,3},{2,0},{3,1},{4,6},{5,7},{6,4},{7,5},{8,10},{9,11},{10,... | collective-permute-start | bytes 638984 | tf_op jit(solution)/shard_map/ppermute | solution.py:439
  415.9 19.8 %collective-permute-start.71 = (bf16[32,3328]{1,0:T(8,128)(2,1)}, bf16[32,3328]{1,0:T(8,128)(2,1)}, u32[]{:S(2)}, u32[]{:S(2)}) collective-permute-start(bf16[32,3328]{1,0:T(8,128)(2,1)} %get-tuple-element.334), channel_id=1, source_target_pairs={{0,3},{1,2},{2,1},{3,0},{4,7},{5,6},{6,5},{7,4},{8,11},{9,10},{10,... | collective-permute-start | bytes 638984 | tf_op jit(solution)/shard_map/ppermute | solution.py:439
  (68 other events, 623.8 us)

commit v5 on v4

--- a/solution.py
+++ b/solution.py
@@ -737,12 +737,13 @@
     pay_ref[256:288, :] = jnp.concatenate([rows(code), high, middle_part, low], axis=1).astype(BF16)
 
 
-def turn_body(e_ref, sum_ref, add_ref, grad_ref, middle_ref, gates_ref, small_ref, normed2_ref, mixed_ref,
+def turn_body(e_ref, sum_ref, mine_ref, other_ref, add_ref, grad_ref, middle_ref, gates_ref, small_ref, normed2_ref, mixed_ref,
               *refs):
     w_refs, (own_ref, far_ref, mixed_grad_ref, middle_grad_ref, side_ref) = (refs[0:4], refs[4:8]), refs[8:]
     e = e_ref[0]
-    upstream = sum_ref[0:256, :].astype(F32) + add_ref[0:256, :].astype(F32)
-    table = sum_ref[256:272, :].astype(F32) + add_ref[256:272, :].astype(F32)
+    addends = (sum_ref, mine_ref, other_ref, add_ref)
+    upstream = sum(ref[0:256, :].astype(F32) for ref in addends)
+    table = sum(ref[256:272, :].astype(F32) for ref in addends)
     dots = jnp.concatenate([table[:, :256], table[:, 256:512]], axis=0) + jnp.concatenate(
         [table[:, 512:768], table[:, 768:]], axis=0
     )
@@ -998,13 +999,15 @@
     plane = xor_order([pack] + [over_shard(pack, k) for k in (1, 2, 3)], z)
     out_pair = over_shard(grad_early, 1)
     out_x, out_y = over_x(grad_early), over_y(grad_early)
-    slices = [expert_slices(w, 0) for w in (expert_in, expert_out)]
-    second = jnp.concatenate([expert_slices(w, 1) for w in (expert_in, expert_out)], axis=1)
+    slices = [
+        jnp.concatenate([expert_slices(w, part) for w in (expert_in, expert_out)], axis=1)
+        for part in range(OWN)
+    ]
     plane, out_x, out_y, slices[0] = together(plane, out_x, out_y, slices[0])
     left = spread(plane[:, :1152], over_x, over_y)
     right = spread(plane[:, 1152:2176], over_y, over_x)
     slices[0], out_pair, left[1], right[2] = together(slices[0], out_pair, left[1], right[2])
-    in0 = exchange(slices[0])
+    weights0 = exchange(slices[0])
     swap = lambda values: [over_expert(value, 1) for value in values]
     left_far, right_far = swap(left), swap(right)
     left[3], right[3], plane, out_pair, out_x = together(left[3], right[3], plane, out_pair, out_x)
@@ -1037,15 +1040,14 @@
     pay_pair = over_shard(payload, 1)
     pay_x, pay_y = over_x(payload), over_y(payload)
     pay_x, pay_y, pay_pair, *out_blocks = together(pay_x, pay_y, pay_pair, *out_blocks)
-    slices[1], in0, pay_pair = together(slices[1], in0, pay_pair)
-    out0 = exchange(slices[1])
+    slices[1], weights0, pay_pair = together(slices[1], weights0, pay_pair)
+    weights1 = [exchange(slices[1])]
     out_blocks.append(over_x(out_blocks[6]))
     tok_own = [payload, pay_x, pay_y, over_y(pay_x)]
     tok_pair = [pay_pair, over_x(pay_pair), over_y(pay_pair)]
-    *tok_pair, out_blocks[7], out0, second = together(*tok_pair, out_blocks[7], out0, second)
+    tok_pair[2], out_blocks[7] = together(tok_pair[2], out_blocks[7])
     tok_pair.append(over_x(tok_pair[2]))
-    weights0 = [in0, out0]
-    weights1 = [exchange(second)]
+    weights0 = [weights0]
     weights0_far = swap(weights0)
     tokens = tok_own + tok_pair
     first = (e * 4 + z % PAIR * OWN).reshape(1)
@@ -1075,30 +1077,31 @@
     moe_mine, moe_own_mine = over_x(moes[5]), over_y(moes[2])
     owned = owner_sum(0, slices0)
     own_other, *owned = together(own_other, *owned)
-    row_own = bf_sum(own[0], own_mine, own_other)
-    returned, expert_grad1, slices0 = together(returned, expert_grad1, slices0)
+    own_other, expert_grad1 = together(own_other, expert_grad1)
     slices1 = exchange(expert_grad1)
     early_own, early_far, mixed_grad, middle_grad = local_kernel(
         turn_body, "turn", [((512, 1152), BF16), ((512, 1152), BF16), (wide, BF16), (wide, F32)],
-        [((1024, LANES), F32)], place, row_own, returned, cotangent, middle, gates,
+        [((1024, LANES), F32)], place, own[0], own_mine, own_other, returned, cotangent, middle, gates,
         small_all, payload, mixed, *out_w,
     )
-    middle_grad, moe_mine, moe_own_mine = together(middle_grad, moe_mine, moe_own_mine)
     moe_rest, moe_own_rest = over_y(bf_sum(moes[6], moe_pass)), over_x(bf_sum(moes[1], moe_own_pass))
     left_own, left_far, right_own, right_far, grad_embedded = local_kernel(
         attend_back_body, "attend_back", [((512, 1152), BF16)] * 2 + [((512, 1024), BF16)] * 2 + [(wide, BF16)],
         [((SEQUENCE, 2048), BF16), (wide, F32)], place, embedded, column, row, cosine, sine,
         queries, keys, values, mixed_grad, normed, middle_grad, *weights,
     )
-    left_far, right_far, moe_rest, moe_own_rest = together(left_far, right_far, moe_rest, moe_own_rest)
+    left_far, right_far, moe_rest, moe_own_rest, moe_mine, moe_own_mine = together(
+        left_far, right_far, moe_rest, moe_own_rest, moe_mine, moe_own_mine
+    )
     moe_pair = bf_sum(moes[4], moe_mine, moe_rest)
     moe_own = bf_sum(moes[0], moe_own_mine, moe_own_rest)
     moe_other = over_shard(moe_pair, 1)
     addends = plane_fold(core_sum(left_own, left_far), over_x, over_y)
     addends += plane_fold(core_sum(right_own, right_far), over_y, over_x)
     addends += plane_fold(core_sum(early_own, early_far), over_y, over_x)
-    addends[0], slices1 = together(addends[0], slices1)
     planes = local_kernel(plane_body, "plane", [((32, 3328), BF16)] * 4, [], z.reshape(1), *addends)
+    planes = list(planes)
+    planes[3], slices1 = together(planes[3], slices1)
     planes = [planes[0]] + [over_shard(planes[k], k) for k in (1, 2, 3)]
     shapes = [(32, 1024), (32, 512), (32, 512), (32, 1024), (32, EXPERTS), (1, 32), (1, 32)]
     late_query, late_key, late_value, early_out, router, gain_attn, gain_ffn = local_kernel(

time: 447 us -> 436 us (0.975)
  the two profiles are of different devices: /device:TPU:8 before, /device:TPU:0 now
where the time goes in v5:
time: 436 us; the launch traced here: 428 us
  Pallas kernels  147 us (34%)
  waiting for transfers between devices  140 us (32%)
  starting transfers between devices  84.8 us (19%)
  other arithmetic  38.5 us (9%)
  local copies, waits for them, and re-layouts  15.3 us (4%)
    ppermute x61, waiting for transfers between devices, over_expert(): return lax.ppermute(value, 'expert', [(i, i ^ bits) for i in range(8)])  105 us
    pallas_call x4, Pallas kernels, expert_call(): pl.pallas_call(functools.partial(expert_body, before is None, len(weights...  97.2 us
    ppermute x61, starting transfers between devices, over_expert(): return lax.ppermute(value, 'expert', [(i, i ^ bits) for i in range(8)])  49.8 us
    pallas_call x6, Pallas kernels, local_kernel(): pl.pallas_call(body, out_shape=[jax.ShapeDtypeStruct(shape, dtype) for sh...  41.8 us
    all_to_all x4, starting transfers between devices, exchange(): lax.all_to_all(slices, 'shard', split_axis=0, concat_axis=0, tiled=True)  18.3 us
    all_to_all x4, waiting for transfers between devices, exchange(): lax.all_to_all(slices, 'shard', split_axis=0, concat_axis=0, tiled=True)  17.9 us
    ppermute x10, waiting for transfers between devices, over_shard(): return lax.ppermute(value, 'shard', [(i, i ^ bits) for i in range(4)])  17.7 us
    ppermute x10, starting transfers between devices, over_shard(): return lax.ppermute(value, 'shard', [(i, i ^ bits) for i in range(4)])  16.7 us
  transfers between devices with their start and end apart: 75, of which 25 were waited for; matrix products, arithmetic and copies ran while one was open for 11% of the time, Pallas kernels for 33%

profile of v5, /device:TPU:0, one launch (start us, length us, event | category | flops | bytes accessed | tf_op | source)
XLA Modules:
  0.0 428.4 jit_solution(8926821071586009772)
XLA Ops:
  0.7 1.9 pack.1
  2.6 3.1 collective-permute-start
  5.6 2.6 collective-permute-start.1
  8.2 1.7 collective-permute-start.3
  9.9 1.5 collective-permute-start.4
  11.5 2.6 fusion.3
  15.0 1.8 maximum_maximum_fusion
  17.5 6.0 %collective-permute-done.1 = bf16[32,3200]{1,0:T(8,128)(2,1)S(1)} collective-permute-done((bf16[32,3200]{1,0:T(8,128)(2,1)}, bf16[32,3200]{1,0:T(8,128)(2,1)S(1)}, u32[]{:S(2)}, u32[]{:S(2)}) %collective-permute-start.1) | collective-permute-done | bytes 204832 | tf_op jit(solution)/shard_map/ppermute | solution.py:439
  23.9 1.6 collective-permute-start.5
  25.5 1.6 collective-permute-start.7
  27.1 6.5 %collective-permute-done.9.refs_12_ = bf16[256,1024]{1,0:T(8,128)(2,1)S(1)} collective-permute-done((bf16[256,1024]{1,0:T(8,128)(2,1)S(1)}, bf16[256,1024]{1,0:T(8,128)(2,1)S(1)}, u32[]{:S(2)}, u32[]{:S(2)}) %collective-permute-start.9) | collective-permute-done | bytes 524320 | tf_op jit(solution)/shard_map/ppermute | solution.py:439
  35.2 3.7 all-to-all-start
  43.0 5.5 %collective-permute-done.18.refs_9_ = bf16[128,1024]{1,0:T(8,128)(2,1)} collective-permute-done((bf16[128,1024]{1,0:T(8,128)(2,1)}, bf16[128,1024]{1,0:T(8,128)(2,1)}, u32[]{:S(2)}, u32[]{:S(2)}) %collective-permute-start.18) | collective-permute-done | bytes 262176 | tf_op jit(solution)/shard_map/ppermute | solution.py:435
  48.4 1.5 collective-permute-start.6
  52.7 2.8 collective-permute-done.6.refs_3_
  55.6 1.7 slice.101.refs_0_
  60.8 1.5 collective-permute-start.30
  65.1 2.5 pad_maximum_fusion.2
  67.6 9.7 %attend.1 = (bf16[256,1024]{1,0:T(8,128)(2,1)}, bf16[256,1024]{1,0:T(8,128)(2,1)}, bf16[256,512]{1,0:T(8,128)(2,1)}, bf16[256,512]{1,0:T(8,128)(2,1)}, bf16[256,...) custom-call(s32[1]{0:T(128)} %bitcast.e_ref, bf16[256,1024]{1,0:T(8,128)(2,1)} %x_ref.5, s32[256,1]{1,0:T(8,128)} %copy.30.column_ref, ...), custom_call_target="tpu_custom_call" | custom-call | flops 1000 | bytes 1000 | tf_op jit(solution)/shard_map/attend/pallas_call | solution.py:848
  81.2 4.5 %route.1 = (bf16[288,1024]{1,0:T(8,128)(2,1)}, f32[256,128]{1,0:T(8,128)}, f32[256,1024]{1,0:T(8,128)}) custom-call(s32[1]{0:T(128)} %bitcast.e_ref, bf16[256,1024]{1,0:T(8,128)(2,1)} %x_ref.5, bf16[256,1024]{1,0:T(8,128)(2,1)} %get-tuple-element.186.mixed_ref, bf16[1024,128]{1,0:T(8,128)(2,1)} %get-tuple-element.187.small_ref, ...), custom_call_target="tpu_custom_call" | custom-call | flops 1000 | bytes 1000 | tf_op jit(solution)/shard_map/route/pallas_call | solution.py:848
  87.4 2.0 collective-permute-start.29
  90.1 1.6 collective-permute-start.32
  91.7 1.8 maximum_maximum_fusion.1
  93.6 19.1 %collective-permute-done.31.refs_13_ = bf16[256,1024]{1,0:T(8,128)(2,1)S(1)} collective-permute-done((bf16[256,1024]{1,0:T(8,128)(2,1)S(1)}, bf16[256,1024]{1,0:T(8,128)(2,1)S(1)}, u32[]{:S(2)}, u32[]{:S(2)}) %collective-permute-start.31) | collective-permute-done | bytes 524320 | tf_op jit(solution)/shard_map/ppermute | solution.py:435
  115.2 3.7 collective-permute-done.29.refs_4_
  121.3 5.3 %all-to-all-start.1 = ((bf16[4,384,1024]{2,1,0:T(8,128)(2,1)}), bf16[4,384,1024]{2,1,0:T(8,128)(2,1)}, u32[]{:S(2)}, u32[]{:S(2)}) async-start(bf16[4,384,1024]{2,1,0:T(8,128)(2,1)} %maximum_maximum_fusion.1), calls=%async_computation.1 | async-start | bytes 6291456 | tf_op jit(solution)/shard_map/all_to_all | solution.py:876
  128.5 6.9 %collective-permute-done.36.refs_15_ = bf16[256,1024]{1,0:T(8,128)(2,1)} collective-permute-done((bf16[256,1024]{1,0:T(8,128)(2,1)}, bf16[256,1024]{1,0:T(8,128)(2,1)}, u32[]{:S(2)}, u32[]{:S(2)}) %collective-permute-start.36) | collective-permute-done | bytes 524320 | tf_op jit(solution)/shard_map/ppermute | solution.py:435
  136.4 11.3 %collective-permute-done.33.refs_3_ = bf16[288,1024]{1,0:T(8,128)(2,1)} collective-permute-done((bf16[288,1024]{1,0:T(8,128)(2,1)}, bf16[288,1024]{1,0:T(8,128)(2,1)}, u32[]{:S(2)}, u32[]{:S(2)}) %collective-permute-start.33) | collective-permute-done | bytes 589856 | tf_op jit(solution)/shard_map/ppermute | solution.py:435
  148.0 11.8 %collective-permute-done.37.refs_7_ = bf16[288,1024]{1,0:T(8,128)(2,1)} collective-permute-done((bf16[288,1024]{1,0:T(8,128)(2,1)}, bf16[288,1024]{1,0:T(8,128)(2,1)}, u32[]{:S(2)}, u32[]{:S(2)}) %collective-permute-start.37) | collective-permute-done | bytes 589856 | tf_op jit(solution)/shard_map/ppermute | solution.py:435
  159.8 22.0 %expert.4 = (bf16[272,1024]{1,0:T(8,128)(2,1)}, bf16[272,1024]{1,0:T(8,128)(2,1)}, bf16[272,1024]{1,0:T(8,128)(2,1)}, bf16[272,1024]{1,0:T(8,128)(2,1)}, bf16[27...) custom-call(s32[1]{0:T(128)} %bitcast.15.number_ref, ...), custom_call_target="tpu_custom_call" | custom-call | flops 1000 | bytes 1000 | tf_op jit(solution)/shard_map/expert/pallas_call | solution.py:592
  182.0 24.9 %expert.5 = (bf16[272,1024]{1,0:T(8,128)(2,1)}, bf16[272,1024]{1,0:T(8,128)(2,1)}, bf16[272,1024]{1,0:T(8,128)(2,1)}, bf16[272,1024]{1,0:T(8,128)(2,1)}, bf16[27...) custom-call(s32[1]{0:T(128)} %bitcast.14.number_ref, ...), custom_call_target="tpu_custom_call" | custom-call | flops 1000 | bytes 1000 | tf_op jit(solution)/shard_map/expert/pallas_call | solution.py:592
  206.9 5.1 %add_convert_fusion.1 = bf16[4,384,1024]{2,1,0:T(8,128)(2,1)} fusion(bf16[4,384,1024]{2,1,0:T(8,128)(2,1)S(1)} %collective-permute-done.39, bf16[4,384,1024]{2,1,0:T(8,128)(2,1)} %get-tuple-element.228), kind=kLoop, calls=%fused_computation.1 | loop fusion | flops 6291456 | bytes 9437184 | tf_op jit(solution)/shard_map/convert_element_type | solution.py:865
  212.4 5.6 %all-to-all-start.2 = ((bf16[4,384,1024]{2,1,0:T(8,128)(2,1)}), bf16[4,384,1024]{2,1,0:T(8,128)(2,1)S(1)}, u32[]{:S(2)}, u32[]{:S(2)}) async-start(bf16[4,384,1024]{2,1,0:T(8,128)(2,1)} %add_convert_fusion.1), calls=%async_computation.2 | async-start | bytes 6291456 | tf_op jit(solution)/shard_map/all_to_all | solution.py:876
  218.1 25.1 %expert.6 = (bf16[272,1024]{1,0:T(8,128)(2,1)}, bf16[272,1024]{1,0:T(8,128)(2,1)}, bf16[272,1024]{1,0:T(8,128)(2,1)}, bf16[272,1024]{1,0:T(8,128)(2,1)}, bf16[27...) custom-call(s32[1]{0:T(128)S(6)} %add.100.number_ref, ...), custom_call_target="tpu_custom_call" | custom-call | flops 1000 | bytes 1000 | tf_op jit(solution)/shard_map/expert/pallas_call | solution.py:592
  243.6 25.0 %expert.7 = (bf16[272,1024]{1,0:T(8,128)(2,1)}, bf16[272,1024]{1,0:T(8,128)(2,1)}, bf16[272,1024]{1,0:T(8,128)(2,1)}, bf16[272,1024]{1,0:T(8,128)(2,1)}, bf16[27...) custom-call(s32[1]{0:T(128)S(6)} %add.97.number_ref, ...), custom_call_target="tpu_custom_call" | custom-call | flops 1000 | bytes 1000 | tf_op jit(solution)/shard_map/expert/pallas_call | solution.py:592
  271.6 6.1 %add_convert_fusion = bf16[4,384,1024]{2,1,0:T(8,128)(2,1)} fusion(bf16[4,384,1024]{2,1,0:T(8,128)(2,1)} %collective-permute-done.43, bf16[4,384,1024]{2,1,0:T(8,128)(2,1)} %get-tuple-element.268), kind=kLoop, calls=%fused_computation | loop fusion | flops 6291456 | bytes 9437184 | tf_op jit(solution)/shard_map/convert_element_type | solution.py:865
  277.7 6.9 %collective-permute-done.42 = bf16[272,1024]{1,0:T(8,128)(2,1)} collective-permute-done((bf16[272,1024]{1,0:T(8,128)(2,1)}, bf16[272,1024]{1,0:T(8,128)(2,1)}, u32[]{:S(2)}, u32[]{:S(2)}) %collective-permute-start.42) | collective-permute-done | bytes 557088 | tf_op jit(solution)/shard_map/ppermute | solution.py:435
  284.6 4.3 %all-to-all-done.2.one_ref.two_ref = bf16[4,384,1024]{2,1,0:T(8,128)(2,1)S(1)} async-done(((bf16[4,384,1024]{2,1,0:T(8,128)(2,1)}), bf16[4,384,1024]{2,1,0:T(8,128)(2,1)S(1)}, u32[]{:S(2)}, u32[]{:S(2)}) %all-to-all-start.2) | async-done | bytes 3145760 | tf_op jit(solution)/shard_map/all_to_all | solution.py:876
  288.9 2.3 add_convert_fusion.7
  292.1 2.3 add_convert_fusion.5
  296.6 10.2 %collective-permute-done.44 = bf16[272,1024]{1,0:T(8,128)(2,1)S(1)} collective-permute-done((bf16[272,1024]{1,0:T(8,128)(2,1)S(1)}, bf16[272,1024]{1,0:T(8,128)(2,1)S(1)}, u32[]{:S(2)}, u32[]{:S(2)}) %collective-permute-start.44) | collective-permute-done | bytes 557088 | tf_op jit(solution)/shard_map/ppermute | solution.py:435
  306.8 2.2 add_convert_fusion.6
  310.5 3.3 owner_sum.2
  313.9 5.0 %collective-permute-done.45.mine_ref = bf16[272,1024]{1,0:T(8,128)(2,1)} collective-permute-done((bf16[272,1024]{1,0:T(8,128)(2,1)}, bf16[272,1024]{1,0:T(8,128)(2,1)}, u32[]{:S(2)}, u32[]{:S(2)}) %collective-permute-start.45) | collective-permute-done | bytes 557088 | tf_op jit(solution)/shard_map/ppermute | solution.py:435
  320.3 6.6 %turn.1 = (bf16[512,1152]{1,0:T(8,128)(2,1)}, bf16[512,1152]{1,0:T(8,128)(2,1)}, bf16[256,1024]{1,0:T(8,128)(2,1)}, f32[256,1024]{1,0:T(8,128)}) custom-call(s32[1]{0:T(128)} %bitcast.e_ref, bf16[272,1024]{1,0:T(8,128)(2,1)} %get-tuple-element.284.sum_ref, bf16[272,1024]{1,0:T(8,128)(2,1)} %collective-permute-done.45.mine_ref, ...), custom_call_target="tpu_custom_call" | custom-call | flops 1000 | bytes 1000 | tf_op jit(solution)/shard_map/turn/pallas_call | solution.py:848
  328.6 2.1 add_convert_fusion.11
  331.9 2.0 add_convert_fusion.12
  335.2 3.7 all-to-all-start.3
  338.9 16.2 %attend_back.1 = (bf16[512,1152]{1,0:T(8,128)(2,1)}, bf16[512,1152]{1,0:T(8,128)(2,1)}, bf16[512,1024]{1,0:T(8,128)(2,1)}, bf16[512,1024]{1,0:T(8,128)(2,1)}, bf16[256,1024]{1,0:T(8,128)(2,1)}) custom-call(s32[1]{0:T(128)} %bitcast.e_ref, bf16[256,1024]{1,0:T(8,128)(2,1)} %x_ref.5, s32[256,1]{1,0:T(8,128)} %copy.30.column_ref, s32[1,256]{1,0:T(1,128)} %row_ref.3, ...), custom_call_target="tpu_custom_call" | custom-call | flops 1000 | bytes 1000 | tf_op jit(solution)/shard_map/attend_back/pallas_call | solution.py:848
  355.3 1.6 add_convert_fusion.2
  358.6 2.3 add_convert_fusion.9
  360.9 1.9 collective-permute-start.55
  364.1 3.5 collective-permute-done.66
  372.9 9.0 %collective-permute-done.58 = bf16[128,1152]{1,0:T(8,128)(2,1)S(1)} collective-permute-done((bf16[128,1152]{1,0:T(8,128)(2,1)S(1)}, bf16[128,1152]{1,0:T(8,128)(2,1)S(1)}, u32[]{:S(2)}, u32[]{:S(2)}) %collective-permute-start.58) | collective-permute-done | bytes 294944 | tf_op jit(solution)/shard_map/ppermute | solution.py:435
  383.8 1.5 collective-permute-start.61
  386.3 9.2 %collective-permute-done.61.refs_4_ = bf16[128,1024]{1,0:T(8,128)(2,1)S(1)} collective-permute-done((bf16[128,1024]{1,0:T(8,128)(2,1)S(1)}, bf16[128,1024]{1,0:T(8,128)(2,1)S(1)}, u32[]{:S(2)}, u32[]{:S(2)}) %collective-permute-start.61) | collective-permute-done | bytes 262176 | tf_op jit(solution)/shard_map/ppermute | solution.py:435
  396.6 2.7 plane.1
  399.3 1.8 collective-permute-start.68
  401.1 2.5 collective-permute-start.69
  403.6 13.5 %all-to-all-done.3.one_ref.two_ref = bf16[4,384,1024]{2,1,0:T(8,128)(2,1)S(1)} async-done(((bf16[4,384,1024]{2,1,0:T(8,128)(2,1)}), bf16[4,384,1024]{2,1,0:T(8,128)(2,1)S(1)}, u32[]{:S(2)}, u32[]{:S(2)}) %all-to-all-start.3) | async-done | bytes 3145760 | tf_op jit(solution)/shard_map/all_to_all | solution.py:876
  417.1 2.1 collective-permute-start.70
  419.3 3.1 add_convert_fusion.8
  422.3 3.1 owner_sum.3
  426.2 2.0 settle.1
  (231 shorter events, 58.1 us)
Async XLA Ops:
  2.6 14.2 %collective-permute-start = (bf16[32,3200]{1,0:T(8,128)(2,1)}, bf16[32,3200]{1,0:T(8,128)(2,1)S(1)}, u32[]{:S(2)}, u32[]{:S(2)}) collective-permute-start(bf16[32,3200]{1,0:T(8,128)(2,1)} %pack.1), channel_id=1, source_target_pairs={{0,1},{1,0},{2,3},{3,2},{4,5},{5,4},{6,7},{7,6},{8,9},{9,8},{10,11... | collective-permute-start | bytes 614408 | tf_op jit(solution)/shard_map/ppermute | solution.py:439
  5.6 17.9 %collective-permute-start.1 = (bf16[32,3200]{1,0:T(8,128)(2,1)}, bf16[32,3200]{1,0:T(8,128)(2,1)S(1)}, u32[]{:S(2)}, u32[]{:S(2)}) collective-permute-start(bf16[32,3200]{1,0:T(8,128)(2,1)} %pack.1), channel_id=1, source_target_pairs={{0,2},{1,3},{2,0},{3,1},{4,6},{5,7},{6,4},{7,5},{8,10},{9,11},{10,... | collective-permute-start | bytes 614408 | tf_op jit(solution)/shard_map/ppermute | solution.py:439
  8.2 15.3 %collective-permute-start.2 = (bf16[32,3200]{1,0:T(8,128)(2,1)}, bf16[32,3200]{1,0:T(8,128)(2,1)S(1)}, u32[]{:S(2)}, u32[]{:S(2)}) collective-permute-start(bf16[32,3200]{1,0:T(8,128)(2,1)} %pack.1), channel_id=1, source_target_pairs={{0,3},{1,2},{2,1},{3,0},{4,7},{5,6},{6,5},{7,4},{8,11},{9,10},{10,... | collective-permute-start | bytes 614408 | tf_op jit(solution)/shard_map/ppermute | solution.py:439
  8.2 15.6 %collective-permute-start.3 = (bf16[256,1024]{1,0:T(8,128)(2,1)}, bf16[256,1024]{1,0:T(8,128)(2,1)S(1)}, u32[]{:S(2)}, u32[]{:S(2)}) collective-permute-start(bf16[256,1024]{1,0:T(8,128)(2,1)} %grad_ref.1), channel_id=1, source_target_pairs={{0,8},{4,12},{8,0},{12,4},{16,24},{20,28},{24,16},{28,20},{1,9},{5... | collective-permute-start | bytes 1572872 | tf_op jit(solution)/shard_map/ppermute | solution.py:435
  9.9 13.9 %collective-permute-start.4 = (bf16[256,1024]{1,0:T(8,128)(2,1)}, bf16[256,1024]{1,0:T(8,128)(2,1)S(1)}, u32[]{:S(2)}, u32[]{:S(2)}) collective-permute-start(bf16[256,1024]{1,0:T(8,128)(2,1)} %grad_ref.1), channel_id=1, source_target_pairs={{0,16},{4,20},{8,24},{12,28},{16,0},{20,4},{24,8},{28,12},{1,17},{... | collective-permute-start | bytes 1572872 | tf_op jit(solution)/shard_map/ppermute | solution.py:435
  16.8 16.7 %collective-permute-start.9 = (bf16[256,1024]{1,0:T(8,128)(2,1)S(1)}, bf16[256,1024]{1,0:T(8,128)(2,1)S(1)}, u32[]{:S(2)}, u32[]{:S(2)}) collective-permute-start(bf16[256,1024]{1,0:T(8,128)(2,1)S(1)} %copy-done.2), channel_id=1, source_target_pairs={{0,1},{1,0},{2,3},{3,2},{4,5},{5,4},{6,7},{7,6},{8,9},{9,8},{10,11... | collective-permute-start | bytes 1572872 | tf_op jit(solution)/shard_map/ppermute | solution.py:439
  23.9 10.5 %collective-permute-start.5 = (bf16[128,1152]{1,0:T(8,128)(2,1)S(1)}, bf16[128,1152]{1,0:T(8,128)(2,1)S(1)}, u32[]{:S(2)}, u32[]{:S(2)}) collective-permute-start(bf16[128,1152]{1,0:T(8,128)(2,1)S(1)} %slice.99.refs_0_), channel_id=1, source_target_pairs={{0,8},{4,12},{8,0},{12,4},{16,24},{20,28},{24,16},{28,20},{1,9},{5... | collective-permute-start | bytes 884744 | tf_op jit(solution)/shard_map/ppermute | solution.py:435
  25.5 8.9 %collective-permute-start.7 = (bf16[128,1024]{1,0:T(8,128)(2,1)S(1)}, bf16[128,1024]{1,0:T(8,128)(2,1)S(1)}, u32[]{:S(2)}, u32[]{:S(2)}) collective-permute-start(bf16[128,1024]{1,0:T(8,128)(2,1)S(1)} %slice.100.refs_8_), channel_id=1, source_target_pairs={{0,16},{4,20},{8,24},{12,28},{16,0},{20,4},{24,8},{28,12},{1,17},{... | collective-permute-start | bytes 786440 | tf_op jit(solution)/shard_map/ppermute | solution.py:435
  35.2 83.7 %all-to-all-start = ((bf16[4,384,1024]{2,1,0:T(8,128)(2,1)}), bf16[4,384,1024]{2,1,0:T(8,128)(2,1)S(1)}, u32[]{:S(2)}, u32[]{:S(2)}) async-start(bf16[4,384,1024]{2,1,0:T(8,128)(2,1)} %maximum_maximum_fusion), calls=%async_computation | async-start | bytes 6291456 | tf_op jit(solution)/shard_map/all_to_all | solution.py:876
  38.9 9.5 %collective-permute-start.18 = (bf16[128,1024]{1,0:T(8,128)(2,1)}, bf16[128,1024]{1,0:T(8,128)(2,1)}, u32[]{:S(2)}, u32[]{:S(2)}) collective-permute-start(bf16[128,1024]{1,0:T(8,128)(2,1)} %copy-done.14), channel_id=1, source_target_pairs={{0,8},{4,12},{8,0},{12,4},{16,24},{20,28},{24,16},{28,20},{1,9},{5... | collective-permute-start | bytes 786440 | tf_op jit(solution)/shard_map/ppermute | solution.py:435
  40.3 10.5 %collective-permute-start.13 = (bf16[128,1152]{1,0:T(8,128)(2,1)S(1)}, bf16[128,1152]{1,0:T(8,128)(2,1)}, u32[]{:S(2)}, u32[]{:S(2)}) collective-permute-start(bf16[128,1152]{1,0:T(8,128)(2,1)S(1)} %slice.99.refs_0_), channel_id=1, source_target_pairs={{0,16},{4,20},{8,24},{12,28},{16,0},{20,4},{24,8},{28,12},{1,17},{... | collective-permute-start | bytes 884744 | tf_op jit(solution)/shard_map/ppermute | solution.py:435
  41.5 9.8 %collective-permute-start.14 = (bf16[128,1152]{1,0:T(8,128)(2,1)S(1)}, bf16[128,1152]{1,0:T(8,128)(2,1)}, u32[]{:S(2)}, u32[]{:S(2)}) collective-permute-start(bf16[128,1152]{1,0:T(8,128)(2,1)S(1)} %slice.99.refs_0_), channel_id=1, source_target_pairs={{0,4},{4,0},{8,12},{12,8},{16,20},{20,16},{24,28},{28,24},{1,5},{5... | collective-permute-start | bytes 884744 | tf_op jit(solution)/shard_map/ppermute | solution.py:435
  41.5 9.2 %collective-permute-start.19 = (bf16[128,1024]{1,0:T(8,128)(2,1)}, bf16[128,1024]{1,0:T(8,128)(2,1)}, u32[]{:S(2)}, u32[]{:S(2)}) collective-permute-start(bf16[128,1024]{1,0:T(8,128)(2,1)} %copy-done.14), channel_id=1, source_target_pairs={{0,4},{4,0},{8,12},{12,8},{16,20},{20,16},{24,28},{28,24},{1,5},{5... | collective-permute-start | bytes 786440 | tf_op jit(solution)/shard_map/ppermute | solution.py:435
  42.0 10.7 %collective-permute-start.8 = (bf16[128,1024]{1,0:T(8,128)(2,1)}, bf16[128,1024]{1,0:T(8,128)(2,1)}, u32[]{:S(2)}, u32[]{:S(2)}) collective-permute-start(bf16[128,1024]{1,0:T(8,128)(2,1)} %copy-done.21), channel_id=1, source_target_pairs={{0,8},{4,12},{8,0},{12,4},{16,24},{20,28},{24,16},{28,20},{1,9},{5... | collective-permute-start | bytes 786440 | tf_op jit(solution)/shard_map/ppermute | solution.py:435
  50.8 9.0 %collective-permute-start.15 = (bf16[128,1152]{1,0:T(8,128)(2,1)}, bf16[128,1152]{1,0:T(8,128)(2,1)}, u32[]{:S(2)}, u32[]{:S(2)}) collective-permute-start(bf16[128,1152]{1,0:T(8,128)(2,1)} %copy-done.17), channel_id=1, source_target_pairs={{0,4},{4,0},{8,12},{12,8},{16,20},{20,16},{24,28},{28,24},{1,5},{5... | collective-permute-start | bytes 884744 | tf_op jit(solution)/shard_map/ppermute | solution.py:435
  57.2 20.1 %collective-permute-start.10 = (bf16[128,1024]{1,0:T(8,128)(2,1)}, bf16[128,1024]{1,0:T(8,128)(2,1)}, u32[]{:S(2)}, u32[]{:S(2)}) collective-permute-start(bf16[128,1024]{1,0:T(8,128)(2,1)} %slice.101.refs_0_), channel_id=1, source_target_pairs={{0,8},{4,12},{8,0},{12,4},{16,24},{20,28},{24,16},{28,20},{1,9},{5... | collective-permute-start | bytes 786440 | tf_op jit(solution)/shard_map/ppermute | solution.py:435
  58.6 18.8 %collective-permute-start.11 = (bf16[128,1024]{1,0:T(8,128)(2,1)}, bf16[128,1024]{1,0:T(8,128)(2,1)}, u32[]{:S(2)}, u32[]{:S(2)}) collective-permute-start(bf16[128,1024]{1,0:T(8,128)(2,1)} %slice.101.refs_0_), channel_id=1, source_target_pairs={{0,16},{4,20},{8,24},{12,28},{16,0},{20,4},{24,8},{28,12},{1,17},{... | collective-permute-start | bytes 786440 | tf_op jit(solution)/shard_map/ppermute | solution.py:435
  59.8 17.6 %collective-permute-start.12 = (bf16[128,1024]{1,0:T(8,128)(2,1)}, bf16[128,1024]{1,0:T(8,128)(2,1)}, u32[]{:S(2)}, u32[]{:S(2)}) collective-permute-start(bf16[128,1024]{1,0:T(8,128)(2,1)} %slice.101.refs_0_), channel_id=1, source_target_pairs={{0,24},{4,28},{8,16},{12,20},{16,8},{20,12},{24,0},{28,4},{1,25},{... | collective-permute-start | bytes 786440 | tf_op jit(solution)/shard_map/ppermute | solution.py:435
  60.8 29.4 %collective-permute-start.30 = (bf16[256,1024]{1,0:T(8,128)(2,1)}, bf16[256,1024]{1,0:T(8,128)(2,1)}, u32[]{:S(2)}, u32[]{:S(2)}) collective-permute-start(bf16[256,1024]{1,0:T(8,128)(2,1)} %copy-done.6), channel_id=1, source_target_pairs={{0,16},{4,20},{8,24},{12,28},{16,0},{20,4},{24,8},{28,12},{1,17},{... | collective-permute-start | bytes 1572872 | tf_op jit(solution)/shard_map/ppermute | solution.py:435
  85.6 27.8 %collective-permute-start.27 = (bf16[288,1024]{1,0:T(8,128)(2,1)}, bf16[288,1024]{1,0:T(8,128)(2,1)S(1)}, u32[]{:S(2)}, u32[]{:S(2)}) collective-permute-start(bf16[288,1024]{1,0:T(8,128)(2,1)} %get-tuple-element.193.refs_0_.normed2_ref), channel_id=1, source_target_pairs={{0,8},{4,12},{8,0},{12,4},{16,24},{20,28},{24,16},{28,20},{1,9},{5... | collective-permute-start | bytes 1769480 | tf_op jit(solution)/shard_map/ppermute | solution.py:435
  86.6 26.8 %collective-permute-start.28 = (bf16[288,1024]{1,0:T(8,128)(2,1)}, bf16[288,1024]{1,0:T(8,128)(2,1)S(1)}, u32[]{:S(2)}, u32[]{:S(2)}) collective-permute-start(bf16[288,1024]{1,0:T(8,128)(2,1)} %get-tuple-element.193.refs_0_.normed2_ref), channel_id=1, source_target_pairs={{0,16},{4,20},{8,24},{12,28},{16,0},{20,4},{24,8},{28,12},{1,17},{... | collective-permute-start | bytes 1769480 | tf_op jit(solution)/shard_map/ppermute | solution.py:435
  87.4 31.5 %collective-permute-start.29 = (bf16[288,1024]{1,0:T(8,128)(2,1)}, bf16[288,1024]{1,0:T(8,128)(2,1)}, u32[]{:S(2)}, u32[]{:S(2)}) collective-permute-start(bf16[288,1024]{1,0:T(8,128)(2,1)} %get-tuple-element.193.refs_0_.normed2_ref), channel_id=1, source_target_pairs={{0,1},{1,0},{2,3},{3,2},{4,5},{5,4},{6,7},{7,6},{8,9},{9,8},{10,11... | collective-permute-start | bytes 1769480 | tf_op jit(solution)/shard_map/ppermute | solution.py:439
  89.5 23.2 %collective-permute-start.31 = (bf16[256,1024]{1,0:T(8,128)(2,1)S(1)}, bf16[256,1024]{1,0:T(8,128)(2,1)S(1)}, u32[]{:S(2)}, u32[]{:S(2)}) collective-permute-start(bf16[256,1024]{1,0:T(8,128)(2,1)S(1)} %copy-done.9), channel_id=1, source_target_pairs={{0,8},{4,12},{8,0},{12,4},{16,24},{20,28},{24,16},{28,20},{1,9},{5... | collective-permute-start | bytes 1572872 | tf_op jit(solution)/shard_map/ppermute | solution.py:435
  90.1 23.3 %collective-permute-start.32 = (bf16[256,1024]{1,0:T(8,128)(2,1)S(1)}, bf16[256,1024]{1,0:T(8,128)(2,1)S(1)}, u32[]{:S(2)}, u32[]{:S(2)}) collective-permute-start(bf16[256,1024]{1,0:T(8,128)(2,1)S(1)} %copy-done.9), channel_id=1, source_target_pairs={{0,16},{4,20},{8,24},{12,28},{16,0},{20,4},{24,8},{28,12},{1,17},{... | collective-permute-start | bytes 1572872 | tf_op jit(solution)/shard_map/ppermute | solution.py:435
  118.9 40.9 %collective-permute-start.38 = (bf16[4,384,1024]{2,1,0:T(8,128)(2,1)S(1)}, bf16[4,384,1024]{2,1,0:T(8,128)(2,1)}, u32[]{:S(2)}, u32[]{:S(2)}) collective-permute-start(bf16[4,384,1024]{2,1,0:T(8,128)(2,1)S(1)} %all-to-all-done.refs_16_), channel_id=1, source_target_pairs={{0,4},{4,0},{8,12},{12,8},{16,20},{20,16},{24,28},{28,24},{1,5},{5... | collective-permute-start | bytes 9437192 | tf_op jit(solution)/shard_map/ppermute | solution.py:435
  118.9 16.6 %collective-permute-start.35 = (bf16[288,1024]{1,0:T(8,128)(2,1)}, bf16[288,1024]{1,0:T(8,128)(2,1)}, u32[]{:S(2)}, u32[]{:S(2)}) collective-permute-start(bf16[288,1024]{1,0:T(8,128)(2,1)} %collective-permute-done.29.refs_4_), channel_id=1, source_target_pairs={{0,16},{4,20},{8,24},{12,28},{16,0},{20,4},{24,8},{28,12},{1,17},{... | collective-permute-start | bytes 1769480 | tf_op jit(solution)/shard_map/ppermute | solution.py:435
  120.2 15.1 %collective-permute-start.36 = (bf16[256,1024]{1,0:T(8,128)(2,1)}, bf16[256,1024]{1,0:T(8,128)(2,1)}, u32[]{:S(2)}, u32[]{:S(2)}) collective-permute-start(bf16[256,1024]{1,0:T(8,128)(2,1)} %copy-done.11), channel_id=1, source_target_pairs={{0,8},{4,12},{8,0},{12,4},{16,24},{20,28},{24,16},{28,20},{1,9},{5... | collective-permute-start | bytes 1572872 | tf_op jit(solution)/shard_map/ppermute | solution.py:435
  121.3 90.7 %all-to-all-start.1 = ((bf16[4,384,1024]{2,1,0:T(8,128)(2,1)}), bf16[4,384,1024]{2,1,0:T(8,128)(2,1)}, u32[]{:S(2)}, u32[]{:S(2)}) async-start(bf16[4,384,1024]{2,1,0:T(8,128)(2,1)} %maximum_maximum_fusion.1), calls=%async_computation.1 | async-start | bytes 6291456 | tf_op jit(solution)/shard_map/all_to_all | solution.py:876
  126.6 21.0 %collective-permute-start.33 = (bf16[288,1024]{1,0:T(8,128)(2,1)}, bf16[288,1024]{1,0:T(8,128)(2,1)}, u32[]{:S(2)}, u32[]{:S(2)}) collective-permute-start(bf16[288,1024]{1,0:T(8,128)(2,1)} %copy-done.4), channel_id=1, source_target_pairs={{0,16},{4,20},{8,24},{12,28},{16,0},{20,4},{24,8},{28,12},{1,17},{... | collective-permute-start | bytes 1769480 | tf_op jit(solution)/shard_map/ppermute | solution.py:435
  127.2 20.8 %collective-permute-start.34 = (bf16[288,1024]{1,0:T(8,128)(2,1)}, bf16[288,1024]{1,0:T(8,128)(2,1)}, u32[]{:S(2)}, u32[]{:S(2)}) collective-permute-start(bf16[288,1024]{1,0:T(8,128)(2,1)} %collective-permute-done.29.refs_4_), channel_id=1, source_target_pairs={{0,8},{4,12},{8,0},{12,4},{16,24},{20,28},{24,16},{28,20},{1,9},{5... | collective-permute-start | bytes 1769480 | tf_op jit(solution)/shard_map/ppermute | solution.py:435
  135.5 24.3 %collective-permute-start.37 = (bf16[288,1024]{1,0:T(8,128)(2,1)}, bf16[288,1024]{1,0:T(8,128)(2,1)}, u32[]{:S(2)}, u32[]{:S(2)}) collective-permute-start(bf16[288,1024]{1,0:T(8,128)(2,1)} %collective-permute-done.35.refs_6_), channel_id=1, source_target_pairs={{0,8},{4,12},{8,0},{12,4},{16,24},{20,28},{24,16},{28,20},{1,9},{5... | collective-permute-start | bytes 1769480 | tf_op jit(solution)/shard_map/ppermute | solution.py:435
  181.9 25.0 %collective-permute-start.39 = (bf16[4,384,1024]{2,1,0:T(8,128)(2,1)}, bf16[4,384,1024]{2,1,0:T(8,128)(2,1)S(1)}, u32[]{:S(2)}, u32[]{:S(2)}) collective-permute-start(bf16[4,384,1024]{2,1,0:T(8,128)(2,1)} %get-tuple-element.229), channel_id=1, source_target_pairs={{0,4},{4,0},{8,12},{12,8},{16,20},{20,16},{24,28},{28,24},{1,5},{5... | collective-permute-start | bytes 9437192 | tf_op jit(solution)/shard_map/ppermute | solution.py:435
  212.4 76.5 %all-to-all-start.2 = ((bf16[4,384,1024]{2,1,0:T(8,128)(2,1)}), bf16[4,384,1024]{2,1,0:T(8,128)(2,1)S(1)}, u32[]{:S(2)}, u32[]{:S(2)}) async-start(bf16[4,384,1024]{2,1,0:T(8,128)(2,1)} %add_convert_fusion.1), calls=%async_computation.2 | async-start | bytes 6291456 | tf_op jit(solution)/shard_map/all_to_all | solution.py:876
  243.2 28.4 %collective-permute-start.43 = (bf16[4,384,1024]{2,1,0:T(8,128)(2,1)}, bf16[4,384,1024]{2,1,0:T(8,128)(2,1)}, u32[]{:S(2)}, u32[]{:S(2)}) collective-permute-start(bf16[4,384,1024]{2,1,0:T(8,128)(2,1)} %get-tuple-element.269), channel_id=1, source_target_pairs={{0,4},{4,0},{8,12},{12,8},{16,20},{20,16},{24,28},{28,24},{1,5},{5... | collective-permute-start | bytes 9437192 | tf_op jit(solution)/shard_map/ppermute | solution.py:435
  268.7 15.9 %collective-permute-start.42 = (bf16[272,1024]{1,0:T(8,128)(2,1)}, bf16[272,1024]{1,0:T(8,128)(2,1)}, u32[]{:S(2)}, u32[]{:S(2)}) collective-permute-start(bf16[272,1024]{1,0:T(8,128)(2,1)} %get-tuple-element.267), channel_id=1, source_target_pairs={{0,8},{4,12},{8,0},{12,4},{16,24},{20,28},{24,16},{28,20},{1,9},{5... | collective-permute-start | bytes 1671176 | tf_op jit(solution)/shard_map/ppermute | solution.py:435
  269.8 26.8 %collective-permute-start.41 = (bf16[272,1024]{1,0:T(8,128)(2,1)}, bf16[272,1024]{1,0:T(8,128)(2,1)}, u32[]{:S(2)}, u32[]{:S(2)}) collective-permute-start(bf16[272,1024]{1,0:T(8,128)(2,1)} %get-tuple-element.265), channel_id=1, source_target_pairs={{0,8},{4,12},{8,0},{12,4},{16,24},{20,28},{24,16},{28,20},{1,9},{5... | collective-permute-start | bytes 1671176 | tf_op jit(solution)/shard_map/ppermute | solution.py:435
  270.8 21.3 %collective-permute-start.46 = (bf16[272,1024]{1,0:T(8,128)(2,1)}, bf16[272,1024]{1,0:T(8,128)(2,1)}, u32[]{:S(2)}, u32[]{:S(2)}) collective-permute-start(bf16[272,1024]{1,0:T(8,128)(2,1)} %get-tuple-element.288), channel_id=1, source_target_pairs={{0,16},{4,20},{8,24},{12,28},{16,0},{20,4},{24,8},{28,12},{1,17},{... | collective-permute-start | bytes 1671176 | tf_op jit(solution)/shard_map/ppermute | solution.py:435
  291.2 15.6 %collective-permute-start.44 = (bf16[272,1024]{1,0:T(8,128)(2,1)S(1)}, bf16[272,1024]{1,0:T(8,128)(2,1)S(1)}, u32[]{:S(2)}, u32[]{:S(2)}) collective-permute-start(bf16[272,1024]{1,0:T(8,128)(2,1)S(1)} %add_convert_fusion.7), channel_id=1, source_target_pairs={{0,16},{4,20},{8,24},{12,28},{16,0},{20,4},{24,8},{28,12},{1,17},{... | collective-permute-start | bytes 1671176 | tf_op jit(solution)/shard_map/ppermute | solution.py:435
  294.4 19.5 %collective-permute-start.47 = (bf16[272,1024]{1,0:T(8,128)(2,1)}, bf16[272,1024]{1,0:T(8,128)(2,1)}, u32[]{:S(2)}, u32[]{:S(2)}) collective-permute-start(bf16[272,1024]{1,0:T(8,128)(2,1)} %add_convert_fusion.5), channel_id=1, source_target_pairs={{0,8},{4,12},{8,0},{12,4},{16,24},{20,28},{24,16},{28,20},{1,9},{5... | collective-permute-start | bytes 1671176 | tf_op jit(solution)/shard_map/ppermute | solution.py:435
  295.1 23.7 %collective-permute-start.45 = (bf16[272,1024]{1,0:T(8,128)(2,1)}, bf16[272,1024]{1,0:T(8,128)(2,1)}, u32[]{:S(2)}, u32[]{:S(2)}) collective-permute-start(bf16[272,1024]{1,0:T(8,128)(2,1)} %get-tuple-element.286), channel_id=1, source_target_pairs={{0,16},{4,20},{8,24},{12,28},{16,0},{20,4},{24,8},{28,12},{1,17},{... | collective-permute-start | bytes 1671176 | tf_op jit(solution)/shard_map/ppermute | solution.py:435
  308.9 11.4 %collective-permute-start.48 = (bf16[272,1024]{1,0:T(8,128)(2,1)}, bf16[272,1024]{1,0:T(8,128)(2,1)}, u32[]{:S(2)}, u32[]{:S(2)}) collective-permute-start(bf16[272,1024]{1,0:T(8,128)(2,1)} %add_convert_fusion.6), channel_id=1, source_target_pairs={{0,1},{1,0},{2,3},{3,2},{4,5},{5,4},{6,7},{7,6},{8,9},{9,8},{10,11... | collective-permute-start | bytes 1671176 | tf_op jit(solution)/shard_map/ppermute | solution.py:439
  308.9 19.6 %collective-permute-start.51 = (bf16[256,1024]{1,0:T(8,128)(2,1)}, bf16[256,1024]{1,0:T(8,128)(2,1)}, u32[]{:S(2)}, u32[]{:S(2)}) collective-permute-start(bf16[256,1024]{1,0:T(8,128)(2,1)} %get-tuple-element.304), channel_id=1, source_target_pairs={{0,16},{4,20},{8,24},{12,28},{16,0},{20,4},{24,8},{28,12},{1,17},{... | collective-permute-start | bytes 1572872 | tf_op jit(solution)/shard_map/ppermute | solution.py:435
  309.8 22.1 %collective-permute-start.49 = (bf16[256,1024]{1,0:T(8,128)(2,1)}, bf16[256,1024]{1,0:T(8,128)(2,1)}, u32[]{:S(2)}, u32[]{:S(2)}) collective-permute-start(bf16[256,1024]{1,0:T(8,128)(2,1)} %get-tuple-element.302), channel_id=1, source_target_pairs={{0,8},{4,12},{8,0},{12,4},{16,24},{20,28},{24,16},{28,20},{1,9},{5... | collective-permute-start | bytes 1572872 | tf_op jit(solution)/shard_map/ppermute | solution.py:435
  326.9 28.3 %collective-permute-start.64 = (bf16[512,1152]{1,0:T(8,128)(2,1)}, bf16[512,1152]{1,0:T(8,128)(2,1)}, u32[]{:S(2)}, u32[]{:S(2)}) collective-permute-start(bf16[512,1152]{1,0:T(8,128)(2,1)} %get-tuple-element.318), channel_id=1, source_target_pairs={{0,4},{4,0},{8,12},{12,8},{16,20},{20,16},{24,28},{28,24},{1,5},{5... | collective-permute-start | bytes 3538952 | tf_op jit(solution)/shard_map/ppermute | solution.py:435
  326.9 28.2 %collective-permute-start.53 = (bf16[256,1024]{1,0:T(8,128)(2,1)}, bf16[256,1024]{1,0:T(8,128)(2,1)}, u32[]{:S(2)}, u32[]{:S(2)}) collective-permute-start(bf16[256,1024]{1,0:T(8,128)(2,1)} %get-tuple-element.305), channel_id=1, source_target_pairs={{0,8},{4,12},{8,0},{12,4},{16,24},{20,28},{24,16},{28,20},{1,9},{5... | collective-permute-start | bytes 1572872 | tf_op jit(solution)/shard_map/ppermute | solution.py:435
  328.0 27.2 %collective-permute-start.54 = (bf16[256,1024]{1,0:T(8,128)(2,1)}, bf16[256,1024]{1,0:T(8,128)(2,1)}, u32[]{:S(2)}, u32[]{:S(2)}) collective-permute-start(bf16[256,1024]{1,0:T(8,128)(2,1)} %get-tuple-element.306), channel_id=1, source_target_pairs={{0,16},{4,20},{8,24},{12,28},{16,0},{20,4},{24,8},{28,12},{1,17},{... | collective-permute-start | bytes 1572872 | tf_op jit(solution)/shard_map/ppermute | solution.py:435
  330.6 24.5 %collective-permute-start.52 = (bf16[256,1024]{1,0:T(8,128)(2,1)}, bf16[256,1024]{1,0:T(8,128)(2,1)}, u32[]{:S(2)}, u32[]{:S(2)}) collective-permute-start(bf16[256,1024]{1,0:T(8,128)(2,1)} %add_convert_fusion.11), channel_id=1, source_target_pairs={{0,8},{4,12},{8,0},{12,4},{16,24},{20,28},{24,16},{28,20},{1,9},{5... | collective-permute-start | bytes 1572872 | tf_op jit(solution)/shard_map/ppermute | solution.py:435
  333.9 21.2 %collective-permute-start.50 = (bf16[256,1024]{1,0:T(8,128)(2,1)}, bf16[256,1024]{1,0:T(8,128)(2,1)}, u32[]{:S(2)}, u32[]{:S(2)}) collective-permute-start(bf16[256,1024]{1,0:T(8,128)(2,1)} %add_convert_fusion.12), channel_id=1, source_target_pairs={{0,16},{4,20},{8,24},{12,28},{16,0},{20,4},{24,8},{28,12},{1,17},{... | collective-permute-start | bytes 1572872 | tf_op jit(solution)/shard_map/ppermute | solution.py:435
  335.2 82.0 %all-to-all-start.3 = ((bf16[4,384,1024]{2,1,0:T(8,128)(2,1)}), bf16[4,384,1024]{2,1,0:T(8,128)(2,1)S(1)}, u32[]{:S(2)}, u32[]{:S(2)}) async-start(bf16[4,384,1024]{2,1,0:T(8,128)(2,1)} %add_convert_fusion), calls=%async_computation.3 | async-start | bytes 6291456 | tf_op jit(solution)/shard_map/all_to_all | solution.py:876
  355.2 13.6 %collective-permute-start.56 = (bf16[512,1152]{1,0:T(8,128)(2,1)}, bf16[512,1152]{1,0:T(8,128)(2,1)S(1)}, u32[]{:S(2)}, u32[]{:S(2)}) collective-permute-start(bf16[512,1152]{1,0:T(8,128)(2,1)} %get-tuple-element.314), channel_id=1, source_target_pairs={{0,4},{4,0},{8,12},{12,8},{16,20},{20,16},{24,28},{28,24},{1,5},{5... | collective-permute-start | bytes 3538952 | tf_op jit(solution)/shard_map/ppermute | solution.py:435
  357.7 9.9 %collective-permute-start.66 = (bf16[128,1152]{1,0:T(8,128)(2,1)S(1)}, bf16[128,1152]{1,0:T(8,128)(2,1)S(1)}, u32[]{:S(2)}, u32[]{:S(2)}) collective-permute-start(bf16[128,1152]{1,0:T(8,128)(2,1)S(1)} %get-tuple-element.341), channel_id=1, source_target_pairs={{0,16},{4,20},{8,24},{12,28},{16,0},{20,4},{24,8},{28,12},{1,17},{... | collective-permute-start | bytes 884744 | tf_op jit(solution)/shard_map/ppermute | solution.py:435
  358.5 12.4 %collective-permute-start.60 = (bf16[512,1024]{1,0:T(8,128)(2,1)S(1)}, bf16[512,1024]{1,0:T(8,128)(2,1)S(1)}, u32[]{:S(2)}, u32[]{:S(2)}) collective-permute-start(bf16[512,1024]{1,0:T(8,128)(2,1)S(1)} %copy-done.44), channel_id=1, source_target_pairs={{0,4},{4,0},{8,12},{12,8},{16,20},{20,16},{24,28},{28,24},{1,5},{5... | collective-permute-start | bytes 3145736 | tf_op jit(solution)/shard_map/ppermute | solution.py:435
  360.9 58.4 %collective-permute-start.55 = (bf16[256,1024]{1,0:T(8,128)(2,1)}, bf16[256,1024]{1,0:T(8,128)(2,1)}, u32[]{:S(2)}, u32[]{:S(2)}) collective-permute-start(bf16[256,1024]{1,0:T(8,128)(2,1)} %add_convert_fusion.9), channel_id=1, source_target_pairs={{0,1},{1,0},{2,3},{3,2},{4,5},{5,4},{6,7},{7,6},{8,9},{9,8},{10,11... | collective-permute-start | bytes 1572872 | tf_op jit(solution)/shard_map/ppermute | solution.py:439
  362.8 20.9 %collective-permute-start.65 = (bf16[128,1152]{1,0:T(8,128)(2,1)S(1)}, bf16[128,1152]{1,0:T(8,128)(2,1)S(1)}, u32[]{:S(2)}, u32[]{:S(2)}) collective-permute-start(bf16[128,1152]{1,0:T(8,128)(2,1)S(1)} %get-tuple-element.342), channel_id=1, source_target_pairs={{0,16},{4,20},{8,24},{12,28},{16,0},{20,4},{24,8},{28,12},{1,17},{... | collective-permute-start | bytes 884744 | tf_op jit(solution)/shard_map/ppermute | solution.py:435
  367.7 17.6 %collective-permute-start.67 = (bf16[128,1152]{1,0:T(8,128)(2,1)S(1)}, bf16[128,1152]{1,0:T(8,128)(2,1)S(1)}, u32[]{:S(2)}, u32[]{:S(2)}) collective-permute-start(bf16[128,1152]{1,0:T(8,128)(2,1)S(1)} %add_convert_fusion.13), channel_id=1, source_target_pairs={{0,8},{4,12},{8,0},{12,4},{16,24},{20,28},{24,16},{28,20},{1,9},{5... | collective-permute-start | bytes 884744 | tf_op jit(solution)/shard_map/ppermute | solution.py:435
  369.9 12.1 %collective-permute-start.58 = (bf16[128,1152]{1,0:T(8,128)(2,1)S(1)}, bf16[128,1152]{1,0:T(8,128)(2,1)S(1)}, u32[]{:S(2)}, u32[]{:S(2)}) collective-permute-start(bf16[128,1152]{1,0:T(8,128)(2,1)S(1)} %get-tuple-element.344), channel_id=1, source_target_pairs={{0,8},{4,12},{8,0},{12,4},{16,24},{20,28},{24,16},{28,20},{1,9},{5... | collective-permute-start | bytes 884744 | tf_op jit(solution)/shard_map/ppermute | solution.py:435
  372.1 10.9 %collective-permute-start.62 = (bf16[128,1024]{1,0:T(8,128)(2,1)S(1)}, bf16[128,1024]{1,0:T(8,128)(2,1)S(1)}, u32[]{:S(2)}, u32[]{:S(2)}) collective-permute-start(bf16[128,1024]{1,0:T(8,128)(2,1)S(1)} %get-tuple-element.347), channel_id=1, source_target_pairs={{0,16},{4,20},{8,24},{12,28},{16,0},{20,4},{24,8},{28,12},{1,17},{... | collective-permute-start | bytes 786440 | tf_op jit(solution)/shard_map/ppermute | solution.py:435
  381.9 13.6 %collective-permute-start.57 = (bf16[128,1152]{1,0:T(8,128)(2,1)S(1)}, bf16[128,1152]{1,0:T(8,128)(2,1)S(1)}, u32[]{:S(2)}, u32[]{:S(2)}) collective-permute-start(bf16[128,1152]{1,0:T(8,128)(2,1)S(1)} %get-tuple-element.345), channel_id=1, source_target_pairs={{0,8},{4,12},{8,0},{12,4},{16,24},{20,28},{24,16},{28,20},{1,9},{5... | collective-permute-start | bytes 884744 | tf_op jit(solution)/shard_map/ppermute | solution.py:435
  383.0 12.6 %collective-permute-start.59 = (bf16[128,1152]{1,0:T(8,128)(2,1)S(1)}, bf16[128,1152]{1,0:T(8,128)(2,1)S(1)}, u32[]{:S(2)}, u32[]{:S(2)}) collective-permute-start(bf16[128,1152]{1,0:T(8,128)(2,1)S(1)} %add_convert_fusion.14), channel_id=1, source_target_pairs={{0,16},{4,20},{8,24},{12,28},{16,0},{20,4},{24,8},{28,12},{1,17},{... | collective-permute-start | bytes 884744 | tf_op jit(solution)/shard_map/ppermute | solution.py:435
  383.8 11.8 %collective-permute-start.61 = (bf16[128,1024]{1,0:T(8,128)(2,1)S(1)}, bf16[128,1024]{1,0:T(8,128)(2,1)S(1)}, u32[]{:S(2)}, u32[]{:S(2)}) collective-permute-start(bf16[128,1024]{1,0:T(8,128)(2,1)S(1)} %get-tuple-element.348), channel_id=1, source_target_pairs={{0,16},{4,20},{8,24},{12,28},{16,0},{20,4},{24,8},{28,12},{1,17},{... | collective-permute-start | bytes 786440 | tf_op jit(solution)/shard_map/ppermute | solution.py:435
  385.3 10.3 %collective-permute-start.63 = (bf16[128,1024]{1,0:T(8,128)(2,1)S(1)}, bf16[128,1024]{1,0:T(8,128)(2,1)S(1)}, u32[]{:S(2)}, u32[]{:S(2)}) collective-permute-start(bf16[128,1024]{1,0:T(8,128)(2,1)S(1)} %add_convert_fusion.15), channel_id=1, source_target_pairs={{0,8},{4,12},{8,0},{12,4},{16,24},{20,28},{24,16},{28,20},{1,9},{5... | collective-permute-start | bytes 786440 | tf_op jit(solution)/shard_map/ppermute | solution.py:435
  399.3 26.2 %collective-permute-start.68 = (bf16[32,3328]{1,0:T(8,128)(2,1)}, bf16[32,3328]{1,0:T(8,128)(2,1)S(1)}, u32[]{:S(2)}, u32[]{:S(2)}) collective-permute-start(bf16[32,3328]{1,0:T(8,128)(2,1)} %get-tuple-element.320), channel_id=1, source_target_pairs={{0,1},{1,0},{2,3},{3,2},{4,5},{5,4},{6,7},{7,6},{8,9},{9,8},{10,11... | collective-permute-start | bytes 638984 | tf_op jit(solution)/shard_map/ppermute | solution.py:439
  401.1 24.3 %collective-permute-start.69 = (bf16[32,3328]{1,0:T(8,128)(2,1)}, bf16[32,3328]{1,0:T(8,128)(2,1)}, u32[]{:S(2)}, u32[]{:S(2)}) collective-permute-start(bf16[32,3328]{1,0:T(8,128)(2,1)} %get-tuple-element.321), channel_id=1, source_target_pairs={{0,2},{1,3},{2,0},{3,1},{4,6},{5,7},{6,4},{7,5},{8,10},{9,11},{10,... | collective-permute-start | bytes 638984 | tf_op jit(solution)/shard_map/ppermute | solution.py:439
  417.1 8.3 %collective-permute-start.70 = (bf16[32,3328]{1,0:T(8,128)(2,1)}, bf16[32,3328]{1,0:T(8,128)(2,1)}, u32[]{:S(2)}, u32[]{:S(2)}) collective-permute-start(bf16[32,3328]{1,0:T(8,128)(2,1)} %get-tuple-element.324), channel_id=1, source_target_pairs={{0,3},{1,2},{2,1},{3,0},{4,7},{5,6},{6,5},{7,4},{8,11},{9,10},{10,... | collective-permute-start | bytes 638984 | tf_op jit(solution)/shard_map/ppermute | solution.py:439
  (56 other events, 458.7 us)

commit v6 on v5

--- a/solution.py
+++ b/solution.py
@@ -1065,9 +1065,9 @@
     own, pair = rows[:4], rows[4:]
     pair_pass, own_pass = over_x(pair[3]), over_y(own[3])
     pair_mine = over_x(pair[1])
-    pair_pass, expert_grad1, slices0 = together(pair_pass, expert_grad1, slices0)
+    pair_pass, expert_grad1 = together(pair_pass, expert_grad1)
     pair_other = over_y(bf_sum(pair[2], pair_pass))
-    mine, pair_pass = together(own[2], pair_pass)
+    mine, pair_pass, slices0 = together(own[2], pair_pass, slices0)
     own_mine = over_y(mine)
     own_other = over_x(bf_sum(own[1], own_pass))
     row_pair = bf_sum(pair[0], pair_mine, pair_other)

time: 436 us -> 431 us (0.989)
  waiting for transfers between devices: 140 us -> 135 us
  transfers between devices with their start and end apart: 75 -> 75, of which waited for: 25 -> 26; matrix products, arithmetic and copies ran while one was open for 11% -> 11% of each run, Pallas kernels for 33% -> 34%
where the time goes in v6:
time: 431 us; the launch traced here: 423 us
  Pallas kernels  147 us (34%)
  waiting for transfers between devices  135 us (31%)
  starting transfers between devices  86.5 us (20%)
  other arithmetic  36.4 us (8%)
  local copies, waits for them, and re-layouts  15.3 us (4%)
    ppermute x61, waiting for transfers between devices, over_expert(): return lax.ppermute(value, 'expert', [(i, i ^ bits) for i in range(8)])  103 us
    pallas_call x4, Pallas kernels, expert_call(): pl.pallas_call(functools.partial(expert_body, before is None, len(weights...  97 us
    ppermute x61, starting transfers between devices, over_expert(): return lax.ppermute(value, 'expert', [(i, i ^ bits) for i in range(8)])  49 us
    pallas_call x6, Pallas kernels, local_kernel(): pl.pallas_call(body, out_shape=[jax.ShapeDtypeStruct(shape, dtype) for sh...  41.8 us
    ppermute x10, starting transfers between devices, over_shard(): return lax.ppermute(value, 'shard', [(i, i ^ bits) for i in range(4)])  18.9 us
    all_to_all x4, starting transfers between devices, exchange(): lax.all_to_all(slices, 'shard', split_axis=0, concat_axis=0, tiled=True)  18.7 us
    ppermute x10, waiting for transfers between devices, over_shard(): return lax.ppermute(value, 'shard', [(i, i ^ bits) for i in range(4)])  17.9 us
    all_to_all x4, waiting for transfers between devices, exchange(): lax.all_to_all(slices, 'shard', split_axis=0, concat_axis=0, tiled=True)  14.1 us
  transfers between devices with their start and end apart: 75, of which 26 were waited for; matrix products, arithmetic and copies ran while one was open for 11% of the time, Pallas kernels for 34%

profile of v6, /device:TPU:0, one launch (start us, length us, event | category | flops | bytes accessed | tf_op | source)
XLA Modules:
  0.0 423.2 jit_solution(12920449212240914172)
XLA Ops:
  0.7 1.9 pack.1
  2.6 3.1 collective-permute-start
  5.6 2.6 collective-permute-start.1
  8.2 1.7 collective-permute-start.3
  9.9 1.5 collective-permute-start.4
  11.5 2.6 fusion.3
  15.0 1.8 maximum_maximum_fusion
  17.5 6.0 %collective-permute-done.1 = bf16[32,3200]{1,0:T(8,128)(2,1)S(1)} collective-permute-done((bf16[32,3200]{1,0:T(8,128)(2,1)}, bf16[32,3200]{1,0:T(8,128)(2,1)S(1)}, u32[]{:S(2)}, u32[]{:S(2)}) %collective-permute-start.1) | collective-permute-done | bytes 204832 | tf_op jit(solution)/shard_map/ppermute | solution.py:439
  23.9 1.6 collective-permute-start.5
  25.5 1.6 collective-permute-start.7
  27.1 6.5 %collective-permute-done.9.refs_12_ = bf16[256,1024]{1,0:T(8,128)(2,1)S(1)} collective-permute-done((bf16[256,1024]{1,0:T(8,128)(2,1)S(1)}, bf16[256,1024]{1,0:T(8,128)(2,1)S(1)}, u32[]{:S(2)}, u32[]{:S(2)}) %collective-permute-start.9) | collective-permute-done | bytes 524320 | tf_op jit(solution)/shard_map/ppermute | solution.py:439
  35.2 3.7 all-to-all-start
  43.0 5.5 %collective-permute-done.18.refs_9_ = bf16[128,1024]{1,0:T(8,128)(2,1)} collective-permute-done((bf16[128,1024]{1,0:T(8,128)(2,1)}, bf16[128,1024]{1,0:T(8,128)(2,1)}, u32[]{:S(2)}, u32[]{:S(2)}) %collective-permute-start.18) | collective-permute-done | bytes 262176 | tf_op jit(solution)/shard_map/ppermute | solution.py:435
  48.4 1.5 collective-permute-start.6
  52.7 2.8 collective-permute-done.6.refs_3_
  55.6 1.7 slice.101.refs_0_
  60.8 1.5 collective-permute-start.30
  65.1 2.5 pad_maximum_fusion.2
  67.6 9.7 %attend.1 = (bf16[256,1024]{1,0:T(8,128)(2,1)}, bf16[256,1024]{1,0:T(8,128)(2,1)}, bf16[256,512]{1,0:T(8,128)(2,1)}, bf16[256,512]{1,0:T(8,128)(2,1)}, bf16[256,...) custom-call(s32[1]{0:T(128)} %bitcast.e_ref, bf16[256,1024]{1,0:T(8,128)(2,1)} %x_ref.5, s32[256,1]{1,0:T(8,128)} %copy.30.column_ref, ...), custom_call_target="tpu_custom_call" | custom-call | flops 1000 | bytes 1000 | tf_op jit(solution)/shard_map/attend/pallas_call | solution.py:848
  81.2 4.5 %route.1 = (bf16[288,1024]{1,0:T(8,128)(2,1)}, f32[256,128]{1,0:T(8,128)}, f32[256,1024]{1,0:T(8,128)}) custom-call(s32[1]{0:T(128)} %bitcast.e_ref, bf16[256,1024]{1,0:T(8,128)(2,1)} %x_ref.5, bf16[256,1024]{1,0:T(8,128)(2,1)} %get-tuple-element.186.mixed_ref, bf16[1024,128]{1,0:T(8,128)(2,1)} %get-tuple-element.187.small_ref, ...), custom_call_target="tpu_custom_call" | custom-call | flops 1000 | bytes 1000 | tf_op jit(solution)/shard_map/route/pallas_call | solution.py:848
  87.4 2.0 collective-permute-start.29
  90.2 1.6 collective-permute-start.32
  91.7 1.8 maximum_maximum_fusion.1
  93.6 19.1 %collective-permute-done.31.refs_13_ = bf16[256,1024]{1,0:T(8,128)(2,1)S(1)} collective-permute-done((bf16[256,1024]{1,0:T(8,128)(2,1)S(1)}, bf16[256,1024]{1,0:T(8,128)(2,1)S(1)}, u32[]{:S(2)}, u32[]{:S(2)}) %collective-permute-start.31) | collective-permute-done | bytes 524320 | tf_op jit(solution)/shard_map/ppermute | solution.py:435
  115.2 3.7 collective-permute-done.29.refs_4_
  121.3 5.3 %all-to-all-start.1 = ((bf16[4,384,1024]{2,1,0:T(8,128)(2,1)}), bf16[4,384,1024]{2,1,0:T(8,128)(2,1)}, u32[]{:S(2)}, u32[]{:S(2)}) async-start(bf16[4,384,1024]{2,1,0:T(8,128)(2,1)} %maximum_maximum_fusion.1), calls=%async_computation.1 | async-start | bytes 6291456 | tf_op jit(solution)/shard_map/all_to_all | solution.py:876
  128.5 6.8 %collective-permute-done.36.refs_15_ = bf16[256,1024]{1,0:T(8,128)(2,1)} collective-permute-done((bf16[256,1024]{1,0:T(8,128)(2,1)}, bf16[256,1024]{1,0:T(8,128)(2,1)}, u32[]{:S(2)}, u32[]{:S(2)}) %collective-permute-start.36) | collective-permute-done | bytes 524320 | tf_op jit(solution)/shard_map/ppermute | solution.py:435
  136.4 11.3 %collective-permute-done.33.refs_3_ = bf16[288,1024]{1,0:T(8,128)(2,1)} collective-permute-done((bf16[288,1024]{1,0:T(8,128)(2,1)}, bf16[288,1024]{1,0:T(8,128)(2,1)}, u32[]{:S(2)}, u32[]{:S(2)}) %collective-permute-start.33) | collective-permute-done | bytes 589856 | tf_op jit(solution)/shard_map/ppermute | solution.py:435
  148.0 11.8 %collective-permute-done.37.refs_7_ = bf16[288,1024]{1,0:T(8,128)(2,1)} collective-permute-done((bf16[288,1024]{1,0:T(8,128)(2,1)}, bf16[288,1024]{1,0:T(8,128)(2,1)}, u32[]{:S(2)}, u32[]{:S(2)}) %collective-permute-start.37) | collective-permute-done | bytes 589856 | tf_op jit(solution)/shard_map/ppermute | solution.py:435
  159.8 22.0 %expert.4 = (bf16[272,1024]{1,0:T(8,128)(2,1)}, bf16[272,1024]{1,0:T(8,128)(2,1)}, bf16[272,1024]{1,0:T(8,128)(2,1)}, bf16[272,1024]{1,0:T(8,128)(2,1)}, bf16[27...) custom-call(s32[1]{0:T(128)} %bitcast.15.number_ref, ...), custom_call_target="tpu_custom_call" | custom-call | flops 1000 | bytes 1000 | tf_op jit(solution)/shard_map/expert/pallas_call | solution.py:592
  181.9 24.9 %expert.5 = (bf16[272,1024]{1,0:T(8,128)(2,1)}, bf16[272,1024]{1,0:T(8,128)(2,1)}, bf16[272,1024]{1,0:T(8,128)(2,1)}, bf16[272,1024]{1,0:T(8,128)(2,1)}, bf16[27...) custom-call(s32[1]{0:T(128)} %bitcast.14.number_ref, ...), custom_call_target="tpu_custom_call" | custom-call | flops 1000 | bytes 1000 | tf_op jit(solution)/shard_map/expert/pallas_call | solution.py:592
  206.9 5.1 %add_convert_fusion.1 = bf16[4,384,1024]{2,1,0:T(8,128)(2,1)} fusion(bf16[4,384,1024]{2,1,0:T(8,128)(2,1)S(1)} %collective-permute-done.39, bf16[4,384,1024]{2,1,0:T(8,128)(2,1)} %get-tuple-element.228), kind=kLoop, calls=%fused_computation.1 | loop fusion | flops 6291456 | bytes 9437184 | tf_op jit(solution)/shard_map/convert_element_type | solution.py:865
  212.4 5.6 %all-to-all-start.2 = ((bf16[4,384,1024]{2,1,0:T(8,128)(2,1)}), bf16[4,384,1024]{2,1,0:T(8,128)(2,1)S(1)}, u32[]{:S(2)}, u32[]{:S(2)}) async-start(bf16[4,384,1024]{2,1,0:T(8,128)(2,1)} %add_convert_fusion.1), calls=%async_computation.2 | async-start | bytes 6291456 | tf_op jit(solution)/shard_map/all_to_all | solution.py:876
  218.0 25.0 %expert.6 = (bf16[272,1024]{1,0:T(8,128)(2,1)}, bf16[272,1024]{1,0:T(8,128)(2,1)}, bf16[272,1024]{1,0:T(8,128)(2,1)}, bf16[272,1024]{1,0:T(8,128)(2,1)}, bf16[27...) custom-call(s32[1]{0:T(128)S(6)} %add.100.number_ref, ...), custom_call_target="tpu_custom_call" | custom-call | flops 1000 | bytes 1000 | tf_op jit(solution)/shard_map/expert/pallas_call | solution.py:592
  243.5 25.0 %expert.7 = (bf16[272,1024]{1,0:T(8,128)(2,1)}, bf16[272,1024]{1,0:T(8,128)(2,1)}, bf16[272,1024]{1,0:T(8,128)(2,1)}, bf16[272,1024]{1,0:T(8,128)(2,1)}, bf16[27...) custom-call(s32[1]{0:T(128)S(6)} %add.97.number_ref, ...), custom_call_target="tpu_custom_call" | custom-call | flops 1000 | bytes 1000 | tf_op jit(solution)/shard_map/expert/pallas_call | solution.py:592
  271.4 6.2 %add_convert_fusion = bf16[4,384,1024]{2,1,0:T(8,128)(2,1)} fusion(bf16[4,384,1024]{2,1,0:T(8,128)(2,1)} %collective-permute-done.43, bf16[4,384,1024]{2,1,0:T(8,128)(2,1)} %get-tuple-element.268), kind=kLoop, calls=%fused_computation | loop fusion | flops 6291456 | bytes 9437184 | tf_op jit(solution)/shard_map/convert_element_type | solution.py:865
  277.6 6.7 %collective-permute-done.42 = bf16[272,1024]{1,0:T(8,128)(2,1)S(1)} collective-permute-done((bf16[272,1024]{1,0:T(8,128)(2,1)}, bf16[272,1024]{1,0:T(8,128)(2,1)S(1)}, u32[]{:S(2)}, u32[]{:S(2)}) %collective-permute-start.42) | collective-permute-done | bytes 557088 | tf_op jit(solution)/shard_map/ppermute | solution.py:435
  289.7 6.6 %collective-permute-done.41 = bf16[272,1024]{1,0:T(8,128)(2,1)} collective-permute-done((bf16[272,1024]{1,0:T(8,128)(2,1)}, bf16[272,1024]{1,0:T(8,128)(2,1)}, u32[]{:S(2)}, u32[]{:S(2)}) %collective-permute-start.41) | collective-permute-done | bytes 557088 | tf_op jit(solution)/shard_map/ppermute | solution.py:435
  296.3 4.8 %collective-permute-done.44 = bf16[272,1024]{1,0:T(8,128)(2,1)} collective-permute-done((bf16[272,1024]{1,0:T(8,128)(2,1)}, bf16[272,1024]{1,0:T(8,128)(2,1)}, u32[]{:S(2)}, u32[]{:S(2)}) %collective-permute-start.44) | collective-permute-done | bytes 557088 | tf_op jit(solution)/shard_map/ppermute | solution.py:435
  301.1 2.5 add_convert_fusion.6
  303.6 1.7 collective-permute-start.48
  306.9 3.3 owner_sum.2
  310.2 2.8 collective-permute-done.45.mine_ref
  313.1 1.7 collective-permute-done.48.add_ref
  314.7 6.6 %turn.1 = (bf16[512,1152]{1,0:T(8,128)(2,1)}, bf16[512,1152]{1,0:T(8,128)(2,1)}, bf16[256,1024]{1,0:T(8,128)(2,1)}, f32[256,1024]{1,0:T(8,128)}) custom-call(s32[1]{0:T(128)} %bitcast.e_ref, bf16[272,1024]{1,0:T(8,128)(2,1)} %get-tuple-element.283.sum_ref, bf16[272,1024]{1,0:T(8,128)(2,1)} %collective-permute-done.45.mine_ref, ...), custom_call_target="tpu_custom_call" | custom-call | flops 1000 | bytes 1000 | tf_op jit(solution)/shard_map/turn/pallas_call | solution.py:848
  323.0 2.0 add_convert_fusion.11
  326.4 2.0 add_convert_fusion.12
  329.6 4.0 all-to-all-start.3
  333.6 16.2 %attend_back.1 = (bf16[512,1152]{1,0:T(8,128)(2,1)}, bf16[512,1152]{1,0:T(8,128)(2,1)}, bf16[512,1024]{1,0:T(8,128)(2,1)}, bf16[512,1024]{1,0:T(8,128)(2,1)}, bf16[256,1024]{1,0:T(8,128)(2,1)}) custom-call(s32[1]{0:T(128)} %bitcast.e_ref, bf16[256,1024]{1,0:T(8,128)(2,1)} %x_ref.5, s32[256,1]{1,0:T(8,128)} %copy.30.column_ref, s32[1,256]{1,0:T(1,128)} %row_ref.3, ...), custom_call_target="tpu_custom_call" | custom-call | flops 1000 | bytes 1000 | tf_op jit(solution)/shard_map/attend_back/pallas_call | solution.py:848
  350.0 1.6 add_convert_fusion.2
  353.4 2.3 add_convert_fusion.9
  355.6 2.0 collective-permute-start.55
  358.9 3.4 collective-permute-done.66
  367.6 9.0 %collective-permute-done.58 = bf16[128,1152]{1,0:T(8,128)(2,1)S(1)} collective-permute-done((bf16[128,1152]{1,0:T(8,128)(2,1)S(1)}, bf16[128,1152]{1,0:T(8,128)(2,1)S(1)}, u32[]{:S(2)}, u32[]{:S(2)}) %collective-permute-start.58) | collective-permute-done | bytes 294944 | tf_op jit(solution)/shard_map/ppermute | solution.py:435
  378.4 1.6 collective-permute-start.61
  381.0 9.2 %collective-permute-done.61.refs_4_ = bf16[128,1024]{1,0:T(8,128)(2,1)S(1)} collective-permute-done((bf16[128,1024]{1,0:T(8,128)(2,1)S(1)}, bf16[128,1024]{1,0:T(8,128)(2,1)S(1)}, u32[]{:S(2)}, u32[]{:S(2)}) %collective-permute-start.61) | collective-permute-done | bytes 262176 | tf_op jit(solution)/shard_map/ppermute | solution.py:435
  391.3 2.8 plane.1
  394.1 1.9 collective-permute-start.68
  396.0 2.5 collective-permute-start.69
  398.5 13.1 %all-to-all-done.3.one_ref.two_ref = bf16[4,384,1024]{2,1,0:T(8,128)(2,1)S(1)} async-done(((bf16[4,384,1024]{2,1,0:T(8,128)(2,1)}), bf16[4,384,1024]{2,1,0:T(8,128)(2,1)S(1)}, u32[]{:S(2)}, u32[]{:S(2)}) %all-to-all-start.3) | async-done | bytes 3145760 | tf_op jit(solution)/shard_map/all_to_all | solution.py:876
  411.6 2.4 collective-permute-start.70
  414.1 3.1 add_convert_fusion.8
  417.1 3.1 owner_sum.3
  420.9 2.0 settle.1
  (233 shorter events, 58.9 us)
Async XLA Ops:
  2.6 14.3 %collective-permute-start = (bf16[32,3200]{1,0:T(8,128)(2,1)}, bf16[32,3200]{1,0:T(8,128)(2,1)S(1)}, u32[]{:S(2)}, u32[]{:S(2)}) collective-permute-start(bf16[32,3200]{1,0:T(8,128)(2,1)} %pack.1), channel_id=1, source_target_pairs={{0,1},{1,0},{2,3},{3,2},{4,5},{5,4},{6,7},{7,6},{8,9},{9,8},{10,11... | collective-permute-start | bytes 614408 | tf_op jit(solution)/shard_map/ppermute | solution.py:439
  5.6 17.9 %collective-permute-start.1 = (bf16[32,3200]{1,0:T(8,128)(2,1)}, bf16[32,3200]{1,0:T(8,128)(2,1)S(1)}, u32[]{:S(2)}, u32[]{:S(2)}) collective-permute-start(bf16[32,3200]{1,0:T(8,128)(2,1)} %pack.1), channel_id=1, source_target_pairs={{0,2},{1,3},{2,0},{3,1},{4,6},{5,7},{6,4},{7,5},{8,10},{9,11},{10,... | collective-permute-start | bytes 614408 | tf_op jit(solution)/shard_map/ppermute | solution.py:439
  8.2 15.3 %collective-permute-start.2 = (bf16[32,3200]{1,0:T(8,128)(2,1)}, bf16[32,3200]{1,0:T(8,128)(2,1)S(1)}, u32[]{:S(2)}, u32[]{:S(2)}) collective-permute-start(bf16[32,3200]{1,0:T(8,128)(2,1)} %pack.1), channel_id=1, source_target_pairs={{0,3},{1,2},{2,1},{3,0},{4,7},{5,6},{6,5},{7,4},{8,11},{9,10},{10,... | collective-permute-start | bytes 614408 | tf_op jit(solution)/shard_map/ppermute | solution.py:439
  8.2 15.6 %collective-permute-start.3 = (bf16[256,1024]{1,0:T(8,128)(2,1)}, bf16[256,1024]{1,0:T(8,128)(2,1)S(1)}, u32[]{:S(2)}, u32[]{:S(2)}) collective-permute-start(bf16[256,1024]{1,0:T(8,128)(2,1)} %grad_ref.1), channel_id=1, source_target_pairs={{0,8},{4,12},{8,0},{12,4},{16,24},{20,28},{24,16},{28,20},{1,9},{5... | collective-permute-start | bytes 1572872 | tf_op jit(solution)/shard_map/ppermute | solution.py:435
  9.9 13.9 %collective-permute-start.4 = (bf16[256,1024]{1,0:T(8,128)(2,1)}, bf16[256,1024]{1,0:T(8,128)(2,1)S(1)}, u32[]{:S(2)}, u32[]{:S(2)}) collective-permute-start(bf16[256,1024]{1,0:T(8,128)(2,1)} %grad_ref.1), channel_id=1, source_target_pairs={{0,16},{4,20},{8,24},{12,28},{16,0},{20,4},{24,8},{28,12},{1,17},{... | collective-permute-start | bytes 1572872 | tf_op jit(solution)/shard_map/ppermute | solution.py:435
  16.8 16.7 %collective-permute-start.9 = (bf16[256,1024]{1,0:T(8,128)(2,1)S(1)}, bf16[256,1024]{1,0:T(8,128)(2,1)S(1)}, u32[]{:S(2)}, u32[]{:S(2)}) collective-permute-start(bf16[256,1024]{1,0:T(8,128)(2,1)S(1)} %copy-done.2), channel_id=1, source_target_pairs={{0,1},{1,0},{2,3},{3,2},{4,5},{5,4},{6,7},{7,6},{8,9},{9,8},{10,11... | collective-permute-start | bytes 1572872 | tf_op jit(solution)/shard_map/ppermute | solution.py:439
  23.9 10.5 %collective-permute-start.5 = (bf16[128,1152]{1,0:T(8,128)(2,1)S(1)}, bf16[128,1152]{1,0:T(8,128)(2,1)S(1)}, u32[]{:S(2)}, u32[]{:S(2)}) collective-permute-start(bf16[128,1152]{1,0:T(8,128)(2,1)S(1)} %slice.99.refs_0_), channel_id=1, source_target_pairs={{0,8},{4,12},{8,0},{12,4},{16,24},{20,28},{24,16},{28,20},{1,9},{5... | collective-permute-start | bytes 884744 | tf_op jit(solution)/shard_map/ppermute | solution.py:435
  25.5 8.9 %collective-permute-start.7 = (bf16[128,1024]{1,0:T(8,128)(2,1)S(1)}, bf16[128,1024]{1,0:T(8,128)(2,1)S(1)}, u32[]{:S(2)}, u32[]{:S(2)}) collective-permute-start(bf16[128,1024]{1,0:T(8,128)(2,1)S(1)} %slice.100.refs_8_), channel_id=1, source_target_pairs={{0,16},{4,20},{8,24},{12,28},{16,0},{20,4},{24,8},{28,12},{1,17},{... | collective-permute-start | bytes 786440 | tf_op jit(solution)/shard_map/ppermute | solution.py:435
  35.2 83.8 %all-to-all-start = ((bf16[4,384,1024]{2,1,0:T(8,128)(2,1)}), bf16[4,384,1024]{2,1,0:T(8,128)(2,1)S(1)}, u32[]{:S(2)}, u32[]{:S(2)}) async-start(bf16[4,384,1024]{2,1,0:T(8,128)(2,1)} %maximum_maximum_fusion), calls=%async_computation | async-start | bytes 6291456 | tf_op jit(solution)/shard_map/all_to_all | solution.py:876
  38.9 9.5 %collective-permute-start.18 = (bf16[128,1024]{1,0:T(8,128)(2,1)}, bf16[128,1024]{1,0:T(8,128)(2,1)}, u32[]{:S(2)}, u32[]{:S(2)}) collective-permute-start(bf16[128,1024]{1,0:T(8,128)(2,1)} %copy-done.14), channel_id=1, source_target_pairs={{0,8},{4,12},{8,0},{12,4},{16,24},{20,28},{24,16},{28,20},{1,9},{5... | collective-permute-start | bytes 786440 | tf_op jit(solution)/shard_map/ppermute | solution.py:435
  40.3 10.5 %collective-permute-start.13 = (bf16[128,1152]{1,0:T(8,128)(2,1)S(1)}, bf16[128,1152]{1,0:T(8,128)(2,1)}, u32[]{:S(2)}, u32[]{:S(2)}) collective-permute-start(bf16[128,1152]{1,0:T(8,128)(2,1)S(1)} %slice.99.refs_0_), channel_id=1, source_target_pairs={{0,16},{4,20},{8,24},{12,28},{16,0},{20,4},{24,8},{28,12},{1,17},{... | collective-permute-start | bytes 884744 | tf_op jit(solution)/shard_map/ppermute | solution.py:435
  41.5 9.8 %collective-permute-start.14 = (bf16[128,1152]{1,0:T(8,128)(2,1)S(1)}, bf16[128,1152]{1,0:T(8,128)(2,1)}, u32[]{:S(2)}, u32[]{:S(2)}) collective-permute-start(bf16[128,1152]{1,0:T(8,128)(2,1)S(1)} %slice.99.refs_0_), channel_id=1, source_target_pairs={{0,4},{4,0},{8,12},{12,8},{16,20},{20,16},{24,28},{28,24},{1,5},{5... | collective-permute-start | bytes 884744 | tf_op jit(solution)/shard_map/ppermute | solution.py:435
  41.5 9.2 %collective-permute-start.19 = (bf16[128,1024]{1,0:T(8,128)(2,1)}, bf16[128,1024]{1,0:T(8,128)(2,1)}, u32[]{:S(2)}, u32[]{:S(2)}) collective-permute-start(bf16[128,1024]{1,0:T(8,128)(2,1)} %copy-done.14), channel_id=1, source_target_pairs={{0,4},{4,0},{8,12},{12,8},{16,20},{20,16},{24,28},{28,24},{1,5},{5... | collective-permute-start | bytes 786440 | tf_op jit(solution)/shard_map/ppermute | solution.py:435
  42.0 10.7 %collective-permute-start.8 = (bf16[128,1024]{1,0:T(8,128)(2,1)}, bf16[128,1024]{1,0:T(8,128)(2,1)}, u32[]{:S(2)}, u32[]{:S(2)}) collective-permute-start(bf16[128,1024]{1,0:T(8,128)(2,1)} %copy-done.21), channel_id=1, source_target_pairs={{0,8},{4,12},{8,0},{12,4},{16,24},{20,28},{24,16},{28,20},{1,9},{5... | collective-permute-start | bytes 786440 | tf_op jit(solution)/shard_map/ppermute | solution.py:435
  50.8 9.0 %collective-permute-start.15 = (bf16[128,1152]{1,0:T(8,128)(2,1)}, bf16[128,1152]{1,0:T(8,128)(2,1)}, u32[]{:S(2)}, u32[]{:S(2)}) collective-permute-start(bf16[128,1152]{1,0:T(8,128)(2,1)} %copy-done.17), channel_id=1, source_target_pairs={{0,4},{4,0},{8,12},{12,8},{16,20},{20,16},{24,28},{28,24},{1,5},{5... | collective-permute-start | bytes 884744 | tf_op jit(solution)/shard_map/ppermute | solution.py:435
  57.3 20.1 %collective-permute-start.10 = (bf16[128,1024]{1,0:T(8,128)(2,1)}, bf16[128,1024]{1,0:T(8,128)(2,1)}, u32[]{:S(2)}, u32[]{:S(2)}) collective-permute-start(bf16[128,1024]{1,0:T(8,128)(2,1)} %slice.101.refs_0_), channel_id=1, source_target_pairs={{0,8},{4,12},{8,0},{12,4},{16,24},{20,28},{24,16},{28,20},{1,9},{5... | collective-permute-start | bytes 786440 | tf_op jit(solution)/shard_map/ppermute | solution.py:435
  58.6 18.8 %collective-permute-start.11 = (bf16[128,1024]{1,0:T(8,128)(2,1)}, bf16[128,1024]{1,0:T(8,128)(2,1)}, u32[]{:S(2)}, u32[]{:S(2)}) collective-permute-start(bf16[128,1024]{1,0:T(8,128)(2,1)} %slice.101.refs_0_), channel_id=1, source_target_pairs={{0,16},{4,20},{8,24},{12,28},{16,0},{20,4},{24,8},{28,12},{1,17},{... | collective-permute-start | bytes 786440 | tf_op jit(solution)/shard_map/ppermute | solution.py:435
  59.8 17.6 %collective-permute-start.12 = (bf16[128,1024]{1,0:T(8,128)(2,1)}, bf16[128,1024]{1,0:T(8,128)(2,1)}, u32[]{:S(2)}, u32[]{:S(2)}) collective-permute-start(bf16[128,1024]{1,0:T(8,128)(2,1)} %slice.101.refs_0_), channel_id=1, source_target_pairs={{0,24},{4,28},{8,16},{12,20},{16,8},{20,12},{24,0},{28,4},{1,25},{... | collective-permute-start | bytes 786440 | tf_op jit(solution)/shard_map/ppermute | solution.py:435
  60.8 29.4 %collective-permute-start.30 = (bf16[256,1024]{1,0:T(8,128)(2,1)}, bf16[256,1024]{1,0:T(8,128)(2,1)}, u32[]{:S(2)}, u32[]{:S(2)}) collective-permute-start(bf16[256,1024]{1,0:T(8,128)(2,1)} %copy-done.6), channel_id=1, source_target_pairs={{0,16},{4,20},{8,24},{12,28},{16,0},{20,4},{24,8},{28,12},{1,17},{... | collective-permute-start | bytes 1572872 | tf_op jit(solution)/shard_map/ppermute | solution.py:435
  85.6 27.8 %collective-permute-start.27 = (bf16[288,1024]{1,0:T(8,128)(2,1)}, bf16[288,1024]{1,0:T(8,128)(2,1)S(1)}, u32[]{:S(2)}, u32[]{:S(2)}) collective-permute-start(bf16[288,1024]{1,0:T(8,128)(2,1)} %get-tuple-element.193.refs_0_.normed2_ref), channel_id=1, source_target_pairs={{0,8},{4,12},{8,0},{12,4},{16,24},{20,28},{24,16},{28,20},{1,9},{5... | collective-permute-start | bytes 1769480 | tf_op jit(solution)/shard_map/ppermute | solution.py:435
  86.7 26.8 %collective-permute-start.28 = (bf16[288,1024]{1,0:T(8,128)(2,1)}, bf16[288,1024]{1,0:T(8,128)(2,1)S(1)}, u32[]{:S(2)}, u32[]{:S(2)}) collective-permute-start(bf16[288,1024]{1,0:T(8,128)(2,1)} %get-tuple-element.193.refs_0_.normed2_ref), channel_id=1, source_target_pairs={{0,16},{4,20},{8,24},{12,28},{16,0},{20,4},{24,8},{28,12},{1,17},{... | collective-permute-start | bytes 1769480 | tf_op jit(solution)/shard_map/ppermute | solution.py:435
  87.4 31.5 %collective-permute-start.29 = (bf16[288,1024]{1,0:T(8,128)(2,1)}, bf16[288,1024]{1,0:T(8,128)(2,1)}, u32[]{:S(2)}, u32[]{:S(2)}) collective-permute-start(bf16[288,1024]{1,0:T(8,128)(2,1)} %get-tuple-element.193.refs_0_.normed2_ref), channel_id=1, source_target_pairs={{0,1},{1,0},{2,3},{3,2},{4,5},{5,4},{6,7},{7,6},{8,9},{9,8},{10,11... | collective-permute-start | bytes 1769480 | tf_op jit(solution)/shard_map/ppermute | solution.py:439
  89.5 23.2 %collective-permute-start.31 = (bf16[256,1024]{1,0:T(8,128)(2,1)S(1)}, bf16[256,1024]{1,0:T(8,128)(2,1)S(1)}, u32[]{:S(2)}, u32[]{:S(2)}) collective-permute-start(bf16[256,1024]{1,0:T(8,128)(2,1)S(1)} %copy-done.9), channel_id=1, source_target_pairs={{0,8},{4,12},{8,0},{12,4},{16,24},{20,28},{24,16},{28,20},{1,9},{5... | collective-permute-start | bytes 1572872 | tf_op jit(solution)/shard_map/ppermute | solution.py:435
  90.2 23.3 %collective-permute-start.32 = (bf16[256,1024]{1,0:T(8,128)(2,1)S(1)}, bf16[256,1024]{1,0:T(8,128)(2,1)S(1)}, u32[]{:S(2)}, u32[]{:S(2)}) collective-permute-start(bf16[256,1024]{1,0:T(8,128)(2,1)S(1)} %copy-done.9), channel_id=1, source_target_pairs={{0,16},{4,20},{8,24},{12,28},{16,0},{20,4},{24,8},{28,12},{1,17},{... | collective-permute-start | bytes 1572872 | tf_op jit(solution)/shard_map/ppermute | solution.py:435
  118.9 40.9 %collective-permute-start.38 = (bf16[4,384,1024]{2,1,0:T(8,128)(2,1)S(1)}, bf16[4,384,1024]{2,1,0:T(8,128)(2,1)}, u32[]{:S(2)}, u32[]{:S(2)}) collective-permute-start(bf16[4,384,1024]{2,1,0:T(8,128)(2,1)S(1)} %all-to-all-done.refs_16_), channel_id=1, source_target_pairs={{0,4},{4,0},{8,12},{12,8},{16,20},{20,16},{24,28},{28,24},{1,5},{5... | collective-permute-start | bytes 9437192 | tf_op jit(solution)/shard_map/ppermute | solution.py:435
  118.9 16.6 %collective-permute-start.35 = (bf16[288,1024]{1,0:T(8,128)(2,1)}, bf16[288,1024]{1,0:T(8,128)(2,1)}, u32[]{:S(2)}, u32[]{:S(2)}) collective-permute-start(bf16[288,1024]{1,0:T(8,128)(2,1)} %collective-permute-done.29.refs_4_), channel_id=1, source_target_pairs={{0,16},{4,20},{8,24},{12,28},{16,0},{20,4},{24,8},{28,12},{1,17},{... | collective-permute-start | bytes 1769480 | tf_op jit(solution)/shard_map/ppermute | solution.py:435
  120.2 15.1 %collective-permute-start.36 = (bf16[256,1024]{1,0:T(8,128)(2,1)}, bf16[256,1024]{1,0:T(8,128)(2,1)}, u32[]{:S(2)}, u32[]{:S(2)}) collective-permute-start(bf16[256,1024]{1,0:T(8,128)(2,1)} %copy-done.11), channel_id=1, source_target_pairs={{0,8},{4,12},{8,0},{12,4},{16,24},{20,28},{24,16},{28,20},{1,9},{5... | collective-permute-start | bytes 1572872 | tf_op jit(solution)/shard_map/ppermute | solution.py:435
  121.3 90.7 %all-to-all-start.1 = ((bf16[4,384,1024]{2,1,0:T(8,128)(2,1)}), bf16[4,384,1024]{2,1,0:T(8,128)(2,1)}, u32[]{:S(2)}, u32[]{:S(2)}) async-start(bf16[4,384,1024]{2,1,0:T(8,128)(2,1)} %maximum_maximum_fusion.1), calls=%async_computation.1 | async-start | bytes 6291456 | tf_op jit(solution)/shard_map/all_to_all | solution.py:876
  126.6 21.0 %collective-permute-start.33 = (bf16[288,1024]{1,0:T(8,128)(2,1)}, bf16[288,1024]{1,0:T(8,128)(2,1)}, u32[]{:S(2)}, u32[]{:S(2)}) collective-permute-start(bf16[288,1024]{1,0:T(8,128)(2,1)} %copy-done.4), channel_id=1, source_target_pairs={{0,16},{4,20},{8,24},{12,28},{16,0},{20,4},{24,8},{28,12},{1,17},{... | collective-permute-start | bytes 1769480 | tf_op jit(solution)/shard_map/ppermute | solution.py:435
  127.3 20.7 %collective-permute-start.34 = (bf16[288,1024]{1,0:T(8,128)(2,1)}, bf16[288,1024]{1,0:T(8,128)(2,1)}, u32[]{:S(2)}, u32[]{:S(2)}) collective-permute-start(bf16[288,1024]{1,0:T(8,128)(2,1)} %collective-permute-done.29.refs_4_), channel_id=1, source_target_pairs={{0,8},{4,12},{8,0},{12,4},{16,24},{20,28},{24,16},{28,20},{1,9},{5... | collective-permute-start | bytes 1769480 | tf_op jit(solution)/shard_map/ppermute | solution.py:435
  135.5 24.3 %collective-permute-start.37 = (bf16[288,1024]{1,0:T(8,128)(2,1)}, bf16[288,1024]{1,0:T(8,128)(2,1)}, u32[]{:S(2)}, u32[]{:S(2)}) collective-permute-start(bf16[288,1024]{1,0:T(8,128)(2,1)} %collective-permute-done.35.refs_6_), channel_id=1, source_target_pairs={{0,8},{4,12},{8,0},{12,4},{16,24},{20,28},{24,16},{28,20},{1,9},{5... | collective-permute-start | bytes 1769480 | tf_op jit(solution)/shard_map/ppermute | solution.py:435
  181.8 25.0 %collective-permute-start.39 = (bf16[4,384,1024]{2,1,0:T(8,128)(2,1)}, bf16[4,384,1024]{2,1,0:T(8,128)(2,1)S(1)}, u32[]{:S(2)}, u32[]{:S(2)}) collective-permute-start(bf16[4,384,1024]{2,1,0:T(8,128)(2,1)} %get-tuple-element.229), channel_id=1, source_target_pairs={{0,4},{4,0},{8,12},{12,8},{16,20},{20,16},{24,28},{28,24},{1,5},{5... | collective-permute-start | bytes 9437192 | tf_op jit(solution)/shard_map/ppermute | solution.py:435
  212.4 76.5 %all-to-all-start.2 = ((bf16[4,384,1024]{2,1,0:T(8,128)(2,1)}), bf16[4,384,1024]{2,1,0:T(8,128)(2,1)S(1)}, u32[]{:S(2)}, u32[]{:S(2)}) async-start(bf16[4,384,1024]{2,1,0:T(8,128)(2,1)} %add_convert_fusion.1), calls=%async_computation.2 | async-start | bytes 6291456 | tf_op jit(solution)/shard_map/all_to_all | solution.py:876
  243.1 28.3 %collective-permute-start.43 = (bf16[4,384,1024]{2,1,0:T(8,128)(2,1)}, bf16[4,384,1024]{2,1,0:T(8,128)(2,1)}, u32[]{:S(2)}, u32[]{:S(2)}) collective-permute-start(bf16[4,384,1024]{2,1,0:T(8,128)(2,1)} %get-tuple-element.269), channel_id=1, source_target_pairs={{0,4},{4,0},{8,12},{12,8},{16,20},{20,16},{24,28},{28,24},{1,5},{5... | collective-permute-start | bytes 9437192 | tf_op jit(solution)/shard_map/ppermute | solution.py:435
  268.5 15.8 %collective-permute-start.42 = (bf16[272,1024]{1,0:T(8,128)(2,1)}, bf16[272,1024]{1,0:T(8,128)(2,1)S(1)}, u32[]{:S(2)}, u32[]{:S(2)}) collective-permute-start(bf16[272,1024]{1,0:T(8,128)(2,1)} %get-tuple-element.267), channel_id=1, source_target_pairs={{0,8},{4,12},{8,0},{12,4},{16,24},{20,28},{24,16},{28,20},{1,9},{5... | collective-permute-start | bytes 1671176 | tf_op jit(solution)/shard_map/ppermute | solution.py:435
  269.6 26.7 %collective-permute-start.41 = (bf16[272,1024]{1,0:T(8,128)(2,1)}, bf16[272,1024]{1,0:T(8,128)(2,1)}, u32[]{:S(2)}, u32[]{:S(2)}) collective-permute-start(bf16[272,1024]{1,0:T(8,128)(2,1)} %get-tuple-element.265), channel_id=1, source_target_pairs={{0,8},{4,12},{8,0},{12,4},{16,24},{20,28},{24,16},{28,20},{1,9},{5... | collective-permute-start | bytes 1671176 | tf_op jit(solution)/shard_map/ppermute | solution.py:435
  270.6 15.5 %collective-permute-start.46 = (bf16[272,1024]{1,0:T(8,128)(2,1)}, bf16[272,1024]{1,0:T(8,128)(2,1)S(1)}, u32[]{:S(2)}, u32[]{:S(2)}) collective-permute-start(bf16[272,1024]{1,0:T(8,128)(2,1)} %get-tuple-element.288), channel_id=1, source_target_pairs={{0,16},{4,20},{8,24},{12,28},{16,0},{20,4},{24,8},{28,12},{1,17},{... | collective-permute-start | bytes 1671176 | tf_op jit(solution)/shard_map/ppermute | solution.py:435
  285.3 15.8 %collective-permute-start.44 = (bf16[272,1024]{1,0:T(8,128)(2,1)}, bf16[272,1024]{1,0:T(8,128)(2,1)}, u32[]{:S(2)}, u32[]{:S(2)}) collective-permute-start(bf16[272,1024]{1,0:T(8,128)(2,1)} %add_convert_fusion.7), channel_id=1, source_target_pairs={{0,16},{4,20},{8,24},{12,28},{16,0},{20,4},{24,8},{28,12},{1,17},{... | collective-permute-start | bytes 1671176 | tf_op jit(solution)/shard_map/ppermute | solution.py:435
  287.2 23.1 %collective-permute-start.47 = (bf16[272,1024]{1,0:T(8,128)(2,1)}, bf16[272,1024]{1,0:T(8,128)(2,1)}, u32[]{:S(2)}, u32[]{:S(2)}) collective-permute-start(bf16[272,1024]{1,0:T(8,128)(2,1)} %add_convert_fusion.5), channel_id=1, source_target_pairs={{0,8},{4,12},{8,0},{12,4},{16,24},{20,28},{24,16},{28,20},{1,9},{5... | collective-permute-start | bytes 1671176 | tf_op jit(solution)/shard_map/ppermute | solution.py:435
  288.9 24.2 %collective-permute-start.45 = (bf16[272,1024]{1,0:T(8,128)(2,1)}, bf16[272,1024]{1,0:T(8,128)(2,1)}, u32[]{:S(2)}, u32[]{:S(2)}) collective-permute-start(bf16[272,1024]{1,0:T(8,128)(2,1)} %get-tuple-element.286), channel_id=1, source_target_pairs={{0,16},{4,20},{8,24},{12,28},{16,0},{20,4},{24,8},{28,12},{1,17},{... | collective-permute-start | bytes 1671176 | tf_op jit(solution)/shard_map/ppermute | solution.py:435
  303.6 11.1 %collective-permute-start.48 = (bf16[272,1024]{1,0:T(8,128)(2,1)}, bf16[272,1024]{1,0:T(8,128)(2,1)}, u32[]{:S(2)}, u32[]{:S(2)}) collective-permute-start(bf16[272,1024]{1,0:T(8,128)(2,1)} %add_convert_fusion.6), channel_id=1, source_target_pairs={{0,1},{1,0},{2,3},{3,2},{4,5},{5,4},{6,7},{7,6},{8,9},{9,8},{10,11... | collective-permute-start | bytes 1671176 | tf_op jit(solution)/shard_map/ppermute | solution.py:439
  305.3 17.6 %collective-permute-start.51 = (bf16[256,1024]{1,0:T(8,128)(2,1)}, bf16[256,1024]{1,0:T(8,128)(2,1)}, u32[]{:S(2)}, u32[]{:S(2)}) collective-permute-start(bf16[256,1024]{1,0:T(8,128)(2,1)} %get-tuple-element.304), channel_id=1, source_target_pairs={{0,16},{4,20},{8,24},{12,28},{16,0},{20,4},{24,8},{28,12},{1,17},{... | collective-permute-start | bytes 1572872 | tf_op jit(solution)/shard_map/ppermute | solution.py:435
  306.2 20.2 %collective-permute-start.49 = (bf16[256,1024]{1,0:T(8,128)(2,1)}, bf16[256,1024]{1,0:T(8,128)(2,1)}, u32[]{:S(2)}, u32[]{:S(2)}) collective-permute-start(bf16[256,1024]{1,0:T(8,128)(2,1)} %get-tuple-element.302), channel_id=1, source_target_pairs={{0,8},{4,12},{8,0},{12,4},{16,24},{20,28},{24,16},{28,20},{1,9},{5... | collective-permute-start | bytes 1572872 | tf_op jit(solution)/shard_map/ppermute | solution.py:435
  321.4 28.6 %collective-permute-start.64 = (bf16[512,1152]{1,0:T(8,128)(2,1)}, bf16[512,1152]{1,0:T(8,128)(2,1)}, u32[]{:S(2)}, u32[]{:S(2)}) collective-permute-start(bf16[512,1152]{1,0:T(8,128)(2,1)} %get-tuple-element.318), channel_id=1, source_target_pairs={{0,4},{4,0},{8,12},{12,8},{16,20},{20,16},{24,28},{28,24},{1,5},{5... | collective-permute-start | bytes 3538952 | tf_op jit(solution)/shard_map/ppermute | solution.py:435
  321.4 28.5 %collective-permute-start.53 = (bf16[256,1024]{1,0:T(8,128)(2,1)}, bf16[256,1024]{1,0:T(8,128)(2,1)}, u32[]{:S(2)}, u32[]{:S(2)}) collective-permute-start(bf16[256,1024]{1,0:T(8,128)(2,1)} %get-tuple-element.305), channel_id=1, source_target_pairs={{0,8},{4,12},{8,0},{12,4},{16,24},{20,28},{24,16},{28,20},{1,9},{5... | collective-permute-start | bytes 1572872 | tf_op jit(solution)/shard_map/ppermute | solution.py:435
  322.4 27.4 %collective-permute-start.54 = (bf16[256,1024]{1,0:T(8,128)(2,1)}, bf16[256,1024]{1,0:T(8,128)(2,1)}, u32[]{:S(2)}, u32[]{:S(2)}) collective-permute-start(bf16[256,1024]{1,0:T(8,128)(2,1)} %get-tuple-element.306), channel_id=1, source_target_pairs={{0,16},{4,20},{8,24},{12,28},{16,0},{20,4},{24,8},{28,12},{1,17},{... | collective-permute-start | bytes 1572872 | tf_op jit(solution)/shard_map/ppermute | solution.py:435
  325.0 24.8 %collective-permute-start.52 = (bf16[256,1024]{1,0:T(8,128)(2,1)}, bf16[256,1024]{1,0:T(8,128)(2,1)}, u32[]{:S(2)}, u32[]{:S(2)}) collective-permute-start(bf16[256,1024]{1,0:T(8,128)(2,1)} %add_convert_fusion.11), channel_id=1, source_target_pairs={{0,8},{4,12},{8,0},{12,4},{16,24},{20,28},{24,16},{28,20},{1,9},{5... | collective-permute-start | bytes 1572872 | tf_op jit(solution)/shard_map/ppermute | solution.py:435
  328.4 21.5 %collective-permute-start.50 = (bf16[256,1024]{1,0:T(8,128)(2,1)}, bf16[256,1024]{1,0:T(8,128)(2,1)}, u32[]{:S(2)}, u32[]{:S(2)}) collective-permute-start(bf16[256,1024]{1,0:T(8,128)(2,1)} %add_convert_fusion.12), channel_id=1, source_target_pairs={{0,16},{4,20},{8,24},{12,28},{16,0},{20,4},{24,8},{28,12},{1,17},{... | collective-permute-start | bytes 1572872 | tf_op jit(solution)/shard_map/ppermute | solution.py:435
  329.6 82.1 %all-to-all-start.3 = ((bf16[4,384,1024]{2,1,0:T(8,128)(2,1)}), bf16[4,384,1024]{2,1,0:T(8,128)(2,1)S(1)}, u32[]{:S(2)}, u32[]{:S(2)}) async-start(bf16[4,384,1024]{2,1,0:T(8,128)(2,1)} %add_convert_fusion), calls=%async_computation.3 | async-start | bytes 6291456 | tf_op jit(solution)/shard_map/all_to_all | solution.py:876
  349.9 13.6 %collective-permute-start.56 = (bf16[512,1152]{1,0:T(8,128)(2,1)}, bf16[512,1152]{1,0:T(8,128)(2,1)S(1)}, u32[]{:S(2)}, u32[]{:S(2)}) collective-permute-start(bf16[512,1152]{1,0:T(8,128)(2,1)} %get-tuple-element.314), channel_id=1, source_target_pairs={{0,4},{4,0},{8,12},{12,8},{16,20},{20,16},{24,28},{28,24},{1,5},{5... | collective-permute-start | bytes 3538952 | tf_op jit(solution)/shard_map/ppermute | solution.py:435
  352.4 9.9 %collective-permute-start.66 = (bf16[128,1152]{1,0:T(8,128)(2,1)S(1)}, bf16[128,1152]{1,0:T(8,128)(2,1)S(1)}, u32[]{:S(2)}, u32[]{:S(2)}) collective-permute-start(bf16[128,1152]{1,0:T(8,128)(2,1)S(1)} %get-tuple-element.341), channel_id=1, source_target_pairs={{0,16},{4,20},{8,24},{12,28},{16,0},{20,4},{24,8},{28,12},{1,17},{... | collective-permute-start | bytes 884744 | tf_op jit(solution)/shard_map/ppermute | solution.py:435
  353.3 12.4 %collective-permute-start.60 = (bf16[512,1024]{1,0:T(8,128)(2,1)S(1)}, bf16[512,1024]{1,0:T(8,128)(2,1)S(1)}, u32[]{:S(2)}, u32[]{:S(2)}) collective-permute-start(bf16[512,1024]{1,0:T(8,128)(2,1)S(1)} %copy-done.45), channel_id=1, source_target_pairs={{0,4},{4,0},{8,12},{12,8},{16,20},{20,16},{24,28},{28,24},{1,5},{5... | collective-permute-start | bytes 3145736 | tf_op jit(solution)/shard_map/ppermute | solution.py:435
  355.6 58.4 %collective-permute-start.55 = (bf16[256,1024]{1,0:T(8,128)(2,1)}, bf16[256,1024]{1,0:T(8,128)(2,1)}, u32[]{:S(2)}, u32[]{:S(2)}) collective-permute-start(bf16[256,1024]{1,0:T(8,128)(2,1)} %add_convert_fusion.9), channel_id=1, source_target_pairs={{0,1},{1,0},{2,3},{3,2},{4,5},{5,4},{6,7},{7,6},{8,9},{9,8},{10,11... | collective-permute-start | bytes 1572872 | tf_op jit(solution)/shard_map/ppermute | solution.py:439
  357.7 20.7 %collective-permute-start.65 = (bf16[128,1152]{1,0:T(8,128)(2,1)S(1)}, bf16[128,1152]{1,0:T(8,128)(2,1)S(1)}, u32[]{:S(2)}, u32[]{:S(2)}) collective-permute-start(bf16[128,1152]{1,0:T(8,128)(2,1)S(1)} %get-tuple-element.342), channel_id=1, source_target_pairs={{0,16},{4,20},{8,24},{12,28},{16,0},{20,4},{24,8},{28,12},{1,17},{... | collective-permute-start | bytes 884744 | tf_op jit(solution)/shard_map/ppermute | solution.py:435
  362.4 17.6 %collective-permute-start.67 = (bf16[128,1152]{1,0:T(8,128)(2,1)S(1)}, bf16[128,1152]{1,0:T(8,128)(2,1)S(1)}, u32[]{:S(2)}, u32[]{:S(2)}) collective-permute-start(bf16[128,1152]{1,0:T(8,128)(2,1)S(1)} %add_convert_fusion.13), channel_id=1, source_target_pairs={{0,8},{4,12},{8,0},{12,4},{16,24},{20,28},{24,16},{28,20},{1,9},{5... | collective-permute-start | bytes 884744 | tf_op jit(solution)/shard_map/ppermute | solution.py:435
  364.6 12.1 %collective-permute-start.58 = (bf16[128,1152]{1,0:T(8,128)(2,1)S(1)}, bf16[128,1152]{1,0:T(8,128)(2,1)S(1)}, u32[]{:S(2)}, u32[]{:S(2)}) collective-permute-start(bf16[128,1152]{1,0:T(8,128)(2,1)S(1)} %get-tuple-element.344), channel_id=1, source_target_pairs={{0,8},{4,12},{8,0},{12,4},{16,24},{20,28},{24,16},{28,20},{1,9},{5... | collective-permute-start | bytes 884744 | tf_op jit(solution)/shard_map/ppermute | solution.py:435
  366.8 10.9 %collective-permute-start.62 = (bf16[128,1024]{1,0:T(8,128)(2,1)S(1)}, bf16[128,1024]{1,0:T(8,128)(2,1)S(1)}, u32[]{:S(2)}, u32[]{:S(2)}) collective-permute-start(bf16[128,1024]{1,0:T(8,128)(2,1)S(1)} %get-tuple-element.347), channel_id=1, source_target_pairs={{0,16},{4,20},{8,24},{12,28},{16,0},{20,4},{24,8},{28,12},{1,17},{... | collective-permute-start | bytes 786440 | tf_op jit(solution)/shard_map/ppermute | solution.py:435
  376.7 13.6 %collective-permute-start.57 = (bf16[128,1152]{1,0:T(8,128)(2,1)S(1)}, bf16[128,1152]{1,0:T(8,128)(2,1)S(1)}, u32[]{:S(2)}, u32[]{:S(2)}) collective-permute-start(bf16[128,1152]{1,0:T(8,128)(2,1)S(1)} %get-tuple-element.345), channel_id=1, source_target_pairs={{0,8},{4,12},{8,0},{12,4},{16,24},{20,28},{24,16},{28,20},{1,9},{5... | collective-permute-start | bytes 884744 | tf_op jit(solution)/shard_map/ppermute | solution.py:435
  377.7 12.6 %collective-permute-start.59 = (bf16[128,1152]{1,0:T(8,128)(2,1)S(1)}, bf16[128,1152]{1,0:T(8,128)(2,1)S(1)}, u32[]{:S(2)}, u32[]{:S(2)}) collective-permute-start(bf16[128,1152]{1,0:T(8,128)(2,1)S(1)} %add_convert_fusion.14), channel_id=1, source_target_pairs={{0,16},{4,20},{8,24},{12,28},{16,0},{20,4},{24,8},{28,12},{1,17},{... | collective-permute-start | bytes 884744 | tf_op jit(solution)/shard_map/ppermute | solution.py:435
  378.4 11.8 %collective-permute-start.61 = (bf16[128,1024]{1,0:T(8,128)(2,1)S(1)}, bf16[128,1024]{1,0:T(8,128)(2,1)S(1)}, u32[]{:S(2)}, u32[]{:S(2)}) collective-permute-start(bf16[128,1024]{1,0:T(8,128)(2,1)S(1)} %get-tuple-element.348), channel_id=1, source_target_pairs={{0,16},{4,20},{8,24},{12,28},{16,0},{20,4},{24,8},{28,12},{1,17},{... | collective-permute-start | bytes 786440 | tf_op jit(solution)/shard_map/ppermute | solution.py:435
  380.0 10.3 %collective-permute-start.63 = (bf16[128,1024]{1,0:T(8,128)(2,1)S(1)}, bf16[128,1024]{1,0:T(8,128)(2,1)S(1)}, u32[]{:S(2)}, u32[]{:S(2)}) collective-permute-start(bf16[128,1024]{1,0:T(8,128)(2,1)S(1)} %add_convert_fusion.15), channel_id=1, source_target_pairs={{0,8},{4,12},{8,0},{12,4},{16,24},{20,28},{24,16},{28,20},{1,9},{5... | collective-permute-start | bytes 786440 | tf_op jit(solution)/shard_map/ppermute | solution.py:435
  394.1 26.1 %collective-permute-start.68 = (bf16[32,3328]{1,0:T(8,128)(2,1)}, bf16[32,3328]{1,0:T(8,128)(2,1)S(1)}, u32[]{:S(2)}, u32[]{:S(2)}) collective-permute-start(bf16[32,3328]{1,0:T(8,128)(2,1)} %get-tuple-element.320), channel_id=1, source_target_pairs={{0,1},{1,0},{2,3},{3,2},{4,5},{5,4},{6,7},{7,6},{8,9},{9,8},{10,11... | collective-permute-start | bytes 638984 | tf_op jit(solution)/shard_map/ppermute | solution.py:439
  396.0 24.2 %collective-permute-start.69 = (bf16[32,3328]{1,0:T(8,128)(2,1)}, bf16[32,3328]{1,0:T(8,128)(2,1)}, u32[]{:S(2)}, u32[]{:S(2)}) collective-permute-start(bf16[32,3328]{1,0:T(8,128)(2,1)} %get-tuple-element.321), channel_id=1, source_target_pairs={{0,2},{1,3},{2,0},{3,1},{4,6},{5,7},{6,4},{7,5},{8,10},{9,11},{10,... | collective-permute-start | bytes 638984 | tf_op jit(solution)/shard_map/ppermute | solution.py:439
  411.6 8.6 %collective-permute-start.70 = (bf16[32,3328]{1,0:T(8,128)(2,1)}, bf16[32,3328]{1,0:T(8,128)(2,1)}, u32[]{:S(2)}, u32[]{:S(2)}) collective-permute-start(bf16[32,3328]{1,0:T(8,128)(2,1)} %get-tuple-element.324), channel_id=1, source_target_pairs={{0,3},{1,2},{2,1},{3,0},{4,7},{5,6},{6,5},{7,4},{8,11},{9,10},{10,... | collective-permute-start | bytes 638984 | tf_op jit(solution)/shard_map/ppermute | solution.py:439
  (57 other events, 465.3 us)
